TPU v7x, 32 devices: a whole 2x2x4 slice. The times are simulated.
32 devices in a mesh: dp: 4 (over x, core), ctx: 4 (over z), tensor: 2 (over y).
Axes of the slice: x: 2, y: 2, z: 4, core: 2. Of those that a mesh axis runs over, the one named last changes fastest.
Arguments:
- hidden_in: bfloat16 [8192, 1536], P(('dp', 'ctx')), may hold values from -6 to 6
- attn_gain: float32 [1536], replicated, may hold values from 0.5 to 1.5
- q_weight: bfloat16 [1536, 1536], P(None, 'tensor'), may hold values from -0.21875 to 0.21875
- key_matrix: bfloat16 [1536, 512], P(None, 'tensor'), may hold values from -0.15625 to 0.15625
- value_matrix: bfloat16 [1536, 512], P(None, 'tensor'), may hold values from -0.15625 to 0.15625
- o_weight: bfloat16 [1536, 1536], P(None, 'tensor'), may hold values from -1.75 to 1.75
- moe_gain: float32 [1536], replicated, may hold values from 0.5 to 1.5
- router_weight: bfloat16 [1536, 24], replicated, may hold values from -0.078125 to 0.078125
- gate_weight: bfloat16 [24, 1536, 512], P(None, None, 'tensor'), may hold values from -0.15625 to 0.15625
- up_weight: bfloat16 [24, 1536, 512], P(None, None, 'tensor'), may hold values from -0.15625 to 0.15625
- down_weight: bfloat16 [24, 1536, 512], P(None, None, 'tensor'), may hold values from -1 to 1
- segments: int32 [8192], P('dp'), may hold values from 0 to 1, as said below
- expert_picks: int32 [8192, 8], P(('dp', 'ctx')), may hold values from 0 to 23, all different within a row; in each aligned block of 512 rows (0 to 511, 512 to 1023, ...) at most 341 rows name the same one
- output_grad: bfloat16 [8192, 1536], P(('dp', 'ctx')), may hold values from -6 to 6
Outputs:
- output: bfloat16 [8192, 1536], P(('dp', 'ctx'))
- input_grad: float32 [8192, 1536], P(('dp', 'ctx'))
- grad_attn_gain: float32 [1536], P(('dp', 'ctx'))
- grad_q: float32 [1536, 1536], P(('dp', 'ctx'), 'tensor')
- grad_k: float32 [1536, 512], P(('dp', 'ctx'), 'tensor')
- grad_v: float32 [1536, 512], P(('dp', 'ctx'), 'tensor')
- grad_o: float32 [1536, 1536], P(('dp', 'ctx'), 'tensor')
- grad_moe_gain: float32 [1536], P(('dp', 'ctx'))
- grad_router: float32 [1536, 24], P(('dp', 'ctx'))
- grad_gate: float32 [24, 1536, 512], P(None, ('dp', 'ctx'), 'tensor')
- grad_up: float32 [24, 1536, 512], P(None, ('dp', 'ctx'), 'tensor')
- grad_down: float32 [24, 1536, 512], P(None, ('dp', 'ctx'), 'tensor')
Inputs may be any that keep to these rules, and one draw needn't show every extreme that they name: `segments`: within each sequence of 2048 tokens documents are runs of one number, 1, 2, 3 and so on from its start; each sequence holds exactly 1 documents of 200 to 2000 tokens each; tokens after the last document hold 0. `expert_picks`: the 8 experts of a row are different. In each aligned block of 512 rows (the rows of one device) no expert is named by more than 341 rows.
All inputs are finite; a program needn't handle non-finite values.
Results may differ from a plain program's by a relative error of at most 0.03.
Values may be sent and summed in bfloat16 or wider, within the bound.
A program may use at most 384 MiB of HBM per device.

v0:
```python
import math

import jax
import jax.numpy as jnp
from jax import lax
from jax.sharding import PartitionSpec as P

HEAD_SIZE = 64
NEXP = 24
CAP = 341


EPSILON = 1e-06
ROPE_BASE = 10000.0
NEGATIVE = -1e30
HIGHEST = lax.Precision.HIGHEST


def normalize(rows, gain):
    scale_inv = lax.rsqrt(jnp.mean(rows * rows, axis=-1, keepdims=True) + EPSILON)
    return (rows * scale_inv * gain, scale_inv)


def norm_backward(rows, scale_inv, gain, grad_normed):
    weighted = gain * grad_normed
    grad_gain = jnp.sum(grad_normed * rows * scale_inv, axis=0)
    inner_mean = jnp.mean(weighted * rows, axis=-1, keepdims=True)
    grad_rows = scale_inv * weighted - rows * scale_inv * scale_inv * scale_inv * inner_mean
    return (grad_rows, grad_gain)


def apply_rotary(value_rows, token_positions, direction):
    half_dim = value_rows.shape[-1] // 2
    frequency = ROPE_BASE ** (-jnp.arange(half_dim, dtype=jnp.float32) / half_dim)
    angles = token_positions.astype(jnp.float32)[:, None] * frequency[None, :]
    cosine = jnp.cos(angles)[:, None, :]
    sine_part = direction * jnp.sin(angles)[:, None, :]
    first_half = value_rows[..., :half_dim]
    second = value_rows[..., half_dim:]
    return jnp.concatenate(
        [first_half * cosine - second * sine_part, second * cosine + first_half * sine_part],
        axis=-1,
    )


def contract_rows(left, right):
    return lax.dot_general(
        left, right, (((0,), (0,)), ((), ())), preferred_element_type=jnp.float32
    )


def contract_rows_exact(left, right):
    return lax.dot_general(
        left, right, (((0,), (0,)), ((), ())), precision=HIGHEST, preferred_element_type=jnp.float32
    )


def contract_cols(left, right):
    return lax.dot_general(
        left, right, (((1,), (1,)), ((), ())), preferred_element_type=jnp.float32
    )


def per_device(
    hidden_in,
    attn_gain,
    q_weight,
    key_matrix,
    value_matrix,
    o_weight,
    moe_gain,
    router_weight,
    gate_weight,
    up_weight,
    down_weight,
    segments,
    expert_picks,
    output_grad,
):
    bf16 = jnp.bfloat16
    f32 = jnp.float32
    token_count = hidden_in.shape[0]
    ctx_index = lax.axis_index("ctx")
    heads_local = q_weight.shape[1] // HEAD_SIZE
    kv_local = key_matrix.shape[1] // HEAD_SIZE
    group_size = heads_local // kv_local
    score_scale = 1.0 / math.sqrt(HEAD_SIZE)
    token_positions = ctx_index * token_count + jnp.arange(token_count, dtype=jnp.int32)
    segment_here = lax.dynamic_slice_in_dim(segments, ctx_index * token_count, token_count)
    inputs_f32 = hidden_in.astype(f32)
    normed_f32, scale_one = normalize(inputs_f32, attn_gain)
    normed_one = normed_f32.astype(bf16)
    query_rows = jnp.dot(normed_one, q_weight, preferred_element_type=f32).reshape(
        token_count, heads_local, HEAD_SIZE
    )
    keys_raw = jnp.dot(normed_one, key_matrix, preferred_element_type=f32).reshape(
        token_count, kv_local, HEAD_SIZE
    )
    values_raw = jnp.dot(normed_one, value_matrix, preferred_element_type=f32)
    query_grouped = (
        apply_rotary(query_rows, token_positions, 1.0)
        .astype(bf16)
        .reshape(token_count, kv_local, group_size, HEAD_SIZE)
    )
    key_flat = (
        apply_rotary(keys_raw, token_positions, 1.0)
        .astype(bf16)
        .reshape(token_count, kv_local * HEAD_SIZE)
    )
    value_flat = values_raw.astype(bf16)

    def piece_mask(piece_rows):
        key_pos = jnp.arange(piece_rows, dtype=jnp.int32)
        return (segment_here[:, None] == segments[None, :]) & (
            key_pos[None, :] <= token_positions[:, None]
        )

    pieces = (
        lax.all_gather(key_flat, "ctx", axis=0, tiled=True),
        lax.all_gather(value_flat, "ctx", axis=0, tiled=True),
    )
    run_max = jnp.full((kv_local, group_size, token_count), NEGATIVE, f32)
    piece_rows = pieces[0].shape[0]
    key_piece = pieces[0].reshape(piece_rows, kv_local, HEAD_SIZE)
    value_piece = pieces[1].reshape(piece_rows, kv_local, HEAD_SIZE)
    allowed = piece_mask(piece_rows)
    scores = (
        jnp.einsum("tkgd,nkd->kgtn", query_grouped, key_piece, preferred_element_type=f32)
        * score_scale
    )
    scores = jnp.where(allowed, scores, NEGATIVE)
    new_max = jnp.maximum(run_max, jnp.max(scores, axis=-1))
    weights = jnp.where(allowed, jnp.exp(scores - new_max[..., None]), 0.0)
    run_sum = jnp.sum(weights, axis=-1)
    accumulated = jnp.einsum(
        "kgtn,nkd->kgtd", weights.astype(bf16), value_piece, preferred_element_type=f32
    )
    fold_state = (new_max, run_sum, accumulated)
    run_max, run_sum, accumulated = fold_state
    attn_grouped = accumulated / run_sum[..., None]
    log_sum = run_max + jnp.log(run_sum)
    attn_bf = (
        jnp.transpose(attn_grouped, (2, 0, 1, 3))
        .reshape(token_count, heads_local * HEAD_SIZE)
        .astype(bf16)
    )
    attn_partial = contract_cols(attn_bf, o_weight)
    mixed_attn = lax.psum(attn_partial.astype(jnp.bfloat16), "tensor").astype(jnp.float32)
    resid = inputs_f32 + mixed_attn
    normed_two_f32, scale_two = normalize(resid, moe_gain)
    normed_two = normed_two_f32.astype(bf16)
    logits = jnp.dot(normed_two, router_weight, preferred_element_type=f32)
    expert_range = jnp.arange(NEXP, dtype=jnp.int32)
    picked_onehot = expert_picks[:, :, None] == expert_range[None, None, :]
    picked = jnp.sum(jnp.where(picked_onehot, logits[:, None, :], 0.0), axis=2)
    gate_probs = jax.nn.softmax(picked, axis=-1)
    uses_expert = jnp.sum(picked_onehot.astype(f32), axis=1)
    token_range = jnp.arange(token_count, dtype=jnp.int32)
    earlier_mask = (token_range[None, :] < token_range[:, None]).astype(bf16)
    earlier_count = jnp.dot(earlier_mask, uses_expert.astype(bf16), preferred_element_type=f32)
    slot_place = jnp.transpose(jnp.where(uses_expert > 0.5, earlier_count, -1.0)).astype(jnp.int32)
    gate_token = jnp.transpose(
        jnp.sum(jnp.where(picked_onehot, gate_probs[:, :, None], 0.0), axis=1)
    )
    slot_range = jnp.arange(CAP, dtype=jnp.int32)
    cot_f32 = output_grad.astype(f32)

    def expert_forward(mixed_rows, inputs):
        gate_mat, up_mat, down_mat, place_row, gate_row = inputs
        selector = slot_range[:, None] == place_row[None, :]
        slot_rows = jnp.dot(selector.astype(bf16), normed_two, preferred_element_type=f32).astype(
            bf16
        )
        gate_act = jnp.dot(slot_rows, gate_mat, preferred_element_type=f32)
        up_act = jnp.dot(slot_rows, up_mat, preferred_element_type=f32)
        hidden = (jax.nn.silu(gate_act) * up_act).astype(bf16)
        expert_out = contract_cols(hidden, down_mat)
        token_out = contract_rows_exact(selector.astype(f32), expert_out)
        gate_part = jnp.sum(token_out * cot_f32, axis=1)
        mixed_rows = mixed_rows + gate_row[:, None] * token_out
        return (mixed_rows, (gate_act, up_act, gate_part))

    mixed_rows, (gate_acts, up_acts, gate_parts) = lax.scan(
        expert_forward,
        jnp.zeros((token_count, normed_two.shape[1]), f32),
        (gate_weight, up_weight, down_weight, slot_place, gate_token),
    )
    moe_total = lax.psum(mixed_rows.astype(jnp.bfloat16), "tensor").astype(jnp.float32)
    output = (resid + moe_total).astype(bf16)

    def expert_backward(grad_rows_all, inputs):
        gate_mat, up_mat, down_mat, place_row, gate_row, gate_act, up_act = inputs
        selector = slot_range[:, None] == place_row[None, :]
        selector_bf = selector.astype(bf16)
        slot_rows = jnp.dot(selector_bf, normed_two, preferred_element_type=f32).astype(bf16)
        sigmoid_act = jax.nn.sigmoid(gate_act)
        silu_act = jax.nn.silu(gate_act)
        hidden = (silu_act * up_act).astype(bf16)
        scaled_cot = (gate_row[:, None] * cot_f32).astype(bf16)
        grad_out = jnp.dot(selector_bf, scaled_cot, preferred_element_type=f32).astype(bf16)
        grad_hidden = jnp.dot(grad_out, down_mat, preferred_element_type=f32)
        grad_down_mat = contract_rows(grad_out, hidden)
        grad_gate_act = (
            grad_hidden * up_act * sigmoid_act * (1.0 + gate_act * (1.0 - sigmoid_act))
        ).astype(bf16)
        grad_up_act = (grad_hidden * silu_act).astype(bf16)
        grad_gate_mat = contract_rows(slot_rows, grad_gate_act)
        grad_up_mat = contract_rows(slot_rows, grad_up_act)
        grad_slot = contract_cols(grad_gate_act, gate_mat) + contract_cols(grad_up_act, up_mat)
        grad_rows_all = grad_rows_all + contract_rows_exact(selector.astype(f32), grad_slot)
        return (grad_rows_all, (grad_gate_mat, grad_up_mat, grad_down_mat))

    grad_rows_all, (grad_gate, grad_up, grad_down) = lax.scan(
        expert_backward,
        jnp.zeros((token_count, normed_two.shape[1]), f32),
        (gate_weight, up_weight, down_weight, slot_place, gate_token, gate_acts, up_acts),
    )
    grad_gate_out, grad_up_out, grad_down_out = (
        lax.psum_scatter(
            grad_gate.astype(jnp.bfloat16), ("dp", "ctx"), scatter_dimension=1, tiled=True
        ).astype(jnp.float32),
        lax.psum_scatter(
            grad_up.astype(jnp.bfloat16), ("dp", "ctx"), scatter_dimension=1, tiled=True
        ).astype(jnp.float32),
        lax.psum_scatter(
            grad_down.astype(jnp.bfloat16), ("dp", "ctx"), scatter_dimension=1, tiled=True
        ).astype(jnp.float32),
    )
    gate_pair = jnp.sum(
        jnp.where(picked_onehot, jnp.transpose(gate_parts)[:, None, :], 0.0), axis=2
    )
    moe_summed, gate_summed = (
        lax.psum(grad_rows_all.astype(jnp.bfloat16), "tensor").astype(jnp.float32),
        lax.psum(gate_pair.astype(jnp.bfloat16), "tensor").astype(jnp.float32),
    )
    grad_picked = gate_probs * (
        gate_summed - jnp.sum(gate_probs * gate_summed, axis=1, keepdims=True)
    )
    grad_logits = jnp.sum(jnp.where(picked_onehot, grad_picked[:, :, None], 0.0), axis=1).astype(
        bf16
    )
    grad_router = contract_rows(normed_two, grad_logits)
    grad_normed_two = moe_summed + contract_cols(grad_logits, router_weight)
    grad_two_rows, grad_moe_gain = norm_backward(resid, scale_two, moe_gain, grad_normed_two)
    grad_resid = cot_f32 + grad_two_rows
    grad_mix = grad_resid.astype(bf16)
    grad_o = contract_rows(grad_mix, attn_bf)
    grad_attn = jnp.dot(grad_mix, o_weight, preferred_element_type=f32).astype(bf16)
    grad_attn_grouped = jnp.transpose(
        grad_attn.reshape(token_count, kv_local, group_size, HEAD_SIZE), (1, 2, 0, 3)
    )
    row_delta = jnp.sum(grad_attn_grouped.astype(f32) * attn_grouped, axis=-1)
    pieces = (
        lax.all_gather(key_flat, "ctx", axis=0, tiled=True),
        lax.all_gather(value_flat, "ctx", axis=0, tiled=True),
    )
    piece_rows = pieces[0].shape[0]
    key_piece = pieces[0].reshape(piece_rows, kv_local, HEAD_SIZE)
    value_piece = pieces[1].reshape(piece_rows, kv_local, HEAD_SIZE)
    allowed = piece_mask(piece_rows)
    scores = (
        jnp.einsum("tkgd,nkd->kgtn", query_grouped, key_piece, preferred_element_type=f32)
        * score_scale
    )
    probability = jnp.where(allowed, jnp.exp(scores - log_sum[..., None]), 0.0)
    grad_probs = jnp.einsum(
        "kgtd,nkd->kgtn", grad_attn_grouped, value_piece, preferred_element_type=f32
    )
    grad_scores = (probability * (grad_probs - row_delta[..., None])).astype(bf16)
    grad_query = score_scale * jnp.einsum(
        "kgtn,nkd->kgtd", grad_scores, key_piece, preferred_element_type=f32
    )
    key_part = score_scale * jnp.einsum(
        "kgtn,tkgd->nkd", grad_scores, query_grouped, preferred_element_type=f32
    )
    value_part = jnp.einsum(
        "kgtn,kgtd->nkd", probability.astype(bf16), grad_attn_grouped, preferred_element_type=f32
    )
    grad_keys_all = key_part.reshape(piece_rows, kv_local * HEAD_SIZE)
    grad_values_all = value_part.reshape(piece_rows, kv_local * HEAD_SIZE)
    back_state = (grad_query, grad_keys_all, grad_values_all)
    grad_query, grad_keys_all, grad_values_all = back_state
    grad_keys_here, grad_values_here = (
        lax.psum_scatter(
            grad_keys_all.astype(jnp.bfloat16), "ctx", scatter_dimension=0, tiled=True
        ).astype(jnp.float32),
        lax.psum_scatter(
            grad_values_all.astype(jnp.bfloat16), "ctx", scatter_dimension=0, tiled=True
        ).astype(jnp.float32),
    )
    grad_query_rows = jnp.transpose(grad_query, (2, 0, 1, 3)).reshape(
        token_count, heads_local, HEAD_SIZE
    )
    grad_query_bf = (
        apply_rotary(grad_query_rows, token_positions, -1.0)
        .reshape(token_count, heads_local * HEAD_SIZE)
        .astype(bf16)
    )
    grad_key_bf = (
        apply_rotary(
            grad_keys_here.reshape(token_count, kv_local, HEAD_SIZE), token_positions, -1.0
        )
        .reshape(token_count, kv_local * HEAD_SIZE)
        .astype(bf16)
    )
    grad_value_bf = grad_values_here.astype(bf16)
    grad_q = contract_rows(normed_one, grad_query_bf)
    grad_k = contract_rows(normed_one, grad_key_bf)
    grad_v = contract_rows(normed_one, grad_value_bf)
    partial_one = (
        contract_cols(grad_query_bf, q_weight)
        + contract_cols(grad_key_bf, key_matrix)
        + contract_cols(grad_value_bf, value_matrix)
    )
    grad_normed_one = lax.psum(partial_one.astype(jnp.bfloat16), "tensor").astype(jnp.float32)
    grad_one_rows, grad_attn_gain = norm_backward(inputs_f32, scale_one, attn_gain, grad_normed_one)
    input_grad = grad_resid + grad_one_rows
    dense_out = (
        lax.psum_scatter(
            grad_attn_gain.astype(jnp.bfloat16), ("dp", "ctx"), scatter_dimension=0, tiled=True
        ).astype(jnp.float32),
        lax.psum_scatter(
            grad_q.astype(jnp.bfloat16), ("dp", "ctx"), scatter_dimension=0, tiled=True
        ).astype(jnp.float32),
        lax.psum_scatter(
            grad_k.astype(jnp.bfloat16), ("dp", "ctx"), scatter_dimension=0, tiled=True
        ).astype(jnp.float32),
        lax.psum_scatter(
            grad_v.astype(jnp.bfloat16), ("dp", "ctx"), scatter_dimension=0, tiled=True
        ).astype(jnp.float32),
        lax.psum_scatter(
            grad_o.astype(jnp.bfloat16), ("dp", "ctx"), scatter_dimension=0, tiled=True
        ).astype(jnp.float32),
        lax.psum_scatter(
            grad_moe_gain.astype(jnp.bfloat16), ("dp", "ctx"), scatter_dimension=0, tiled=True
        ).astype(jnp.float32),
        lax.psum_scatter(
            grad_router.astype(jnp.bfloat16), ("dp", "ctx"), scatter_dimension=0, tiled=True
        ).astype(jnp.float32),
    )
    return (
        output,
        input_grad,
        dense_out[0],
        dense_out[1],
        dense_out[2],
        dense_out[3],
        dense_out[4],
        dense_out[5],
        dense_out[6],
        grad_gate_out,
        grad_up_out,
        grad_down_out,
    )


def solution(mesh):
    return jax.shard_map(
        per_device,
        mesh=mesh,
        in_specs=(
            P(("dp", "ctx"), None),
            P(),
            P(None, "tensor"),
            P(None, "tensor"),
            P(None, "tensor"),
            P(None, "tensor"),
            P(),
            P(),
            P(None, None, "tensor"),
            P(None, None, "tensor"),
            P(None, None, "tensor"),
            P("dp"),
            P(("dp", "ctx"), None),
            P(("dp", "ctx"), None),
        ),
        out_specs=(
            P(("dp", "ctx"), None),
            P(("dp", "ctx"), None),
            P(("dp", "ctx")),
            P(("dp", "ctx"), "tensor"),
            P(("dp", "ctx"), "tensor"),
            P(("dp", "ctx"), "tensor"),
            P(("dp", "ctx"), "tensor"),
            P(("dp", "ctx")),
            P(("dp", "ctx"), None),
            P(None, ("dp", "ctx"), "tensor"),
            P(None, ("dp", "ctx"), "tensor"),
            P(None, ("dp", "ctx"), "tensor"),
        ),
        check_vma=False,
    )
```

profile of v0, /device:TPU:0, one launch (start us, length us, event | category | flops | bytes accessed | tf_op | source)
XLA Modules:
  0.0 2344.5 jit_solution(8626117995089846924)
XLA Ops:
  22.4 21.8 all-gather.3.cloned.1.call-done
  44.2 21.3 fusion.52
  65.6 22.2 fusion.54
  90.0 23.0 fusion.84
  120.4 47.5 %all-reduce.8.cloned.1.call-done = bf16[512,1536]{1,0:T(8,128)(2,1)} async-done(((bf16[512,1536]{1,0:T(8,128)(2,1)}), bf16[512,1536]{1,0:T(8,128)(2,1)}) %all-reduce.8.cloned.1.call-update) | async-done | bytes 1572880 | tf_op jit(solution)/shard_map/psum | solution.py:148
  174.7 416.1 %while.34 = (s32[]{:T(128)}, f32[512,1536]{1,0:T(8,128)}, f32[24,341,256]{2,1,0:T(8,128)}, f32[24,341,256]{2,1,0:T(8,128)}, f32[24,512]{1,0:T(8,128)}, /*index=5...) while((s32[]{:T(128)}, f32[512,1536]{1,0:T(8,128)}, ...), condition=%wide.region_12.13_spmd.clone, body=%wide.region_10.12_spmd.clone.sunk | while | flops 4564274688 | bytes 60574968 | solution.py:183
  590.8 585.0 %while.35 = (s32[]{:T(128)}, f32[512,1536]{1,0:T(8,128)}, bf16[24,1536,256]{2,1,0:T(8,128)(2,1)}, bf16[24,1536,256]{2,1,0:T(8,128)(2,1)}, bf16[24,1536,256]{2,1,...) while((s32[]{:T(128)}, f32[512,1536]{1,0:T(8,128)}, ...), condition=%wide.region_15.16_spmd.clone, body=%wide.region_14.15_spmd.clone.sunk | while | flops 5906712064 | bytes 44313928 | solution.py:213
  1185.1 45.6 %all-reduce.10.cloned.1.call-done = bf16[512,1536]{1,0:T(8,128)(2,1)} async-done(((bf16[512,1536]{1,0:T(8,128)(2,1)}), bf16[512,1536]{1,0:T(8,128)(2,1)}) %all-reduce.10.cloned.1.call-update) | async-done | bytes 1572880 | tf_op jit(solution)/shard_map/psum | solution.py:233
  1244.4 28.0 %multiply_convert_fusion.5 = bf16[4,3,512,2048]{2,3,1,0:T(8,128)(2,1)} fusion(f32[4,2048,512,3]{2,1,3,0:T(8,128)} %get-tuple-element.342, f32[4,3,512]{2,1,0:T(4,128)S(1)} %multiply_reduce_fusion.4, f32[4,3,512]{2,1,0:T(4,128)S(1)} %copy-done.32, pred[512,2048]{0,1:T(8,128)(4,1)S(1)} %copy-done.18, bf16[4,3,512,64]{2,3,1,0:T(8,128)(2,1)} %bitcast.275, ...), kind=kOutput, calls=%fused_computation.77 | convolution fusion | flops 1686110208 | bytes 78430208 | tf_op jit(solution)/shard_map/kgtd,nkd->kgtn/dot_general | solution.py:266
  1272.4 13.4 fusion.80
  1286.1 20.8 fusion.81
  1317.4 24.3 %reduce-scatter.15.cloned.1.call-done = bf16[512,256]{0,1:T(8,128)(2,1)} async-done(((bf16[2048,256]{0,1:T(8,128)(2,1)}), bf16[512,256]{0,1:T(8,128)(2,1)}) %reduce-scatter.15.cloned.1.call-update) | async-done | bytes 262160 | tf_op jit(solution)/shard_map/reduce_scatter | solution.py:287
  1345.0 10.7 convolution_multiply_fusion
  1376.6 23.0 reduce-scatter.31.cloned.1.call-done
  1401.0 58.2 %reduce-scatter.19.cloned.1.call-done = bf16[96,256]{1,0:T(8,128)(2,1)} async-done(((bf16[1536,256]{1,0:T(8,128)(2,1)}), bf16[96,256]{1,0:T(8,128)(2,1)}) %reduce-scatter.19.cloned.1.call-update) | async-done | bytes 49168 | tf_op jit(solution)/shard_map/reduce_scatter | solution.py:325
  1460.6 57.7 %reduce-scatter.21.cloned.1.call-done = bf16[96,256]{1,0:T(8,128)(2,1)} async-done(((bf16[1536,256]{1,0:T(8,128)(2,1)}), bf16[96,256]{1,0:T(8,128)(2,1)}) %reduce-scatter.21.cloned.1.call-update) | async-done | bytes 49168 | tf_op jit(solution)/shard_map/reduce_scatter | solution.py:328
  1519.8 65.3 %reduce-scatter.17.cloned.1.call-done = bf16[96,768]{1,0:T(8,128)(2,1)} async-done(((bf16[1536,768]{1,0:T(8,128)(2,1)}), bf16[96,768]{1,0:T(8,128)(2,1)}) %reduce-scatter.17.cloned.1.call-update) | async-done | bytes 147472 | tf_op jit(solution)/shard_map/reduce_scatter | solution.py:322
  1586.7 64.7 %reduce-scatter.23.cloned.1.call-done = bf16[96,768]{1,0:T(8,128)(2,1)} async-done(((bf16[1536,768]{1,0:T(8,128)(2,1)}), bf16[96,768]{1,0:T(8,128)(2,1)}) %reduce-scatter.23.cloned.1.call-update) | async-done | bytes 147472 | tf_op jit(solution)/shard_map/reduce_scatter | solution.py:331
  1653.1 86.9 %all-reduce.12.cloned.1.call-done = (bf16[512,1536]{1,0:T(8,128)(2,1)}, bf16[512,1536]{1,0:T(8,128)(2,1)}) async-done(((bf16[512,1536]{1,0:T(8,128)(2,1)}, bf16[512,1536]{1,0:T(8,128)(2,1)}), (bf16[512,1536]{1,0:T(8,128)(2,1)}, bf16[512,1536]{1,0:T(8,128)(2,1)})) %all-reduce.12.cloned.1.call-update) | async-done | bytes 3145744 | tf_op jit(solution)/shard_map/psum | solution.py:188
  1743.0 34.0 %all-reduce.2 = (bf16[1536]{0:T(1024)(128)(2,1)S(1)}, bf16[1536]{0:T(1024)(128)(2,1)S(1)}) all-reduce(bf16[1536]{0:T(1024)(128)(2,1)S(1)} %get-tuple-element.260, bf16[1536]{0:T(1024)(128)(2,1)S(1)} %get-tuple-element.258), channel_id=4, replica_groups=mesh['dp'=4,'ctx'=4,'tensor'=2] {'dp','ctx'}, use_global_device_ids=true, to_apply=%region_28.29.clone | all-reduce | flops 3072 | bytes 12288
  1777.6 7.5 fusion.70
  1785.1 153.7 %reduce-scatter.25.cloned.1.call-done = bf16[24,96,256]{2,1,0:T(8,128)(2,1)} async-done(((bf16[24,1536,256]{2,1,0:T(8,128)(2,1)}), bf16[24,96,256]{2,1,0:T(8,128)(2,1)}) %reduce-scatter.25.cloned.1.call-update) | async-done | bytes 1179664 | tf_op jit(solution)/shard_map/reduce_scatter | solution.py:219
  1941.8 194.9 %reduce-scatter.27.cloned.1.call-done = bf16[24,96,256]{2,1,0:T(8,128)(2,1)} async-done(((bf16[24,1536,256]{2,1,0:T(8,128)(2,1)}), bf16[24,96,256]{2,1,0:T(8,128)(2,1)}) %reduce-scatter.27.cloned.1.call-update) | async-done | bytes 1179664 | tf_op jit(solution)/shard_map/reduce_scatter | solution.py:222
  2139.6 195.1 %reduce-scatter.29.cloned.1.call-done = bf16[24,96,256]{2,1,0:T(8,128)(2,1)} async-done(((bf16[24,1536,256]{2,1,0:T(8,128)(2,1)}), bf16[24,96,256]{2,1,0:T(8,128)(2,1)}) %reduce-scatter.29.cloned.1.call-update) | async-done | bytes 1179664 | tf_op jit(solution)/shard_map/reduce_scatter | solution.py:225
  (1011 shorter events, 1106.6 us)
Async XLA Ops:
  7.2 105.8 %copy-start = (bf16[1536,768]{1,0:T(8,128)(2,1)S(1)}, bf16[1536,768]{1,0:T(8,128)(2,1)}, u32[]{:S(2)}) copy-start(bf16[1536,768]{1,0:T(8,128)(2,1)} %param.23) | copy-start | bytes 7077892
  7.2 37.1 %all-gather.3.cloned.1.call-start = ((), (), s32[]{:S(2)}) async-start(), calls=%async_computation.10 | async-start | bytes 1310720 | tf_op jit(solution)/shard_map/all_gather | solution.py:119
  10.2 9.8 copy-start.19
  13.5 74.3 %all-gather.5.cloned.1.call-start = ((), (), s32[]{:S(2)}) async-start(), calls=%async_computation.11 | async-start | bytes 1310720 | tf_op jit(solution)/shard_map/all_gather | solution.py:120
  16.3 151.6 %all-reduce.8.cloned.1.call-start = ((), (), s32[]{:S(2)}) async-start(), calls=%async_computation.12 | async-start | bytes 3145728 | tf_op jit(solution)/shard_map/psum | solution.py:148
  22.4 67.6 %copy-start.17 = (pred[512,2048]{0,1:T(8,128)(4,1)}, pred[512,2048]{0,1:T(8,128)(4,1)S(1)}, u32[]{:S(2)}) copy-start(pred[512,2048]{0,1:T(8,128)(4,1)S(1)} %fusion.62) | copy-start | bytes 3145732
  116.8 1114.0 %all-reduce.10.cloned.1.call-start = ((), (), s32[]{:S(2)}) async-start(), calls=%async_computation.13 | async-start | bytes 3145728 | tf_op jit(solution)/shard_map/psum | solution.py:233
  116.9 53.7 %copy-start.33 = (f32[1536]{0:T(1024)S(1)}, f32[1536]{0:T(1024)}, u32[]{:S(2)}) copy-start(f32[1536]{0:T(1024)} %param.24) | copy-start | bytes 18436
  1175.8 54.9 %copy-start.28 = (bf16[1536,24]{0,1:T(8,128)(2,1)S(1)}, bf16[1536,24]{0,1:T(8,128)(2,1)}, u32[]{:S(2)}) copy-start(bf16[1536,24]{0,1:T(8,128)(2,1)} %param.25) | copy-start | bytes 221188
  1179.1 134.1 %reduce-scatter.13.cloned.1.call-start = ((), (), s32[]{:S(2)}) async-start(), calls=%async_computation.14 | async-start | bytes 1310720 | tf_op jit(solution)/shard_map/reduce_scatter | solution.py:284
  1285.8 56.0 %reduce-scatter.15.cloned.1.call-start = ((), (), s32[]{:S(2)}) async-start(), calls=%async_computation.15 | async-start | bytes 1310720 | tf_op jit(solution)/shard_map/reduce_scatter | solution.py:287
  1306.9 7.3 copy-start.20
  1306.9 7.3 copy-start.24
  1306.9 7.4 copy-start.31
  1306.9 7.4 copy-start.35
  1306.9 92.7 %reduce-scatter.31.cloned.1.call-start = ((), (), s32[]{:S(2)}) async-start(), calls=%async_computation.23 | async-start | bytes 417792
  1309.7 149.5 %reduce-scatter.19.cloned.1.call-start = ((), (), s32[]{:S(2)}) async-start(), calls=%async_computation.17 | async-start | bytes 835584 | tf_op jit(solution)/shard_map/reduce_scatter | solution.py:325
  1317.4 200.9 %reduce-scatter.21.cloned.1.call-start = ((), (), s32[]{:S(2)}) async-start(), calls=%async_computation.18 | async-start | bytes 835584 | tf_op jit(solution)/shard_map/reduce_scatter | solution.py:328
  1344.9 240.1 %reduce-scatter.17.cloned.1.call-start = ((), (), s32[]{:S(2)}) async-start(), calls=%async_computation.16 | async-start | bytes 2506752 | tf_op jit(solution)/shard_map/reduce_scatter | solution.py:322
  1360.2 291.2 %reduce-scatter.23.cloned.1.call-start = ((), (), s32[]{:S(2)}) async-start(), calls=%async_computation.19 | async-start | bytes 2506752 | tf_op jit(solution)/shard_map/reduce_scatter | solution.py:331
  1365.2 374.7 %all-reduce.12.cloned.1.call-start = ((), (), s32[]{:S(2)}) async-start(), calls=%async_computation.24 | async-start | bytes 6291456 | tf_op jit(solution)/shard_map/psum | solution.py:188
  1373.3 565.5 %reduce-scatter.25.cloned.1.call-start = ((), (), s32[]{:S(2)}) async-start(), calls=%async_computation.20 | async-start | bytes 20054016 | tf_op jit(solution)/shard_map/reduce_scatter | solution.py:219
  1374.1 762.6 %reduce-scatter.27.cloned.1.call-start = ((), (), s32[]{:S(2)}) async-start(), calls=%async_computation.21 | async-start | bytes 20054016 | tf_op jit(solution)/shard_map/reduce_scatter | solution.py:222
  1374.7 960.0 %reduce-scatter.29.cloned.1.call-start = ((), (), s32[]{:S(2)}) async-start(), calls=%async_computation.22 | async-start | bytes 20054016 | tf_op jit(solution)/shard_map/reduce_scatter | solution.py:225
  (214 other events, 743.0 us)
Sparse Core Ops, SparseCore 0:
  13.6 30.6 all-gather.2
  46.4 27.4 all-gather.4
  116.9 51.0 all-reduce.7
  1179.2 51.4 all-reduce.9
  1285.9 27.1 reduce-scatter.12
  1315.9 25.7 reduce-scatter.14
  1345.3 54.2 reduce-scatter.30
  1403.6 55.5 reduce-scatter.18
  1462.7 55.5 reduce-scatter.20
  1523.0 62.0 reduce-scatter.16
  1589.4 61.9 reduce-scatter.22
  1654.9 84.9 all-reduce.11
  1744.0 194.7 reduce-scatter.24
  1942.8 193.8 reduce-scatter.26
  2140.6 194.0 reduce-scatter.28
where the time goes:
time: 2360 us; the launch traced here: 2340 us
  waiting for transfers between devices  1040 us (44%)
  matrix products  993 us (42%)
  local copies, waits for them, and re-layouts  174 us (7%)
  other arithmetic  74.6 us (3%)
  blocking collectives  39.2 us (2%)
    dot_general x48, matrix products, contract_rows_exact(): lax.dot_general(left, right, (((0,), (0,)), ((), ())), precision=HIGHEST,...  258 us
    reduce_scatter x1, waiting for transfers between devices, per_device(): lax.psum_scatter(grad_down.astype(jnp.bfloat16), ('dp', 'ctx'), scatter_d...  195 us
    reduce_scatter x1, waiting for transfers between devices, per_device(): lax.psum_scatter(grad_up.astype(jnp.bfloat16), ('dp', 'ctx'), scatter_dim...  195 us
    dot_general x77, matrix products, contract_cols(): lax.dot_general(left, right, (((1,), (1,)), ((), ())), preferred_element_...  159 us
    reduce_scatter x1, waiting for transfers between devices, per_device(): lax.psum_scatter(grad_gate.astype(jnp.bfloat16), ('dp', 'ctx'), scatter_d...  154 us
    dot_general x77, matrix products, contract_rows(): lax.dot_general(left, right, (((0,), (0,)), ((), ())), preferred_element_...  153 us
    psum x1, waiting for transfers between devices, per_device(): lax.psum(mixed_rows.astype(jnp.bfloat16), 'tensor').astype(jnp.float32)  86.9 us
    dynamic_slice x96, local copies, waits for them, and re-layouts, per_device(): lax.scan(expert_forward, jnp.zeros((token_count, normed_two.shape[1]), f3...  69.3 us
  transfers between devices with their start and end apart: 15, of which 14 were waited for; matrix products, arithmetic and copies ran while one was open for 6% of the time, Pallas kernels for 0%

commit v1 on v0

--- a/solution.py
+++ b/solution.py
@@ -3,6 +3,8 @@
 import jax
 import jax.numpy as jnp
 from jax import lax
+from jax.experimental import pallas as pl
+from jax.experimental.pallas import tpu as pltpu
 from jax.sharding import PartitionSpec as P
 
 HEAD_SIZE = 64
@@ -59,6 +61,95 @@
     return lax.dot_general(
         left, right, (((1,), (1,)), ((), ())), preferred_element_type=jnp.float32
     )
+
+
+def _expert_body(
+    n2_ref, n2t_ref, dy_ref, dyt_ref, gcol_ref, grow_ref, wg_ref, wu_ref, wd_ref,
+    acc_ref, dgate_ref, gg_ref, gu_ref, gd_ref, dn2_ref,
+):
+    f32 = jnp.float32
+    bf16 = jnp.bfloat16
+    nt = (((1,), (1,)), ((), ()))
+
+    @pl.when(pl.program_id(0) == 0)
+    def _():
+        acc_ref[...] = jnp.zeros_like(acc_ref)
+        dn2_ref[...] = jnp.zeros_like(dn2_ref)
+
+    n2 = n2_ref[...]
+    wg = wg_ref[0]
+    wu = wu_ref[0]
+    wd = wd_ref[0]
+    gate_act = jnp.dot(n2, wg, preferred_element_type=f32)
+    up_act = jnp.dot(n2, wu, preferred_element_type=f32)
+    sig = 1.0 / (1.0 + jnp.exp(-gate_act))
+    silu = gate_act * sig
+    hidden = (silu * up_act).astype(bf16)
+    expert_out = lax.dot_general(hidden, wd, nt, preferred_element_type=f32)
+    gc = gcol_ref[0]
+    acc_ref[...] += gc * expert_out
+    dy = dy_ref[...].astype(f32)
+    dgate_ref[0] = jnp.sum(expert_out * dy, axis=1, keepdims=True)
+    deo = (gc * dy).astype(bf16)
+    grad_hidden = jnp.dot(deo, wd, preferred_element_type=f32)
+    deo_t = (grow_ref[0] * dyt_ref[...].astype(f32)).astype(bf16)
+    gd_ref[0] = jnp.dot(deo_t, hidden, preferred_element_type=f32)
+    grad_gate_act = (grad_hidden * up_act * sig * (1.0 + gate_act * (1.0 - sig))).astype(bf16)
+    grad_up_act = (grad_hidden * silu).astype(bf16)
+    n2t = n2t_ref[...]
+    gg_ref[0] = jnp.dot(n2t, grad_gate_act, preferred_element_type=f32)
+    gu_ref[0] = jnp.dot(n2t, grad_up_act, preferred_element_type=f32)
+    dn2_ref[...] += lax.dot_general(
+        grad_gate_act, wg, nt, preferred_element_type=f32
+    ) + lax.dot_general(grad_up_act, wu, nt, preferred_element_type=f32)
+
+
+def expert_kernel(n2, n2t, dy, dyt, gcol, grow, wg, wu, wd):
+    tokens, width = n2.shape
+    experts, _, hidden = wg.shape
+    f32 = jnp.float32
+    whole = lambda shape: pl.BlockSpec(shape, lambda e: (0,) * len(shape))
+    per_expert = lambda shape: pl.BlockSpec((1,) + shape, lambda e: (e,) + (0,) * len(shape))
+    flops = experts * tokens * width * hidden * 2 * 9
+    return pl.pallas_call(
+        _expert_body,
+        grid=(experts,),
+        in_specs=[
+            whole((tokens, width)),
+            whole((width, tokens)),
+            whole((tokens, width)),
+            whole((width, tokens)),
+            per_expert((tokens, 1)),
+            per_expert((1, tokens)),
+            per_expert((width, hidden)),
+            per_expert((width, hidden)),
+            per_expert((width, hidden)),
+        ],
+        out_specs=[
+            whole((tokens, width)),
+            per_expert((tokens, 1)),
+            per_expert((width, hidden)),
+            per_expert((width, hidden)),
+            per_expert((width, hidden)),
+            whole((tokens, width)),
+        ],
+        out_shape=[
+            jax.ShapeDtypeStruct((tokens, width), f32),
+            jax.ShapeDtypeStruct((experts, tokens, 1), f32),
+            jax.ShapeDtypeStruct((experts, width, hidden), f32),
+            jax.ShapeDtypeStruct((experts, width, hidden), f32),
+            jax.ShapeDtypeStruct((experts, width, hidden), f32),
+            jax.ShapeDtypeStruct((tokens, width), f32),
+        ],
+        compiler_params=pltpu.CompilerParams(
+            dimension_semantics=("arbitrary",), vmem_limit_bytes=64 * 1024 * 1024
+        ),
+        cost_estimate=pl.CostEstimate(
+            flops=flops,
+            transcendentals=experts * tokens * hidden,
+            bytes_accessed=experts * width * hidden * (3 * 2 + 3 * 4) + tokens * width * 16,
+        ),
+    )(n2, n2t, dy, dyt, gcol, grow, wg, wu, wd)
 
 
 def per_device(
@@ -154,67 +245,25 @@
     picked_onehot = expert_picks[:, :, None] == expert_range[None, None, :]
     picked = jnp.sum(jnp.where(picked_onehot, logits[:, None, :], 0.0), axis=2)
     gate_probs = jax.nn.softmax(picked, axis=-1)
-    uses_expert = jnp.sum(picked_onehot.astype(f32), axis=1)
-    token_range = jnp.arange(token_count, dtype=jnp.int32)
-    earlier_mask = (token_range[None, :] < token_range[:, None]).astype(bf16)
-    earlier_count = jnp.dot(earlier_mask, uses_expert.astype(bf16), preferred_element_type=f32)
-    slot_place = jnp.transpose(jnp.where(uses_expert > 0.5, earlier_count, -1.0)).astype(jnp.int32)
-    gate_token = jnp.transpose(
-        jnp.sum(jnp.where(picked_onehot, gate_probs[:, :, None], 0.0), axis=1)
-    )
-    slot_range = jnp.arange(CAP, dtype=jnp.int32)
+    gates_dense = jnp.sum(jnp.where(picked_onehot, gate_probs[:, :, None], 0.0), axis=1)
+    gates_by_expert = jnp.transpose(gates_dense)
+    cot_bf = output_grad
+    moe_acc, gate_parts, grad_gate, grad_up, grad_down, moe_grad_rows = expert_kernel(
+        normed_two,
+        jnp.transpose(normed_two),
+        cot_bf,
+        jnp.transpose(cot_bf),
+        gates_by_expert[:, :, None],
+        gates_by_expert[:, None, :],
+        gate_weight,
+        up_weight,
+        down_weight,
+    )
     cot_f32 = output_grad.astype(f32)
-
-    def expert_forward(mixed_rows, inputs):
-        gate_mat, up_mat, down_mat, place_row, gate_row = inputs
-        selector = slot_range[:, None] == place_row[None, :]
-        slot_rows = jnp.dot(selector.astype(bf16), normed_two, preferred_element_type=f32).astype(
-            bf16
-        )
-        gate_act = jnp.dot(slot_rows, gate_mat, preferred_element_type=f32)
-        up_act = jnp.dot(slot_rows, up_mat, preferred_element_type=f32)
-        hidden = (jax.nn.silu(gate_act) * up_act).astype(bf16)
-        expert_out = contract_cols(hidden, down_mat)
-        token_out = contract_rows_exact(selector.astype(f32), expert_out)
-        gate_part = jnp.sum(token_out * cot_f32, axis=1)
-        mixed_rows = mixed_rows + gate_row[:, None] * token_out
-        return (mixed_rows, (gate_act, up_act, gate_part))
-
-    mixed_rows, (gate_acts, up_acts, gate_parts) = lax.scan(
-        expert_forward,
-        jnp.zeros((token_count, normed_two.shape[1]), f32),
-        (gate_weight, up_weight, down_weight, slot_place, gate_token),
-    )
-    moe_total = lax.psum(mixed_rows.astype(jnp.bfloat16), "tensor").astype(jnp.float32)
+    moe_total = lax.psum(moe_acc.astype(jnp.bfloat16), "tensor").astype(jnp.float32)
     output = (resid + moe_total).astype(bf16)
-
-    def expert_backward(grad_rows_all, inputs):
-        gate_mat, up_mat, down_mat, place_row, gate_row, gate_act, up_act = inputs
-        selector = slot_range[:, None] == place_row[None, :]
-        selector_bf = selector.astype(bf16)
-        slot_rows = jnp.dot(selector_bf, normed_two, preferred_element_type=f32).astype(bf16)
-        sigmoid_act = jax.nn.sigmoid(gate_act)
-        silu_act = jax.nn.silu(gate_act)
-        hidden = (silu_act * up_act).astype(bf16)
-        scaled_cot = (gate_row[:, None] * cot_f32).astype(bf16)
-        grad_out = jnp.dot(selector_bf, scaled_cot, preferred_element_type=f32).astype(bf16)
-        grad_hidden = jnp.dot(grad_out, down_mat, preferred_element_type=f32)
-        grad_down_mat = contract_rows(grad_out, hidden)
-        grad_gate_act = (
-            grad_hidden * up_act * sigmoid_act * (1.0 + gate_act * (1.0 - sigmoid_act))
-        ).astype(bf16)
-        grad_up_act = (grad_hidden * silu_act).astype(bf16)
-        grad_gate_mat = contract_rows(slot_rows, grad_gate_act)
-        grad_up_mat = contract_rows(slot_rows, grad_up_act)
-        grad_slot = contract_cols(grad_gate_act, gate_mat) + contract_cols(grad_up_act, up_mat)
-        grad_rows_all = grad_rows_all + contract_rows_exact(selector.astype(f32), grad_slot)
-        return (grad_rows_all, (grad_gate_mat, grad_up_mat, grad_down_mat))
-
-    grad_rows_all, (grad_gate, grad_up, grad_down) = lax.scan(
-        expert_backward,
-        jnp.zeros((token_count, normed_two.shape[1]), f32),
-        (gate_weight, up_weight, down_weight, slot_place, gate_token, gate_acts, up_acts),
-    )
+    grad_rows_all = moe_grad_rows
+    gate_parts = gate_parts[:, :, 0]
     grad_gate_out, grad_up_out, grad_down_out = (
         lax.psum_scatter(
             grad_gate.astype(jnp.bfloat16), ("dp", "ctx"), scatter_dimension=1, tiled=True

time: 2360 us -> 1460 us (0.62)
  matrix products: 993 us -> 150 us
  local copies, waits for them, and re-layouts: 174 us -> 32.3 us
  Pallas kernels: 0 us -> 113 us
  waiting for transfers between devices: 1040 us -> 982 us
  other arithmetic: 74.6 us -> 124 us
    dot_general x193 -> x0, matrix products: 552 us -> none  [the longest x48 258 us: contract_rows_exact(): lax.dot_general(left, right, (((0,), (0,)), ((), ())), precision=HIGHEST,...]
    dot_general x77 -> x5, matrix products: 159 us -> 13.5 us  [contract_cols(): lax.dot_general(left, right, (((1,), (1,)), ((), ())), preferred_element_...]
    dot_general x77 -> x5, matrix products: 153 us -> 12.1 us  [contract_rows(): lax.dot_general(left, right, (((0,), (0,)), ((), ())), preferred_element_...]
    pallas_call x0 -> x1, Pallas kernels: none -> 113 us  [expert_kernel(): pl.pallas_call(_expert_body, grid=(experts,), in_specs=[whole((tokens, wi...]
    dynamic_slice x96 -> x0, local copies, waits for them, and re-layouts: 69.3 us -> none  [per_device(): lax.scan(expert_forward, jnp.zeros((token_count, normed_two.shape[1]), f3...]
    while x384 -> x0, local copies, waits for them, and re-layouts: 60.6 us -> none
    convert_element_type x3, other arithmetic: 10.1 us -> 61.6 us  [the longest x1 20.6 us: per_device(): grad_up.astype(jnp.bfloat16)]
    reduce_scatter x1, waiting for transfers between devices: 58.2 us -> 21.4 us  [per_device(): lax.psum_scatter(grad_k.astype(jnp.bfloat16), ('dp', 'ctx'), scatter_dime...]
  transfers between devices with their start and end apart: 15 -> 15, of which waited for: 14 -> 13; matrix products, arithmetic and copies ran while one was open for 6% -> 14% of each run, Pallas kernels for 0% -> 0%
where the time goes in v1:
time: 1460 us
  waiting for transfers between devices  982 us (67%)
  matrix products  150 us (10%)
  other arithmetic  124 us (8%)
  Pallas kernels  113 us (8%)
  blocking collectives  39.5 us (3%)
  local copies, waits for them, and re-layouts  32.3 us (2%)
  between operations  15.7 us (1%)
    reduce_scatter x1, waiting for transfers between devices, per_device(): lax.psum_scatter(grad_down.astype(jnp.bfloat16), ('dp', 'ctx'), scatter_d...  195 us
    reduce_scatter x1, waiting for transfers between devices, per_device(): lax.psum_scatter(grad_up.astype(jnp.bfloat16), ('dp', 'ctx'), scatter_dim...  195 us
    reduce_scatter x1, waiting for transfers between devices, per_device(): lax.psum_scatter(grad_gate.astype(jnp.bfloat16), ('dp', 'ctx'), scatter_d...  151 us
    pallas_call x1, Pallas kernels, expert_kernel(): pl.pallas_call(_expert_body, grid=(experts,), in_specs=[whole((tokens, wi...  113 us
    psum x1, waiting for transfers between devices, per_device(): lax.psum(moe_acc.astype(jnp.bfloat16), 'tensor').astype(jnp.float32)  86.8 us
    reduce_scatter x1, waiting for transfers between devices, per_device(): lax.psum_scatter(grad_o.astype(jnp.bfloat16), ('dp', 'ctx'), scatter_dime...  65.3 us
    reduce_scatter x1, waiting for transfers between devices, per_device(): lax.psum_scatter(grad_q.astype(jnp.bfloat16), ('dp', 'ctx'), scatter_dime...  64.7 us
    reduce_scatter x1, waiting for transfers between devices, per_device(): lax.psum_scatter(grad_v.astype(jnp.bfloat16), ('dp', 'ctx'), scatter_dime...  57.6 us
  transfers between devices with their start and end apart: 15, of which 13 were waited for; matrix products, arithmetic and copies ran while one was open for 14% of the time, Pallas kernels for 0%

profile of v1, /device:TPU:0, one launch (start us, length us, event | category | flops | bytes accessed | tf_op | source)
XLA Modules:
  0.0 1456.6 jit_solution(4963956465390512012)
XLA Ops:
  18.8 24.1 %all-gather.3.cloned.1.call-done = bf16[2048,256]{0,1:T(8,128)(2,1)} async-done(((bf16[512,256]{0,1:T(8,128)(2,1)}), bf16[2048,256]{0,1:T(8,128)(2,1)}) %all-gather.3.cloned.1.call-update) | async-done | bytes 1048592 | tf_op jit(solution)/shard_map/all_gather | solution.py:210
  42.9 20.2 %fusion.2 = (f32[4,3,512]{2,1,0:T(4,128)S(1)}, f32[4,2048,512,3]{2,1,3,0:T(8,128)}) fusion(pred[512,2048]{0,1:T(8,128)(4,1)S(1)} %fusion.12, bf16[2048,4,64,1]{0,2,3,1:T(8,128)(2,1)} %bitcast.132, bf16[512,4,3,32]{0,3,2,1:T(8,128)(2,1)S(1)} %bitcast.124, bf16[512,4,3,32]{0,3,2,1:T(8,128)(2,1)S(1)} %bitcast.122), kind=kOutput, calls=%fused_computation.6 | convolution fusion | flops 1649928192 | bytes 53239808 | tf_op jit(solution)/shard_map/tkgd,nkd->kgtn/dot_general | solution.py:219
  63.1 22.1 %fusion.4 = f32[4,3,512]{2,1,0:T(4,128)S(1)} fusion(f32[4,2048,512,3]{2,1,3,0:T(8,128)} %get-tuple-element.94, f32[4,3,512]{2,1,0:T(4,128)S(1)} %broadcast_maximum_fusion, pred[512,2048]{0,1:T(8,128)(4,1)S(1)} %fusion.12), kind=kLoop, calls=%fused_computation.8 | loop fusion | flops 62908416 | bytes 51429376 | tf_op jit(solution)/shard_map/reduce_sum | solution.py:225
  87.6 22.8 %fusion.34 = (bf16[512,4,3,64]{0,3,2,1:T(8,128)(2,1)}, f32[4,3,512,64]{2,3,1,0:T(8,128)}) fusion(f32[512,4,3]{0,2,1:T(4,128)S(1)} %bitcast.139, bf16[2048,4,64,1]{0,2,3,1:T(8,128)(2,1)} %bitcast.128, f32[4,2048,512,3]{2,1,3,0:T(8,128)} %get-tuple-element.94, f32[4,3,512]{2,1,0:T(4,128)S(1)} %broadcast_maximum_fusion, pred[512,2048]{0,1:T(8,128)(4,1)S(1)} %fusion.12), kind=kOutput, calls=%fused_computation.56 | convolution fusion | flops 1674313728 | bytes 54837248 | tf_op jit(solution)/shard_map/kgtn,nkd->kgtd/dot_general | solution.py:226
  117.1 48.9 %all-reduce.8.cloned.1.call-done = bf16[512,1536]{0,1:T(8,128)(2,1)} async-done(((bf16[512,1536]{0,1:T(8,128)(2,1)}), bf16[512,1536]{0,1:T(8,128)(2,1)}) %all-reduce.8.cloned.1.call-update) | async-done | bytes 1572880 | tf_op jit(solution)/shard_map/psum | solution.py:239
  177.4 113.0 %shard_map.229 = (f32[512,1536]{1,0:T(8,128)}, f32[24,512,1]{2,1,0:T(8,128)}, f32[24,1536,256]{2,1,0:T(8,128)}, f32[24,1536,256]{2,1,0:T(8,128)}, f32[24,1536,256]{2,1,0:T(8,128)}, /*index=5*/f32[512,1536]{1,0:T(8,128)}) custom-call(bf16[512,1536]{1,0:T(8,128)(2,1)} %copy.114.n2_ref, bf16[1536,512]{1,0:T(8,128)(2,1)} %bitcast.114, bf16[512,1536]{1,0:T(8,128)(2,1)} %dy_ref.1, ...), custom_call_target="tpu_custom_call" | custom-call | flops 86973087744 | bytes 182452224 | tf_op jit(solution)/shard_map/pallas_call | solution.py:114
  303.9 41.5 %all-reduce.10.cloned.1.call-done = bf16[512,1536]{0,1:T(8,128)(2,1)} async-done(((bf16[512,1536]{0,1:T(8,128)(2,1)}), bf16[512,1536]{0,1:T(8,128)(2,1)}) %all-reduce.10.cloned.1.call-update) | async-done | bytes 1572880 | tf_op jit(solution)/shard_map/psum | solution.py:282
  356.4 28.1 %multiply_convert_fusion = bf16[4,3,512,2048]{2,3,1,0:T(8,128)(2,1)} fusion(f32[4,2048,512,3]{2,1,3,0:T(8,128)} %get-tuple-element.94, f32[4,3,512]{2,1,0:T(4,128)S(1)} %multiply_reduce_fusion.3, f32[4,3,512]{2,1,0:T(4,128)S(1)} %log_add_fusion, pred[512,2048]{0,1:T(8,128)(4,1)S(1)} %copy-done.12, bf16[4,3,512,64]{2,3,1,0:T(8,128)(2,1)} %bitcast.119, ...), kind=kOutput, calls=%fused_computation.4 | convolution fusion | flops 1686110208 | bytes 78430208 | tf_op jit(solution)/shard_map/kgtd,nkd->kgtn/dot_general | solution.py:315
  384.5 13.4 fusion.30
  398.2 21.2 %fusion.31 = bf16[4,64,2048]{2,1,0:T(8,128)(2,1)} fusion(bf16[4,3,512,64]{2,3,1,0:T(8,128)(2,1)} %bitcast.120, f32[4,2048,512,3]{2,1,3,0:T(8,128)} %get-tuple-element.94, f32[4,3,512]{2,1,0:T(4,128)S(1)} %log_add_fusion, pred[512,2048]{0,1:T(8,128)(4,1)} %copy-done.11), kind=kOutput, calls=%fused_computation.51 | convolution fusion | flops 1661468672 | bytes 53239808 | tf_op jit(solution)/shard_map/kgtn,kgtd->nkd/dot_general | solution.py:325
  428.1 25.9 %reduce-scatter.15.cloned.1.call-done = bf16[512,256]{0,1:T(8,128)(2,1)} async-done(((bf16[2048,256]{0,1:T(8,128)(2,1)}), bf16[512,256]{0,1:T(8,128)(2,1)}) %reduce-scatter.15.cloned.1.call-update) | async-done | bytes 262160 | tf_op jit(solution)/shard_map/reduce_scatter | solution.py:336
  461.4 10.8 convolution_multiply_fusion
  484.9 20.5 %convert_element_type.230 = bf16[24,1536,256]{2,1,0:T(8,128)(2,1)} convert(f32[24,1536,256]{2,1,0:T(8,128)} %get-tuple-element.21) | non-fusion elementwise | flops 9437184 | bytes 56623104 | tf_op jit(solution)/shard_map/convert_element_type | solution.py:269
  505.4 20.6 %convert_element_type.232 = bf16[24,1536,256]{2,1,0:T(8,128)(2,1)} convert(f32[24,1536,256]{2,1,0:T(8,128)} %get-tuple-element.22) | non-fusion elementwise | flops 9437184 | bytes 56623104 | tf_op jit(solution)/shard_map/convert_element_type | solution.py:272
  526.1 20.5 %convert_element_type.234 = bf16[24,1536,256]{2,1,0:T(8,128)(2,1)} convert(f32[24,1536,256]{2,1,0:T(8,128)} %get-tuple-element.23) | non-fusion elementwise | flops 9437184 | bytes 56623104 | tf_op jit(solution)/shard_map/convert_element_type | solution.py:275
  550.0 21.4 %reduce-scatter.19.cloned.1.call-done = bf16[96,256]{1,0:T(8,128)(2,1)} async-done(((bf16[1536,256]{1,0:T(8,128)(2,1)}), bf16[96,256]{1,0:T(8,128)(2,1)}) %reduce-scatter.19.cloned.1.call-update) | async-done | bytes 49168 | tf_op jit(solution)/shard_map/reduce_scatter | solution.py:374
  572.8 57.6 %reduce-scatter.21.cloned.1.call-done = bf16[96,256]{1,0:T(8,128)(2,1)} async-done(((bf16[1536,256]{1,0:T(8,128)(2,1)}), bf16[96,256]{1,0:T(8,128)(2,1)}) %reduce-scatter.21.cloned.1.call-update) | async-done | bytes 49168 | tf_op jit(solution)/shard_map/reduce_scatter | solution.py:377
  631.9 65.3 %reduce-scatter.23.cloned.1.call-done = bf16[96,768]{1,0:T(8,128)(2,1)} async-done(((bf16[1536,768]{1,0:T(8,128)(2,1)}), bf16[96,768]{1,0:T(8,128)(2,1)}) %reduce-scatter.23.cloned.1.call-update) | async-done | bytes 147472 | tf_op jit(solution)/shard_map/reduce_scatter | solution.py:380
  698.8 64.7 %reduce-scatter.17.cloned.1.call-done = bf16[96,768]{1,0:T(8,128)(2,1)} async-done(((bf16[1536,768]{1,0:T(8,128)(2,1)}), bf16[96,768]{1,0:T(8,128)(2,1)}) %reduce-scatter.17.cloned.1.call-update) | async-done | bytes 147472 | tf_op jit(solution)/shard_map/reduce_scatter | solution.py:371
  765.2 86.8 %all-reduce.12.cloned.1.call-done = (bf16[512,1536]{0,1:T(8,128)(2,1)}, bf16[512,1536]{0,1:T(8,128)(2,1)}) async-done(((bf16[512,1536]{0,1:T(8,128)(2,1)}, bf16[512,1536]{0,1:T(8,128)(2,1)}), (bf16[512,1536]{0,1:T(8,128)(2,1)}, bf16[512,1536]{0,1:T(8,128)(2,1)})) %all-reduce.12.cloned.1.call-update) | async-done | bytes 3145744 | tf_op jit(solution)/shard_map/psum | solution.py:263
  865.2 34.2 %all-reduce.2 = (bf16[1536]{0:T(1024)(128)(2,1)S(1)}, bf16[1536]{0:T(1024)(128)(2,1)S(1)}) all-reduce(bf16[1536]{0:T(1024)(128)(2,1)S(1)} %get-tuple-element.74, bf16[1536]{0:T(1024)(128)(2,1)S(1)} %copy-done.50), channel_id=4, replica_groups=mesh['dp'=4,'ctx'=4,'tensor'=2] {'dp','ctx'}, use_global_device_ids=true, to_apply=%region_22.23.clone | all-reduce | flops 3072 | bytes 12288
  899.9 151.0 %reduce-scatter.25.cloned.1.call-done = bf16[24,96,256]{2,1,0:T(8,128)(2,1)} async-done(((bf16[24,1536,256]{2,1,0:T(8,128)(2,1)}), bf16[24,96,256]{2,1,0:T(8,128)(2,1)}) %reduce-scatter.25.cloned.1.call-update) | async-done | bytes 1179664 | tf_op jit(solution)/shard_map/reduce_scatter | solution.py:268
  1053.9 194.9 %reduce-scatter.27.cloned.1.call-done = bf16[24,96,256]{2,1,0:T(8,128)(2,1)} async-done(((bf16[24,1536,256]{2,1,0:T(8,128)(2,1)}), bf16[24,96,256]{2,1,0:T(8,128)(2,1)}) %reduce-scatter.27.cloned.1.call-update) | async-done | bytes 1179664 | tf_op jit(solution)/shard_map/reduce_scatter | solution.py:271
  1251.8 195.1 %reduce-scatter.29.cloned.1.call-done = bf16[24,96,256]{2,1,0:T(8,128)(2,1)} async-done(((bf16[24,1536,256]{2,1,0:T(8,128)(2,1)}), bf16[24,96,256]{2,1,0:T(8,128)(2,1)}) %reduce-scatter.29.cloned.1.call-update) | async-done | bytes 1179664 | tf_op jit(solution)/shard_map/reduce_scatter | solution.py:274
  (215 shorter events, 116.2 us)
Async XLA Ops:
  7.2 35.7 %all-gather.3.cloned.1.call-start = ((), (), s32[]{:S(2)}) async-start(), calls=%async_computation.10 | async-start | bytes 1310720 | tf_op jit(solution)/shard_map/all_gather | solution.py:210
  9.1 159.1 %copy-start = (bf16[512,1536]{0,1:T(8,128)(2,1)}, bf16[512,1536]{0,1:T(8,128)(2,1)S(1)}, u32[]{:S(2)}) copy-start(bf16[512,1536]{0,1:T(8,128)(2,1)S(1)} %copy.108) | copy-start | bytes 4718596
  12.1 73.2 %all-gather.5.cloned.1.call-start = ((), (), s32[]{:S(2)}) async-start(), calls=%async_computation.11 | async-start | bytes 1310720 | tf_op jit(solution)/shard_map/all_gather | solution.py:211
  13.8 152.2 %all-reduce.8.cloned.1.call-start = ((), (), s32[]{:S(2)}) async-start(), calls=%async_computation.12 | async-start | bytes 3145728 | tf_op jit(solution)/shard_map/psum | solution.py:239
  18.8 68.8 %copy-start.11 = (pred[512,2048]{0,1:T(8,128)(4,1)}, pred[512,2048]{0,1:T(8,128)(4,1)S(1)}, u32[]{:S(2)}) copy-start(pred[512,2048]{0,1:T(8,128)(4,1)S(1)} %fusion.12) | copy-start | bytes 3145732
  114.9 53.8 %copy-start.43 = (f32[1536]{0:T(1024)S(1)}, f32[1536]{0:T(1024)}, u32[]{:S(2)}) copy-start(f32[1536]{0:T(1024)} %param.20) | copy-start | bytes 18436
  114.9 230.4 %all-reduce.10.cloned.1.call-start = ((), (), s32[]{:S(2)}) async-start(), calls=%async_computation.13 | async-start | bytes 3145728 | tf_op jit(solution)/shard_map/psum | solution.py:282
  293.5 131.8 %reduce-scatter.13.cloned.1.call-start = ((), (), s32[]{:S(2)}) async-start(), calls=%async_computation.14 | async-start | bytes 1310720 | tf_op jit(solution)/shard_map/reduce_scatter | solution.py:333
  293.6 51.7 %copy-start.1 = (bf16[512,1536]{0,1:T(8,128)(2,1)S(1)}, bf16[512,1536]{0,1:T(8,128)(2,1)}, u32[]{:S(2)}) copy-start(bf16[512,1536]{0,1:T(8,128)(2,1)} %copy-done) | copy-start | bytes 4718596
  293.6 51.7 %copy-start.7 = (bf16[512,1536]{0,1:T(8,128)(2,1)S(1)}, bf16[512,1536]{0,1:T(8,128)(2,1)}, u32[]{:S(2)}) copy-start(bf16[512,1536]{0,1:T(8,128)(2,1)} %all-reduce.8.cloned.1.call-done) | copy-start | bytes 4718596
  293.7 51.7 %copy-start.36 = (bf16[1536,24]{0,1:T(8,128)(2,1)S(1)}, bf16[1536,24]{0,1:T(8,128)(2,1)}, u32[]{:S(2)}) copy-start(bf16[1536,24]{0,1:T(8,128)(2,1)} %param.21) | copy-start | bytes 221188
  293.7 51.7 %copy-start.44 = (f32[1536]{0:T(1024)S(1)}, f32[1536]{0:T(1024)}, u32[]{:S(2)}) copy-start(f32[1536]{0:T(1024)} %param.20) | copy-start | bytes 18436
  293.7 51.7 %copy-start.48 = (f32[512]{0:T(512)S(1)}, f32[512]{0:T(512)}, u32[]{:S(2)}) copy-start(f32[512]{0:T(512)} %copy-done.47) | copy-start | bytes 6148
  398.0 56.0 %reduce-scatter.15.cloned.1.call-start = ((), (), s32[]{:S(2)}) async-start(), calls=%async_computation.15 | async-start | bytes 1310720 | tf_op jit(solution)/shard_map/reduce_scatter | solution.py:336
  419.5 129.0 %reduce-scatter.31.cloned.1.call-start = ((), (), s32[]{:S(2)}) async-start(), calls=%async_computation.23 | async-start | bytes 417792
  421.1 150.3 %reduce-scatter.19.cloned.1.call-start = ((), (), s32[]{:S(2)}) async-start(), calls=%async_computation.17 | async-start | bytes 835584 | tf_op jit(solution)/shard_map/reduce_scatter | solution.py:374
  428.0 202.4 %reduce-scatter.21.cloned.1.call-start = ((), (), s32[]{:S(2)}) async-start(), calls=%async_computation.18 | async-start | bytes 835584 | tf_op jit(solution)/shard_map/reduce_scatter | solution.py:377
  456.5 240.7 %reduce-scatter.23.cloned.1.call-start = ((), (), s32[]{:S(2)}) async-start(), calls=%async_computation.19 | async-start | bytes 2506752 | tf_op jit(solution)/shard_map/reduce_scatter | solution.py:380
  461.3 302.2 %reduce-scatter.17.cloned.1.call-start = ((), (), s32[]{:S(2)}) async-start(), calls=%async_computation.16 | async-start | bytes 2506752 | tf_op jit(solution)/shard_map/reduce_scatter | solution.py:371
  475.4 376.6 %all-reduce.12.cloned.1.call-start = ((), (), s32[]{:S(2)}) async-start(), calls=%async_computation.24 | async-start | bytes 6291456 | tf_op jit(solution)/shard_map/psum | solution.py:263
  484.6 566.4 %reduce-scatter.25.cloned.1.call-start = ((), (), s32[]{:S(2)}) async-start(), calls=%async_computation.20 | async-start | bytes 20054016 | tf_op jit(solution)/shard_map/reduce_scatter | solution.py:268
  505.4 743.4 %reduce-scatter.27.cloned.1.call-start = ((), (), s32[]{:S(2)}) async-start(), calls=%async_computation.21 | async-start | bytes 20054016 | tf_op jit(solution)/shard_map/reduce_scatter | solution.py:271
  526.0 920.9 %reduce-scatter.29.cloned.1.call-start = ((), (), s32[]{:S(2)}) async-start(), calls=%async_computation.22 | async-start | bytes 20054016 | tf_op jit(solution)/shard_map/reduce_scatter | solution.py:274
  546.6 308.4 %copy-start.8 = (bf16[512,1536]{0,1:T(8,128)(2,1)S(1)}, bf16[512,1536]{0,1:T(8,128)(2,1)}, u32[]{:S(2)}) copy-start(bf16[512,1536]{0,1:T(8,128)(2,1)} %all-reduce.8.cloned.1.call-done) | copy-start | bytes 4718596
  (44 other events, 390.9 us)
Sparse Core Ops, SparseCore 0:
  12.2 30.6 all-gather.2
  45.0 27.4 all-gather.4
  115.0 50.9 all-reduce.7
  293.6 51.6 all-reduce.9
  398.1 27.1 reduce-scatter.12
  428.1 25.7 reduce-scatter.14
  457.4 54.3 reduce-scatter.30
  515.8 55.5 reduce-scatter.18
  574.9 55.4 reduce-scatter.20
  635.1 62.0 reduce-scatter.22
  701.5 61.9 reduce-scatter.16
  767.0 84.9 all-reduce.11
  856.1 194.7 reduce-scatter.24
  1054.9 193.8 reduce-scatter.26
  1252.8 194.0 reduce-scatter.28

commit v2 on v1

--- a/solution.py
+++ b/solution.py
@@ -1,3 +1,4 @@
+import functools
 import math
 
 import jax
@@ -93,12 +94,12 @@
     deo = (gc * dy).astype(bf16)
     grad_hidden = jnp.dot(deo, wd, preferred_element_type=f32)
     deo_t = (grow_ref[0] * dyt_ref[...].astype(f32)).astype(bf16)
-    gd_ref[0] = jnp.dot(deo_t, hidden, preferred_element_type=f32)
+    gd_ref[0] = jnp.dot(deo_t, hidden, preferred_element_type=f32).astype(bf16)
     grad_gate_act = (grad_hidden * up_act * sig * (1.0 + gate_act * (1.0 - sig))).astype(bf16)
     grad_up_act = (grad_hidden * silu).astype(bf16)
     n2t = n2t_ref[...]
-    gg_ref[0] = jnp.dot(n2t, grad_gate_act, preferred_element_type=f32)
-    gu_ref[0] = jnp.dot(n2t, grad_up_act, preferred_element_type=f32)
+    gg_ref[0] = jnp.dot(n2t, grad_gate_act, preferred_element_type=f32).astype(bf16)
+    gu_ref[0] = jnp.dot(n2t, grad_up_act, preferred_element_type=f32).astype(bf16)
     dn2_ref[...] += lax.dot_general(
         grad_gate_act, wg, nt, preferred_element_type=f32
     ) + lax.dot_general(grad_up_act, wu, nt, preferred_element_type=f32)
@@ -136,9 +137,9 @@
         out_shape=[
             jax.ShapeDtypeStruct((tokens, width), f32),
             jax.ShapeDtypeStruct((experts, tokens, 1), f32),
-            jax.ShapeDtypeStruct((experts, width, hidden), f32),
-            jax.ShapeDtypeStruct((experts, width, hidden), f32),
-            jax.ShapeDtypeStruct((experts, width, hidden), f32),
+            jax.ShapeDtypeStruct((experts, width, hidden), jnp.bfloat16),
+            jax.ShapeDtypeStruct((experts, width, hidden), jnp.bfloat16),
+            jax.ShapeDtypeStruct((experts, width, hidden), jnp.bfloat16),
             jax.ShapeDtypeStruct((tokens, width), f32),
         ],
         compiler_params=pltpu.CompilerParams(
@@ -147,9 +148,80 @@
         cost_estimate=pl.CostEstimate(
             flops=flops,
             transcendentals=experts * tokens * hidden,
-            bytes_accessed=experts * width * hidden * (3 * 2 + 3 * 4) + tokens * width * 16,
+            bytes_accessed=experts * width * hidden * (3 * 2 + 3 * 2) + tokens * width * 16,
         ),
     )(n2, n2t, dy, dyt, gcol, grow, wg, wu, wd)
+
+
+MESH = pl.DeviceIdType.MESH
+
+
+def _exchange_body(axis, n, per_peer, src_ref, out_ref, send_sems, recv_sems):
+    me = lax.axis_index(axis)
+    barrier = pltpu.get_barrier_semaphore()
+    for k in range(1, n):
+        peer = lax.rem(me + k, n)
+        pl.semaphore_signal(barrier, 1, device_id={axis: peer}, device_id_type=MESH)
+    pl.semaphore_wait(barrier, n - 1)
+    sends = []
+    for k in range(1, n):
+        peer = lax.rem(me + k, n)
+        copy = pltpu.make_async_remote_copy(
+            src_ref=src_ref.at[peer] if per_peer else src_ref,
+            dst_ref=out_ref.at[me],
+            send_sem=send_sems.at[k - 1],
+            recv_sem=recv_sems.at[k - 1],
+            device_id={axis: peer},
+            device_id_type=MESH,
+        )
+        copy.start()
+        sends.append(copy)
+    for k in range(1, n):
+        source = lax.rem(me + n - k, n)
+        pltpu.make_async_remote_copy(
+            src_ref=src_ref.at[source] if per_peer else src_ref,
+            dst_ref=out_ref.at[source],
+            send_sem=send_sems.at[k - 1],
+            recv_sem=recv_sems.at[k - 1],
+            device_id={axis: source},
+            device_id_type=MESH,
+        ).wait_recv()
+    for copy in sends:
+        copy.wait_send()
+
+
+def exchange(x, axis, n, per_peer, collective_id):
+    block = x.shape[1:] if per_peer else x.shape
+    nbytes = math.prod(block) * x.dtype.itemsize
+    return pl.pallas_call(
+        functools.partial(_exchange_body, axis, n, per_peer),
+        out_shape=jax.ShapeDtypeStruct((n,) + tuple(block), x.dtype),
+        in_specs=[pl.BlockSpec(memory_space=pl.ANY)],
+        out_specs=pl.BlockSpec(memory_space=pl.ANY),
+        scratch_shapes=[pltpu.SemaphoreType.DMA((n - 1,)), pltpu.SemaphoreType.DMA((n - 1,))],
+        compiler_params=pltpu.CompilerParams(collective_id=collective_id, has_side_effects=True),
+        cost_estimate=pl.CostEstimate(flops=0, transcendentals=0, bytes_accessed=2 * (n - 1) * nbytes),
+    )(x)
+
+
+def gather_axis(x, axis, n, collective_id):
+    got = exchange(x, axis, n, False, collective_id)
+    return lax.dynamic_update_slice_in_dim(got, x[None], lax.axis_index(axis), 0)
+
+
+def sum_axis(x, axis, collective_id):
+    got = exchange(x, axis, 2, False, collective_id)
+    me = lax.axis_index(axis)
+    other = lax.dynamic_index_in_dim(got, 1 - me, 0, keepdims=False)
+    return x.astype(jnp.float32) + other.astype(jnp.float32)
+
+
+def scatter_sum_axis(x, axis, n, collective_id):
+    got = exchange(x, axis, n, True, collective_id)
+    me = lax.axis_index(axis)
+    own = lax.dynamic_index_in_dim(x, me, 0, keepdims=True)
+    full = lax.dynamic_update_slice_in_dim(got, own, me, 0)
+    return jnp.sum(full.astype(jnp.float32), axis=0)
 
 
 def per_device(
@@ -206,14 +278,13 @@
             key_pos[None, :] <= token_positions[:, None]
         )
 
-    pieces = (
-        lax.all_gather(key_flat, "ctx", axis=0, tiled=True),
-        lax.all_gather(value_flat, "ctx", axis=0, tiled=True),
-    )
+    ctx_count = segments.shape[0] // token_count
+    kv_both = gather_axis(jnp.concatenate([key_flat, value_flat], axis=1), "ctx", ctx_count, 1)
     run_max = jnp.full((kv_local, group_size, token_count), NEGATIVE, f32)
-    piece_rows = pieces[0].shape[0]
-    key_piece = pieces[0].reshape(piece_rows, kv_local, HEAD_SIZE)
-    value_piece = pieces[1].reshape(piece_rows, kv_local, HEAD_SIZE)
+    piece_rows = ctx_count * token_count
+    kv_width = kv_local * HEAD_SIZE
+    key_piece = kv_both[:, :, :kv_width].reshape(piece_rows, kv_local, HEAD_SIZE)
+    value_piece = kv_both[:, :, kv_width:].reshape(piece_rows, kv_local, HEAD_SIZE)
     allowed = piece_mask(piece_rows)
     scores = (
         jnp.einsum("tkgd,nkd->kgtn", query_grouped, key_piece, preferred_element_type=f32)
@@ -236,7 +307,7 @@
         .astype(bf16)
     )
     attn_partial = contract_cols(attn_bf, o_weight)
-    mixed_attn = lax.psum(attn_partial.astype(jnp.bfloat16), "tensor").astype(jnp.float32)
+    mixed_attn = sum_axis(attn_partial.astype(bf16), "tensor", 2)
     resid = inputs_f32 + mixed_attn
     normed_two_f32, scale_two = normalize(resid, moe_gain)
     normed_two = normed_two_f32.astype(bf16)
@@ -260,28 +331,26 @@
         down_weight,
     )
     cot_f32 = output_grad.astype(f32)
-    moe_total = lax.psum(moe_acc.astype(jnp.bfloat16), "tensor").astype(jnp.float32)
+    moe_total = sum_axis(moe_acc.astype(bf16), "tensor", 3)
     output = (resid + moe_total).astype(bf16)
     grad_rows_all = moe_grad_rows
     gate_parts = gate_parts[:, :, 0]
     grad_gate_out, grad_up_out, grad_down_out = (
-        lax.psum_scatter(
-            grad_gate.astype(jnp.bfloat16), ("dp", "ctx"), scatter_dimension=1, tiled=True
-        ).astype(jnp.float32),
-        lax.psum_scatter(
-            grad_up.astype(jnp.bfloat16), ("dp", "ctx"), scatter_dimension=1, tiled=True
-        ).astype(jnp.float32),
-        lax.psum_scatter(
-            grad_down.astype(jnp.bfloat16), ("dp", "ctx"), scatter_dimension=1, tiled=True
-        ).astype(jnp.float32),
+        lax.psum_scatter(grad_gate, ("dp", "ctx"), scatter_dimension=1, tiled=True).astype(
+            jnp.float32
+        ),
+        lax.psum_scatter(grad_up, ("dp", "ctx"), scatter_dimension=1, tiled=True).astype(
+            jnp.float32
+        ),
+        lax.psum_scatter(grad_down, ("dp", "ctx"), scatter_dimension=1, tiled=True).astype(
+            jnp.float32
+        ),
     )
     gate_pair = jnp.sum(
         jnp.where(picked_onehot, jnp.transpose(gate_parts)[:, None, :], 0.0), axis=2
     )
-    moe_summed, gate_summed = (
-        lax.psum(grad_rows_all.astype(jnp.bfloat16), "tensor").astype(jnp.float32),
-        lax.psum(gate_pair.astype(jnp.bfloat16), "tensor").astype(jnp.float32),
-    )
+    moe_summed = sum_axis(grad_rows_all.astype(bf16), "tensor", 4)
+    gate_summed = sum_axis(gate_pair.astype(bf16), "tensor", 5)
     grad_picked = gate_probs * (
         gate_summed - jnp.sum(gate_probs * gate_summed, axis=1, keepdims=True)
     )
@@ -299,13 +368,6 @@
         grad_attn.reshape(token_count, kv_local, group_size, HEAD_SIZE), (1, 2, 0, 3)
     )
     row_delta = jnp.sum(grad_attn_grouped.astype(f32) * attn_grouped, axis=-1)
-    pieces = (
-        lax.all_gather(key_flat, "ctx", axis=0, tiled=True),
-        lax.all_gather(value_flat, "ctx", axis=0, tiled=True),
-    )
-    piece_rows = pieces[0].shape[0]
-    key_piece = pieces[0].reshape(piece_rows, kv_local, HEAD_SIZE)
-    value_piece = pieces[1].reshape(piece_rows, kv_local, HEAD_SIZE)
     allowed = piece_mask(piece_rows)
     scores = (
         jnp.einsum("tkgd,nkd->kgtn", query_grouped, key_piece, preferred_element_type=f32)
@@ -329,14 +391,16 @@
     grad_values_all = value_part.reshape(piece_rows, kv_local * HEAD_SIZE)
     back_state = (grad_query, grad_keys_all, grad_values_all)
     grad_query, grad_keys_all, grad_values_all = back_state
-    grad_keys_here, grad_values_here = (
-        lax.psum_scatter(
-            grad_keys_all.astype(jnp.bfloat16), "ctx", scatter_dimension=0, tiled=True
-        ).astype(jnp.float32),
-        lax.psum_scatter(
-            grad_values_all.astype(jnp.bfloat16), "ctx", scatter_dimension=0, tiled=True
-        ).astype(jnp.float32),
-    )
+    grad_kv_here = scatter_sum_axis(
+        jnp.concatenate([grad_keys_all, grad_values_all], axis=1)
+        .astype(bf16)
+        .reshape(ctx_count, token_count, 2 * kv_width),
+        "ctx",
+        ctx_count,
+        6,
+    )
+    grad_keys_here = grad_kv_here[:, :kv_width]
+    grad_values_here = grad_kv_here[:, kv_width:]
     grad_query_rows = jnp.transpose(grad_query, (2, 0, 1, 3)).reshape(
         token_count, heads_local, HEAD_SIZE
     )
@@ -361,31 +425,36 @@
         + contract_cols(grad_key_bf, key_matrix)
         + contract_cols(grad_value_bf, value_matrix)
     )
-    grad_normed_one = lax.psum(partial_one.astype(jnp.bfloat16), "tensor").astype(jnp.float32)
+    grad_normed_one = sum_axis(partial_one.astype(bf16), "tensor", 7)
     grad_one_rows, grad_attn_gain = norm_backward(inputs_f32, scale_one, attn_gain, grad_normed_one)
     input_grad = grad_resid + grad_one_rows
+    q_cols, o_cols, k_cols = grad_q.shape[1], grad_o.shape[1], grad_k.shape[1]
+    dense_all = jnp.concatenate(
+        [
+            grad_q.astype(bf16),
+            grad_o.astype(bf16),
+            grad_k.astype(bf16),
+            grad_v.astype(bf16),
+            grad_router.astype(bf16),
+            grad_attn_gain[:, None].astype(bf16),
+            grad_moe_gain[:, None].astype(bf16),
+        ],
+        axis=1,
+    )
+    dense_here = lax.psum_scatter(dense_all, ("dp", "ctx"), scatter_dimension=0, tiled=True).astype(
+        f32
+    )
+    spans = [q_cols, o_cols, k_cols, k_cols, router_weight.shape[1], 1, 1]
+    cuts = [sum(spans[:i]) for i in range(len(spans) + 1)]
+    pieces_out = [dense_here[:, cuts[i] : cuts[i + 1]] for i in range(len(spans))]
     dense_out = (
-        lax.psum_scatter(
-            grad_attn_gain.astype(jnp.bfloat16), ("dp", "ctx"), scatter_dimension=0, tiled=True
-        ).astype(jnp.float32),
-        lax.psum_scatter(
-            grad_q.astype(jnp.bfloat16), ("dp", "ctx"), scatter_dimension=0, tiled=True
-        ).astype(jnp.float32),
-        lax.psum_scatter(
-            grad_k.astype(jnp.bfloat16), ("dp", "ctx"), scatter_dimension=0, tiled=True
-        ).astype(jnp.float32),
-        lax.psum_scatter(
-            grad_v.astype(jnp.bfloat16), ("dp", "ctx"), scatter_dimension=0, tiled=True
-        ).astype(jnp.float32),
-        lax.psum_scatter(
-            grad_o.astype(jnp.bfloat16), ("dp", "ctx"), scatter_dimension=0, tiled=True
-        ).astype(jnp.float32),
-        lax.psum_scatter(
-            grad_moe_gain.astype(jnp.bfloat16), ("dp", "ctx"), scatter_dimension=0, tiled=True
-        ).astype(jnp.float32),
-        lax.psum_scatter(
-            grad_router.astype(jnp.bfloat16), ("dp", "ctx"), scatter_dimension=0, tiled=True
-        ).astype(jnp.float32),
+        pieces_out[5][:, 0],
+        pieces_out[0],
+        pieces_out[2],
+        pieces_out[3],
+        pieces_out[1],
+        pieces_out[6][:, 0],
+        pieces_out[4],
     )
     return (
         output,

time: 1460 us -> 1340 us (0.918)
  waiting for transfers between devices: 982 us -> 675 us
  Pallas kernels: 113 us -> 343 us
  other arithmetic: 124 us -> 70.8 us
  local copies, waits for them, and re-layouts: 32.3 us -> 79.7 us
  blocking collectives: 39.5 us -> 0 us
    pallas_call x0 -> x7, Pallas kernels: none -> 230 us  [exchange(): pl.pallas_call(functools.partial(_exchange_body, axis, n, per_peer), out_...]
    reduce_scatter x9 -> x3, waiting for transfers between devices: 780 us -> 583 us  [the longest x1 195 us: per_device(): lax.psum_scatter(grad_up, ('dp', 'ctx'), scatter_dimension=1, tiled=True)]
    psum x3 -> x0, waiting for transfers between devices: 177 us -> none  [the longest x1 86.8 us: per_device(): lax.psum(moe_acc.astype(jnp.bfloat16), 'tensor').astype(jnp.float32)]
    unnamed x16 -> x5, waiting for transfers between devices: 0.27 us -> 92.1 us
    convert_element_type x13 -> x6, other arithmetic: 77.9 us -> 15.3 us  [the longest x1 3.21 us: per_device(): moe_summed = sum_axis(grad_rows_all.astype(bf16), 'tensor', 4)]
    concatenate x0 -> x5, local copies, waits for them, and re-layouts: none -> 37.5 us  [the longest x1 30.9 us: per_device(): jnp.concatenate([grad_q.astype(bf16), grad_o.astype(bf16), grad_k.astype(...]
    unnamed x1 -> x0, blocking collectives: 34.2 us -> none
    all_gather x2 -> x0, waiting for transfers between devices: 24.1 us -> none  [the longest x1 24.1 us: per_device(): lax.all_gather(key_flat, 'ctx', axis=0, tiled=True)]
  transfers between devices with their start and end apart: 15 -> 4, of which waited for: 13 -> 4; matrix products, arithmetic and copies ran while one was open for 14% -> 1% of each run, Pallas kernels for 0% -> 0%
where the time goes in v2:
time: 1340 us; the launch traced here: 1330 us
  waiting for transfers between devices  675 us (50%)
  Pallas kernels  343 us (26%)
  matrix products  150 us (11%)
  local copies, waits for them, and re-layouts  79.7 us (6%)
  other arithmetic  70.8 us (5%)
  between operations  15.1 us (1%)
    pallas_call x7, Pallas kernels, exchange(): pl.pallas_call(functools.partial(_exchange_body, axis, n, per_peer), out_...  230 us
    reduce_scatter x1, waiting for transfers between devices, per_device(): lax.psum_scatter(grad_up, ('dp', 'ctx'), scatter_dimension=1, tiled=True)  195 us
    reduce_scatter x1, waiting for transfers between devices, per_device(): lax.psum_scatter(grad_gate, ('dp', 'ctx'), scatter_dimension=1, tiled=True)  195 us
    reduce_scatter x1, waiting for transfers between devices, per_device(): lax.psum_scatter(grad_down, ('dp', 'ctx'), scatter_dimension=1, tiled=True)  192 us
    pallas_call x1, Pallas kernels, expert_kernel(): pl.pallas_call(_expert_body, grid=(experts,), in_specs=[whole((tokens, wi...  113 us
    unnamed x5, waiting for transfers between devices  92.1 us
    concatenate x1, local copies, waits for them, and re-layouts, per_device(): jnp.concatenate([grad_q.astype(bf16), grad_o.astype(bf16), grad_k.astype(...  30.9 us
    dot_general x1, matrix products, per_device(): jnp.einsum('kgtd,nkd->kgtn', grad_attn_grouped, value_piece, preferred_el...  28.6 us
  transfers between devices with their start and end apart: 4, of which 4 were waited for; matrix products, arithmetic and copies ran while one was open for 1% of the time, Pallas kernels for 0%

profile of v2, /device:TPU:0, one launch (start us, length us, event | category | flops | bytes accessed | tf_op | source)
XLA Modules:
  0.0 1332.9 jit_solution(4211109373423959887)
XLA Ops:
  14.3 40.1 %shard_map.229 = bf16[4,512,512]{2,1,0:T(8,128)(2,1)} custom-call(bf16[512,512]{1,0:T(8,128)(2,1)} %pad_maximum_fusion.3.src_ref), custom_call_target="tpu_custom_call" | custom-call | bytes 3145728 | tf_op jit(solution)/shard_map/pallas_call | solution.py:196
  69.8 20.5 %fusion.2 = (f32[4,3,512]{2,1,0:T(4,128)S(1)}, f32[4,2048,512,3]{2,1,3,0:T(8,128)}) fusion(pred[512,2048]{0,1:T(8,128)(4,1)S(1)} %fusion.12, bf16[512,4,3,32]{0,3,2,1:T(8,128)(2,1)S(1)} %bitcast.157, bf16[512,4,3,32]{0,3,2,1:T(8,128)(2,1)S(1)} %bitcast.155, bf16[2048,4,64,1]{0,2,1,3:T(8,128)(2,1)} %reshape.324), kind=kOutput, calls=%fused_computation.6 | convolution fusion | flops 1649928192 | bytes 53239808 | tf_op jit(solution)/shard_map/tkgd,nkd->kgtn/dot_general | solution.py:290
  90.3 22.0 %fusion.4 = f32[4,3,512]{2,1,0:T(4,128)S(1)} fusion(f32[4,2048,512,3]{2,1,3,0:T(8,128)} %get-tuple-element.114, f32[4,3,512]{2,1,0:T(4,128)S(1)} %broadcast_maximum_fusion, pred[512,2048]{0,1:T(8,128)(4,1)S(1)} %fusion.12), kind=kLoop, calls=%fused_computation.8 | loop fusion | flops 62908416 | bytes 51429376 | tf_op jit(solution)/shard_map/reduce_sum | solution.py:296
  113.0 22.9 %fusion.40 = (bf16[512,4,3,64]{0,3,2,1:T(8,128)(2,1)S(1)}, f32[4,3,512,64]{2,3,1,0:T(8,128)}) fusion(f32[512,4,3]{0,2,1:T(4,128)S(1)} %bitcast.167, f32[4,2048,512,3]{2,1,3,0:T(8,128)} %get-tuple-element.114, f32[4,3,512]{2,1,0:T(4,128)S(1)} %broadcast_maximum_fusion, pred[512,2048]{0,1:T(8,128)(4,1)S(1)} %fusion.12, bf16[2048,4,64,1]{0,2,1,3:T(8,128)(2,1)} %reshape.325), kind=kOutput, calls=%fused_computation.66 | convolution fusion | flops 1674313728 | bytes 54837248 | tf_op jit(solution)/shard_map/kgtn,nkd->kgtd/dot_general | solution.py:297
  136.8 4.2 convolution_convert_fusion.2.src_ref
  141.1 36.6 %shard_map.230 = bf16[2,512,1536]{2,1,0:T(8,128)(2,1)} custom-call(bf16[512,1536]{1,0:T(8,128)(2,1)} %convolution_convert_fusion.2.src_ref), custom_call_target="tpu_custom_call" | custom-call | bytes 3145728 | tf_op jit(solution)/shard_map/pallas_call | solution.py:196
  191.9 112.7 %shard_map.231 = (f32[512,1536]{1,0:T(8,128)}, f32[24,512,1]{2,1,0:T(8,128)}, bf16[24,1536,256]{2,1,0:T(8,128)(2,1)}, bf16[24,1536,256]{2,1,0:T(8,128)(2,1)}, bf...) custom-call(bf16[512,1536]{1,0:T(8,128)(2,1)} %copy-done.5, bf16[1536,512]{1,0:T(8,128)(2,1)} %copy.140.n2t_ref, ...), custom_call_target="tpu_custom_call" | custom-call | flops 86973087744 | bytes 125829120 | tf_op jit(solution)/shard_map/pallas_call | solution.py:115
  307.8 4.6 reduce
  313.3 5.3 shard_map.234
  325.4 34.5 %shard_map.232 = bf16[2,512,1536]{2,1,0:T(8,128)(2,1)} custom-call(bf16[512,1536]{1,0:T(8,128)(2,1)} %convert_element_type.212.src_ref), custom_call_target="tpu_custom_call" | custom-call | bytes 3145728 | tf_op jit(solution)/shard_map/pallas_call | solution.py:196
  359.9 33.4 %shard_map.233 = bf16[2,512,1536]{2,1,0:T(8,128)(2,1)} custom-call(bf16[512,1536]{1,0:T(8,128)(2,1)} %convert_element_type.218.src_ref), custom_call_target="tpu_custom_call" | custom-call | bytes 3145728 | tf_op jit(solution)/shard_map/pallas_call | solution.py:196
  405.9 19.7 %fusion.37 = bf16[2048,4,64]{0,2,1:T(8,128)(2,1)} fusion(bf16[4,3,512,64]{2,3,1,0:T(8,128)(2,1)S(1)} %bitcast.150, f32[4,2048,512,3]{2,1,3,0:T(8,128)} %get-tuple-element.114, f32[4,3,512]{2,1,0:T(4,128)S(1)} %copy-done.48, pred[512,2048]{0,1:T(8,128)(4,1)S(1)} %copy-done.18), kind=kOutput, calls=%fused_computation.60 | convolution fusion | flops 1661468672 | bytes 53239808 | tf_op jit(solution)/shard_map/kgtn,kgtd->nkd/dot_general | solution.py:387
  425.5 28.6 %multiply_convert_fusion = bf16[4,3,512,2048]{2,3,1,0:T(8,128)(2,1)} fusion(f32[4,2048,512,3]{2,1,3,0:T(8,128)} %get-tuple-element.114, f32[4,3,512]{2,1,0:T(4,128)S(1)} %multiply_reduce_fusion.3, f32[4,3,512]{2,1,0:T(4,128)S(1)} %copy-done.48, pred[512,2048]{0,1:T(8,128)(4,1)S(1)} %copy-done.18, bf16[4,3,512,64]{2,3,1,0:T(8,128)(2,1)S(1)} %bitcast.151, ...), kind=kOutput, calls=%fused_computation.4 | convolution fusion | flops 1686110208 | bytes 78430208 | tf_op jit(solution)/shard_map/kgtd,nkd->kgtn/dot_general | solution.py:377
  454.1 12.6 fusion.36
  466.7 11.8 convolution_multiply_fusion
  489.7 45.7 %shard_map.235 = bf16[4,512,512]{2,1,0:T(8,128)(2,1)} custom-call(bf16[4,512,512]{2,1,0:T(8,128)(2,1)} %pad_maximum_fusion.src_ref), custom_call_target="tpu_custom_call" | custom-call | bytes 3145728 | tf_op jit(solution)/shard_map/pallas_call | solution.py:196
  553.7 34.6 %shard_map.236 = bf16[2,512,1536]{2,1,0:T(8,128)(2,1)} custom-call(bf16[512,1536]{1,0:T(8,128)(2,1)} %fusion.26.src_ref), custom_call_target="tpu_custom_call" | custom-call | bytes 3145728 | tf_op jit(solution)/shard_map/pallas_call | solution.py:196
  591.0 30.9 %concatenate.46 = bf16[1536,2074]{0,1:T(8,128)(2,1)} concatenate(bf16[1536,768]{0,1:T(8,128)(2,1)} %convolution_convert_fusion.1, bf16[1536,768]{0,1:T(8,128)(2,1)} %convolution_convert_fusion, bf16[1536,256]{0,1:T(8,128)(2,1)} %convolution_convert_fusion.3, bf16[1536,256]{0,1:T(8,128)(2,1)} %convolution_convert_fusion.4, bf16[1536,24]{0,1:T(8,128)(2,1)S(1)} %copy-done.39, ...), dimensions={1} | concatenate | bytes 12742656 | tf_op jit(solution)/shard_map/concatenate | solution.py:432
  621.9 9.2 copy.167
  633.3 5.3 fusion.19
  638.5 90.2 %reduce-scatter.13.cloned.1.call-done = bf16[96,2074]{1,0:T(8,128)(2,1)} async-done(((bf16[1536,2074]{1,0:T(8,128)(2,1)}), bf16[96,2074]{1,0:T(8,128)(2,1)}) %reduce-scatter.13.cloned.1.call-update) | async-done | bytes 398224
  734.5 192.3 %reduce-scatter.11.cloned.1.call-done = bf16[24,96,256]{2,1,0:T(8,128)(2,1)} async-done(((bf16[24,1536,256]{2,1,0:T(8,128)(2,1)}), bf16[24,96,256]{2,1,0:T(8,128)(2,1)}) %reduce-scatter.11.cloned.1.call-update) | async-done | bytes 1179664 | tf_op jit(solution)/shard_map/reduce_scatter | solution.py:345
  929.7 195.3 %reduce-scatter.9.cloned.1.call-done = bf16[24,96,256]{2,1,0:T(8,128)(2,1)} async-done(((bf16[24,1536,256]{2,1,0:T(8,128)(2,1)}), bf16[24,96,256]{2,1,0:T(8,128)(2,1)}) %reduce-scatter.9.cloned.1.call-update) | async-done | bytes 1179664 | tf_op jit(solution)/shard_map/reduce_scatter | solution.py:342
  1127.9 195.1 %reduce-scatter.7.cloned.1.call-done = bf16[24,96,256]{2,1,0:T(8,128)(2,1)} async-done(((bf16[24,1536,256]{2,1,0:T(8,128)(2,1)}), bf16[24,96,256]{2,1,0:T(8,128)(2,1)}) %reduce-scatter.7.cloned.1.call-update) | async-done | bytes 1179664 | tf_op jit(solution)/shard_map/reduce_scatter | solution.py:339
  (220 shorter events, 109.7 us)
Async XLA Ops:
  7.2 721.5 %reduce-scatter.13.cloned.1.call-start = ((), (), s32[]{:S(2)}) async-start(), calls=%async_computation.7 | async-start | bytes 7102464
  9.2 56.0 %copy-start.51 = (f32[512]{0:T(512)}, f32[512]{0:T(512)S(1)}, u32[]{:S(2)}) copy-start(f32[512]{0:T(512)S(1)} %add_rsqrt_fusion.1) | copy-start | bytes 6148
  13.3 55.2 %copy-start.23 = (f32[512,32]{0,1:T(8,128)}, f32[512,32]{0,1:T(8,128)S(1)}, u32[]{:S(2)}) copy-start(f32[512,32]{0,1:T(8,128)S(1)} %get-tuple-element.112) | copy-start | bytes 196612
  68.7 21.6 %copy-start.26 = (bf16[512,12,32]{0,2,1:T(8,128)(2,1)}, bf16[512,12,32]{0,2,1:T(8,128)(2,1)S(1)}, u32[]{:S(2)}) copy-start(bf16[512,12,32]{0,2,1:T(8,128)(2,1)S(1)} %get-tuple-element.98) | copy-start | bytes 1179652
  68.7 21.6 %copy-start.28 = (bf16[512,12,32]{0,2,1:T(8,128)(2,1)}, bf16[512,12,32]{0,2,1:T(8,128)(2,1)S(1)}, u32[]{:S(2)}) copy-start(bf16[512,12,32]{0,2,1:T(8,128)(2,1)S(1)} %get-tuple-element.99) | copy-start | bytes 1179652
  69.7 43.2 %copy-start.17 = (pred[512,2048]{0,1:T(8,128)(4,1)}, pred[512,2048]{0,1:T(8,128)(4,1)S(1)}, u32[]{:S(2)}) copy-start(pred[512,2048]{0,1:T(8,128)(4,1)S(1)} %fusion.12) | copy-start | bytes 3145732
  112.3 23.6 %copy-start.35 = (f32[4,3,512]{2,1,0:T(4,128)}, f32[4,3,512]{2,1,0:T(4,128)S(1)}, u32[]{:S(2)}) copy-start(f32[4,3,512]{2,1,0:T(4,128)S(1)} %fusion.4) | copy-start | bytes 73732
  141.1 36.6 %copy-start.12 = (bf16[512,1536]{1,0:T(8,128)(2,1)S(1)}, bf16[512,1536]{1,0:T(8,128)(2,1)}, u32[]{:S(2)}) copy-start(bf16[512,1536]{1,0:T(8,128)(2,1)} %convolution_convert_fusion.2.src_ref) | copy-start | bytes 4718596
  307.8 10.8 copy-start.47
  307.8 13.4 %copy-start.6 = (bf16[512,1536]{1,0:T(8,128)(2,1)S(1)}, bf16[512,1536]{1,0:T(8,128)(2,1)}, u32[]{:S(2)}) copy-start(bf16[512,1536]{1,0:T(8,128)(2,1)} %copy-done.5) | copy-start | bytes 4718596
  359.9 33.5 %copy-start.1 = (f32[512,1536]{1,0:T(8,128)S(1)}, f32[512,1536]{1,0:T(8,128)}, u32[]{:S(2)}) copy-start(f32[512,1536]{1,0:T(8,128)} %copy-done) | copy-start | bytes 9437188
  359.9 33.5 %copy-start.38 = (bf16[1536,24]{0,1:T(8,128)(2,1)S(1)}, bf16[1536,24]{0,1:T(8,128)(2,1)}, u32[]{:S(2)}) copy-start(bf16[1536,24]{0,1:T(8,128)(2,1)} %param.21) | copy-start | bytes 221188
  359.9 33.5 %copy-start.43 = (f32[1536]{0:T(1024)S(1)}, f32[1536]{0:T(1024)}, u32[]{:S(2)}) copy-start(f32[1536]{0:T(1024)} %param.20) | copy-start | bytes 18436
  359.9 33.5 %copy-start.45 = (f32[512]{0:T(512)S(1)}, f32[512]{0:T(512)}, u32[]{:S(2)}) copy-start(f32[512]{0:T(512)} %copy-done.44) | copy-start | bytes 6148
  425.5 28.6 %copy-start.27 = (bf16[512,12,32]{0,2,1:T(8,128)(2,1)S(1)}, bf16[512,12,32]{0,2,1:T(8,128)(2,1)}, u32[]{:S(2)}) copy-start(bf16[512,12,32]{0,2,1:T(8,128)(2,1)} %copy-done.26) | copy-start | bytes 1179652
  425.5 28.6 %copy-start.29 = (bf16[512,12,32]{0,2,1:T(8,128)(2,1)S(1)}, bf16[512,12,32]{0,2,1:T(8,128)(2,1)}, u32[]{:S(2)}) copy-start(bf16[512,12,32]{0,2,1:T(8,128)(2,1)} %copy-done.28) | copy-start | bytes 1179652
  454.1 12.6 copy-start.21
  466.7 11.9 copy-start.9
  466.7 11.8 copy-start.59
  553.7 34.6 %copy-start.4 = (bf16[512,1536]{1,0:T(8,128)(2,1)S(1)}, bf16[512,1536]{1,0:T(8,128)(2,1)}, u32[]{:S(2)}) copy-start(bf16[512,1536]{1,0:T(8,128)(2,1)} %fusion.26.src_ref) | copy-start | bytes 4718596
  553.7 34.6 %copy-start.53 = (f32[512]{0:T(512)S(1)}, f32[512]{0:T(512)}, u32[]{:S(2)}) copy-start(f32[512]{0:T(512)} %copy-done.51) | copy-start | bytes 6148
  631.2 295.5 %reduce-scatter.11.cloned.1.call-start = ((), (), s32[]{:S(2)}) async-start(), calls=%async_computation.6 | async-start | bytes 20054016 | tf_op jit(solution)/shard_map/reduce_scatter | solution.py:345
  631.9 493.0 %reduce-scatter.9.cloned.1.call-start = ((), (), s32[]{:S(2)}) async-start(), calls=%async_computation.5 | async-start | bytes 20054016 | tf_op jit(solution)/shard_map/reduce_scatter | solution.py:342
  632.7 690.3 %reduce-scatter.7.cloned.1.call-start = ((), (), s32[]{:S(2)}) async-start(), calls=%async_computation.4 | async-start | bytes 20054016 | tf_op jit(solution)/shard_map/reduce_scatter | solution.py:339
  (41 other events, 134.5 us)
Sparse Core Ops, SparseCore 0:
  631.3 97.3 reduce-scatter.12
  732.8 193.8 reduce-scatter.10
  930.9 194.0 reduce-scatter.8
  1128.9 194.0 reduce-scatter.6

commit v3 on v2

--- a/solution.py
+++ b/solution.py
@@ -441,6 +441,9 @@
         ],
         axis=1,
     )
+    dense_all, grad_gate_out, grad_up_out, grad_down_out = lax.optimization_barrier(
+        (dense_all, grad_gate_out, grad_up_out, grad_down_out)
+    )
     dense_here = lax.psum_scatter(dense_all, ("dp", "ctx"), scatter_dimension=0, tiled=True).astype(
         f32
     )

time: 1340 us -> 1060 us (0.79)
  waiting for transfers between devices: 675 us -> 374 us
  Pallas kernels: 343 us -> 368 us
    reduce_scatter x1, waiting for transfers between devices: 192 us -> 0.01 us  [per_device(): lax.psum_scatter(grad_down, ('dp', 'ctx'), scatter_dimension=1, tiled=True)]
    reduce_scatter x1, waiting for transfers between devices: 195 us -> 95.7 us  [per_device(): lax.psum_scatter(grad_up, ('dp', 'ctx'), scatter_dimension=1, tiled=True)]
    pallas_call x7, Pallas kernels: 230 us -> 255 us  [exchange(): pl.pallas_call(functools.partial(_exchange_body, axis, n, per_peer), out_...]
  transfers between devices with their start and end apart: 4 -> 4, of which waited for: 4 -> 3; matrix products, arithmetic and copies ran while one was open for 1% -> 15% of each run, Pallas kernels for 0% -> 17%
where the time goes in v3:
time: 1060 us; the launch traced here: 1050 us
  waiting for transfers between devices  374 us (35%)
  Pallas kernels  368 us (35%)
  matrix products  144 us (14%)
  local copies, waits for them, and re-layouts  81.6 us (8%)
  other arithmetic  68.1 us (6%)
  between operations  15.2 us (1%)
    pallas_call x7, Pallas kernels, exchange(): pl.pallas_call(functools.partial(_exchange_body, axis, n, per_peer), out_...  255 us
    reduce_scatter x1, waiting for transfers between devices, per_device(): lax.psum_scatter(grad_gate, ('dp', 'ctx'), scatter_dimension=1, tiled=True)  195 us
    pallas_call x1, Pallas kernels, expert_kernel(): pl.pallas_call(_expert_body, grid=(experts,), in_specs=[whole((tokens, wi...  113 us
    reduce_scatter x1, waiting for transfers between devices, per_device(): lax.psum_scatter(grad_up, ('dp', 'ctx'), scatter_dimension=1, tiled=True)  95.7 us
    unnamed x5, waiting for transfers between devices  83.2 us
    concatenate x1, local copies, waits for them, and re-layouts, per_device(): jnp.concatenate([grad_q.astype(bf16), grad_o.astype(bf16), grad_k.astype(...  30.9 us
    dot_general x1, matrix products, per_device(): jnp.einsum('kgtd,nkd->kgtn', grad_attn_grouped, value_piece, preferred_el...  28.3 us
    unnamed x127, local copies, waits for them, and re-layouts  26.1 us
  transfers between devices with their start and end apart: 4, of which 3 were waited for; matrix products, arithmetic and copies ran while one was open for 15% of the time, Pallas kernels for 17%

profile of v3, /device:TPU:0, one launch (start us, length us, event | category | flops | bytes accessed | tf_op | source)
XLA Modules:
  0.0 1051.2 jit_solution(4081919553868312247)
XLA Ops:
  14.3 40.1 %shard_map.229 = bf16[4,512,512]{2,1,0:T(8,128)(2,1)} custom-call(bf16[512,512]{1,0:T(8,128)(2,1)} %pad_maximum_fusion.3.src_ref), custom_call_target="tpu_custom_call" | custom-call | bytes 3145728 | tf_op jit(solution)/shard_map/pallas_call | solution.py:196
  69.8 20.4 %fusion.2 = (f32[4,3,512]{2,1,0:T(4,128)S(1)}, f32[4,2048,512,3]{2,1,3,0:T(8,128)}) fusion(pred[512,2048]{0,1:T(8,128)(4,1)S(1)} %fusion.12, bf16[512,4,3,32]{0,3,2,1:T(8,128)(2,1)S(1)} %bitcast.157, bf16[512,4,3,32]{0,3,2,1:T(8,128)(2,1)S(1)} %bitcast.155, bf16[2048,4,64,1]{0,2,1,3:T(8,128)(2,1)} %reshape.324), kind=kOutput, calls=%fused_computation.6 | convolution fusion | flops 1649928192 | bytes 53239808 | tf_op jit(solution)/shard_map/tkgd,nkd->kgtn/dot_general | solution.py:290
  90.9 22.0 %fusion.4 = f32[4,3,512]{2,1,0:T(4,128)S(1)} fusion(f32[4,2048,512,3]{2,1,3,0:T(8,128)} %get-tuple-element.122, f32[4,3,512]{2,1,0:T(4,128)S(1)} %broadcast_maximum_fusion, pred[512,2048]{0,1:T(8,128)(4,1)S(1)} %fusion.12), kind=kLoop, calls=%fused_computation.8 | loop fusion | flops 62908416 | bytes 51429376 | tf_op jit(solution)/shard_map/reduce_sum | solution.py:296
  112.9 22.7 %fusion.40 = (bf16[512,4,3,64]{0,3,2,1:T(8,128)(2,1)S(1)}, f32[4,3,512,64]{2,3,1,0:T(8,128)}) fusion(f32[512,4,3]{0,2,1:T(4,128)S(1)} %bitcast.167, f32[4,2048,512,3]{2,1,3,0:T(8,128)} %get-tuple-element.122, f32[4,3,512]{2,1,0:T(4,128)S(1)} %broadcast_maximum_fusion, pred[512,2048]{0,1:T(8,128)(4,1)S(1)} %fusion.12, bf16[2048,4,64,1]{0,2,1,3:T(8,128)(2,1)} %reshape.325), kind=kOutput, calls=%fused_computation.66 | convolution fusion | flops 1674313728 | bytes 54837248 | tf_op jit(solution)/shard_map/kgtn,nkd->kgtd/dot_general | solution.py:297
  136.5 4.2 convolution_convert_fusion.2.src_ref
  140.7 36.5 %shard_map.230 = bf16[2,512,1536]{2,1,0:T(8,128)(2,1)} custom-call(bf16[512,1536]{1,0:T(8,128)(2,1)} %convolution_convert_fusion.2.src_ref), custom_call_target="tpu_custom_call" | custom-call | bytes 3145728 | tf_op jit(solution)/shard_map/pallas_call | solution.py:196
  187.7 4.0 copy.141.gcol_ref
  191.7 112.6 %shard_map.231 = (f32[512,1536]{1,0:T(8,128)}, f32[24,512,1]{2,1,0:T(8,128)}, bf16[24,1536,256]{2,1,0:T(8,128)(2,1)}, bf16[24,1536,256]{2,1,0:T(8,128)(2,1)}, bf...) custom-call(bf16[512,1536]{1,0:T(8,128)(2,1)} %copy-done.5, bf16[1536,512]{1,0:T(8,128)(2,1)} %copy.140.n2t_ref, ...), custom_call_target="tpu_custom_call" | custom-call | flops 86973087744 | bytes 125829120 | tf_op jit(solution)/shard_map/pallas_call | solution.py:115
  308.3 4.6 reduce
  313.9 5.3 shard_map.234
  324.8 34.7 %shard_map.232 = bf16[2,512,1536]{2,1,0:T(8,128)(2,1)} custom-call(bf16[512,1536]{1,0:T(8,128)(2,1)} %convert_element_type.212.src_ref), custom_call_target="tpu_custom_call" | custom-call | bytes 3145728 | tf_op jit(solution)/shard_map/pallas_call | solution.py:196
  359.5 33.8 %shard_map.233 = bf16[2,512,1536]{2,1,0:T(8,128)(2,1)} custom-call(bf16[512,1536]{1,0:T(8,128)(2,1)} %convert_element_type.218.src_ref), custom_call_target="tpu_custom_call" | custom-call | bytes 3145728 | tf_op jit(solution)/shard_map/pallas_call | solution.py:196
  404.0 20.0 %fusion.37 = bf16[2048,4,64]{0,2,1:T(8,128)(2,1)} fusion(bf16[4,3,512,64]{2,3,1,0:T(8,128)(2,1)S(1)} %bitcast.149, f32[4,2048,512,3]{2,1,3,0:T(8,128)} %get-tuple-element.122, f32[4,3,512]{2,1,0:T(4,128)S(1)} %log_add_fusion, pred[512,2048]{0,1:T(8,128)(4,1)S(1)} %copy-done.17), kind=kOutput, calls=%fused_computation.60 | convolution fusion | flops 1661468672 | bytes 53239808 | tf_op jit(solution)/shard_map/kgtn,kgtd->nkd/dot_general | solution.py:387
  428.6 28.3 %multiply_convert_fusion = bf16[4,3,512,2048]{2,3,1,0:T(8,128)(2,1)} fusion(f32[4,2048,512,3]{2,1,3,0:T(8,128)} %get-tuple-element.122, f32[4,3,512]{2,1,0:T(4,128)S(1)} %multiply_reduce_fusion.3, f32[4,3,512]{2,1,0:T(4,128)S(1)} %log_add_fusion, pred[512,2048]{0,1:T(8,128)(4,1)S(1)} %copy-done.17, bf16[4,3,512,64]{2,3,1,0:T(8,128)(2,1)} %bitcast.151, ...), kind=kOutput, calls=%fused_computation.4 | convolution fusion | flops 1686110208 | bytes 78430208 | tf_op jit(solution)/shard_map/kgtd,nkd->kgtn/dot_general | solution.py:377
  456.9 12.7 %fusion.36 = bf16[2048,4,64]{0,2,1:T(8,128)(2,1)S(1)} fusion(bf16[4,3,512,2048]{2,3,1,0:T(8,128)(2,1)} %multiply_convert_fusion, bf16[512,4,3,32]{0,3,2,1:T(8,128)(2,1)S(1)} %bitcast.158, bf16[512,4,3,32]{0,3,2,1:T(8,128)(2,1)S(1)} %bitcast.156), kind=kOutput, calls=%fused_computation.59 | convolution fusion | flops 1613234176 | bytes 27000832 | tf_op jit(solution)/shard_map/kgtn,tkgd->nkd/dot_general | solution.py:384
  472.9 69.4 %shard_map.235 = bf16[4,512,512]{2,1,0:T(8,128)(2,1)} custom-call(bf16[4,512,512]{2,1,0:T(8,128)(2,1)} %pad_maximum_fusion.src_ref), custom_call_target="tpu_custom_call" | custom-call | bytes 3145728 | tf_op jit(solution)/shard_map/pallas_call | solution.py:196
  545.7 11.6 %convolution_multiply_fusion = f32[4,3,512,64]{2,3,1,0:T(8,128)S(1)} fusion(bf16[4,3,512,2048]{2,3,1,0:T(8,128)(2,1)} %multiply_convert_fusion, bf16[2048,4,64,1]{0,2,1,3:T(8,128)(2,1)S(1)} %copy-done.20), kind=kOutput, calls=%fused_computation.68 | convolution fusion | flops 1611005952 | bytes 27787264 | tf_op jit(solution)/shard_map/kgtn,nkd->kgtd/dot_general | solution.py:381
  564.2 35.1 %shard_map.236 = bf16[2,512,1536]{2,1,0:T(8,128)(2,1)} custom-call(bf16[512,1536]{1,0:T(8,128)(2,1)} %fusion.26.src_ref), custom_call_target="tpu_custom_call" | custom-call | bytes 3145728 | tf_op jit(solution)/shard_map/pallas_call | solution.py:196
  611.4 30.9 %concatenate.46 = bf16[1536,2074]{0,1:T(8,128)(2,1)} concatenate(bf16[1536,768]{0,1:T(8,128)(2,1)} %convolution_convert_fusion.1, bf16[1536,768]{0,1:T(8,128)(2,1)} %convolution_convert_fusion, bf16[1536,256]{0,1:T(8,128)(2,1)} %convolution_convert_fusion.3, bf16[1536,256]{0,1:T(8,128)(2,1)} %convolution_convert_fusion.4, bf16[1536,24]{0,1:T(8,128)(2,1)S(1)} %convolution_convert_fusion.5, ...), dimensions={1} | concatenate | bytes 12742656 | tf_op jit(solution)/shard_map/concatenate | solution.py:432
  645.3 95.7 %reduce-scatter.9.cloned.1.call-done = bf16[24,96,256]{2,1,0:T(8,128)(2,1)} async-done(((bf16[24,1536,256]{2,1,0:T(8,128)(2,1)}), bf16[24,96,256]{2,1,0:T(8,128)(2,1)}) %reduce-scatter.9.cloned.1.call-update) | async-done | bytes 1179664 | tf_op jit(solution)/shard_map/reduce_scatter | solution.py:342
  744.0 195.2 %reduce-scatter.7.cloned.1.call-done = bf16[24,96,256]{2,1,0:T(8,128)(2,1)} async-done(((bf16[24,1536,256]{2,1,0:T(8,128)(2,1)}), bf16[24,96,256]{2,1,0:T(8,128)(2,1)}) %reduce-scatter.7.cloned.1.call-update) | async-done | bytes 1179664 | tf_op jit(solution)/shard_map/reduce_scatter | solution.py:339
  942.1 9.2 copy.167
  951.4 5.3 fusion.19
  956.7 81.8 %reduce-scatter.13.cloned.1.call-done = bf16[96,2074]{1,0:T(8,128)(2,1)} async-done(((bf16[1536,2074]{1,0:T(8,128)(2,1)}), bf16[96,2074]{1,0:T(8,128)(2,1)}) %reduce-scatter.13.cloned.1.call-update) | async-done | bytes 398224
  (219 shorter events, 99.8 us)
Async XLA Ops:
  7.2 635.1 %reduce-scatter.11.cloned.1.call-start = ((), (), s32[]{:S(2)}) async-start(), calls=%async_computation.6 | async-start | bytes 20054016 | tf_op jit(solution)/shard_map/reduce_scatter | solution.py:345
  9.2 56.0 %copy-start.53 = (f32[512]{0:T(512)}, f32[512]{0:T(512)S(1)}, u32[]{:S(2)}) copy-start(f32[512]{0:T(512)S(1)} %add_rsqrt_fusion.1) | copy-start | bytes 6148
  13.3 55.2 %copy-start.23 = (f32[512,32]{0,1:T(8,128)}, f32[512,32]{0,1:T(8,128)S(1)}, u32[]{:S(2)}) copy-start(f32[512,32]{0,1:T(8,128)S(1)} %get-tuple-element.120) | copy-start | bytes 196612
  68.7 21.5 %copy-start.25 = (bf16[512,12,32]{0,2,1:T(8,128)(2,1)}, bf16[512,12,32]{0,2,1:T(8,128)(2,1)S(1)}, u32[]{:S(2)}) copy-start(bf16[512,12,32]{0,2,1:T(8,128)(2,1)S(1)} %get-tuple-element.106) | copy-start | bytes 1179652
  68.7 21.5 %copy-start.27 = (bf16[512,12,32]{0,2,1:T(8,128)(2,1)}, bf16[512,12,32]{0,2,1:T(8,128)(2,1)S(1)}, u32[]{:S(2)}) copy-start(bf16[512,12,32]{0,2,1:T(8,128)(2,1)S(1)} %get-tuple-element.107) | copy-start | bytes 1179652
  69.8 43.1 %copy-start.16 = (pred[512,2048]{0,1:T(8,128)(4,1)}, pred[512,2048]{0,1:T(8,128)(4,1)S(1)}, u32[]{:S(2)}) copy-start(pred[512,2048]{0,1:T(8,128)(4,1)S(1)} %fusion.12) | copy-start | bytes 3145732
  112.9 22.7 %copy-start.35 = (f32[4,3,512]{2,1,0:T(4,128)}, f32[4,3,512]{2,1,0:T(4,128)S(1)}, u32[]{:S(2)}) copy-start(f32[4,3,512]{2,1,0:T(4,128)S(1)} %fusion.4) | copy-start | bytes 73732
  140.7 36.6 %copy-start.12 = (bf16[512,1536]{1,0:T(8,128)(2,1)S(1)}, bf16[512,1536]{1,0:T(8,128)(2,1)}, u32[]{:S(2)}) copy-start(bf16[512,1536]{1,0:T(8,128)(2,1)} %convolution_convert_fusion.2.src_ref) | copy-start | bytes 4718596
  304.3 436.7 %reduce-scatter.9.cloned.1.call-start = ((), (), s32[]{:S(2)}) async-start(), calls=%async_computation.5 | async-start | bytes 20054016 | tf_op jit(solution)/shard_map/reduce_scatter | solution.py:342
  305.1 634.1 %reduce-scatter.7.cloned.1.call-start = ((), (), s32[]{:S(2)}) async-start(), calls=%async_computation.4 | async-start | bytes 20054016 | tf_op jit(solution)/shard_map/reduce_scatter | solution.py:339
  305.8 732.7 %reduce-scatter.13.cloned.1.call-start = ((), (), s32[]{:S(2)}) async-start(), calls=%async_computation.7 | async-start | bytes 7102464
  308.3 15.1 %copy-start.7 = (f32[512,1536]{1,0:T(8,128)S(1)}, f32[512,1536]{1,0:T(8,128)}, u32[]{:S(2)}) copy-start(f32[512,1536]{1,0:T(8,128)} %get-tuple-element.22) | copy-start | bytes 9437188
  359.5 33.9 %copy-start.1 = (f32[512,1536]{1,0:T(8,128)S(1)}, f32[512,1536]{1,0:T(8,128)}, u32[]{:S(2)}) copy-start(f32[512,1536]{1,0:T(8,128)} %copy-done) | copy-start | bytes 9437188
  359.5 33.9 %copy-start.38 = (bf16[1536,24]{0,1:T(8,128)(2,1)S(1)}, bf16[1536,24]{0,1:T(8,128)(2,1)}, u32[]{:S(2)}) copy-start(bf16[1536,24]{0,1:T(8,128)(2,1)} %param.21) | copy-start | bytes 221188
  359.5 33.9 %copy-start.44 = (f32[1536]{0:T(1024)S(1)}, f32[1536]{0:T(1024)}, u32[]{:S(2)}) copy-start(f32[1536]{0:T(1024)} %param.20) | copy-start | bytes 18436
  359.5 33.9 %copy-start.48 = (f32[512]{0:T(512)S(1)}, f32[512]{0:T(512)}, u32[]{:S(2)}) copy-start(f32[512]{0:T(512)} %copy-done.47) | copy-start | bytes 6148
  404.0 20.0 %copy-start.22 = (bf16[512,768]{0,1:T(8,128)(2,1)}, bf16[512,768]{0,1:T(8,128)(2,1)S(1)}, u32[]{:S(2)}) copy-start(bf16[512,768]{0,1:T(8,128)(2,1)S(1)} %copy.144) | copy-start | bytes 2359300
  428.6 28.3 %copy-start.26 = (bf16[512,12,32]{0,2,1:T(8,128)(2,1)S(1)}, bf16[512,12,32]{0,2,1:T(8,128)(2,1)}, u32[]{:S(2)}) copy-start(bf16[512,12,32]{0,2,1:T(8,128)(2,1)} %copy-done.25) | copy-start | bytes 1179652
  428.6 28.3 %copy-start.28 = (bf16[512,12,32]{0,2,1:T(8,128)(2,1)S(1)}, bf16[512,12,32]{0,2,1:T(8,128)(2,1)}, u32[]{:S(2)}) copy-start(bf16[512,12,32]{0,2,1:T(8,128)(2,1)} %copy-done.27) | copy-start | bytes 1179652
  545.3 16.5 %copy-start.14 = (f32[512,512]{1,0:T(8,128)}, f32[512,512]{1,0:T(8,128)S(1)}, u32[]{:S(2)}) copy-start(f32[512,512]{1,0:T(8,128)S(1)} %convert_reduce_fusion) | copy-start | bytes 3145732
  564.2 35.1 %copy-start.3 = (bf16[512,1536]{1,0:T(8,128)(2,1)S(1)}, bf16[512,1536]{1,0:T(8,128)(2,1)}, u32[]{:S(2)}) copy-start(bf16[512,1536]{1,0:T(8,128)(2,1)} %param.14) | copy-start | bytes 4718596
  564.2 35.1 %copy-start.4 = (bf16[512,1536]{1,0:T(8,128)(2,1)S(1)}, bf16[512,1536]{1,0:T(8,128)(2,1)}, u32[]{:S(2)}) copy-start(bf16[512,1536]{1,0:T(8,128)(2,1)} %fusion.26.src_ref) | copy-start | bytes 4718596
  564.2 35.1 %copy-start.52 = (f32[1536]{0:T(1024)S(1)}, f32[1536]{0:T(1024)}, u32[]{:S(2)}) copy-start(f32[1536]{0:T(1024)} %param.15) | copy-start | bytes 18436
  564.2 35.1 %copy-start.54 = (f32[512]{0:T(512)S(1)}, f32[512]{0:T(512)}, u32[]{:S(2)}) copy-start(f32[512]{0:T(512)} %copy-done.53) | copy-start | bytes 6148
  (40 other events, 133.6 us)
Sparse Core Ops, SparseCore 0:
  304.4 238.4 reduce-scatter.10
  547.1 193.9 reduce-scatter.8
  745.2 193.9 reduce-scatter.6
  951.5 86.9 reduce-scatter.12

commit v4 on v3

--- a/solution.py
+++ b/solution.py
@@ -62,6 +62,14 @@
     return lax.dot_general(
         left, right, (((1,), (1,)), ((), ())), preferred_element_type=jnp.float32
     )
+
+
+def _store_split(out_ref, value):
+    cores, _, groups, rows, _ = out_ref.shape
+    for x in range(groups):
+        for c in range(cores):
+            start = (x * cores + c) * rows
+            out_ref[c, 0, x] = value[start : start + rows].astype(out_ref.dtype)
 
 
 def _expert_body(
@@ -94,24 +102,26 @@
     deo = (gc * dy).astype(bf16)
     grad_hidden = jnp.dot(deo, wd, preferred_element_type=f32)
     deo_t = (grow_ref[0] * dyt_ref[...].astype(f32)).astype(bf16)
-    gd_ref[0] = jnp.dot(deo_t, hidden, preferred_element_type=f32).astype(bf16)
+    _store_split(gd_ref, jnp.dot(deo_t, hidden, preferred_element_type=f32))
     grad_gate_act = (grad_hidden * up_act * sig * (1.0 + gate_act * (1.0 - sig))).astype(bf16)
     grad_up_act = (grad_hidden * silu).astype(bf16)
     n2t = n2t_ref[...]
-    gg_ref[0] = jnp.dot(n2t, grad_gate_act, preferred_element_type=f32).astype(bf16)
-    gu_ref[0] = jnp.dot(n2t, grad_up_act, preferred_element_type=f32).astype(bf16)
+    _store_split(gg_ref, jnp.dot(n2t, grad_gate_act, preferred_element_type=f32))
+    _store_split(gu_ref, jnp.dot(n2t, grad_up_act, preferred_element_type=f32))
     dn2_ref[...] += lax.dot_general(
         grad_gate_act, wg, nt, preferred_element_type=f32
     ) + lax.dot_general(grad_up_act, wu, nt, preferred_element_type=f32)
 
 
-def expert_kernel(n2, n2t, dy, dyt, gcol, grow, wg, wu, wd):
+def expert_kernel(n2, n2t, dy, dyt, gcol, grow, wg, wu, wd, groups):
     tokens, width = n2.shape
     experts, _, hidden = wg.shape
     f32 = jnp.float32
     whole = lambda shape: pl.BlockSpec(shape, lambda e: (0,) * len(shape))
     per_expert = lambda shape: pl.BlockSpec((1,) + shape, lambda e: (e,) + (0,) * len(shape))
     flops = experts * tokens * width * hidden * 2 * 9
+    split_rows = width // (groups * 2)
+    split = pl.BlockSpec((2, 1, groups, split_rows, hidden), lambda e: (0, e, 0, 0, 0))
     return pl.pallas_call(
         _expert_body,
         grid=(experts,),
@@ -129,17 +139,17 @@
         out_specs=[
             whole((tokens, width)),
             per_expert((tokens, 1)),
-            per_expert((width, hidden)),
-            per_expert((width, hidden)),
-            per_expert((width, hidden)),
+            split,
+            split,
+            split,
             whole((tokens, width)),
         ],
         out_shape=[
             jax.ShapeDtypeStruct((tokens, width), f32),
             jax.ShapeDtypeStruct((experts, tokens, 1), f32),
-            jax.ShapeDtypeStruct((experts, width, hidden), jnp.bfloat16),
-            jax.ShapeDtypeStruct((experts, width, hidden), jnp.bfloat16),
-            jax.ShapeDtypeStruct((experts, width, hidden), jnp.bfloat16),
+            jax.ShapeDtypeStruct((2, experts, groups, split_rows, hidden), jnp.bfloat16),
+            jax.ShapeDtypeStruct((2, experts, groups, split_rows, hidden), jnp.bfloat16),
+            jax.ShapeDtypeStruct((2, experts, groups, split_rows, hidden), jnp.bfloat16),
             jax.ShapeDtypeStruct((tokens, width), f32),
         ],
         compiler_params=pltpu.CompilerParams(
@@ -216,6 +226,14 @@
     return x.astype(jnp.float32) + other.astype(jnp.float32)
 
 
+def core_reduce(x, collective_id):
+    got = exchange(x, "core", 2, True, collective_id)
+    me = lax.axis_index("core")
+    own = lax.dynamic_index_in_dim(x, me, 0, keepdims=False)
+    other = lax.dynamic_index_in_dim(got, 1 - me, 0, keepdims=False)
+    return (own.astype(jnp.float32) + other.astype(jnp.float32)).astype(jnp.bfloat16)
+
+
 def scatter_sum_axis(x, axis, n, collective_id):
     got = exchange(x, axis, n, True, collective_id)
     me = lax.axis_index(axis)
@@ -225,6 +243,7 @@
 
 
 def per_device(
+    dpx_count,
     hidden_in,
     attn_gain,
     q_weight,
@@ -329,23 +348,22 @@
         gate_weight,
         up_weight,
         down_weight,
+        dpx_count,
     )
     cot_f32 = output_grad.astype(f32)
     moe_total = sum_axis(moe_acc.astype(bf16), "tensor", 3)
     output = (resid + moe_total).astype(bf16)
     grad_rows_all = moe_grad_rows
     gate_parts = gate_parts[:, :, 0]
-    grad_gate_out, grad_up_out, grad_down_out = (
-        lax.psum_scatter(grad_gate, ("dp", "ctx"), scatter_dimension=1, tiled=True).astype(
-            jnp.float32
-        ),
-        lax.psum_scatter(grad_up, ("dp", "ctx"), scatter_dimension=1, tiled=True).astype(
-            jnp.float32
-        ),
-        lax.psum_scatter(grad_down, ("dp", "ctx"), scatter_dimension=1, tiled=True).astype(
-            jnp.float32
-        ),
-    )
+    grad_gate_out, grad_up_out, grad_down_out = [
+        lax.psum_scatter(
+            core_reduce(g, cid).reshape(g.shape[1], -1, g.shape[4]),
+            ("dpx", "ctx"),
+            scatter_dimension=1,
+            tiled=True,
+        ).astype(jnp.float32)
+        for g, cid in ((grad_gate, 8), (grad_up, 9), (grad_down, 10))
+    ]
     gate_pair = jnp.sum(
         jnp.where(picked_onehot, jnp.transpose(gate_parts)[:, None, :], 0.0), axis=2
     )
@@ -429,24 +447,29 @@
     grad_one_rows, grad_attn_gain = norm_backward(inputs_f32, scale_one, attn_gain, grad_normed_one)
     input_grad = grad_resid + grad_one_rows
     q_cols, o_cols, k_cols = grad_q.shape[1], grad_o.shape[1], grad_k.shape[1]
-    dense_all = jnp.concatenate(
+    small = jnp.concatenate(
         [
-            grad_q.astype(bf16),
-            grad_o.astype(bf16),
-            grad_k.astype(bf16),
-            grad_v.astype(bf16),
-            grad_router.astype(bf16),
-            grad_attn_gain[:, None].astype(bf16),
-            grad_moe_gain[:, None].astype(bf16),
+            grad_router,
+            grad_attn_gain[:, None],
+            grad_moe_gain[:, None],
+            jnp.zeros((grad_router.shape[0], 128 - grad_router.shape[1] - 2), f32),
         ],
         axis=1,
     )
+    dense_all = jnp.concatenate(
+        [grad_q, grad_o, grad_k, grad_v, small], axis=1
+    ).astype(bf16)
+    width = dense_all.shape[0]
+    dense_all = jnp.transpose(
+        dense_all.reshape(dpx_count, 2, width // (2 * dpx_count), dense_all.shape[1]), (1, 0, 2, 3)
+    )
     dense_all, grad_gate_out, grad_up_out, grad_down_out = lax.optimization_barrier(
         (dense_all, grad_gate_out, grad_up_out, grad_down_out)
     )
-    dense_here = lax.psum_scatter(dense_all, ("dp", "ctx"), scatter_dimension=0, tiled=True).astype(
-        f32
-    )
+    dense_half = core_reduce(dense_all, 11)
+    dense_here = lax.psum_scatter(
+        dense_half.reshape(-1, dense_half.shape[-1]), ("dpx", "ctx"), scatter_dimension=0, tiled=True
+    ).astype(f32)
     spans = [q_cols, o_cols, k_cols, k_cols, router_weight.shape[1], 1, 1]
     cuts = [sum(spans[:i]) for i in range(len(spans) + 1)]
     pieces_out = [dense_here[:, cuts[i] : cuts[i + 1]] for i in range(len(spans))]
@@ -476,11 +499,15 @@
 
 
 def solution(mesh):
+    dp_count, ctx_count, tensor_count = (mesh.shape[a] for a in ("dp", "ctx", "tensor"))
+    split_mesh = jax.sharding.Mesh(
+        mesh.devices.reshape(dp_count // 2, 2, ctx_count, tensor_count), ("dpx", "core", "ctx", "tensor")
+    )
     return jax.shard_map(
-        per_device,
-        mesh=mesh,
+        functools.partial(per_device, dp_count // 2),
+        mesh=split_mesh,
         in_specs=(
-            P(("dp", "ctx"), None),
+            P(("dpx", "core", "ctx"), None),
             P(),
             P(None, "tensor"),
             P(None, "tensor"),
@@ -491,23 +518,23 @@
             P(None, None, "tensor"),
             P(None, None, "tensor"),
             P(None, None, "tensor"),
-            P("dp"),
-            P(("dp", "ctx"), None),
-            P(("dp", "ctx"), None),
+            P(("dpx", "core")),
+            P(("dpx", "core", "ctx"), None),
+            P(("dpx", "core", "ctx"), None),
         ),
         out_specs=(
-            P(("dp", "ctx"), None),
-            P(("dp", "ctx"), None),
-            P(("dp", "ctx")),
-            P(("dp", "ctx"), "tensor"),
-            P(("dp", "ctx"), "tensor"),
-            P(("dp", "ctx"), "tensor"),
-            P(("dp", "ctx"), "tensor"),
-            P(("dp", "ctx")),
-            P(("dp", "ctx"), None),
-            P(None, ("dp", "ctx"), "tensor"),
-            P(None, ("dp", "ctx"), "tensor"),
-            P(None, ("dp", "ctx"), "tensor"),
+            P(("dpx", "core", "ctx"), None),
+            P(("dpx", "core", "ctx"), None),
+            P(("dpx", "core", "ctx")),
+            P(("dpx", "core", "ctx"), "tensor"),
+            P(("dpx", "core", "ctx"), "tensor"),
+            P(("dpx", "core", "ctx"), "tensor"),
+            P(("dpx", "core", "ctx"), "tensor"),
+            P(("dpx", "core", "ctx")),
+            P(("dpx", "core", "ctx"), None),
+            P(None, ("dpx", "core", "ctx"), "tensor"),
+            P(None, ("dpx", "core", "ctx"), "tensor"),
+            P(None, ("dpx", "core", "ctx"), "tensor"),
         ),
         check_vma=False,
     )

time: 1060 us -> 978 us (0.923)
  waiting for transfers between devices: 374 us -> 212 us
  other arithmetic: 68.1 us -> 116 us
  Pallas kernels: 368 us -> 415 us
  local copies, waits for them, and re-layouts: 81.6 us -> 64.1 us
    reduce_scatter x3, waiting for transfers between devices: 291 us -> 135 us  [per_device(): lax.psum_scatter(core_reduce(g, cid).reshape(g.shape[1], -1, g.shape[4]),...]
    pallas_call x7 -> x11, Pallas kernels: 255 us -> 302 us  [exchange(): pl.pallas_call(functools.partial(_exchange_body, axis, n, per_peer), out_...]
    convert_element_type x4 -> x10, other arithmetic: 8.94 us -> 49.7 us  [the longest x4 40.7 us: core_reduce(): (own.astype(jnp.float32) + other.astype(jnp.float32)).astype(jnp.bfloat16)]
    concatenate x1 -> x8, local copies, waits for them, and re-layouts: 30.9 us -> 14.3 us  [per_device(): jnp.concatenate([grad_q, grad_o, grad_k, grad_v, small], axis=1)]
    dot_general x0 -> x2, other arithmetic: none -> 12.4 us  [contract_rows(): lax.dot_general(left, right, (((0,), (0,)), ((), ())), preferred_element_...]
    unnamed x127 -> x116, local copies, waits for them, and re-layouts: 26.1 us -> 14.3 us
  transfers between devices with their start and end apart: 4 -> 4, of which waited for: 3 -> 2; matrix products, arithmetic and copies ran while one was open for 15% -> 19% of each run, Pallas kernels for 17% -> 21%
where the time goes in v4:
time: 978 us; the launch traced here: 969 us
  Pallas kernels  415 us (42%)
  waiting for transfers between devices  212 us (22%)
  matrix products  147 us (15%)
  other arithmetic  116 us (12%)
  local copies, waits for them, and re-layouts  64.1 us (7%)
  between operations  15.2 us (2%)
    pallas_call x11, Pallas kernels, exchange(): pl.pallas_call(functools.partial(_exchange_body, axis, n, per_peer), out_...  302 us
    reduce_scatter x3, waiting for transfers between devices, per_device(): lax.psum_scatter(core_reduce(g, cid).reshape(g.shape[1], -1, g.shape[4]),...  135 us
    pallas_call x1, Pallas kernels, expert_kernel(): pl.pallas_call(_expert_body, grid=(experts,), in_specs=[whole((tokens, wi...  113 us
    unnamed x5, waiting for transfers between devices  76.8 us
    convert_element_type x4, other arithmetic, core_reduce(): (own.astype(jnp.float32) + other.astype(jnp.float32)).astype(jnp.bfloat16)  40.7 us
    dot_general x1, matrix products, per_device(): jnp.einsum('kgtd,nkd->kgtn', grad_attn_grouped, value_piece, preferred_el...  28.2 us
    dot_general x1, matrix products, per_device(): jnp.einsum('kgtn,nkd->kgtd', weights.astype(bf16), value_piece, preferred...  22.7 us
    reduce_sum x1, other arithmetic, per_device(): run_sum = jnp.sum(weights, axis=-1)  22 us
  transfers between devices with their start and end apart: 4, of which 2 were waited for; matrix products, arithmetic and copies ran while one was open for 19% of the time, Pallas kernels for 21%

profile of v4, /device:TPU:0, one launch (start us, length us, event | category | flops | bytes accessed | tf_op | source)
XLA Modules:
  0.0 969.1 jit_solution(4293343967688258232)
XLA Ops:
  14.3 40.1 %shard_map.229 = bf16[4,512,512]{2,1,0:T(8,128)(2,1)} custom-call(bf16[512,512]{1,0:T(8,128)(2,1)} %pad_maximum_fusion.2.src_ref), custom_call_target="tpu_custom_call" | custom-call | bytes 3145728 | tf_op jit(solution)/shard_map/pallas_call | solution.py:206
  69.8 20.4 %fusion.2 = (f32[4,3,512]{2,1,0:T(4,128)S(1)}, f32[4,2048,512,3]{2,1,3,0:T(8,128)}) fusion(pred[512,2048]{0,1:T(8,128)(4,1)S(1)} %fusion.12, bf16[512,4,3,32]{0,3,2,1:T(8,128)(2,1)S(1)} %bitcast.193, bf16[512,4,3,32]{0,3,2,1:T(8,128)(2,1)S(1)} %bitcast.191, bf16[2048,4,64,1]{0,2,1,3:T(8,128)(2,1)} %reshape.363), kind=kOutput, calls=%fused_computation.6 | convolution fusion | flops 1649928192 | bytes 53239808 | tf_op jit(solution)/shard_map/tkgd,nkd->kgtn/dot_general | solution.py:309
  90.8 22.0 %fusion.4 = f32[4,3,512]{2,1,0:T(4,128)S(1)} fusion(f32[4,2048,512,3]{2,1,3,0:T(8,128)} %get-tuple-element.125, f32[4,3,512]{2,1,0:T(4,128)S(1)} %broadcast_maximum_fusion, pred[512,2048]{0,1:T(8,128)(4,1)S(1)} %fusion.12), kind=kLoop, calls=%fused_computation.8 | loop fusion | flops 62908416 | bytes 51429376 | tf_op jit(solution)/shard_map/reduce_sum | solution.py:315
  112.9 22.7 %fusion.40 = (bf16[512,4,3,64]{0,3,2,1:T(8,128)(2,1)S(1)}, f32[4,3,512,64]{2,3,1,0:T(8,128)}) fusion(f32[512,4,3]{0,2,1:T(4,128)S(1)} %bitcast.202, f32[4,2048,512,3]{2,1,3,0:T(8,128)} %get-tuple-element.125, f32[4,3,512]{2,1,0:T(4,128)S(1)} %broadcast_maximum_fusion, pred[512,2048]{0,1:T(8,128)(4,1)S(1)} %fusion.12, bf16[2048,4,64,1]{0,2,1,3:T(8,128)(2,1)} %reshape.364), kind=kOutput, calls=%fused_computation.70 | convolution fusion | flops 1674313728 | bytes 54837248 | tf_op jit(solution)/shard_map/kgtn,nkd->kgtd/dot_general | solution.py:316
  140.7 36.6 %shard_map.230 = bf16[2,512,1536]{2,1,0:T(8,128)(2,1)} custom-call(bf16[512,1536]{1,0:T(8,128)(2,1)} %convolution_convert_fusion.src_ref), custom_call_target="tpu_custom_call" | custom-call | bytes 3145728 | tf_op jit(solution)/shard_map/pallas_call | solution.py:206
  192.7 113.0 %shard_map.231 = (f32[512,1536]{1,0:T(8,128)}, f32[24,512,1]{2,1,0:T(8,128)}, bf16[2,24,2,384,256]{4,3,2,1,0:T(8,128)(2,1)}, bf16[2,24,2,384,256]{4,3,2,1,0:T(8,...) custom-call(bf16[512,1536]{1,0:T(8,128)(2,1)} %copy-done.5, bf16[1536,512]{1,0:T(8,128)(2,1)} %copy.188.n2t_ref, ...), custom_call_target="tpu_custom_call" | custom-call | flops 86973087744 | bytes 125829120 | tf_op jit(solution)/shard_map/pallas_call | solution.py:125
  305.7 15.1 %shard_map.237 = bf16[2,24,2,384,256]{4,3,2,1,0:T(8,128)(2,1)} custom-call(bf16[2,24,2,384,256]{4,3,2,1,0:T(8,128)(2,1)} %get-tuple-element.25.src_ref), custom_call_target="tpu_custom_call" | custom-call | bytes 18874368 | tf_op jit(solution)/shard_map/pallas_call | solution.py:206
  320.8 11.9 %add_convert_fusion.2 = bf16[1,24,2,384,256]{4,3,2,1,0:T(8,128)(2,1)} fusion(bf16[2,24,2,384,256]{4,3,2,1,0:T(8,128)(2,1)} %shard_map.237, s32[]{:T(128)S(6)} %select_n.67, bf16[2,24,2,384,256]{4,3,2,1,0:T(8,128)(2,1)} %get-tuple-element.25.src_ref, s32[]{:T(128)S(6)} %select_n.66), kind=kLoop, calls=%fused_computation.16 | loop fusion | flops 18874368 | bytes 28311560 | tf_op jit(solution)/shard_map/convert_element_type | solution.py:234
  332.8 15.1 %shard_map.238 = bf16[2,24,2,384,256]{4,3,2,1,0:T(8,128)(2,1)} custom-call(bf16[2,24,2,384,256]{4,3,2,1,0:T(8,128)(2,1)} %get-tuple-element.26.src_ref), custom_call_target="tpu_custom_call" | custom-call | bytes 18874368 | tf_op jit(solution)/shard_map/pallas_call | solution.py:206
  347.8 11.2 %add_convert_fusion.1 = bf16[1,24,2,384,256]{4,3,2,1,0:T(8,128)(2,1)} fusion(bf16[2,24,2,384,256]{4,3,2,1,0:T(8,128)(2,1)} %shard_map.238, s32[]{:T(128)S(6)} %select_n.67, bf16[2,24,2,384,256]{4,3,2,1,0:T(8,128)(2,1)} %get-tuple-element.26.src_ref, s32[]{:T(128)S(6)} %select_n.66), kind=kLoop, calls=%fused_computation.15 | loop fusion | flops 18874368 | bytes 28311560 | tf_op jit(solution)/shard_map/convert_element_type | solution.py:234
  359.1 15.1 %shard_map.239 = bf16[2,24,2,384,256]{4,3,2,1,0:T(8,128)(2,1)} custom-call(bf16[2,24,2,384,256]{4,3,2,1,0:T(8,128)(2,1)} %get-tuple-element.27.src_ref), custom_call_target="tpu_custom_call" | custom-call | bytes 18874368 | tf_op jit(solution)/shard_map/pallas_call | solution.py:206
  374.2 12.1 %add_convert_fusion = bf16[1,24,2,384,256]{4,3,2,1,0:T(8,128)(2,1)} fusion(bf16[2,24,2,384,256]{4,3,2,1,0:T(8,128)(2,1)} %shard_map.239, s32[]{:T(128)S(6)} %select_n.67, bf16[2,24,2,384,256]{4,3,2,1,0:T(8,128)(2,1)} %get-tuple-element.27.src_ref, s32[]{:T(128)S(6)} %select_n.66), kind=kLoop, calls=%fused_computation.14 | loop fusion | flops 18874368 | bytes 28311560 | tf_op jit(solution)/shard_map/convert_element_type | solution.py:234
  408.1 35.9 %shard_map.232 = bf16[2,512,1536]{2,1,0:T(8,128)(2,1)} custom-call(bf16[512,1536]{1,0:T(8,128)(2,1)} %convert_element_type.254.src_ref), custom_call_target="tpu_custom_call" | custom-call | bytes 3145728 | tf_op jit(solution)/shard_map/pallas_call | solution.py:206
  444.1 35.0 %shard_map.233 = bf16[2,512,1536]{2,1,0:T(8,128)(2,1)} custom-call(bf16[512,1536]{1,0:T(8,128)(2,1)} %convert_element_type.260.src_ref), custom_call_target="tpu_custom_call" | custom-call | bytes 3145728 | tf_op jit(solution)/shard_map/pallas_call | solution.py:206
  484.0 6.4 convert_bitcast_fusion
  499.5 19.9 %fusion.37 = bf16[2048,4,64]{0,2,1:T(8,128)(2,1)} fusion(bf16[4,3,512,64]{2,3,1,0:T(8,128)(2,1)S(1)} %bitcast.182, f32[4,2048,512,3]{2,1,3,0:T(8,128)} %get-tuple-element.125, f32[4,3,512]{2,1,0:T(4,128)S(1)} %log_add_fusion, pred[512,2048]{0,1:T(8,128)(4,1)} %copy-done.11), kind=kOutput, calls=%fused_computation.61 | convolution fusion | flops 1661468672 | bytes 53239808 | tf_op jit(solution)/shard_map/kgtn,kgtd->nkd/dot_general | solution.py:405
  524.1 28.2 %multiply_convert_fusion = bf16[4,3,512,2048]{2,3,1,0:T(8,128)(2,1)} fusion(f32[4,2048,512,3]{2,1,3,0:T(8,128)} %get-tuple-element.125, f32[4,3,512]{2,1,0:T(4,128)S(1)} %multiply_reduce_fusion.3, f32[4,3,512]{2,1,0:T(4,128)S(1)} %log_add_fusion, pred[512,2048]{0,1:T(8,128)(4,1)S(1)} %copy-done.12, bf16[4,3,512,64]{2,3,1,0:T(8,128)(2,1)} %bitcast.184, ...), kind=kOutput, calls=%fused_computation.4 | convolution fusion | flops 1686110208 | bytes 78430208 | tf_op jit(solution)/shard_map/kgtd,nkd->kgtn/dot_general | solution.py:395
  552.3 13.0 %fusion.36 = bf16[2048,4,64]{0,2,1:T(8,128)(2,1)S(1)} fusion(bf16[4,3,512,2048]{2,3,1,0:T(8,128)(2,1)} %multiply_convert_fusion, bf16[512,4,3,32]{0,3,2,1:T(8,128)(2,1)S(1)} %bitcast.194, bf16[512,4,3,32]{0,3,2,1:T(8,128)(2,1)S(1)} %bitcast.192), kind=kOutput, calls=%fused_computation.60 | convolution fusion | flops 1613234176 | bytes 27000832 | tf_op jit(solution)/shard_map/kgtn,tkgd->nkd/dot_general | solution.py:402
  568.6 61.8 %shard_map.235 = bf16[4,512,512]{2,1,0:T(8,128)(2,1)} custom-call(bf16[4,512,512]{2,1,0:T(8,128)(2,1)} %pad_maximum_fusion.src_ref), custom_call_target="tpu_custom_call" | custom-call | bytes 3145728 | tf_op jit(solution)/shard_map/pallas_call | solution.py:206
  637.5 10.4 %convolution_multiply_fusion = f32[4,3,512,64]{2,3,1,0:T(8,128)S(1)} fusion(bf16[4,3,512,2048]{2,3,1,0:T(8,128)(2,1)} %multiply_convert_fusion, bf16[2048,4,64,1]{0,2,1,3:T(8,128)(2,1)S(1)} %copy-done.15), kind=kOutput, calls=%fused_computation.73 | convolution fusion | flops 1611005952 | bytes 27787264 | tf_op jit(solution)/shard_map/kgtn,nkd->kgtd/dot_general | solution.py:399
  654.3 35.9 %shard_map.236 = bf16[2,512,1536]{2,1,0:T(8,128)(2,1)} custom-call(bf16[512,1536]{1,0:T(8,128)(2,1)} %fusion.26.src_ref), custom_call_target="tpu_custom_call" | custom-call | bytes 3145728 | tf_op jit(solution)/shard_map/pallas_call | solution.py:206
  712.8 11.1 %concatenate.58 = bf16[2,2,384,2176]{3,2,0,1:T(8,128)(2,1)} concatenate(bf16[2,2,384,768]{3,2,0,1:T(8,128)(2,1)} %convolution_convert_fusion.4, bf16[2,2,384,768]{3,2,0,1:T(8,128)(2,1)} %convolution_convert_fusion.3, bf16[2,2,384,256]{3,2,0,1:T(8,128)(2,1)S(1)} %convolution_convert_fusion.5, bf16[2,2,384,256]{3,2,0,1:T(8,128)(2,1)S(1)} %copy-done.16, ...), dimensions={3} | concatenate | bytes 13369344 | tf_op jit(solution)/shard_map/concatenate | solution.py:459
  729.7 135.2 %reduce-scatter.11.cloned.1.call-done = bf16[24,96,256]{2,1,0:T(8,128)(2,1)} async-done(((bf16[24,768,256]{2,1,0:T(8,128)(2,1)}), bf16[24,96,256]{2,1,0:T(8,128)(2,1)}) %reduce-scatter.11.cloned.1.call-update) | async-done | bytes 1179664 | tf_op jit(solution)/shard_map/reduce_scatter | solution.py:359
  879.6 76.7 %reduce-scatter.13.cloned.1.call-done = bf16[96,2176]{1,0:T(8,128)(2,1)} async-done(((bf16[768,2176]{1,0:T(8,128)(2,1)}), bf16[96,2176]{1,0:T(8,128)(2,1)}) %reduce-scatter.13.cloned.1.call-update) | async-done | bytes 417808
  (225 shorter events, 149.1 us)
Async XLA Ops:
  7.2 716.6 %reduce-scatter.7.cloned.1.call-start = ((), (), s32[]{:S(2)}) async-start(), calls=%async_computation.4 | async-start | bytes 10616832 | tf_op jit(solution)/shard_map/reduce_scatter | solution.py:359
  9.2 56.0 %copy-start.49 = (f32[512]{0:T(512)}, f32[512]{0:T(512)S(1)}, u32[]{:S(2)}) copy-start(f32[512]{0:T(512)S(1)} %add_rsqrt_fusion.1) | copy-start | bytes 6148
  13.3 55.2 %copy-start.19 = (f32[512,32]{0,1:T(8,128)}, f32[512,32]{0,1:T(8,128)S(1)}, u32[]{:S(2)}) copy-start(f32[512,32]{0,1:T(8,128)S(1)} %get-tuple-element.123) | copy-start | bytes 196612
  68.7 21.5 %copy-start.22 = (bf16[512,12,32]{0,2,1:T(8,128)(2,1)}, bf16[512,12,32]{0,2,1:T(8,128)(2,1)S(1)}, u32[]{:S(2)}) copy-start(bf16[512,12,32]{0,2,1:T(8,128)(2,1)S(1)} %get-tuple-element.107) | copy-start | bytes 1179652
  68.7 21.5 %copy-start.24 = (bf16[512,12,32]{0,2,1:T(8,128)(2,1)}, bf16[512,12,32]{0,2,1:T(8,128)(2,1)S(1)}, u32[]{:S(2)}) copy-start(bf16[512,12,32]{0,2,1:T(8,128)(2,1)S(1)} %get-tuple-element.108) | copy-start | bytes 1179652
  69.7 43.1 %copy-start.11 = (pred[512,2048]{0,1:T(8,128)(4,1)}, pred[512,2048]{0,1:T(8,128)(4,1)S(1)}, u32[]{:S(2)}) copy-start(pred[512,2048]{0,1:T(8,128)(4,1)S(1)} %fusion.12) | copy-start | bytes 3145732
  112.9 22.7 %copy-start.33 = (f32[4,3,512]{2,1,0:T(4,128)}, f32[4,3,512]{2,1,0:T(4,128)S(1)}, u32[]{:S(2)}) copy-start(f32[4,3,512]{2,1,0:T(4,128)S(1)} %fusion.4) | copy-start | bytes 73732
  140.7 36.6 %copy-start.10 = (bf16[512,1536]{1,0:T(8,128)(2,1)S(1)}, bf16[512,1536]{1,0:T(8,128)(2,1)}, u32[]{:S(2)}) copy-start(bf16[512,1536]{1,0:T(8,128)(2,1)} %convolution_convert_fusion.src_ref) | copy-start | bytes 4718596
  186.0 6.7 copy-start.45
  186.1 6.6 copy-start.13
  332.7 394.1 %reduce-scatter.9.cloned.1.call-start = ((), (), s32[]{:S(2)}) async-start(), calls=%async_computation.5 | async-start | bytes 10616832 | tf_op jit(solution)/shard_map/reduce_scatter | solution.py:359
  359.1 505.8 %reduce-scatter.11.cloned.1.call-start = ((), (), s32[]{:S(2)}) async-start(), calls=%async_computation.6 | async-start | bytes 10616832 | tf_op jit(solution)/shard_map/reduce_scatter | solution.py:359
  386.3 570.0 %reduce-scatter.13.cloned.1.call-start = ((), (), s32[]{:S(2)}) async-start(), calls=%async_computation.7 | async-start | bytes 3760128
  389.7 11.3 %copy-start.14 = (f32[512,8]{1,0:T(8,128)S(1)}, f32[512,8]{1,0:T(8,128)}, u32[]{:S(2)}) copy-start(f32[512,8]{1,0:T(8,128)} %copy-done.13) | copy-start | bytes 49156
  389.7 11.3 %copy-start.46 = (f32[512]{0:T(512)S(1)}, f32[512]{0:T(512)}, u32[]{:S(2)}) copy-start(f32[512]{0:T(512)} %copy-done.45) | copy-start | bytes 6148
  389.7 13.9 %copy-start.6 = (bf16[512,1536]{1,0:T(8,128)(2,1)S(1)}, bf16[512,1536]{1,0:T(8,128)(2,1)}, u32[]{:S(2)}) copy-start(bf16[512,1536]{1,0:T(8,128)(2,1)} %copy-done.5) | copy-start | bytes 4718596
  444.0 35.1 %copy-start.1 = (f32[512,1536]{1,0:T(8,128)S(1)}, f32[512,1536]{1,0:T(8,128)}, u32[]{:S(2)}) copy-start(f32[512,1536]{1,0:T(8,128)} %copy-done) | copy-start | bytes 9437188
  444.1 35.1 %copy-start.36 = (bf16[1536,24]{0,1:T(8,128)(2,1)S(1)}, bf16[1536,24]{0,1:T(8,128)(2,1)}, u32[]{:S(2)}) copy-start(bf16[1536,24]{0,1:T(8,128)(2,1)} %param.21) | copy-start | bytes 221188
  444.1 35.1 %copy-start.40 = (f32[1536]{0:T(1024)S(1)}, f32[1536]{0:T(1024)}, u32[]{:S(2)}) copy-start(f32[1536]{0:T(1024)} %param.20) | copy-start | bytes 18436
  444.1 35.1 %copy-start.44 = (f32[512]{0:T(512)S(1)}, f32[512]{0:T(512)}, u32[]{:S(2)}) copy-start(f32[512]{0:T(512)} %copy-done.43) | copy-start | bytes 6148
  499.5 20.0 %copy-start.18 = (bf16[512,768]{0,1:T(8,128)(2,1)}, bf16[512,768]{0,1:T(8,128)(2,1)S(1)}, u32[]{:S(2)}) copy-start(bf16[512,768]{0,1:T(8,128)(2,1)S(1)} %copy.192) | copy-start | bytes 2359300
  524.1 28.2 %copy-start.23 = (bf16[512,12,32]{0,2,1:T(8,128)(2,1)S(1)}, bf16[512,12,32]{0,2,1:T(8,128)(2,1)}, u32[]{:S(2)}) copy-start(bf16[512,12,32]{0,2,1:T(8,128)(2,1)} %copy-done.22) | copy-start | bytes 1179652
  524.1 28.2 %copy-start.25 = (bf16[512,12,32]{0,2,1:T(8,128)(2,1)S(1)}, bf16[512,12,32]{0,2,1:T(8,128)(2,1)}, u32[]{:S(2)}) copy-start(bf16[512,12,32]{0,2,1:T(8,128)(2,1)} %copy-done.24) | copy-start | bytes 1179652
  654.3 35.9 %copy-start.4 = (bf16[512,1536]{1,0:T(8,128)(2,1)S(1)}, bf16[512,1536]{1,0:T(8,128)(2,1)}, u32[]{:S(2)}) copy-start(bf16[512,1536]{1,0:T(8,128)(2,1)} %fusion.26.src_ref) | copy-start | bytes 4718596
  (35 other events, 108.2 us)
Sparse Core Ops, SparseCore 0:
  332.8 173.6 reduce-scatter.6
  510.1 188.5 reduce-scatter.8
  702.3 162.4 reduce-scatter.10
  879.7 76.5 reduce-scatter.12

commit v5 on v4

--- a/solution.py
+++ b/solution.py
@@ -242,6 +242,86 @@
     return jnp.sum(full.astype(jnp.float32), axis=0)
 
 
+def _flash_body(ctx_ref, q_ref, k_ref, v_ref, qseg_ref, qpos_ref, kseg_ref, o_ref, lse_ref, m_sc, l_sc, acc_sc):
+    f32 = jnp.float32
+    block = pl.program_id(1)
+
+    @pl.when(block == 0)
+    def _():
+        m_sc[...] = jnp.full_like(m_sc, NEGATIVE)
+        l_sc[...] = jnp.zeros_like(l_sc)
+        acc_sc[...] = jnp.zeros_like(acc_sc)
+
+    @pl.when(block <= ctx_ref[0])
+    def _():
+        keys = k_ref[0]
+        width = keys.shape[0]
+        scores = lax.dot_general(
+            q_ref[0], keys, (((1,), (1,)), ((), ())), preferred_element_type=f32
+        ) * (1.0 / math.sqrt(HEAD_SIZE))
+        key_pos = block * width + lax.broadcasted_iota(jnp.int32, (1, width), 1)
+        allowed = (qseg_ref[...] == kseg_ref[...]) & (key_pos <= qpos_ref[...])
+        scores = jnp.where(allowed, scores, NEGATIVE)
+        m_old = m_sc[...]
+        m_new = jnp.maximum(m_old, jnp.max(scores, axis=1, keepdims=True))
+        alpha = jnp.exp(m_old - m_new)
+        weights = jnp.where(allowed, jnp.exp(scores - m_new), 0.0)
+        l_sc[...] = alpha * l_sc[...] + jnp.sum(weights, axis=1, keepdims=True)
+        acc_sc[...] = alpha * acc_sc[...] + jnp.dot(
+            weights.astype(jnp.bfloat16), v_ref[0], preferred_element_type=f32
+        )
+        m_sc[...] = m_new
+
+    @pl.when(block == pl.num_programs(1) - 1)
+    def _():
+        o_ref[0] = acc_sc[...] / l_sc[...]
+        lse_ref[0] = m_sc[...] + jnp.log(l_sc[...])
+
+
+def flash_forward(ctx_index, q, k, v, qseg, qpos, kseg, width):
+    heads, rows, depth = q.shape
+    blocks = k.shape[1] // width
+    f32 = jnp.float32
+    capped = lambda h, b, c: (h, jnp.minimum(b, c[0]), 0)
+    grid_spec = pltpu.PrefetchScalarGridSpec(
+        num_scalar_prefetch=1,
+        grid=(heads, blocks),
+        in_specs=[
+            pl.BlockSpec((1, rows, depth), lambda h, b, c: (h, 0, 0)),
+            pl.BlockSpec((1, width, depth), capped),
+            pl.BlockSpec((1, width, depth), capped),
+            pl.BlockSpec((rows, 1), lambda h, b, c: (0, 0)),
+            pl.BlockSpec((rows, 1), lambda h, b, c: (0, 0)),
+            pl.BlockSpec((1, width), lambda h, b, c: (0, jnp.minimum(b, c[0]))),
+        ],
+        out_specs=[
+            pl.BlockSpec((1, rows, depth), lambda h, b, c: (h, 0, 0)),
+            pl.BlockSpec((1, rows, 1), lambda h, b, c: (h, 0, 0)),
+        ],
+        scratch_shapes=[
+            pltpu.VMEM((rows, 1), f32),
+            pltpu.VMEM((rows, 1), f32),
+            pltpu.VMEM((rows, depth), f32),
+        ],
+    )
+    return pl.pallas_call(
+        _flash_body,
+        grid_spec=grid_spec,
+        out_shape=[
+            jax.ShapeDtypeStruct((heads, rows, depth), f32),
+            jax.ShapeDtypeStruct((heads, rows, 1), f32),
+        ],
+        compiler_params=pltpu.CompilerParams(
+            dimension_semantics=("arbitrary", "arbitrary"), vmem_limit_bytes=48 * 1024 * 1024
+        ),
+        cost_estimate=pl.CostEstimate(
+            flops=heads * rows * k.shape[1] * depth * 4,
+            transcendentals=heads * rows * k.shape[1],
+            bytes_accessed=(q.size + k.size + v.size) * 2 + heads * rows * depth * 4,
+        ),
+    )(jnp.reshape(ctx_index, (1,)).astype(jnp.int32), q, k, v, qseg, qpos, kseg)
+
+
 def per_device(
     dpx_count,
     hidden_in,
@@ -270,6 +350,7 @@
     token_positions = ctx_index * token_count + jnp.arange(token_count, dtype=jnp.int32)
     segment_here = lax.dynamic_slice_in_dim(segments, ctx_index * token_count, token_count)
     inputs_f32 = hidden_in.astype(f32)
+    o_full = lax.all_gather(o_weight, "tensor", axis=1, tiled=True)
     normed_f32, scale_one = normalize(inputs_f32, attn_gain)
     normed_one = normed_f32.astype(bf16)
     query_rows = jnp.dot(normed_one, q_weight, preferred_element_type=f32).reshape(
@@ -299,34 +380,33 @@
 
     ctx_count = segments.shape[0] // token_count
     kv_both = gather_axis(jnp.concatenate([key_flat, value_flat], axis=1), "ctx", ctx_count, 1)
-    run_max = jnp.full((kv_local, group_size, token_count), NEGATIVE, f32)
     piece_rows = ctx_count * token_count
     kv_width = kv_local * HEAD_SIZE
     key_piece = kv_both[:, :, :kv_width].reshape(piece_rows, kv_local, HEAD_SIZE)
     value_piece = kv_both[:, :, kv_width:].reshape(piece_rows, kv_local, HEAD_SIZE)
-    allowed = piece_mask(piece_rows)
-    scores = (
-        jnp.einsum("tkgd,nkd->kgtn", query_grouped, key_piece, preferred_element_type=f32)
-        * score_scale
-    )
-    scores = jnp.where(allowed, scores, NEGATIVE)
-    new_max = jnp.maximum(run_max, jnp.max(scores, axis=-1))
-    weights = jnp.where(allowed, jnp.exp(scores - new_max[..., None]), 0.0)
-    run_sum = jnp.sum(weights, axis=-1)
-    accumulated = jnp.einsum(
-        "kgtn,nkd->kgtd", weights.astype(bf16), value_piece, preferred_element_type=f32
-    )
-    fold_state = (new_max, run_sum, accumulated)
-    run_max, run_sum, accumulated = fold_state
-    attn_grouped = accumulated / run_sum[..., None]
-    log_sum = run_max + jnp.log(run_sum)
+    row_segments = jnp.tile(segment_here, group_size)[:, None]
+    row_positions = jnp.tile(token_positions, group_size)[:, None]
+    attn_rows, lse_rows = flash_forward(
+        ctx_index,
+        jnp.transpose(query_grouped, (1, 2, 0, 3)).reshape(kv_local, group_size * token_count, HEAD_SIZE),
+        jnp.transpose(key_piece, (1, 0, 2)),
+        jnp.transpose(value_piece, (1, 0, 2)),
+        row_segments,
+        row_positions,
+        segments[None, :],
+        token_count,
+    )
+    attn_grouped = attn_rows.reshape(kv_local, group_size, token_count, HEAD_SIZE)
+    log_sum = lse_rows.reshape(kv_local, group_size, token_count)
     attn_bf = (
         jnp.transpose(attn_grouped, (2, 0, 1, 3))
         .reshape(token_count, heads_local * HEAD_SIZE)
         .astype(bf16)
     )
-    attn_partial = contract_cols(attn_bf, o_weight)
-    mixed_attn = sum_axis(attn_partial.astype(bf16), "tensor", 2)
+    tensor_count = o_weight.shape[0] // o_weight.shape[1]
+    attn_all = gather_axis(attn_bf, "tensor", tensor_count, 2)
+    attn_full = jnp.transpose(attn_all, (1, 0, 2)).reshape(token_count, tensor_count * attn_bf.shape[1])
+    mixed_attn = contract_cols(attn_full, o_full)
     resid = inputs_f32 + mixed_attn
     normed_two_f32, scale_two = normalize(resid, moe_gain)
     normed_two = normed_two_f32.astype(bf16)

time: 978 us -> 937 us (0.958)
  waiting for transfers between devices: 212 us -> 177 us
  matrix products: 147 us -> 118 us
  Pallas kernels: 415 us -> 443 us
  other arithmetic: 116 us -> 90.4 us
  local copies, waits for them, and re-layouts: 64.1 us -> 88.8 us
    reduce_scatter x3, waiting for transfers between devices: 135 us -> 99.9 us  [per_device(): lax.psum_scatter(core_reduce(g, cid).reshape(g.shape[1], -1, g.shape[4]),...]
    dot_general x1 -> x0, matrix products: 22.7 us -> none  [per_device(): jnp.einsum('kgtn,nkd->kgtd', weights.astype(bf16), value_piece, preferred...]
    reduce_sum x1 -> x0, other arithmetic: 22 us -> none  [per_device(): run_sum = jnp.sum(weights, axis=-1)]
    pallas_call x0 -> x1, Pallas kernels: none -> 17 us  [flash_forward(): pl.pallas_call(_flash_body, grid_spec=grid_spec, out_shape=[jax.ShapeDtyp...]
    pallas_call x11, Pallas kernels: 302 us -> 313 us  [exchange(): pl.pallas_call(functools.partial(_exchange_body, axis, n, per_peer), out_...]
    unnamed x116 -> x158, local copies, waits for them, and re-layouts: 14.3 us -> 23.6 us
    unnamed x5 -> x6, waiting for transfers between devices: 76.8 us -> 77.3 us
  transfers between devices with their start and end apart: 4 -> 5, of which waited for: 2 -> 2; matrix products, arithmetic and copies ran while one was open for 19% -> 26% of each run, Pallas kernels for 21% -> 33%
where the time goes in v5:
time: 937 us; the launch traced here: 933 us
  Pallas kernels  443 us (47%)
  waiting for transfers between devices  177 us (19%)
  matrix products  118 us (13%)
  other arithmetic  90.4 us (10%)
  local copies, waits for them, and re-layouts  88.8 us (9%)
  between operations  15.2 us (2%)
    pallas_call x11, Pallas kernels, exchange(): pl.pallas_call(functools.partial(_exchange_body, axis, n, per_peer), out_...  313 us
    pallas_call x1, Pallas kernels, expert_kernel(): pl.pallas_call(_expert_body, grid=(experts,), in_specs=[whole((tokens, wi...  113 us
    reduce_scatter x3, waiting for transfers between devices, per_device(): lax.psum_scatter(core_reduce(g, cid).reshape(g.shape[1], -1, g.shape[4]),...  99.9 us
    unnamed x6, waiting for transfers between devices  77.3 us
    convert_element_type x4, other arithmetic, core_reduce(): (own.astype(jnp.float32) + other.astype(jnp.float32)).astype(jnp.bfloat16)  41.4 us
    dot_general x1, matrix products, per_device(): jnp.einsum('kgtd,nkd->kgtn', grad_attn_grouped, value_piece, preferred_el...  28.1 us
    unnamed x158, local copies, waits for them, and re-layouts  23.6 us
    dot_general x1, matrix products, per_device(): jnp.einsum('tkgd,nkd->kgtn', query_grouped, key_piece, preferred_element_...  20.2 us
  transfers between devices with their start and end apart: 5, of which 2 were waited for; matrix products, arithmetic and copies ran while one was open for 26% of the time, Pallas kernels for 33%

profile of v5, /device:TPU:0, one launch (start us, length us, event | category | flops | bytes accessed | tf_op | source)
XLA Modules:
  0.0 932.6 jit_solution(10595819142393984970)
XLA Ops:
  12.5 40.1 %shard_map.229 = bf16[4,512,512]{2,1,0:T(8,128)(2,1)} custom-call(bf16[512,512]{1,0:T(8,128)(2,1)} %pad_maximum_fusion.2.src_ref), custom_call_target="tpu_custom_call" | custom-call | bytes 3145728 | tf_op jit(solution)/shard_map/pallas_call | solution.py:206
  74.0 17.0 %shard_map.230 = (f32[4,1536,64]{2,1,0:T(8,128)}, f32[4,1536,1]{2,1,0:T(8,128)}) custom-call(s32[1]{0:T(128)} %bitcast.ctx_ref, bf16[4,1536,64]{2,1,0:T(8,128)(2,1)S(1)} %bitcast.176, bf16[4,2048,64]{2,1,0:T(8,128)(2,1)S(1)} %bitcast.175, bf16[4,2048,64]{2,1,0:T(8,128)(2,1)} %bitcast.203, s32[1536,1]{1,0:T(8,128)S(1)} %bitcast.177, s32[1536,1]{1,0:T(8,128)S(1)} %bitcast.178, ...), custom_call_target="tpu_custom_call" | custom-call | flops 3221225472 | bytes 4456448 | tf_op jit(solution)/shard_map/pallas_call | solution.py:307
  94.9 19.7 %shard_map.231 = bf16[2,512,768]{2,1,0:T(8,128)(2,1)} custom-call(bf16[512,768]{1,0:T(8,128)(2,1)} %copy.218.src_ref), custom_call_target="tpu_custom_call" | custom-call | bytes 1572864 | tf_op jit(solution)/shard_map/pallas_call | solution.py:206
  134.8 112.5 %shard_map.232 = (f32[512,1536]{1,0:T(8,128)}, f32[24,512,1]{2,1,0:T(8,128)}, bf16[2,24,2,384,256]{4,3,2,1,0:T(8,128)(2,1)}, bf16[2,24,2,384,256]{4,3,2,1,0:T(8,...) custom-call(bf16[512,1536]{1,0:T(8,128)(2,1)} %copy-done.7, bf16[1536,512]{1,0:T(8,128)(2,1)} %copy.226.n2t_ref, ...), custom_call_target="tpu_custom_call" | custom-call | flops 86973087744 | bytes 125829120 | tf_op jit(solution)/shard_map/pallas_call | solution.py:125
  247.3 15.1 %shard_map.238 = bf16[2,24,2,384,256]{4,3,2,1,0:T(8,128)(2,1)} custom-call(bf16[2,24,2,384,256]{4,3,2,1,0:T(8,128)(2,1)} %get-tuple-element.29.src_ref), custom_call_target="tpu_custom_call" | custom-call | bytes 18874368 | tf_op jit(solution)/shard_map/pallas_call | solution.py:206
  262.4 11.9 %add_convert_fusion.2 = bf16[1,24,2,384,256]{4,3,2,1,0:T(8,128)(2,1)} fusion(bf16[2,24,2,384,256]{4,3,2,1,0:T(8,128)(2,1)} %shard_map.238, s32[]{:T(128)S(6)} %select_n.62, bf16[2,24,2,384,256]{4,3,2,1,0:T(8,128)(2,1)} %get-tuple-element.29.src_ref, s32[]{:T(128)S(6)} %select_n.61), kind=kLoop, calls=%fused_computation.9 | loop fusion | flops 18874368 | bytes 28311560 | tf_op jit(solution)/shard_map/convert_element_type | solution.py:234
  274.4 15.1 %shard_map.239 = bf16[2,24,2,384,256]{4,3,2,1,0:T(8,128)(2,1)} custom-call(bf16[2,24,2,384,256]{4,3,2,1,0:T(8,128)(2,1)} %get-tuple-element.30.src_ref), custom_call_target="tpu_custom_call" | custom-call | bytes 18874368 | tf_op jit(solution)/shard_map/pallas_call | solution.py:206
  289.5 11.9 %add_convert_fusion.1 = bf16[1,24,2,384,256]{4,3,2,1,0:T(8,128)(2,1)} fusion(bf16[2,24,2,384,256]{4,3,2,1,0:T(8,128)(2,1)} %shard_map.239, s32[]{:T(128)S(6)} %select_n.62, bf16[2,24,2,384,256]{4,3,2,1,0:T(8,128)(2,1)} %get-tuple-element.30.src_ref, s32[]{:T(128)S(6)} %select_n.61), kind=kLoop, calls=%fused_computation.8 | loop fusion | flops 18874368 | bytes 28311560 | tf_op jit(solution)/shard_map/convert_element_type | solution.py:234
  303.5 15.1 %shard_map.240 = bf16[2,24,2,384,256]{4,3,2,1,0:T(8,128)(2,1)} custom-call(bf16[2,24,2,384,256]{4,3,2,1,0:T(8,128)(2,1)} %get-tuple-element.31.src_ref), custom_call_target="tpu_custom_call" | custom-call | bytes 18874368 | tf_op jit(solution)/shard_map/pallas_call | solution.py:206
  318.5 12.1 %add_convert_fusion = bf16[1,24,2,384,256]{4,3,2,1,0:T(8,128)(2,1)} fusion(bf16[2,24,2,384,256]{4,3,2,1,0:T(8,128)(2,1)} %shard_map.240, s32[]{:T(128)S(6)} %select_n.62, bf16[2,24,2,384,256]{4,3,2,1,0:T(8,128)(2,1)} %get-tuple-element.31.src_ref, s32[]{:T(128)S(6)} %select_n.61), kind=kLoop, calls=%fused_computation.7 | loop fusion | flops 18874368 | bytes 28311560 | tf_op jit(solution)/shard_map/convert_element_type | solution.py:234
  331.7 20.2 %fusion.37 = f32[4,2048,512,3]{2,1,3,0:T(8,128)} fusion(bf16[2048,4,64,1]{0,2,1,3:T(8,128)(2,1)S(1)} %reshape.383, bf16[512,4,3,32]{0,3,2,1:T(8,128)(2,1)S(1)} %bitcast.193, bf16[512,4,3,32]{0,3,2,1:T(8,128)(2,1)S(1)} %bitcast.190), kind=kOutput, calls=%fused_computation.68 | convolution fusion | flops 1612185600 | bytes 52166656 | tf_op jit(solution)/shard_map/tkgd,nkd->kgtn/dot_general | solution.py:471
  361.7 36.7 %shard_map.234 = bf16[2,512,1536]{2,1,0:T(8,128)(2,1)} custom-call(bf16[512,1536]{1,0:T(8,128)(2,1)} %convert_element_type.244.src_ref), custom_call_target="tpu_custom_call" | custom-call | bytes 3145728 | tf_op jit(solution)/shard_map/pallas_call | solution.py:206
  418.4 34.6 %shard_map.233 = bf16[2,512,1536]{2,1,0:T(8,128)(2,1)} custom-call(bf16[512,1536]{1,0:T(8,128)(2,1)} %convert_element_type.238.src_ref), custom_call_target="tpu_custom_call" | custom-call | bytes 3145728 | tf_op jit(solution)/shard_map/pallas_call | solution.py:206
  465.7 18.8 %fusion.31 = bf16[2048,4,64]{0,2,1:T(8,128)(2,1)S(1)} fusion(bf16[4,3,512,64]{2,3,1,0:T(8,128)(2,1)S(1)} %bitcast.198, f32[4,2048,512,3]{2,1,3,0:T(8,128)} %fusion.37, f32[4,3,512]{2,1,0:T(4,128)S(1)} %copy-done.63, pred[512,2048]{0,1:T(8,128)(4,1)S(1)} %copy-done.45), kind=kOutput, calls=%fused_computation.52 | convolution fusion | flops 1661468672 | bytes 53239808 | tf_op jit(solution)/shard_map/kgtn,kgtd->nkd/dot_general | solution.py:485
  489.4 28.1 %multiply_convert_fusion = bf16[4,3,512,2048]{2,3,1,0:T(8,128)(2,1)} fusion(f32[4,2048,512,3]{2,1,3,0:T(8,128)} %fusion.37, f32[4,3,512]{2,1,0:T(4,128)S(1)} %multiply_reduce_fusion.3, f32[4,3,512]{2,1,0:T(4,128)S(1)} %copy-done.63, pred[512,2048]{0,1:T(8,128)(4,1)} %fusion.6, bf16[4,3,512,64]{2,3,1,0:T(8,128)(2,1)} %bitcast.200, ...), kind=kOutput, calls=%fused_computation.3 | convolution fusion | flops 1686110208 | bytes 78430208 | tf_op jit(solution)/shard_map/kgtd,nkd->kgtn/dot_general | solution.py:475
  517.5 12.7 %fusion.30 = bf16[2048,4,64]{0,2,1:T(8,128)(2,1)S(1)} fusion(bf16[4,3,512,2048]{2,3,1,0:T(8,128)(2,1)} %multiply_convert_fusion, bf16[512,4,3,32]{0,3,2,1:T(8,128)(2,1)S(1)} %bitcast.194, bf16[512,4,3,32]{0,3,2,1:T(8,128)(2,1)S(1)} %bitcast.191), kind=kOutput, calls=%fused_computation.51 | convolution fusion | flops 1613234176 | bytes 27000832 | tf_op jit(solution)/shard_map/kgtn,tkgd->nkd/dot_general | solution.py:482
  534.9 88.8 %shard_map.236 = bf16[4,512,512]{2,1,0:T(8,128)(2,1)} custom-call(bf16[4,512,512]{2,1,0:T(8,128)(2,1)} %pad_maximum_fusion.src_ref), custom_call_target="tpu_custom_call" | custom-call | bytes 3145728 | tf_op jit(solution)/shard_map/pallas_call | solution.py:206
  627.1 10.8 %convolution_multiply_fusion = f32[4,3,512,64]{2,3,1,0:T(8,128)S(1)} fusion(bf16[4,3,512,2048]{2,3,1,0:T(8,128)(2,1)} %multiply_convert_fusion, bf16[2048,4,64,1]{0,2,1,3:T(8,128)(2,1)S(1)} %copy-done.23), kind=kOutput, calls=%fused_computation.62 | convolution fusion | flops 1611005952 | bytes 27787264 | tf_op jit(solution)/shard_map/kgtn,nkd->kgtd/dot_general | solution.py:479
  644.3 36.4 %shard_map.237 = bf16[2,512,1536]{2,1,0:T(8,128)(2,1)} custom-call(bf16[512,1536]{1,0:T(8,128)(2,1)} %fusion.20.src_ref), custom_call_target="tpu_custom_call" | custom-call | bytes 3145728 | tf_op jit(solution)/shard_map/pallas_call | solution.py:206
  683.5 5.6 fusion.51
  711.7 11.2 %concatenate.58 = bf16[2,2,384,2176]{3,2,0,1:T(8,128)(2,1)} concatenate(bf16[2,2,384,768]{3,2,0,1:T(8,128)(2,1)} %convolution_convert_fusion.3, bf16[2,2,384,768]{3,2,0,1:T(8,128)(2,1)} %convolution_convert_fusion.2, bf16[2,2,384,256]{3,2,0,1:T(8,128)(2,1)S(1)} %convolution_convert_fusion.4, bf16[2,2,384,256]{3,2,0,1:T(8,128)(2,1)S(1)} %copy-done.36, ...), dimensions={3} | concatenate | bytes 13369344 | tf_op jit(solution)/shard_map/concatenate | solution.py:539
  728.7 99.9 %reduce-scatter.11.cloned.1.call-done = bf16[24,96,256]{2,1,0:T(8,128)(2,1)} async-done(((bf16[24,768,256]{2,1,0:T(8,128)(2,1)}), bf16[24,96,256]{2,1,0:T(8,128)(2,1)}) %reduce-scatter.11.cloned.1.call-update) | async-done | bytes 1179664 | tf_op jit(solution)/shard_map/reduce_scatter | solution.py:439
  831.6 6.3 shard_map.241
  843.4 76.6 %reduce-scatter.13.cloned.1.call-done = bf16[96,2176]{1,0:T(8,128)(2,1)} async-done(((bf16[768,2176]{1,0:T(8,128)(2,1)}), bf16[96,2176]{1,0:T(8,128)(2,1)}) %reduce-scatter.13.cloned.1.call-update) | async-done | bytes 417808
  (280 shorter events, 160.3 us)
Async XLA Ops:
  7.2 113.1 %all-gather.2.cloned.1.call-start = ((), (), s32[]{:S(2)}) async-start(), calls=%async_computation.4 | async-start | bytes 7077888 | tf_op jit(solution)/shard_map/all_gather | solution.py:353
  7.9 714.9 %reduce-scatter.7.cloned.1.call-start = ((), (), s32[]{:S(2)}) async-start(), calls=%async_computation.5 | async-start | bytes 10616832 | tf_op jit(solution)/shard_map/reduce_scatter | solution.py:439
  8.6 61.6 %copy-start.66 = (s32[512]{0:T(512)}, s32[512]{0:T(512)S(1)}, u32[]{:S(2)}) copy-start(s32[512]{0:T(512)S(1)} %get-tuple-element.129) | copy-start | bytes 6148
  9.0 53.8 %copy-start.70 = (f32[512]{0:T(512)}, f32[512]{0:T(512)S(1)}, u32[]{:S(2)}) copy-start(f32[512]{0:T(512)S(1)} %add_rsqrt_fusion.1) | copy-start | bytes 6148
  10.0 56.5 %copy-start.39 = (f32[512,32]{0,1:T(8,128)}, f32[512,32]{0,1:T(8,128)S(1)}, u32[]{:S(2)}) copy-start(f32[512,32]{0,1:T(8,128)S(1)} %get-tuple-element.125) | copy-start | bytes 196612
  93.3 21.3 %copy-start.9 = (f32[4,3,512,64]{2,3,1,0:T(8,128)}, f32[4,3,512,64]{2,3,1,0:T(8,128)S(1)}, u32[]{:S(2)}) copy-start(f32[4,3,512,64]{2,3,1,0:T(8,128)S(1)} %copy.217) | copy-start | bytes 4718596
  93.4 22.4 %copy-start.25 = (bf16[4,3,512,64]{2,3,1,0:T(8,128)(2,1)}, bf16[4,3,512,64]{2,3,1,0:T(8,128)(2,1)S(1)}, u32[]{:S(2)}) copy-start(bf16[4,3,512,64]{2,3,1,0:T(8,128)(2,1)S(1)} %convert_element_type.233) | copy-start | bytes 2359300
  120.3 5.0 copy-start.58
  274.4 451.4 %reduce-scatter.9.cloned.1.call-start = ((), (), s32[]{:S(2)}) async-start(), calls=%async_computation.6 | async-start | bytes 10616832 | tf_op jit(solution)/shard_map/reduce_scatter | solution.py:439
  301.4 527.2 %reduce-scatter.11.cloned.1.call-start = ((), (), s32[]{:S(2)}) async-start(), calls=%async_computation.7 | async-start | bytes 10616832 | tf_op jit(solution)/shard_map/reduce_scatter | solution.py:439
  303.4 27.2 %copy-start.22 = (bf16[2048,4,64,1]{0,2,1,3:T(8,128)(2,1)}, bf16[2048,4,64,1]{0,2,1,3:T(8,128)(2,1)S(1)}, u32[]{:S(2)}) copy-start(bf16[2048,4,64,1]{0,2,1,3:T(8,128)(2,1)S(1)} %reshape.383) | copy-start | bytes 3145732
  330.6 21.3 %copy-start.19 = (bf16[4,512,256]{1,0,2:T(4,128)(2,1)S(1)}, bf16[4,512,256]{1,0,2:T(4,128)(2,1)}, u32[]{:S(2)}) copy-start(bf16[4,512,256]{1,0,2:T(4,128)(2,1)} %copy-done.18) | copy-start | bytes 3145732
  330.6 589.4 %reduce-scatter.13.cloned.1.call-start = ((), (), s32[]{:S(2)}) async-start(), calls=%async_computation.8 | async-start | bytes 3760128
  398.3 5.4 copy-start.55
  398.4 18.7 %copy-start.15 = (f32[512,1536]{1,0:T(8,128)S(1)}, f32[512,1536]{1,0:T(8,128)}, u32[]{:S(2)}) copy-start(f32[512,1536]{1,0:T(8,128)} %get-tuple-element.25) | copy-start | bytes 9437188
  418.4 35.4 %copy-start.5 = (f32[512,1536]{1,0:T(8,128)S(1)}, f32[512,1536]{1,0:T(8,128)}, u32[]{:S(2)}) copy-start(f32[512,1536]{1,0:T(8,128)} %copy-done.4) | copy-start | bytes 9437188
  458.2 4.9 copy-start.38
  489.4 28.1 %copy-start.31 = (bf16[512,12,32]{0,2,1:T(8,128)(2,1)S(1)}, bf16[512,12,32]{0,2,1:T(8,128)(2,1)}, u32[]{:S(2)}) copy-start(bf16[512,12,32]{0,2,1:T(8,128)(2,1)} %copy-done.29) | copy-start | bytes 1179652
  626.7 15.3 %copy-start.34 = (f32[512,512]{1,0:T(8,128)}, f32[512,512]{1,0:T(8,128)S(1)}, u32[]{:S(2)}) copy-start(f32[512,512]{1,0:T(8,128)S(1)} %convert_reduce_fusion) | copy-start | bytes 3145732
  644.3 36.4 %copy-start.6 = (bf16[512,1536]{1,0:T(8,128)(2,1)S(1)}, bf16[512,1536]{1,0:T(8,128)(2,1)}, u32[]{:S(2)}) copy-start(bf16[512,1536]{1,0:T(8,128)(2,1)} %fusion.20.src_ref) | copy-start | bytes 4718596
  644.3 36.4 %copy-start.13 = (bf16[512,1536]{1,0:T(8,128)(2,1)S(1)}, bf16[512,1536]{1,0:T(8,128)(2,1)}, u32[]{:S(2)}) copy-start(bf16[512,1536]{1,0:T(8,128)(2,1)} %param.14) | copy-start | bytes 4718596
  644.3 36.4 %copy-start.65 = (f32[1536]{0:T(1024)S(1)}, f32[1536]{0:T(1024)}, u32[]{:S(2)}) copy-start(f32[1536]{0:T(1024)} %param.15) | copy-start | bytes 18436
  644.3 36.4 %copy-start.71 = (f32[512]{0:T(512)S(1)}, f32[512]{0:T(512)}, u32[]{:S(2)}) copy-start(f32[512]{0:T(512)} %copy-done.70) | copy-start | bytes 6148
  700.0 5.2 copy-start.33
  (54 other events, 134.5 us)
Sparse Core Ops, SparseCore 0:
  9.6 65.3 all-gather.1
  274.5 203.9 reduce-scatter.6
  482.0 177.9 reduce-scatter.8
  663.5 165.1 reduce-scatter.10
  843.5 76.4 reduce-scatter.12

commit v6 on v5

--- a/solution.py
+++ b/solution.py
@@ -72,58 +72,62 @@
             out_ref[c, 0, x] = value[start : start + rows].astype(out_ref.dtype)
 
 
-def _expert_body(
+def _grad_body(
     n2_ref, n2t_ref, dy_ref, dyt_ref, gcol_ref, grow_ref, wg_ref, wu_ref, wd_ref,
-    acc_ref, dgate_ref, gg_ref, gu_ref, gd_ref, dn2_ref,
+    gg_ref, gu_ref, gd_ref, hid_ref, dga_ref, dua_ref,
 ):
     f32 = jnp.float32
     bf16 = jnp.bfloat16
-    nt = (((1,), (1,)), ((), ()))
-
-    @pl.when(pl.program_id(0) == 0)
-    def _():
-        acc_ref[...] = jnp.zeros_like(acc_ref)
-        dn2_ref[...] = jnp.zeros_like(dn2_ref)
-
     n2 = n2_ref[...]
-    wg = wg_ref[0]
-    wu = wu_ref[0]
     wd = wd_ref[0]
-    gate_act = jnp.dot(n2, wg, preferred_element_type=f32)
-    up_act = jnp.dot(n2, wu, preferred_element_type=f32)
+    gate_act = jnp.dot(n2, wg_ref[0], preferred_element_type=f32)
+    up_act = jnp.dot(n2, wu_ref[0], preferred_element_type=f32)
     sig = 1.0 / (1.0 + jnp.exp(-gate_act))
     silu = gate_act * sig
     hidden = (silu * up_act).astype(bf16)
-    expert_out = lax.dot_general(hidden, wd, nt, preferred_element_type=f32)
-    gc = gcol_ref[0]
-    acc_ref[...] += gc * expert_out
-    dy = dy_ref[...].astype(f32)
-    dgate_ref[0] = jnp.sum(expert_out * dy, axis=1, keepdims=True)
-    deo = (gc * dy).astype(bf16)
+    hid_ref[0] = hidden
+    deo = (gcol_ref[0] * dy_ref[...].astype(f32)).astype(bf16)
     grad_hidden = jnp.dot(deo, wd, preferred_element_type=f32)
     deo_t = (grow_ref[0] * dyt_ref[...].astype(f32)).astype(bf16)
     _store_split(gd_ref, jnp.dot(deo_t, hidden, preferred_element_type=f32))
     grad_gate_act = (grad_hidden * up_act * sig * (1.0 + gate_act * (1.0 - sig))).astype(bf16)
     grad_up_act = (grad_hidden * silu).astype(bf16)
+    dga_ref[0] = grad_gate_act
+    dua_ref[0] = grad_up_act
     n2t = n2t_ref[...]
     _store_split(gg_ref, jnp.dot(n2t, grad_gate_act, preferred_element_type=f32))
     _store_split(gu_ref, jnp.dot(n2t, grad_up_act, preferred_element_type=f32))
+
+
+def _rows_body(hid_ref, dga_ref, dua_ref, dy_ref, gcol_ref, wg_ref, wu_ref, wd_ref, acc_ref, dgate_ref, dn2_ref):
+    f32 = jnp.float32
+    nt = (((1,), (1,)), ((), ()))
+
+    @pl.when(pl.program_id(0) == 0)
+    def _():
+        acc_ref[...] = jnp.zeros_like(acc_ref)
+        dn2_ref[...] = jnp.zeros_like(dn2_ref)
+
+    expert_out = lax.dot_general(hid_ref[0], wd_ref[0], nt, preferred_element_type=f32)
+    acc_ref[...] += gcol_ref[0] * expert_out
+    dgate_ref[0] = jnp.sum(expert_out * dy_ref[...].astype(f32), axis=1, keepdims=True)
     dn2_ref[...] += lax.dot_general(
-        grad_gate_act, wg, nt, preferred_element_type=f32
-    ) + lax.dot_general(grad_up_act, wu, nt, preferred_element_type=f32)
-
-
-def expert_kernel(n2, n2t, dy, dyt, gcol, grow, wg, wu, wd, groups):
+        dga_ref[0], wg_ref[0], nt, preferred_element_type=f32
+    ) + lax.dot_general(dua_ref[0], wu_ref[0], nt, preferred_element_type=f32)
+
+
+def expert_grad_kernel(n2, n2t, dy, dyt, gcol, grow, wg, wu, wd, groups):
     tokens, width = n2.shape
     experts, _, hidden = wg.shape
-    f32 = jnp.float32
+    bf16 = jnp.bfloat16
     whole = lambda shape: pl.BlockSpec(shape, lambda e: (0,) * len(shape))
     per_expert = lambda shape: pl.BlockSpec((1,) + shape, lambda e: (e,) + (0,) * len(shape))
-    flops = experts * tokens * width * hidden * 2 * 9
     split_rows = width // (groups * 2)
     split = pl.BlockSpec((2, 1, groups, split_rows, hidden), lambda e: (0, e, 0, 0, 0))
+    split_shape = jax.ShapeDtypeStruct((2, experts, groups, split_rows, hidden), bf16)
+    act_shape = jax.ShapeDtypeStruct((experts, tokens, hidden), bf16)
     return pl.pallas_call(
-        _expert_body,
+        _grad_body,
         grid=(experts,),
         in_specs=[
             whole((tokens, width)),
@@ -136,32 +140,54 @@
             per_expert((width, hidden)),
             per_expert((width, hidden)),
         ],
-        out_specs=[
+        out_specs=[split, split, split]
+        + [per_expert((tokens, hidden))] * 3,
+        out_shape=[split_shape] * 3 + [act_shape] * 3,
+        compiler_params=pltpu.CompilerParams(
+            dimension_semantics=("arbitrary",), vmem_limit_bytes=64 * 1024 * 1024
+        ),
+        cost_estimate=pl.CostEstimate(
+            flops=experts * tokens * width * hidden * 2 * 6,
+            transcendentals=experts * tokens * hidden,
+            bytes_accessed=experts * width * hidden * 12 + tokens * width * 8 + experts * tokens * hidden * 6,
+        ),
+    )(n2, n2t, dy, dyt, gcol, grow, wg, wu, wd)
+
+
+def expert_rows_kernel(hid, dga, dua, dy, gcol, wg, wu, wd):
+    experts, tokens, hidden = hid.shape
+    width = dy.shape[1]
+    f32 = jnp.float32
+    whole = lambda shape: pl.BlockSpec(shape, lambda e: (0,) * len(shape))
+    per_expert = lambda shape: pl.BlockSpec((1,) + shape, lambda e: (e,) + (0,) * len(shape))
+    return pl.pallas_call(
+        _rows_body,
+        grid=(experts,),
+        in_specs=[
+            per_expert((tokens, hidden)),
+            per_expert((tokens, hidden)),
+            per_expert((tokens, hidden)),
             whole((tokens, width)),
             per_expert((tokens, 1)),
-            split,
-            split,
-            split,
-            whole((tokens, width)),
-        ],
+            per_expert((width, hidden)),
+            per_expert((width, hidden)),
+            per_expert((width, hidden)),
+        ],
+        out_specs=[whole((tokens, width)), per_expert((tokens, 1)), whole((tokens, width))],
         out_shape=[
             jax.ShapeDtypeStruct((tokens, width), f32),
             jax.ShapeDtypeStruct((experts, tokens, 1), f32),
-            jax.ShapeDtypeStruct((2, experts, groups, split_rows, hidden), jnp.bfloat16),
-            jax.ShapeDtypeStruct((2, experts, groups, split_rows, hidden), jnp.bfloat16),
-            jax.ShapeDtypeStruct((2, experts, groups, split_rows, hidden), jnp.bfloat16),
             jax.ShapeDtypeStruct((tokens, width), f32),
         ],
         compiler_params=pltpu.CompilerParams(
             dimension_semantics=("arbitrary",), vmem_limit_bytes=64 * 1024 * 1024
         ),
         cost_estimate=pl.CostEstimate(
-            flops=flops,
-            transcendentals=experts * tokens * hidden,
-            bytes_accessed=experts * width * hidden * (3 * 2 + 3 * 2) + tokens * width * 16,
-        ),
-    )(n2, n2t, dy, dyt, gcol, grow, wg, wu, wd)
-
+            flops=experts * tokens * width * hidden * 2 * 3,
+            transcendentals=0,
+            bytes_accessed=experts * width * hidden * 6 + tokens * width * 10 + experts * tokens * hidden * 6,
+        ),
+    )(hid, dga, dua, dy, gcol, wg, wu, wd)
 
 MESH = pl.DeviceIdType.MESH
 
@@ -418,17 +444,25 @@
     gates_dense = jnp.sum(jnp.where(picked_onehot, gate_probs[:, :, None], 0.0), axis=1)
     gates_by_expert = jnp.transpose(gates_dense)
     cot_bf = output_grad
-    moe_acc, gate_parts, grad_gate, grad_up, grad_down, moe_grad_rows = expert_kernel(
+    gcol = gates_by_expert[:, :, None]
+    grad_gate, grad_up, grad_down, hid_all, dga_all, dua_all = expert_grad_kernel(
         normed_two,
         jnp.transpose(normed_two),
         cot_bf,
         jnp.transpose(cot_bf),
-        gates_by_expert[:, :, None],
+        gcol,
         gates_by_expert[:, None, :],
         gate_weight,
         up_weight,
         down_weight,
         dpx_count,
+    )
+    gate_half = core_reduce(grad_gate, 8)
+    gate_half, hid_all, dga_all, dua_all = lax.optimization_barrier(
+        (gate_half, hid_all, dga_all, dua_all)
+    )
+    moe_acc, gate_parts, moe_grad_rows = expert_rows_kernel(
+        hid_all, dga_all, dua_all, cot_bf, gcol, gate_weight, up_weight, down_weight
     )
     cot_f32 = output_grad.astype(f32)
     moe_total = sum_axis(moe_acc.astype(bf16), "tensor", 3)
@@ -437,12 +471,9 @@
     gate_parts = gate_parts[:, :, 0]
     grad_gate_out, grad_up_out, grad_down_out = [
         lax.psum_scatter(
-            core_reduce(g, cid).reshape(g.shape[1], -1, g.shape[4]),
-            ("dpx", "ctx"),
-            scatter_dimension=1,
-            tiled=True,
+            g.reshape(g.shape[0], -1, g.shape[3]), ("dpx", "ctx"), scatter_dimension=1, tiled=True
         ).astype(jnp.float32)
-        for g, cid in ((grad_gate, 8), (grad_up, 9), (grad_down, 10))
+        for g in (gate_half, core_reduce(grad_up, 9), core_reduce(grad_down, 10))
     ]
     gate_pair = jnp.sum(
         jnp.where(picked_onehot, jnp.transpose(gate_parts)[:, None, :], 0.0), axis=2

time: 937 us -> 912 us (0.973)
  waiting for transfers between devices: 177 us -> 137 us
  Pallas kernels: 443 us -> 461 us
    reduce_scatter x3, waiting for transfers between devices: 99.9 us -> 59.3 us  [per_device(): lax.psum_scatter(g.reshape(g.shape[0], -1, g.shape[3]), ('dpx', 'ctx'), s...]
    pallas_call x11, Pallas kernels: 313 us -> 323 us  [exchange(): pl.pallas_call(functools.partial(_exchange_body, axis, n, per_peer), out_...]
    pallas_call x1 -> x2, Pallas kernels: 113 us -> 121 us  [the longest x1 73.5 us: expert_grad_kernel(): pl.pallas_call(_grad_body, grid=(experts,), in_specs=[whole((tokens, widt...]
    unnamed x158 -> x164, local copies, waits for them, and re-layouts: 23.6 us -> 21.6 us
  transfers between devices with their start and end apart: 5 -> 5, of which waited for: 2 -> 2; matrix products, arithmetic and copies ran while one was open for 26% -> 27% of each run, Pallas kernels for 33% -> 40%
where the time goes in v6:
time: 912 us; the launch traced here: 907 us
  Pallas kernels  461 us (51%)
  waiting for transfers between devices  137 us (15%)
  matrix products  121 us (13%)
  local copies, waits for them, and re-layouts  86.6 us (9%)
  other arithmetic  85.9 us (9%)
  between operations  15.6 us (2%)
    pallas_call x11, Pallas kernels, exchange(): pl.pallas_call(functools.partial(_exchange_body, axis, n, per_peer), out_...  323 us
    unnamed x6, waiting for transfers between devices  77.3 us
    pallas_call x1, Pallas kernels, expert_grad_kernel(): pl.pallas_call(_grad_body, grid=(experts,), in_specs=[whole((tokens, widt...  73.5 us
    reduce_scatter x3, waiting for transfers between devices, per_device(): lax.psum_scatter(g.reshape(g.shape[0], -1, g.shape[3]), ('dpx', 'ctx'), s...  59.3 us
    pallas_call x1, Pallas kernels, expert_rows_kernel(): pl.pallas_call(_rows_body, grid=(experts,), in_specs=[per_expert((tokens,...  47.9 us
    convert_element_type x4, other arithmetic, core_reduce(): (own.astype(jnp.float32) + other.astype(jnp.float32)).astype(jnp.bfloat16)  41.4 us
    dot_general x1, matrix products, per_device(): jnp.einsum('kgtd,nkd->kgtn', grad_attn_grouped, value_piece, preferred_el...  29.2 us
    unnamed x164, local copies, waits for them, and re-layouts  21.6 us
  transfers between devices with their start and end apart: 5, of which 2 were waited for; matrix products, arithmetic and copies ran while one was open for 27% of the time, Pallas kernels for 40%

profile of v6, /device:TPU:0, one launch (start us, length us, event | category | flops | bytes accessed | tf_op | source)
XLA Modules:
  0.0 907.1 jit_solution(16827082585101723221)
XLA Ops:
  12.5 40.1 %shard_map.229 = bf16[4,512,512]{2,1,0:T(8,128)(2,1)} custom-call(bf16[512,512]{1,0:T(8,128)(2,1)} %pad_maximum_fusion.2.src_ref), custom_call_target="tpu_custom_call" | custom-call | bytes 3145728 | tf_op jit(solution)/shard_map/pallas_call | solution.py:232
  74.0 17.0 %shard_map.230 = (f32[4,1536,64]{2,1,0:T(8,128)}, f32[4,1536,1]{2,1,0:T(8,128)}) custom-call(s32[1]{0:T(128)} %bitcast.ctx_ref, bf16[4,1536,64]{2,1,0:T(8,128)(2,1)S(1)} %bitcast.178, bf16[4,2048,64]{2,1,0:T(8,128)(2,1)S(1)} %bitcast.177, bf16[4,2048,64]{2,1,0:T(8,128)(2,1)} %bitcast.205, s32[1536,1]{1,0:T(8,128)S(1)} %bitcast.179, s32[1536,1]{1,0:T(8,128)S(1)} %bitcast.180, ...), custom_call_target="tpu_custom_call" | custom-call | flops 3221225472 | bytes 4456448 | tf_op jit(solution)/shard_map/pallas_call | solution.py:333
  94.9 19.7 %shard_map.231 = bf16[2,512,768]{2,1,0:T(8,128)(2,1)} custom-call(bf16[512,768]{1,0:T(8,128)(2,1)} %copy.221.src_ref), custom_call_target="tpu_custom_call" | custom-call | bytes 1572864 | tf_op jit(solution)/shard_map/pallas_call | solution.py:232
  134.9 73.5 %shard_map.232 = (bf16[2,24,2,384,256]{4,3,2,1,0:T(8,128)(2,1)}, bf16[2,24,2,384,256]{4,3,2,1,0:T(8,128)(2,1)}, bf16[2,24,2,384,256]{4,3,2,1,0:T(8,128)(2,1)}, b...) custom-call(bf16[512,1536]{1,0:T(8,128)(2,1)} %copy-done.7, ...), custom_call_target="tpu_custom_call" | custom-call | flops 57982058496 | bytes 138412032 | tf_op jit(solution)/shard_map/pallas_call | solution.py:129
  208.4 15.1 %shard_map.240 = bf16[2,24,2,384,256]{4,3,2,1,0:T(8,128)(2,1)} custom-call(bf16[2,24,2,384,256]{4,3,2,1,0:T(8,128)(2,1)} %get-tuple-element.44.src_ref), custom_call_target="tpu_custom_call" | custom-call | bytes 18874368 | tf_op jit(solution)/shard_map/pallas_call | solution.py:232
  223.4 12.0 %add_convert_fusion.1 = bf16[1,24,2,384,256]{4,3,2,1,0:T(8,128)(2,1)} fusion(bf16[2,24,2,384,256]{4,3,2,1,0:T(8,128)(2,1)} %shard_map.240, s32[]{:T(128)S(6)} %select_n.58, bf16[2,24,2,384,256]{4,3,2,1,0:T(8,128)(2,1)} %get-tuple-element.44.src_ref, s32[]{:T(128)S(6)} %select_n.57), kind=kLoop, calls=%fused_computation.8 | loop fusion | flops 18874368 | bytes 28311560 | tf_op jit(solution)/shard_map/convert_element_type | solution.py:260
  235.5 15.1 %shard_map.241 = bf16[2,24,2,384,256]{4,3,2,1,0:T(8,128)(2,1)} custom-call(bf16[2,24,2,384,256]{4,3,2,1,0:T(8,128)(2,1)} %get-tuple-element.45.src_ref), custom_call_target="tpu_custom_call" | custom-call | bytes 18874368 | tf_op jit(solution)/shard_map/pallas_call | solution.py:232
  250.6 11.9 %add_convert_fusion = bf16[1,24,2,384,256]{4,3,2,1,0:T(8,128)(2,1)} fusion(bf16[2,24,2,384,256]{4,3,2,1,0:T(8,128)(2,1)} %shard_map.241, s32[]{:T(128)S(6)} %select_n.58, bf16[2,24,2,384,256]{4,3,2,1,0:T(8,128)(2,1)} %get-tuple-element.45.src_ref, s32[]{:T(128)S(6)} %select_n.57), kind=kLoop, calls=%fused_computation.7 | loop fusion | flops 18874368 | bytes 28311560 | tf_op jit(solution)/shard_map/convert_element_type | solution.py:260
  271.0 20.2 %fusion.38 = f32[4,2048,512,3]{2,1,3,0:T(8,128)} fusion(bf16[2048,4,64,1]{0,2,1,3:T(8,128)(2,1)S(1)} %reshape.384, bf16[512,4,3,32]{0,3,2,1:T(8,128)(2,1)S(1)} %bitcast.195, bf16[512,4,3,32]{0,3,2,1:T(8,128)(2,1)S(1)} %bitcast.192), kind=kOutput, calls=%fused_computation.69 | convolution fusion | flops 1612185600 | bytes 52166656 | tf_op jit(solution)/shard_map/tkgd,nkd->kgtn/dot_general | solution.py:502
  291.2 15.0 %shard_map.233 = bf16[2,24,2,384,256]{4,3,2,1,0:T(8,128)(2,1)} custom-call(bf16[2,24,2,384,256]{4,3,2,1,0:T(8,128)(2,1)} %get-tuple-element.32.src_ref), custom_call_target="tpu_custom_call" | custom-call | bytes 18874368 | tf_op jit(solution)/shard_map/pallas_call | solution.py:232
  306.2 12.0 %fusion.6 = bf16[24,2,384,256]{3,2,1,0:T(8,128)(2,1)} fusion(bf16[2,24,2,384,256]{4,3,2,1,0:T(8,128)(2,1)} %shard_map.233, s32[]{:T(128)S(6)} %select_n.58, bf16[2,24,2,384,256]{4,3,2,1,0:T(8,128)(2,1)} %get-tuple-element.32.src_ref, s32[]{:T(128)S(6)} %select_n.57), kind=kLoop, calls=%fused_computation.10 | loop fusion | flops 18874368 | bytes 28311560 | tf_op jit(solution)/shard_map/convert_element_type | solution.py:260
  318.3 47.9 %shard_map.234 = (f32[512,1536]{1,0:T(8,128)}, f32[24,512,1]{2,1,0:T(8,128)}, f32[512,1536]{1,0:T(8,128)}) custom-call(bf16[24,512,256]{2,1,0:T(8,128)(2,1)} %get-tuple-element.36.hid_ref, bf16[24,512,256]{2,1,0:T(8,128)(2,1)} %get-tuple-element.37.dga_ref, bf16[24,512,256]{2,1,0:T(8,128)(2,1)} %get-tuple-element.38.dua_ref, bf16[512,1536]{1,0:T(8,128)(2,1)} %dy_ref.3, ...), custom_call_target="tpu_custom_call" | custom-call | flops 28991029248 | bytes 83361792 | tf_op jit(solution)/shard_map/pallas_call | solution.py:163
  369.4 36.7 %shard_map.236 = bf16[2,512,1536]{2,1,0:T(8,128)(2,1)} custom-call(bf16[512,1536]{1,0:T(8,128)(2,1)} %convert_element_type.245.src_ref), custom_call_target="tpu_custom_call" | custom-call | bytes 3145728 | tf_op jit(solution)/shard_map/pallas_call | solution.py:232
  422.5 35.0 %shard_map.235 = bf16[2,512,1536]{2,1,0:T(8,128)(2,1)} custom-call(bf16[512,1536]{1,0:T(8,128)(2,1)} %convert_element_type.239.src_ref), custom_call_target="tpu_custom_call" | custom-call | bytes 3145728 | tf_op jit(solution)/shard_map/pallas_call | solution.py:232
  468.5 19.0 %fusion.32 = bf16[2048,4,64]{0,2,1:T(8,128)(2,1)S(1)} fusion(bf16[4,3,512,64]{2,3,1,0:T(8,128)(2,1)S(1)} %bitcast.200, f32[4,2048,512,3]{2,1,3,0:T(8,128)} %fusion.38, f32[4,3,512]{2,1,0:T(4,128)S(1)} %copy-done.66, pred[512,2048]{0,1:T(8,128)(4,1)S(1)} %copy-done.46), kind=kOutput, calls=%fused_computation.53 | convolution fusion | flops 1661468672 | bytes 53239808 | tf_op jit(solution)/shard_map/kgtn,kgtd->nkd/dot_general | solution.py:516
  491.1 29.2 %multiply_convert_fusion = bf16[4,3,512,2048]{2,3,1,0:T(8,128)(2,1)} fusion(f32[4,2048,512,3]{2,1,3,0:T(8,128)} %fusion.38, f32[4,3,512]{2,1,0:T(4,128)S(1)} %multiply_reduce_fusion.3, f32[4,3,512]{2,1,0:T(4,128)S(1)} %copy-done.66, pred[512,2048]{0,1:T(8,128)(4,1)} %fusion.7, bf16[4,3,512,64]{2,3,1,0:T(8,128)(2,1)S(1)} %bitcast.202, ...), kind=kOutput, calls=%fused_computation.3 | convolution fusion | flops 1686110208 | bytes 78430208 | tf_op jit(solution)/shard_map/kgtd,nkd->kgtn/dot_general | solution.py:506
  520.3 13.7 %fusion.31 = bf16[2048,4,64]{0,2,1:T(8,128)(2,1)} fusion(bf16[4,3,512,2048]{2,3,1,0:T(8,128)(2,1)} %multiply_convert_fusion, bf16[512,4,3,32]{0,3,2,1:T(8,128)(2,1)S(1)} %bitcast.196, bf16[512,4,3,32]{0,3,2,1:T(8,128)(2,1)S(1)} %bitcast.193), kind=kOutput, calls=%fused_computation.52 | convolution fusion | flops 1613234176 | bytes 27000832 | tf_op jit(solution)/shard_map/kgtn,tkgd->nkd/dot_general | solution.py:513
  539.7 98.3 %shard_map.238 = bf16[4,512,512]{2,1,0:T(8,128)(2,1)} custom-call(bf16[4,512,512]{2,1,0:T(8,128)(2,1)} %pad_maximum_fusion.src_ref), custom_call_target="tpu_custom_call" | custom-call | bytes 3145728 | tf_op jit(solution)/shard_map/pallas_call | solution.py:232
  641.4 11.5 %convolution_multiply_fusion = f32[4,3,512,64]{2,3,1,0:T(8,128)S(1)} fusion(bf16[4,3,512,2048]{2,3,1,0:T(8,128)(2,1)} %multiply_convert_fusion, bf16[2048,4,64,1]{0,2,1,3:T(8,128)(2,1)S(1)} %copy-done.23), kind=kOutput, calls=%fused_computation.63 | convolution fusion | flops 1611005952 | bytes 27787264 | tf_op jit(solution)/shard_map/kgtn,nkd->kgtd/dot_general | solution.py:510
  659.2 36.4 %shard_map.239 = bf16[2,512,1536]{2,1,0:T(8,128)(2,1)} custom-call(bf16[512,1536]{1,0:T(8,128)(2,1)} %fusion.21.src_ref), custom_call_target="tpu_custom_call" | custom-call | bytes 3145728 | tf_op jit(solution)/shard_map/pallas_call | solution.py:232
  726.7 11.1 %concatenate.58 = bf16[2,2,384,2176]{3,2,0,1:T(8,128)(2,1)} concatenate(bf16[2,2,384,768]{3,2,0,1:T(8,128)(2,1)} %convolution_convert_fusion.3, bf16[2,2,384,768]{3,2,0,1:T(8,128)(2,1)} %convolution_convert_fusion.2, bf16[2,2,384,256]{3,2,0,1:T(8,128)(2,1)S(1)} %convolution_convert_fusion.4, bf16[2,2,384,256]{3,2,0,1:T(8,128)(2,1)S(1)} %copy-done.38, ...), dimensions={3} | concatenate | bytes 13369344 | tf_op jit(solution)/shard_map/concatenate | solution.py:570
  743.8 59.3 %reduce-scatter.7.cloned.1.call-done = bf16[24,96,256]{2,1,0:T(8,128)(2,1)} async-done(((bf16[24,768,256]{2,1,0:T(8,128)(2,1)}), bf16[24,96,256]{2,1,0:T(8,128)(2,1)}) %reduce-scatter.7.cloned.1.call-update) | async-done | bytes 1179664 | tf_op jit(solution)/shard_map/reduce_scatter | solution.py:473
  806.0 6.3 shard_map.242
  817.7 76.5 %reduce-scatter.13.cloned.1.call-done = bf16[96,2176]{1,0:T(8,128)(2,1)} async-done(((bf16[768,2176]{1,0:T(8,128)(2,1)}), bf16[96,2176]{1,0:T(8,128)(2,1)}) %reduce-scatter.13.cloned.1.call-update) | async-done | bytes 417808
  (287 shorter events, 159.3 us)
Async XLA Ops:
  7.2 113.1 %all-gather.2.cloned.1.call-start = ((), (), s32[]{:S(2)}) async-start(), calls=%async_computation.4 | async-start | bytes 7077888 | tf_op jit(solution)/shard_map/all_gather | solution.py:379
  7.9 729.9 %reduce-scatter.9.cloned.1.call-start = ((), (), s32[]{:S(2)}) async-start(), calls=%async_computation.6 | async-start | bytes 10616832 | tf_op jit(solution)/shard_map/reduce_scatter | solution.py:473
  8.6 61.6 %copy-start.69 = (s32[512]{0:T(512)}, s32[512]{0:T(512)S(1)}, u32[]{:S(2)}) copy-start(s32[512]{0:T(512)S(1)} %get-tuple-element.143) | copy-start | bytes 6148
  9.0 53.9 %copy-start.73 = (f32[512]{0:T(512)}, f32[512]{0:T(512)S(1)}, u32[]{:S(2)}) copy-start(f32[512]{0:T(512)S(1)} %add_rsqrt_fusion.1) | copy-start | bytes 6148
  10.0 56.6 %copy-start.40 = (f32[512,32]{0,1:T(8,128)}, f32[512,32]{0,1:T(8,128)S(1)}, u32[]{:S(2)}) copy-start(f32[512,32]{0,1:T(8,128)S(1)} %get-tuple-element.139) | copy-start | bytes 196612
  93.3 21.3 %copy-start.9 = (f32[4,3,512,64]{2,3,1,0:T(8,128)}, f32[4,3,512,64]{2,3,1,0:T(8,128)S(1)}, u32[]{:S(2)}) copy-start(f32[4,3,512,64]{2,3,1,0:T(8,128)S(1)} %copy.220) | copy-start | bytes 4718596
  93.4 22.4 %copy-start.25 = (bf16[4,3,512,64]{2,3,1,0:T(8,128)(2,1)}, bf16[4,3,512,64]{2,3,1,0:T(8,128)(2,1)S(1)}, u32[]{:S(2)}) copy-start(bf16[4,3,512,64]{2,3,1,0:T(8,128)(2,1)S(1)} %convert_element_type.230) | copy-start | bytes 2359300
  235.5 505.4 %reduce-scatter.11.cloned.1.call-start = ((), (), s32[]{:S(2)}) async-start(), calls=%async_computation.7 | async-start | bytes 10616832 | tf_op jit(solution)/shard_map/reduce_scatter | solution.py:473
  262.5 540.5 %reduce-scatter.7.cloned.1.call-start = ((), (), s32[]{:S(2)}) async-start(), calls=%async_computation.5 | async-start | bytes 10616832 | tf_op jit(solution)/shard_map/reduce_scatter | solution.py:473
  318.3 576.0 %reduce-scatter.13.cloned.1.call-start = ((), (), s32[]{:S(2)}) async-start(), calls=%async_computation.8 | async-start | bytes 3760128
  406.1 10.9 %copy-start.37 = (f32[512,8]{1,0:T(8,128)S(1)}, f32[512,8]{1,0:T(8,128)}, u32[]{:S(2)}) copy-start(f32[512,8]{1,0:T(8,128)} %copy-done.36) | copy-start | bytes 49156
  406.1 10.9 %copy-start.65 = (f32[512]{0:T(512)S(1)}, f32[512]{0:T(512)}, u32[]{:S(2)}) copy-start(f32[512]{0:T(512)} %copy-done.64) | copy-start | bytes 6148
  406.1 15.1 %copy-start.15 = (f32[512,1536]{1,0:T(8,128)S(1)}, f32[512,1536]{1,0:T(8,128)}, u32[]{:S(2)}) copy-start(f32[512,1536]{1,0:T(8,128)} %get-tuple-element.39) | copy-start | bytes 9437188
  422.5 35.1 %copy-start.5 = (f32[512,1536]{1,0:T(8,128)S(1)}, f32[512,1536]{1,0:T(8,128)}, u32[]{:S(2)}) copy-start(f32[512,1536]{1,0:T(8,128)} %copy-done.4) | copy-start | bytes 9437188
  422.5 35.1 %copy-start.55 = (bf16[1536,24]{0,1:T(8,128)(2,1)S(1)}, bf16[1536,24]{0,1:T(8,128)(2,1)}, u32[]{:S(2)}) copy-start(bf16[1536,24]{0,1:T(8,128)(2,1)} %param.21) | copy-start | bytes 221188
  422.5 35.1 %copy-start.61 = (f32[1536]{0:T(1024)S(1)}, f32[1536]{0:T(1024)}, u32[]{:S(2)}) copy-start(f32[1536]{0:T(1024)} %param.20) | copy-start | bytes 18436
  422.5 35.1 %copy-start.63 = (f32[512]{0:T(512)S(1)}, f32[512]{0:T(512)}, u32[]{:S(2)}) copy-start(f32[512]{0:T(512)} %copy-done.62) | copy-start | bytes 6148
  491.1 29.2 %copy-start.29 = (bf16[512,12,32]{0,2,1:T(8,128)(2,1)S(1)}, bf16[512,12,32]{0,2,1:T(8,128)(2,1)}, u32[]{:S(2)}) copy-start(bf16[512,12,32]{0,2,1:T(8,128)(2,1)} %copy-done.27) | copy-start | bytes 1179652
  491.1 29.2 %copy-start.32 = (bf16[512,12,32]{0,2,1:T(8,128)(2,1)S(1)}, bf16[512,12,32]{0,2,1:T(8,128)(2,1)}, u32[]{:S(2)}) copy-start(bf16[512,12,32]{0,2,1:T(8,128)(2,1)} %copy-done.30) | copy-start | bytes 1179652
  641.0 16.0 %copy-start.35 = (f32[512,512]{1,0:T(8,128)}, f32[512,512]{1,0:T(8,128)S(1)}, u32[]{:S(2)}) copy-start(f32[512,512]{1,0:T(8,128)S(1)} %convert_reduce_fusion) | copy-start | bytes 3145732
  659.2 36.4 %copy-start.6 = (bf16[512,1536]{1,0:T(8,128)(2,1)S(1)}, bf16[512,1536]{1,0:T(8,128)(2,1)}, u32[]{:S(2)}) copy-start(bf16[512,1536]{1,0:T(8,128)(2,1)} %fusion.21.src_ref) | copy-start | bytes 4718596
  659.2 36.4 %copy-start.13 = (bf16[512,1536]{1,0:T(8,128)(2,1)S(1)}, bf16[512,1536]{1,0:T(8,128)(2,1)}, u32[]{:S(2)}) copy-start(bf16[512,1536]{1,0:T(8,128)(2,1)} %param.14) | copy-start | bytes 4718596
  659.2 36.4 %copy-start.68 = (f32[1536]{0:T(1024)S(1)}, f32[1536]{0:T(1024)}, u32[]{:S(2)}) copy-start(f32[1536]{0:T(1024)} %param.15) | copy-start | bytes 18436
  659.2 36.4 %copy-start.74 = (f32[512]{0:T(512)S(1)}, f32[512]{0:T(512)}, u32[]{:S(2)}) copy-start(f32[512]{0:T(512)} %copy-done.73) | copy-start | bytes 6148
  (57 other events, 162.2 us)
Sparse Core Ops, SparseCore 0:
  9.6 65.3 all-gather.1
  235.6 203.8 reduce-scatter.8
  443.1 195.1 reduce-scatter.10
  641.7 161.2 reduce-scatter.6
  817.9 76.3 reduce-scatter.12

commit v7 on v6

--- a/solution.py
+++ b/solution.py
@@ -192,7 +192,7 @@
 MESH = pl.DeviceIdType.MESH
 
 
-def _exchange_body(axis, n, per_peer, src_ref, out_ref, send_sems, recv_sems):
+def _exchange_body(axis, n, per_peer, downward, src_ref, out_ref, send_sems, recv_sems):
     me = lax.axis_index(axis)
     barrier = pltpu.get_barrier_semaphore()
     for k in range(1, n):
@@ -210,27 +210,37 @@
             device_id={axis: peer},
             device_id_type=MESH,
         )
-        copy.start()
-        sends.append(copy)
+        sends.append((peer, copy))
+        if downward:
+            pl.when(peer < me)(copy.start)
+        else:
+            copy.start()
     for k in range(1, n):
         source = lax.rem(me + n - k, n)
-        pltpu.make_async_remote_copy(
+        incoming = pltpu.make_async_remote_copy(
             src_ref=src_ref.at[source] if per_peer else src_ref,
             dst_ref=out_ref.at[source],
             send_sem=send_sems.at[k - 1],
             recv_sem=recv_sems.at[k - 1],
             device_id={axis: source},
             device_id_type=MESH,
-        ).wait_recv()
-    for copy in sends:
-        copy.wait_send()
-
-
-def exchange(x, axis, n, per_peer, collective_id):
+        )
+        if downward:
+            pl.when(source > me)(incoming.wait_recv)
+        else:
+            incoming.wait_recv()
+    for peer, copy in sends:
+        if downward:
+            pl.when(peer < me)(copy.wait_send)
+        else:
+            copy.wait_send()
+
+
+def exchange(x, axis, n, per_peer, collective_id, downward=False):
     block = x.shape[1:] if per_peer else x.shape
     nbytes = math.prod(block) * x.dtype.itemsize
     return pl.pallas_call(
-        functools.partial(_exchange_body, axis, n, per_peer),
+        functools.partial(_exchange_body, axis, n, per_peer, downward),
         out_shape=jax.ShapeDtypeStruct((n,) + tuple(block), x.dtype),
         in_specs=[pl.BlockSpec(memory_space=pl.ANY)],
         out_specs=pl.BlockSpec(memory_space=pl.ANY),
@@ -260,12 +270,12 @@
     return (own.astype(jnp.float32) + other.astype(jnp.float32)).astype(jnp.bfloat16)
 
 
-def scatter_sum_axis(x, axis, n, collective_id):
-    got = exchange(x, axis, n, True, collective_id)
+def scatter_sum_downward(x, axis, n, collective_id):
+    got = exchange(x, axis, n, True, collective_id, downward=True)
     me = lax.axis_index(axis)
-    own = lax.dynamic_index_in_dim(x, me, 0, keepdims=True)
-    full = lax.dynamic_update_slice_in_dim(got, own, me, 0)
-    return jnp.sum(full.astype(jnp.float32), axis=0)
+    own = lax.dynamic_index_in_dim(x, me, 0, keepdims=False).astype(jnp.float32)
+    above = (jnp.arange(n, dtype=jnp.int32) > me).reshape((n,) + (1,) * (x.ndim - 1))
+    return own + jnp.sum(jnp.where(above, got.astype(jnp.float32), 0.0), axis=0)
 
 
 def _flash_body(ctx_ref, q_ref, k_ref, v_ref, qseg_ref, qpos_ref, kseg_ref, o_ref, lse_ref, m_sc, l_sc, acc_sc):
@@ -520,7 +530,7 @@
     grad_values_all = value_part.reshape(piece_rows, kv_local * HEAD_SIZE)
     back_state = (grad_query, grad_keys_all, grad_values_all)
     grad_query, grad_keys_all, grad_values_all = back_state
-    grad_kv_here = scatter_sum_axis(
+    grad_kv_here = scatter_sum_downward(
         jnp.concatenate([grad_keys_all, grad_values_all], axis=1)
         .astype(bf16)
         .reshape(ctx_count, token_count, 2 * kv_width),

time: 912 us -> 912 us (level)
  no operation moved by 1% of the time
where the time goes in v7:
time: 912 us; the launch traced here: 907 us
  Pallas kernels  461 us (51%)
  waiting for transfers between devices  135 us (15%)
  matrix products  121 us (13%)
  local copies, waits for them, and re-layouts  88.8 us (10%)
  other arithmetic  85.7 us (9%)
  between operations  15.6 us (2%)
    pallas_call x11, Pallas kernels, exchange(): pl.pallas_call(functools.partial(_exchange_body, axis, n, per_peer, downw...  322 us
    unnamed x6, waiting for transfers between devices  77.3 us
    pallas_call x1, Pallas kernels, expert_grad_kernel(): pl.pallas_call(_grad_body, grid=(experts,), in_specs=[whole((tokens, widt...  73.5 us
    reduce_scatter x3, waiting for transfers between devices, per_device(): lax.psum_scatter(g.reshape(g.shape[0], -1, g.shape[3]), ('dpx', 'ctx'), s...  57.8 us
    pallas_call x1, Pallas kernels, expert_rows_kernel(): pl.pallas_call(_rows_body, grid=(experts,), in_specs=[per_expert((tokens,...  47.8 us
    convert_element_type x4, other arithmetic, core_reduce(): (own.astype(jnp.float32) + other.astype(jnp.float32)).astype(jnp.bfloat16)  41.4 us
    dot_general x1, matrix products, per_device(): jnp.einsum('kgtd,nkd->kgtn', grad_attn_grouped, value_piece, preferred_el...  29.2 us
    unnamed x164, local copies, waits for them, and re-layouts  23.8 us
  transfers between devices with their start and end apart: 5, of which 2 were waited for; matrix products, arithmetic and copies ran while one was open for 27% of the time, Pallas kernels for 40%

profile of v7, /device:TPU:0, one launch (start us, length us, event | category | flops | bytes accessed | tf_op | source)
XLA Modules:
  0.0 907.2 jit_solution(11024312756365234904)
XLA Ops:
  12.5 40.1 %shard_map.229 = bf16[4,512,512]{2,1,0:T(8,128)(2,1)} custom-call(bf16[512,512]{1,0:T(8,128)(2,1)} %pad_maximum_fusion.2.src_ref), custom_call_target="tpu_custom_call" | custom-call | bytes 3145728 | tf_op jit(solution)/shard_map/pallas_call | solution.py:242
  74.0 17.0 %shard_map.230 = (f32[4,1536,64]{2,1,0:T(8,128)}, f32[4,1536,1]{2,1,0:T(8,128)}) custom-call(s32[1]{0:T(128)} %bitcast.ctx_ref, bf16[4,1536,64]{2,1,0:T(8,128)(2,1)S(1)} %bitcast.183, bf16[4,2048,64]{2,1,0:T(8,128)(2,1)S(1)} %bitcast.182, bf16[4,2048,64]{2,1,0:T(8,128)(2,1)} %bitcast.210, s32[1536,1]{1,0:T(8,128)S(1)} %bitcast.184, s32[1536,1]{1,0:T(8,128)S(1)} %bitcast.185, ...), custom_call_target="tpu_custom_call" | custom-call | flops 3221225472 | bytes 4456448 | tf_op jit(solution)/shard_map/pallas_call | solution.py:343
  94.9 19.7 %shard_map.231 = bf16[2,512,768]{2,1,0:T(8,128)(2,1)} custom-call(bf16[512,768]{1,0:T(8,128)(2,1)} %copy.222.src_ref), custom_call_target="tpu_custom_call" | custom-call | bytes 1572864 | tf_op jit(solution)/shard_map/pallas_call | solution.py:242
  134.9 73.5 %shard_map.232 = (bf16[2,24,2,384,256]{4,3,2,1,0:T(8,128)(2,1)}, bf16[2,24,2,384,256]{4,3,2,1,0:T(8,128)(2,1)}, bf16[2,24,2,384,256]{4,3,2,1,0:T(8,128)(2,1)}, b...) custom-call(bf16[512,1536]{1,0:T(8,128)(2,1)} %copy-done.7, ...), custom_call_target="tpu_custom_call" | custom-call | flops 57982058496 | bytes 138412032 | tf_op jit(solution)/shard_map/pallas_call | solution.py:129
  208.4 15.1 %shard_map.240 = bf16[2,24,2,384,256]{4,3,2,1,0:T(8,128)(2,1)} custom-call(bf16[2,24,2,384,256]{4,3,2,1,0:T(8,128)(2,1)} %get-tuple-element.44.src_ref), custom_call_target="tpu_custom_call" | custom-call | bytes 18874368 | tf_op jit(solution)/shard_map/pallas_call | solution.py:242
  223.4 12.0 %add_convert_fusion.1 = bf16[1,24,2,384,256]{4,3,2,1,0:T(8,128)(2,1)} fusion(bf16[2,24,2,384,256]{4,3,2,1,0:T(8,128)(2,1)} %shard_map.240, s32[]{:T(128)S(6)} %select_n.61, bf16[2,24,2,384,256]{4,3,2,1,0:T(8,128)(2,1)} %get-tuple-element.44.src_ref, s32[]{:T(128)S(6)} %select_n.60), kind=kLoop, calls=%fused_computation.8 | loop fusion | flops 18874368 | bytes 28311560 | tf_op jit(solution)/shard_map/convert_element_type | solution.py:270
  235.5 15.1 %shard_map.241 = bf16[2,24,2,384,256]{4,3,2,1,0:T(8,128)(2,1)} custom-call(bf16[2,24,2,384,256]{4,3,2,1,0:T(8,128)(2,1)} %get-tuple-element.45.src_ref), custom_call_target="tpu_custom_call" | custom-call | bytes 18874368 | tf_op jit(solution)/shard_map/pallas_call | solution.py:242
  250.6 11.9 %add_convert_fusion = bf16[1,24,2,384,256]{4,3,2,1,0:T(8,128)(2,1)} fusion(bf16[2,24,2,384,256]{4,3,2,1,0:T(8,128)(2,1)} %shard_map.241, s32[]{:T(128)S(6)} %select_n.61, bf16[2,24,2,384,256]{4,3,2,1,0:T(8,128)(2,1)} %get-tuple-element.45.src_ref, s32[]{:T(128)S(6)} %select_n.60), kind=kLoop, calls=%fused_computation.7 | loop fusion | flops 18874368 | bytes 28311560 | tf_op jit(solution)/shard_map/convert_element_type | solution.py:270
  271.5 20.2 %fusion.38 = f32[4,2048,512,3]{2,1,3,0:T(8,128)} fusion(bf16[2048,4,64,1]{0,2,1,3:T(8,128)(2,1)S(1)} %reshape.392, bf16[512,4,3,32]{0,3,2,1:T(8,128)(2,1)S(1)} %bitcast.200, bf16[512,4,3,32]{0,3,2,1:T(8,128)(2,1)S(1)} %bitcast.197), kind=kOutput, calls=%fused_computation.70 | convolution fusion | flops 1612185600 | bytes 52166656 | tf_op jit(solution)/shard_map/tkgd,nkd->kgtn/dot_general | solution.py:512
  291.7 15.0 %shard_map.233 = bf16[2,24,2,384,256]{4,3,2,1,0:T(8,128)(2,1)} custom-call(bf16[2,24,2,384,256]{4,3,2,1,0:T(8,128)(2,1)} %get-tuple-element.32.src_ref), custom_call_target="tpu_custom_call" | custom-call | bytes 18874368 | tf_op jit(solution)/shard_map/pallas_call | solution.py:242
  306.7 12.0 %fusion.6 = bf16[24,2,384,256]{3,2,1,0:T(8,128)(2,1)} fusion(bf16[2,24,2,384,256]{4,3,2,1,0:T(8,128)(2,1)} %shard_map.233, s32[]{:T(128)S(6)} %select_n.61, bf16[2,24,2,384,256]{4,3,2,1,0:T(8,128)(2,1)} %get-tuple-element.32.src_ref, s32[]{:T(128)S(6)} %select_n.60), kind=kLoop, calls=%fused_computation.10 | loop fusion | flops 18874368 | bytes 28311560 | tf_op jit(solution)/shard_map/convert_element_type | solution.py:270
  318.8 47.8 %shard_map.234 = (f32[512,1536]{1,0:T(8,128)}, f32[24,512,1]{2,1,0:T(8,128)}, f32[512,1536]{1,0:T(8,128)}) custom-call(bf16[24,512,256]{2,1,0:T(8,128)(2,1)} %get-tuple-element.36.hid_ref, bf16[24,512,256]{2,1,0:T(8,128)(2,1)} %get-tuple-element.37.dga_ref, bf16[24,512,256]{2,1,0:T(8,128)(2,1)} %get-tuple-element.38.dua_ref, bf16[512,1536]{1,0:T(8,128)(2,1)} %dy_ref.3, ...), custom_call_target="tpu_custom_call" | custom-call | flops 28991029248 | bytes 83361792 | tf_op jit(solution)/shard_map/pallas_call | solution.py:163
  369.8 36.5 %shard_map.236 = bf16[2,512,1536]{2,1,0:T(8,128)(2,1)} custom-call(bf16[512,1536]{1,0:T(8,128)(2,1)} %convert_element_type.251.src_ref), custom_call_target="tpu_custom_call" | custom-call | bytes 3145728 | tf_op jit(solution)/shard_map/pallas_call | solution.py:242
  422.8 34.9 %shard_map.235 = bf16[2,512,1536]{2,1,0:T(8,128)(2,1)} custom-call(bf16[512,1536]{1,0:T(8,128)(2,1)} %convert_element_type.245.src_ref), custom_call_target="tpu_custom_call" | custom-call | bytes 3145728 | tf_op jit(solution)/shard_map/pallas_call | solution.py:242
  468.6 19.0 %fusion.32 = bf16[2048,4,64]{0,2,1:T(8,128)(2,1)S(1)} fusion(bf16[4,3,512,64]{2,3,1,0:T(8,128)(2,1)S(1)} %bitcast.205, f32[4,2048,512,3]{2,1,3,0:T(8,128)} %fusion.38, f32[4,3,512]{2,1,0:T(4,128)S(1)} %copy-done.65, pred[512,2048]{0,1:T(8,128)(4,1)S(1)} %copy-done.47), kind=kOutput, calls=%fused_computation.53 | convolution fusion | flops 1661468672 | bytes 53239808 | tf_op jit(solution)/shard_map/kgtn,kgtd->nkd/dot_general | solution.py:526
  491.2 29.2 %multiply_convert_fusion = bf16[4,3,512,2048]{2,3,1,0:T(8,128)(2,1)} fusion(f32[4,2048,512,3]{2,1,3,0:T(8,128)} %fusion.38, f32[4,3,512]{2,1,0:T(4,128)S(1)} %multiply_reduce_fusion.3, f32[4,3,512]{2,1,0:T(4,128)S(1)} %copy-done.65, pred[512,2048]{0,1:T(8,128)(4,1)} %fusion.7, bf16[4,3,512,64]{2,3,1,0:T(8,128)(2,1)S(1)} %bitcast.207, ...), kind=kOutput, calls=%fused_computation.3 | convolution fusion | flops 1686110208 | bytes 78430208 | tf_op jit(solution)/shard_map/kgtd,nkd->kgtn/dot_general | solution.py:516
  520.4 13.7 %fusion.31 = bf16[2048,4,64]{0,2,1:T(8,128)(2,1)} fusion(bf16[4,3,512,2048]{2,3,1,0:T(8,128)(2,1)} %multiply_convert_fusion, bf16[512,4,3,32]{0,3,2,1:T(8,128)(2,1)S(1)} %bitcast.201, bf16[512,4,3,32]{0,3,2,1:T(8,128)(2,1)S(1)} %bitcast.198), kind=kOutput, calls=%fused_computation.52 | convolution fusion | flops 1613234176 | bytes 27000832 | tf_op jit(solution)/shard_map/kgtn,tkgd->nkd/dot_general | solution.py:523
  539.9 98.1 %shard_map.238 = bf16[4,512,512]{2,1,0:T(8,128)(2,1)} custom-call(bf16[4,512,512]{2,1,0:T(8,128)(2,1)} %pad_maximum_fusion.src_ref), custom_call_target="tpu_custom_call" | custom-call | bytes 3145728 | tf_op jit(solution)/shard_map/pallas_call | solution.py:242
  642.6 11.5 %convolution_multiply_fusion = f32[4,3,512,64]{2,3,1,0:T(8,128)S(1)} fusion(bf16[4,3,512,2048]{2,3,1,0:T(8,128)(2,1)} %multiply_convert_fusion, bf16[2048,4,64,1]{0,2,1,3:T(8,128)(2,1)S(1)} %copy-done.23), kind=kOutput, calls=%fused_computation.63 | convolution fusion | flops 1611005952 | bytes 27787264 | tf_op jit(solution)/shard_map/kgtn,nkd->kgtd/dot_general | solution.py:520
  660.8 36.4 %shard_map.239 = bf16[2,512,1536]{2,1,0:T(8,128)(2,1)} custom-call(bf16[512,1536]{1,0:T(8,128)(2,1)} %fusion.21.src_ref), custom_call_target="tpu_custom_call" | custom-call | bytes 3145728 | tf_op jit(solution)/shard_map/pallas_call | solution.py:242
  728.3 11.1 %concatenate.58 = bf16[2,2,384,2176]{3,2,0,1:T(8,128)(2,1)} concatenate(bf16[2,2,384,768]{3,2,0,1:T(8,128)(2,1)} %convolution_convert_fusion.3, bf16[2,2,384,768]{3,2,0,1:T(8,128)(2,1)} %convolution_convert_fusion.2, bf16[2,2,384,256]{3,2,0,1:T(8,128)(2,1)S(1)} %convolution_convert_fusion.4, bf16[2,2,384,256]{3,2,0,1:T(8,128)(2,1)S(1)} %copy-done.39, ...), dimensions={3} | concatenate | bytes 13369344 | tf_op jit(solution)/shard_map/concatenate | solution.py:580
  745.3 57.8 %reduce-scatter.7.cloned.1.call-done = bf16[24,96,256]{2,1,0:T(8,128)(2,1)} async-done(((bf16[24,768,256]{2,1,0:T(8,128)(2,1)}), bf16[24,96,256]{2,1,0:T(8,128)(2,1)}) %reduce-scatter.7.cloned.1.call-update) | async-done | bytes 1179664 | tf_op jit(solution)/shard_map/reduce_scatter | solution.py:483
  806.0 6.3 shard_map.242
  817.8 76.6 %reduce-scatter.13.cloned.1.call-done = bf16[96,2176]{1,0:T(8,128)(2,1)} async-done(((bf16[768,2176]{1,0:T(8,128)(2,1)}), bf16[96,2176]{1,0:T(8,128)(2,1)}) %reduce-scatter.13.cloned.1.call-update) | async-done | bytes 417808
  (288 shorter events, 161.3 us)
Async XLA Ops:
  7.2 113.1 %all-gather.2.cloned.1.call-start = ((), (), s32[]{:S(2)}) async-start(), calls=%async_computation.4 | async-start | bytes 7077888 | tf_op jit(solution)/shard_map/all_gather | solution.py:389
  7.9 731.4 %reduce-scatter.9.cloned.1.call-start = ((), (), s32[]{:S(2)}) async-start(), calls=%async_computation.6 | async-start | bytes 10616832 | tf_op jit(solution)/shard_map/reduce_scatter | solution.py:483
  8.6 61.6 %copy-start.68 = (s32[512]{0:T(512)}, s32[512]{0:T(512)S(1)}, u32[]{:S(2)}) copy-start(s32[512]{0:T(512)S(1)} %get-tuple-element.143) | copy-start | bytes 6148
  9.0 53.9 %copy-start.72 = (f32[512]{0:T(512)}, f32[512]{0:T(512)S(1)}, u32[]{:S(2)}) copy-start(f32[512]{0:T(512)S(1)} %add_rsqrt_fusion.1) | copy-start | bytes 6148
  10.0 56.6 %copy-start.41 = (f32[512,32]{0,1:T(8,128)}, f32[512,32]{0,1:T(8,128)S(1)}, u32[]{:S(2)}) copy-start(f32[512,32]{0,1:T(8,128)S(1)} %get-tuple-element.139) | copy-start | bytes 196612
  93.3 21.3 %copy-start.9 = (f32[4,3,512,64]{2,3,1,0:T(8,128)}, f32[4,3,512,64]{2,3,1,0:T(8,128)S(1)}, u32[]{:S(2)}) copy-start(f32[4,3,512,64]{2,3,1,0:T(8,128)S(1)} %copy.221) | copy-start | bytes 4718596
  93.4 22.4 %copy-start.25 = (bf16[4,3,512,64]{2,3,1,0:T(8,128)(2,1)}, bf16[4,3,512,64]{2,3,1,0:T(8,128)(2,1)S(1)}, u32[]{:S(2)}) copy-start(bf16[4,3,512,64]{2,3,1,0:T(8,128)(2,1)S(1)} %convert_element_type.236) | copy-start | bytes 2359300
  235.5 506.9 %reduce-scatter.11.cloned.1.call-start = ((), (), s32[]{:S(2)}) async-start(), calls=%async_computation.7 | async-start | bytes 10616832 | tf_op jit(solution)/shard_map/reduce_scatter | solution.py:483
  262.5 540.5 %reduce-scatter.7.cloned.1.call-start = ((), (), s32[]{:S(2)}) async-start(), calls=%async_computation.5 | async-start | bytes 10616832 | tf_op jit(solution)/shard_map/reduce_scatter | solution.py:483
  318.8 575.6 %reduce-scatter.13.cloned.1.call-start = ((), (), s32[]{:S(2)}) async-start(), calls=%async_computation.8 | async-start | bytes 3760128
  406.4 10.9 %copy-start.38 = (f32[512,8]{1,0:T(8,128)S(1)}, f32[512,8]{1,0:T(8,128)}, u32[]{:S(2)}) copy-start(f32[512,8]{1,0:T(8,128)} %copy-done.37) | copy-start | bytes 49156
  406.4 10.9 %copy-start.64 = (f32[512]{0:T(512)S(1)}, f32[512]{0:T(512)}, u32[]{:S(2)}) copy-start(f32[512]{0:T(512)} %copy-done.63) | copy-start | bytes 6148
  406.4 15.0 %copy-start.15 = (f32[512,1536]{1,0:T(8,128)S(1)}, f32[512,1536]{1,0:T(8,128)}, u32[]{:S(2)}) copy-start(f32[512,1536]{1,0:T(8,128)} %get-tuple-element.39) | copy-start | bytes 9437188
  422.8 34.9 %copy-start.5 = (f32[512,1536]{1,0:T(8,128)S(1)}, f32[512,1536]{1,0:T(8,128)}, u32[]{:S(2)}) copy-start(f32[512,1536]{1,0:T(8,128)} %copy-done.4) | copy-start | bytes 9437188
  422.8 34.9 %copy-start.56 = (bf16[1536,24]{0,1:T(8,128)(2,1)S(1)}, bf16[1536,24]{0,1:T(8,128)(2,1)}, u32[]{:S(2)}) copy-start(bf16[1536,24]{0,1:T(8,128)(2,1)} %param.21) | copy-start | bytes 221188
  422.8 34.9 %copy-start.60 = (f32[1536]{0:T(1024)S(1)}, f32[1536]{0:T(1024)}, u32[]{:S(2)}) copy-start(f32[1536]{0:T(1024)} %param.20) | copy-start | bytes 18436
  422.8 35.0 %copy-start.62 = (f32[512]{0:T(512)S(1)}, f32[512]{0:T(512)}, u32[]{:S(2)}) copy-start(f32[512]{0:T(512)} %copy-done.61) | copy-start | bytes 6148
  491.2 29.2 %copy-start.29 = (bf16[512,12,32]{0,2,1:T(8,128)(2,1)S(1)}, bf16[512,12,32]{0,2,1:T(8,128)(2,1)}, u32[]{:S(2)}) copy-start(bf16[512,12,32]{0,2,1:T(8,128)(2,1)} %copy-done.27) | copy-start | bytes 1179652
  491.2 29.2 %copy-start.32 = (bf16[512,12,32]{0,2,1:T(8,128)(2,1)S(1)}, bf16[512,12,32]{0,2,1:T(8,128)(2,1)}, u32[]{:S(2)}) copy-start(bf16[512,12,32]{0,2,1:T(8,128)(2,1)} %copy-done.30) | copy-start | bytes 1179652
  539.9 98.2 %copy-start.74 = (pred[4]{0:T(512)(128)(4,1)S(1)}, pred[4]{0:T(512)(128)(4,1)}, u32[]{:S(2)}) copy-start(pred[4]{0:T(512)(128)(4,1)} %iota_compare_fusion.2) | copy-start | bytes 16
  660.8 36.4 %copy-start.6 = (bf16[512,1536]{1,0:T(8,128)(2,1)S(1)}, bf16[512,1536]{1,0:T(8,128)(2,1)}, u32[]{:S(2)}) copy-start(bf16[512,1536]{1,0:T(8,128)(2,1)} %fusion.21.src_ref) | copy-start | bytes 4718596
  660.8 36.4 %copy-start.13 = (bf16[512,1536]{1,0:T(8,128)(2,1)S(1)}, bf16[512,1536]{1,0:T(8,128)(2,1)}, u32[]{:S(2)}) copy-start(bf16[512,1536]{1,0:T(8,128)(2,1)} %param.14) | copy-start | bytes 4718596
  660.8 36.4 %copy-start.67 = (f32[1536]{0:T(1024)S(1)}, f32[1536]{0:T(1024)}, u32[]{:S(2)}) copy-start(f32[1536]{0:T(1024)} %param.15) | copy-start | bytes 18436
  660.8 36.4 %copy-start.73 = (f32[512]{0:T(512)S(1)}, f32[512]{0:T(512)}, u32[]{:S(2)}) copy-start(f32[512]{0:T(512)} %copy-done.72) | copy-start | bytes 6148
  (57 other events, 157.4 us)
Sparse Core Ops, SparseCore 0:
  9.6 65.3 all-gather.1
  235.6 203.8 reduce-scatter.8
  443.1 195.1 reduce-scatter.10
  641.7 161.3 reduce-scatter.6
  817.9 76.4 reduce-scatter.12

commit v8 on v7

--- a/solution.py
+++ b/solution.py
@@ -70,6 +70,12 @@
         for c in range(cores):
             start = (x * cores + c) * rows
             out_ref[c, 0, x] = value[start : start + rows].astype(out_ref.dtype)
+
+
+def _gate_column(gates_ref):
+    gates = gates_ref[...]
+    lane = lax.broadcasted_iota(jnp.int32, gates.shape, 1)
+    return jnp.sum(jnp.where(lane == pl.program_id(0), gates, 0.0), axis=1, keepdims=True)
 
 
 def _grad_body(
@@ -86,7 +92,7 @@
     silu = gate_act * sig
     hidden = (silu * up_act).astype(bf16)
     hid_ref[0] = hidden
-    deo = (gcol_ref[0] * dy_ref[...].astype(f32)).astype(bf16)
+    deo = (_gate_column(gcol_ref) * dy_ref[...].astype(f32)).astype(bf16)
     grad_hidden = jnp.dot(deo, wd, preferred_element_type=f32)
     deo_t = (grow_ref[0] * dyt_ref[...].astype(f32)).astype(bf16)
     _store_split(gd_ref, jnp.dot(deo_t, hidden, preferred_element_type=f32))
@@ -109,7 +115,7 @@
         dn2_ref[...] = jnp.zeros_like(dn2_ref)
 
     expert_out = lax.dot_general(hid_ref[0], wd_ref[0], nt, preferred_element_type=f32)
-    acc_ref[...] += gcol_ref[0] * expert_out
+    acc_ref[...] += _gate_column(gcol_ref) * expert_out
     dgate_ref[0] = jnp.sum(expert_out * dy_ref[...].astype(f32), axis=1, keepdims=True)
     dn2_ref[...] += lax.dot_general(
         dga_ref[0], wg_ref[0], nt, preferred_element_type=f32
@@ -134,7 +140,7 @@
             whole((width, tokens)),
             whole((tokens, width)),
             whole((width, tokens)),
-            per_expert((tokens, 1)),
+            whole((tokens, experts)),
             per_expert((1, tokens)),
             per_expert((width, hidden)),
             per_expert((width, hidden)),
@@ -168,7 +174,7 @@
             per_expert((tokens, hidden)),
             per_expert((tokens, hidden)),
             whole((tokens, width)),
-            per_expert((tokens, 1)),
+            whole((tokens, experts)),
             per_expert((width, hidden)),
             per_expert((width, hidden)),
             per_expert((width, hidden)),
@@ -262,12 +268,31 @@
     return x.astype(jnp.float32) + other.astype(jnp.float32)
 
 
+def _pair_add_body(me_ref, own_ref, other_ref, out_ref):
+    out_ref[...] = (own_ref[...].astype(jnp.float32) + other_ref[...].astype(jnp.float32)).astype(out_ref.dtype)
+
+
 def core_reduce(x, collective_id):
     got = exchange(x, "core", 2, True, collective_id)
     me = lax.axis_index("core")
-    own = lax.dynamic_index_in_dim(x, me, 0, keepdims=False)
-    other = lax.dynamic_index_in_dim(got, 1 - me, 0, keepdims=False)
-    return (own.astype(jnp.float32) + other.astype(jnp.float32)).astype(jnp.bfloat16)
+    count = x.shape[1]
+    rest = x.shape[2:]
+    zeros = (0,) * len(rest)
+    grid_spec = pltpu.PrefetchScalarGridSpec(
+        num_scalar_prefetch=1,
+        grid=(count,),
+        in_specs=[
+            pl.BlockSpec((None, None) + rest, lambda i, c: (c[0], i) + zeros),
+            pl.BlockSpec((None, None) + rest, lambda i, c: (1 - c[0], i) + zeros),
+        ],
+        out_specs=pl.BlockSpec((None,) + rest, lambda i, c: (i,) + zeros),
+    )
+    return pl.pallas_call(
+        _pair_add_body,
+        grid_spec=grid_spec,
+        out_shape=jax.ShapeDtypeStruct(x.shape[1:], jnp.bfloat16),
+        cost_estimate=pl.CostEstimate(flops=x.size // 2, transcendentals=0, bytes_accessed=x.size * 3),
+    )(jnp.reshape(me, (1,)).astype(jnp.int32), x, got)
 
 
 def scatter_sum_downward(x, axis, n, collective_id):
@@ -454,7 +479,7 @@
     gates_dense = jnp.sum(jnp.where(picked_onehot, gate_probs[:, :, None], 0.0), axis=1)
     gates_by_expert = jnp.transpose(gates_dense)
     cot_bf = output_grad
-    gcol = gates_by_expert[:, :, None]
+    gcol = gates_dense
     grad_gate, grad_up, grad_down, hid_all, dga_all, dua_all = expert_grad_kernel(
         normed_two,
         jnp.transpose(normed_two),

time: 912 us -> 917 us (level)
  Pallas kernels: 461 us -> 507 us
  other arithmetic: 85.7 us -> 44.6 us
    pallas_call x0 -> x4, Pallas kernels: none -> 60 us  [core_reduce(): pl.pallas_call(_pair_add_body, grid_spec=grid_spec, out_shape=jax.ShapeDt...]
    convert_element_type x4 -> x0, other arithmetic: 41.4 us -> none  [core_reduce(): (own.astype(jnp.float32) + other.astype(jnp.float32)).astype(jnp.bfloat16)]
    pallas_call x11, Pallas kernels: 322 us -> 310 us  [exchange(): pl.pallas_call(functools.partial(_exchange_body, axis, n, per_peer, downw...]
  transfers between devices with their start and end apart: 5 -> 5, of which waited for: 2 -> 2; matrix products, arithmetic and copies ran while one was open for 27% -> 24% of each run, Pallas kernels for 40% -> 43%
where the time goes in v8:
time: 917 us; the launch traced here: 911 us
  Pallas kernels  507 us (55%)
  waiting for transfers between devices  138 us (15%)
  matrix products  121 us (13%)
  local copies, waits for them, and re-layouts  85.6 us (9%)
  other arithmetic  44.6 us (5%)
  between operations  15.3 us (2%)
    pallas_call x11, Pallas kernels, exchange(): pl.pallas_call(functools.partial(_exchange_body, axis, n, per_peer, downw...  310 us
    unnamed x6, waiting for transfers between devices  77.2 us
    pallas_call x1, Pallas kernels, expert_grad_kernel(): pl.pallas_call(_grad_body, grid=(experts,), in_specs=[whole((tokens, widt...  73.6 us
    reduce_scatter x3, waiting for transfers between devices, per_device(): lax.psum_scatter(g.reshape(g.shape[0], -1, g.shape[3]), ('dpx', 'ctx'), s...  60.7 us
    pallas_call x4, Pallas kernels, core_reduce(): pl.pallas_call(_pair_add_body, grid_spec=grid_spec, out_shape=jax.ShapeDt...  60 us
    pallas_call x1, Pallas kernels, expert_rows_kernel(): pl.pallas_call(_rows_body, grid=(experts,), in_specs=[per_expert((tokens,...  46.6 us
    dot_general x1, matrix products, per_device(): jnp.einsum('kgtd,nkd->kgtn', grad_attn_grouped, value_piece, preferred_el...  29 us
    unnamed x164, local copies, waits for them, and re-layouts  23.9 us
  transfers between devices with their start and end apart: 5, of which 2 were waited for; matrix products, arithmetic and copies ran while one was open for 24% of the time, Pallas kernels for 43%

profile of v8, /device:TPU:0, one launch (start us, length us, event | category | flops | bytes accessed | tf_op | source)
XLA Modules:
  0.0 911.2 jit_solution(6193172716991810770)
XLA Ops:
  12.5 40.1 %shard_map.229 = bf16[4,512,512]{2,1,0:T(8,128)(2,1)} custom-call(bf16[512,512]{1,0:T(8,128)(2,1)} %pad_maximum_fusion.2.src_ref), custom_call_target="tpu_custom_call" | custom-call | bytes 3145728 | tf_op jit(solution)/shard_map/pallas_call | solution.py:248
  74.0 17.0 %shard_map.230 = (f32[4,1536,64]{2,1,0:T(8,128)}, f32[4,1536,1]{2,1,0:T(8,128)}) custom-call(s32[1]{0:T(128)} %bitcast.ctx_ref, bf16[4,1536,64]{2,1,0:T(8,128)(2,1)S(1)} %bitcast.180, bf16[4,2048,64]{2,1,0:T(8,128)(2,1)S(1)} %bitcast.179, bf16[4,2048,64]{2,1,0:T(8,128)(2,1)} %bitcast.207, s32[1536,1]{1,0:T(8,128)S(1)} %bitcast.181, s32[1536,1]{1,0:T(8,128)S(1)} %bitcast.182, ...), custom_call_target="tpu_custom_call" | custom-call | flops 3221225472 | bytes 4456448 | tf_op jit(solution)/shard_map/pallas_call | solution.py:368
  94.9 19.7 %shard_map.231 = bf16[2,512,768]{2,1,0:T(8,128)(2,1)} custom-call(bf16[512,768]{1,0:T(8,128)(2,1)} %copy.220.src_ref), custom_call_target="tpu_custom_call" | custom-call | bytes 1572864 | tf_op jit(solution)/shard_map/pallas_call | solution.py:248
  131.6 73.6 %shard_map.232 = (bf16[2,24,2,384,256]{4,3,2,1,0:T(8,128)(2,1)}, bf16[2,24,2,384,256]{4,3,2,1,0:T(8,128)(2,1)}, bf16[2,24,2,384,256]{4,3,2,1,0:T(8,128)(2,1)}, b...) custom-call(bf16[512,1536]{1,0:T(8,128)(2,1)} %copy-done.7, ...), custom_call_target="tpu_custom_call" | custom-call | flops 57982058496 | bytes 138412032 | tf_op jit(solution)/shard_map/pallas_call | solution.py:135
  205.1 15.1 %shard_map.241.other_ref = bf16[2,24,2,384,256]{4,3,2,1,0:T(8,128)(2,1)} custom-call(bf16[2,24,2,384,256]{4,3,2,1,0:T(8,128)(2,1)} %get-tuple-element.44.src_ref.own_ref), custom_call_target="tpu_custom_call" | custom-call | bytes 18874368 | tf_op jit(solution)/shard_map/pallas_call | solution.py:248
  220.2 18.4 %shard_map.242 = bf16[24,2,384,256]{3,2,1,0:T(8,128)(2,1)} custom-call(s32[1]{0:T(128)} %bitcast.18.me_ref, bf16[2,24,2,384,256]{4,3,2,1,0:T(8,128)(2,1)} %get-tuple-element.44.src_ref.own_ref, bf16[2,24,2,384,256]{4,3,2,1,0:T(8,128)(2,1)} %shard_map.241.other_ref), custom_call_target="tpu_custom_call" | custom-call | flops 4718592 | bytes 28311552 | tf_op jit(solution)/shard_map/pallas_call | solution.py:290
  238.6 15.1 %shard_map.243.other_ref = bf16[2,24,2,384,256]{4,3,2,1,0:T(8,128)(2,1)} custom-call(bf16[2,24,2,384,256]{4,3,2,1,0:T(8,128)(2,1)} %get-tuple-element.45.src_ref.own_ref), custom_call_target="tpu_custom_call" | custom-call | bytes 18874368 | tf_op jit(solution)/shard_map/pallas_call | solution.py:248
  253.7 18.4 %shard_map.244 = bf16[24,2,384,256]{3,2,1,0:T(8,128)(2,1)} custom-call(s32[1]{0:T(128)} %bitcast.18.me_ref, bf16[2,24,2,384,256]{4,3,2,1,0:T(8,128)(2,1)} %get-tuple-element.45.src_ref.own_ref, bf16[2,24,2,384,256]{4,3,2,1,0:T(8,128)(2,1)} %shard_map.243.other_ref), custom_call_target="tpu_custom_call" | custom-call | flops 4718592 | bytes 28311552 | tf_op jit(solution)/shard_map/pallas_call | solution.py:290
  281.1 20.4 %fusion.37 = f32[4,2048,512,3]{2,1,3,0:T(8,128)} fusion(bf16[2048,4,64,1]{0,2,1,3:T(8,128)(2,1)S(1)} %reshape.386, bf16[512,4,3,32]{0,3,2,1:T(8,128)(2,1)S(1)} %bitcast.197, bf16[512,4,3,32]{0,3,2,1:T(8,128)(2,1)S(1)} %bitcast.194), kind=kOutput, calls=%fused_computation.65 | convolution fusion | flops 1612185600 | bytes 52166656 | tf_op jit(solution)/shard_map/tkgd,nkd->kgtn/dot_general | solution.py:537
  301.4 15.0 %shard_map.233.other_ref = bf16[2,24,2,384,256]{4,3,2,1,0:T(8,128)(2,1)} custom-call(bf16[2,24,2,384,256]{4,3,2,1,0:T(8,128)(2,1)} %get-tuple-element.32.src_ref.own_ref), custom_call_target="tpu_custom_call" | custom-call | bytes 18874368 | tf_op jit(solution)/shard_map/pallas_call | solution.py:248
  316.5 18.8 %shard_map.234 = bf16[24,2,384,256]{3,2,1,0:T(8,128)(2,1)} custom-call(s32[1]{0:T(128)} %bitcast.18.me_ref, bf16[2,24,2,384,256]{4,3,2,1,0:T(8,128)(2,1)} %get-tuple-element.32.src_ref.own_ref, bf16[2,24,2,384,256]{4,3,2,1,0:T(8,128)(2,1)} %shard_map.233.other_ref), custom_call_target="tpu_custom_call" | custom-call | flops 4718592 | bytes 28311552 | tf_op jit(solution)/shard_map/pallas_call | solution.py:290
  335.3 46.6 %shard_map.235 = (f32[512,1536]{1,0:T(8,128)}, f32[24,512,1]{2,1,0:T(8,128)}, f32[512,1536]{1,0:T(8,128)}) custom-call(bf16[24,512,256]{2,1,0:T(8,128)(2,1)} %get-tuple-element.36.hid_ref, bf16[24,512,256]{2,1,0:T(8,128)(2,1)} %get-tuple-element.37.dga_ref, bf16[24,512,256]{2,1,0:T(8,128)(2,1)} %get-tuple-element.38.dua_ref, bf16[512,1536]{1,0:T(8,128)(2,1)} %dy_ref.3, ...), custom_call_target="tpu_custom_call" | custom-call | flops 28991029248 | bytes 83361792 | tf_op jit(solution)/shard_map/pallas_call | solution.py:169
  385.2 36.6 %shard_map.237 = bf16[2,512,1536]{2,1,0:T(8,128)(2,1)} custom-call(bf16[512,1536]{1,0:T(8,128)(2,1)} %convert_element_type.182.src_ref), custom_call_target="tpu_custom_call" | custom-call | bytes 3145728 | tf_op jit(solution)/shard_map/pallas_call | solution.py:248
  438.3 35.0 %shard_map.236 = bf16[2,512,1536]{2,1,0:T(8,128)(2,1)} custom-call(bf16[512,1536]{1,0:T(8,128)(2,1)} %convert_element_type.176.src_ref), custom_call_target="tpu_custom_call" | custom-call | bytes 3145728 | tf_op jit(solution)/shard_map/pallas_call | solution.py:248
  484.3 19.4 %fusion.31 = bf16[2048,4,64]{0,2,1:T(8,128)(2,1)S(1)} fusion(bf16[4,3,512,64]{2,3,1,0:T(8,128)(2,1)S(1)} %bitcast.202, f32[4,2048,512,3]{2,1,3,0:T(8,128)} %fusion.37, f32[4,3,512]{2,1,0:T(4,128)S(1)} %copy-done.65, pred[512,2048]{0,1:T(8,128)(4,1)S(1)} %copy-done.47), kind=kOutput, calls=%fused_computation.48 | convolution fusion | flops 1661468672 | bytes 53239808 | tf_op jit(solution)/shard_map/kgtn,kgtd->nkd/dot_general | solution.py:551
  507.3 29.0 %multiply_convert_fusion = bf16[4,3,512,2048]{2,3,1,0:T(8,128)(2,1)} fusion(f32[4,2048,512,3]{2,1,3,0:T(8,128)} %fusion.37, f32[4,3,512]{2,1,0:T(4,128)S(1)} %multiply_reduce_fusion.3, f32[4,3,512]{2,1,0:T(4,128)S(1)} %copy-done.65, pred[512,2048]{0,1:T(8,128)(4,1)} %fusion.6, bf16[4,3,512,64]{2,3,1,0:T(8,128)(2,1)S(1)} %bitcast.204, ...), kind=kOutput, calls=%fused_computation.3 | convolution fusion | flops 1686110208 | bytes 78430208 | tf_op jit(solution)/shard_map/kgtd,nkd->kgtn/dot_general | solution.py:541
  536.4 13.7 %fusion.30 = bf16[2048,4,64]{0,2,1:T(8,128)(2,1)} fusion(bf16[4,3,512,2048]{2,3,1,0:T(8,128)(2,1)} %multiply_convert_fusion, bf16[512,4,3,32]{0,3,2,1:T(8,128)(2,1)S(1)} %bitcast.198, bf16[512,4,3,32]{0,3,2,1:T(8,128)(2,1)S(1)} %bitcast.195), kind=kOutput, calls=%fused_computation.47 | convolution fusion | flops 1613234176 | bytes 27000832 | tf_op jit(solution)/shard_map/kgtn,tkgd->nkd/dot_general | solution.py:548
  555.8 85.8 %shard_map.239 = bf16[4,512,512]{2,1,0:T(8,128)(2,1)} custom-call(bf16[4,512,512]{2,1,0:T(8,128)(2,1)} %pad_maximum_fusion.src_ref), custom_call_target="tpu_custom_call" | custom-call | bytes 3145728 | tf_op jit(solution)/shard_map/pallas_call | solution.py:248
  646.2 10.6 %convolution_multiply_fusion = f32[4,3,512,64]{2,3,1,0:T(8,128)S(1)} fusion(bf16[4,3,512,2048]{2,3,1,0:T(8,128)(2,1)} %multiply_convert_fusion, bf16[2048,4,64,1]{0,2,1,3:T(8,128)(2,1)S(1)} %copy-done.23), kind=kOutput, calls=%fused_computation.58 | convolution fusion | flops 1611005952 | bytes 27787264 | tf_op jit(solution)/shard_map/kgtn,nkd->kgtd/dot_general | solution.py:545
  663.5 36.0 %shard_map.240 = bf16[2,512,1536]{2,1,0:T(8,128)(2,1)} custom-call(bf16[512,1536]{1,0:T(8,128)(2,1)} %fusion.20.src_ref), custom_call_target="tpu_custom_call" | custom-call | bytes 3145728 | tf_op jit(solution)/shard_map/pallas_call | solution.py:248
  730.6 11.1 %concatenate.58 = bf16[2,2,384,2176]{3,2,0,1:T(8,128)(2,1)} concatenate(bf16[2,2,384,768]{3,2,0,1:T(8,128)(2,1)} %convolution_convert_fusion.3, bf16[2,2,384,768]{3,2,0,1:T(8,128)(2,1)} %convolution_convert_fusion.2, bf16[2,2,384,256]{3,2,0,1:T(8,128)(2,1)S(1)} %convolution_convert_fusion.4, bf16[2,2,384,256]{3,2,0,1:T(8,128)(2,1)S(1)} %copy-done.39, ...), dimensions={3} | concatenate | bytes 13369344 | tf_op jit(solution)/shard_map/concatenate | solution.py:605
  747.7 60.7 %reduce-scatter.7.cloned.1.call-done = bf16[24,96,256]{2,1,0:T(8,128)(2,1)} async-done(((bf16[24,768,256]{2,1,0:T(8,128)(2,1)}), bf16[24,96,256]{2,1,0:T(8,128)(2,1)}) %reduce-scatter.7.cloned.1.call-update) | async-done | bytes 1179664 | tf_op jit(solution)/shard_map/reduce_scatter | solution.py:508
  811.3 6.3 shard_map.245.other_ref
  822.1 76.5 %reduce-scatter.13.cloned.1.call-done = bf16[96,2176]{1,0:T(8,128)(2,1)} async-done(((bf16[768,2176]{1,0:T(8,128)(2,1)}), bf16[96,2176]{1,0:T(8,128)(2,1)}) %reduce-scatter.13.cloned.1.call-update) | async-done | bytes 417808
  (288 shorter events, 157.3 us)
Async XLA Ops:
  7.2 113.1 %all-gather.2.cloned.1.call-start = ((), (), s32[]{:S(2)}) async-start(), calls=%async_computation.4 | async-start | bytes 7077888 | tf_op jit(solution)/shard_map/all_gather | solution.py:414
  7.9 733.7 %reduce-scatter.9.cloned.1.call-start = ((), (), s32[]{:S(2)}) async-start(), calls=%async_computation.6 | async-start | bytes 10616832 | tf_op jit(solution)/shard_map/reduce_scatter | solution.py:508
  8.6 61.7 %copy-start.68 = (s32[512]{0:T(512)}, s32[512]{0:T(512)S(1)}, u32[]{:S(2)}) copy-start(s32[512]{0:T(512)S(1)} %get-tuple-element.143) | copy-start | bytes 6148
  9.0 53.8 %copy-start.72 = (f32[512]{0:T(512)}, f32[512]{0:T(512)S(1)}, u32[]{:S(2)}) copy-start(f32[512]{0:T(512)S(1)} %add_rsqrt_fusion.1) | copy-start | bytes 6148
  10.0 56.5 %copy-start.41 = (f32[512,32]{0,1:T(8,128)}, f32[512,32]{0,1:T(8,128)S(1)}, u32[]{:S(2)}) copy-start(f32[512,32]{0,1:T(8,128)S(1)} %get-tuple-element.139) | copy-start | bytes 196612
  93.4 21.3 %copy-start.9 = (f32[4,3,512,64]{2,3,1,0:T(8,128)}, f32[4,3,512,64]{2,3,1,0:T(8,128)S(1)}, u32[]{:S(2)}) copy-start(f32[4,3,512,64]{2,3,1,0:T(8,128)S(1)} %copy.219) | copy-start | bytes 4718596
  93.5 22.4 %copy-start.25 = (bf16[4,3,512,64]{2,3,1,0:T(8,128)(2,1)}, bf16[4,3,512,64]{2,3,1,0:T(8,128)(2,1)S(1)}, u32[]{:S(2)}) copy-start(bf16[4,3,512,64]{2,3,1,0:T(8,128)(2,1)S(1)} %convert_element_type.171) | copy-start | bytes 2359300
  238.6 506.1 %reduce-scatter.11.cloned.1.call-start = ((), (), s32[]{:S(2)}) async-start(), calls=%async_computation.7 | async-start | bytes 10616832 | tf_op jit(solution)/shard_map/reduce_scatter | solution.py:508
  272.1 536.2 %reduce-scatter.7.cloned.1.call-start = ((), (), s32[]{:S(2)}) async-start(), calls=%async_computation.5 | async-start | bytes 10616832 | tf_op jit(solution)/shard_map/reduce_scatter | solution.py:508
  335.3 563.4 %reduce-scatter.13.cloned.1.call-start = ((), (), s32[]{:S(2)}) async-start(), calls=%async_computation.8 | async-start | bytes 3760128
  421.8 11.0 %copy-start.38 = (f32[512,8]{1,0:T(8,128)S(1)}, f32[512,8]{1,0:T(8,128)}, u32[]{:S(2)}) copy-start(f32[512,8]{1,0:T(8,128)} %copy-done.37) | copy-start | bytes 49156
  421.8 11.0 %copy-start.64 = (f32[512]{0:T(512)S(1)}, f32[512]{0:T(512)}, u32[]{:S(2)}) copy-start(f32[512]{0:T(512)} %copy-done.63) | copy-start | bytes 6148
  421.8 15.1 %copy-start.15 = (f32[512,1536]{1,0:T(8,128)S(1)}, f32[512,1536]{1,0:T(8,128)}, u32[]{:S(2)}) copy-start(f32[512,1536]{1,0:T(8,128)} %get-tuple-element.39) | copy-start | bytes 9437188
  438.3 35.0 %copy-start.5 = (f32[512,1536]{1,0:T(8,128)S(1)}, f32[512,1536]{1,0:T(8,128)}, u32[]{:S(2)}) copy-start(f32[512,1536]{1,0:T(8,128)} %copy-done.4) | copy-start | bytes 9437188
  438.3 35.0 %copy-start.56 = (bf16[1536,24]{0,1:T(8,128)(2,1)S(1)}, bf16[1536,24]{0,1:T(8,128)(2,1)}, u32[]{:S(2)}) copy-start(bf16[1536,24]{0,1:T(8,128)(2,1)} %param.21) | copy-start | bytes 221188
  438.3 35.0 %copy-start.60 = (f32[1536]{0:T(1024)S(1)}, f32[1536]{0:T(1024)}, u32[]{:S(2)}) copy-start(f32[1536]{0:T(1024)} %param.20) | copy-start | bytes 18436
  438.3 35.0 %copy-start.62 = (f32[512]{0:T(512)S(1)}, f32[512]{0:T(512)}, u32[]{:S(2)}) copy-start(f32[512]{0:T(512)} %copy-done.61) | copy-start | bytes 6148
  507.3 29.1 %copy-start.29 = (bf16[512,12,32]{0,2,1:T(8,128)(2,1)S(1)}, bf16[512,12,32]{0,2,1:T(8,128)(2,1)}, u32[]{:S(2)}) copy-start(bf16[512,12,32]{0,2,1:T(8,128)(2,1)} %copy-done.27) | copy-start | bytes 1179652
  507.3 29.1 %copy-start.32 = (bf16[512,12,32]{0,2,1:T(8,128)(2,1)S(1)}, bf16[512,12,32]{0,2,1:T(8,128)(2,1)}, u32[]{:S(2)}) copy-start(bf16[512,12,32]{0,2,1:T(8,128)(2,1)} %copy-done.30) | copy-start | bytes 1179652
  555.8 85.8 %copy-start.74 = (pred[4]{0:T(512)(128)(4,1)S(1)}, pred[4]{0:T(512)(128)(4,1)}, u32[]{:S(2)}) copy-start(pred[4]{0:T(512)(128)(4,1)} %iota_compare_fusion.2) | copy-start | bytes 16
  663.5 36.1 %copy-start.6 = (bf16[512,1536]{1,0:T(8,128)(2,1)S(1)}, bf16[512,1536]{1,0:T(8,128)(2,1)}, u32[]{:S(2)}) copy-start(bf16[512,1536]{1,0:T(8,128)(2,1)} %fusion.20.src_ref) | copy-start | bytes 4718596
  663.5 36.1 %copy-start.13 = (bf16[512,1536]{1,0:T(8,128)(2,1)S(1)}, bf16[512,1536]{1,0:T(8,128)(2,1)}, u32[]{:S(2)}) copy-start(bf16[512,1536]{1,0:T(8,128)(2,1)} %param.14) | copy-start | bytes 4718596
  663.5 36.1 %copy-start.67 = (f32[1536]{0:T(1024)S(1)}, f32[1536]{0:T(1024)}, u32[]{:S(2)}) copy-start(f32[1536]{0:T(1024)} %param.15) | copy-start | bytes 18436
  663.5 36.1 %copy-start.73 = (f32[512]{0:T(512)S(1)}, f32[512]{0:T(512)}, u32[]{:S(2)}) copy-start(f32[512]{0:T(512)} %copy-done.72) | copy-start | bytes 6148
  (57 other events, 156.4 us)
Sparse Core Ops, SparseCore 0:
  9.6 65.3 all-gather.1
  238.7 203.8 reduce-scatter.8
  446.2 189.6 reduce-scatter.10
  639.3 169.0 reduce-scatter.6
  822.3 76.3 reduce-scatter.12

commit v9 on v8

--- a/solution.py
+++ b/solution.py
@@ -278,19 +278,22 @@
     count = x.shape[1]
     rest = x.shape[2:]
     zeros = (0,) * len(rest)
+    item_bytes = math.prod(rest) * x.dtype.itemsize
+    step = max(d for d in range(1, count + 1) if count % d == 0 and d * item_bytes <= 4 * 1024 * 1024)
     grid_spec = pltpu.PrefetchScalarGridSpec(
         num_scalar_prefetch=1,
-        grid=(count,),
+        grid=(count // step,),
         in_specs=[
-            pl.BlockSpec((None, None) + rest, lambda i, c: (c[0], i) + zeros),
-            pl.BlockSpec((None, None) + rest, lambda i, c: (1 - c[0], i) + zeros),
-        ],
-        out_specs=pl.BlockSpec((None,) + rest, lambda i, c: (i,) + zeros),
+            pl.BlockSpec((None, step) + rest, lambda i, c: (c[0], i) + zeros),
+            pl.BlockSpec((None, step) + rest, lambda i, c: (1 - c[0], i) + zeros),
+        ],
+        out_specs=pl.BlockSpec((step,) + rest, lambda i, c: (i,) + zeros),
     )
     return pl.pallas_call(
         _pair_add_body,
         grid_spec=grid_spec,
         out_shape=jax.ShapeDtypeStruct(x.shape[1:], jnp.bfloat16),
+        compiler_params=pltpu.CompilerParams(vmem_limit_bytes=56 * 1024 * 1024),
         cost_estimate=pl.CostEstimate(flops=x.size // 2, transcendentals=0, bytes_accessed=x.size * 3),
     )(jnp.reshape(me, (1,)).astype(jnp.int32), x, got)
 

time: 917 us -> 909 us (level)
    pallas_call x4, Pallas kernels: 60 us -> 39.5 us  [core_reduce(): pl.pallas_call(_pair_add_body, grid_spec=grid_spec, out_shape=jax.ShapeDt...]
    pallas_call x11, Pallas kernels: 310 us -> 325 us  [exchange(): pl.pallas_call(functools.partial(_exchange_body, axis, n, per_peer, downw...]
where the time goes in v9:
time: 909 us; the launch traced here: 905 us
  Pallas kernels  501 us (55%)
  waiting for transfers between devices  137 us (15%)
  matrix products  121 us (13%)
  local copies, waits for them, and re-layouts  85.6 us (9%)
  other arithmetic  44.6 us (5%)
  between operations  15.5 us (2%)
    pallas_call x11, Pallas kernels, exchange(): pl.pallas_call(functools.partial(_exchange_body, axis, n, per_peer, downw...  325 us
    unnamed x6, waiting for transfers between devices  77.3 us
    pallas_call x1, Pallas kernels, expert_grad_kernel(): pl.pallas_call(_grad_body, grid=(experts,), in_specs=[whole((tokens, widt...  73.6 us
    reduce_scatter x3, waiting for transfers between devices, per_device(): lax.psum_scatter(g.reshape(g.shape[0], -1, g.shape[3]), ('dpx', 'ctx'), s...  59.3 us
    pallas_call x1, Pallas kernels, expert_rows_kernel(): pl.pallas_call(_rows_body, grid=(experts,), in_specs=[per_expert((tokens,...  46.4 us
    pallas_call x4, Pallas kernels, core_reduce(): pl.pallas_call(_pair_add_body, grid_spec=grid_spec, out_shape=jax.ShapeDt...  39.5 us
    dot_general x1, matrix products, per_device(): jnp.einsum('kgtd,nkd->kgtn', grad_attn_grouped, value_piece, preferred_el...  29.2 us
    unnamed x164, local copies, waits for them, and re-layouts  23.8 us
  transfers between devices with their start and end apart: 5, of which 2 were waited for; matrix products, arithmetic and copies ran while one was open for 24% of the time, Pallas kernels for 43%

profile of v9, /device:TPU:0, one launch (start us, length us, event | category | flops | bytes accessed | tf_op | source)
XLA Modules:
  0.0 904.8 jit_solution(12083123930668575095)
XLA Ops:
  12.5 40.1 %shard_map.229 = bf16[4,512,512]{2,1,0:T(8,128)(2,1)} custom-call(bf16[512,512]{1,0:T(8,128)(2,1)} %pad_maximum_fusion.2.src_ref), custom_call_target="tpu_custom_call" | custom-call | bytes 3145728 | tf_op jit(solution)/shard_map/pallas_call | solution.py:248
  74.1 17.0 %shard_map.230 = (f32[4,1536,64]{2,1,0:T(8,128)}, f32[4,1536,1]{2,1,0:T(8,128)}) custom-call(s32[1]{0:T(128)} %bitcast.ctx_ref, bf16[4,1536,64]{2,1,0:T(8,128)(2,1)S(1)} %bitcast.180, bf16[4,2048,64]{2,1,0:T(8,128)(2,1)S(1)} %bitcast.179, bf16[4,2048,64]{2,1,0:T(8,128)(2,1)} %bitcast.207, s32[1536,1]{1,0:T(8,128)S(1)} %bitcast.181, s32[1536,1]{1,0:T(8,128)S(1)} %bitcast.182, ...), custom_call_target="tpu_custom_call" | custom-call | flops 3221225472 | bytes 4456448 | tf_op jit(solution)/shard_map/pallas_call | solution.py:371
  95.0 19.7 %shard_map.231 = bf16[2,512,768]{2,1,0:T(8,128)(2,1)} custom-call(bf16[512,768]{1,0:T(8,128)(2,1)} %copy.220.src_ref), custom_call_target="tpu_custom_call" | custom-call | bytes 1572864 | tf_op jit(solution)/shard_map/pallas_call | solution.py:248
  131.8 73.6 %shard_map.232 = (bf16[2,24,2,384,256]{4,3,2,1,0:T(8,128)(2,1)}, bf16[2,24,2,384,256]{4,3,2,1,0:T(8,128)(2,1)}, bf16[2,24,2,384,256]{4,3,2,1,0:T(8,128)(2,1)}, b...) custom-call(bf16[512,1536]{1,0:T(8,128)(2,1)} %copy-done.7, ...), custom_call_target="tpu_custom_call" | custom-call | flops 57982058496 | bytes 138412032 | tf_op jit(solution)/shard_map/pallas_call | solution.py:135
  205.4 15.1 %shard_map.241.other_ref = bf16[2,24,2,384,256]{4,3,2,1,0:T(8,128)(2,1)} custom-call(bf16[2,24,2,384,256]{4,3,2,1,0:T(8,128)(2,1)} %get-tuple-element.44.src_ref.own_ref), custom_call_target="tpu_custom_call" | custom-call | bytes 18874368 | tf_op jit(solution)/shard_map/pallas_call | solution.py:248
  220.4 11.5 %shard_map.242 = bf16[24,2,384,256]{3,2,1,0:T(8,128)(2,1)} custom-call(s32[1]{0:T(128)} %bitcast.18.me_ref, bf16[2,24,2,384,256]{4,3,2,1,0:T(8,128)(2,1)} %get-tuple-element.44.src_ref.own_ref, bf16[2,24,2,384,256]{4,3,2,1,0:T(8,128)(2,1)} %shard_map.241.other_ref), custom_call_target="tpu_custom_call" | custom-call | flops 4718592 | bytes 28311552 | tf_op jit(solution)/shard_map/pallas_call | solution.py:292
  232.0 15.1 %shard_map.243.other_ref = bf16[2,24,2,384,256]{4,3,2,1,0:T(8,128)(2,1)} custom-call(bf16[2,24,2,384,256]{4,3,2,1,0:T(8,128)(2,1)} %get-tuple-element.45.src_ref.own_ref), custom_call_target="tpu_custom_call" | custom-call | bytes 18874368 | tf_op jit(solution)/shard_map/pallas_call | solution.py:248
  247.1 11.3 %shard_map.244 = bf16[24,2,384,256]{3,2,1,0:T(8,128)(2,1)} custom-call(s32[1]{0:T(128)} %bitcast.18.me_ref, bf16[2,24,2,384,256]{4,3,2,1,0:T(8,128)(2,1)} %get-tuple-element.45.src_ref.own_ref, bf16[2,24,2,384,256]{4,3,2,1,0:T(8,128)(2,1)} %shard_map.243.other_ref), custom_call_target="tpu_custom_call" | custom-call | flops 4718592 | bytes 28311552 | tf_op jit(solution)/shard_map/pallas_call | solution.py:292
  267.3 20.2 %fusion.37 = f32[4,2048,512,3]{2,1,3,0:T(8,128)} fusion(bf16[2048,4,64,1]{0,2,1,3:T(8,128)(2,1)S(1)} %reshape.386, bf16[512,4,3,32]{0,3,2,1:T(8,128)(2,1)S(1)} %bitcast.197, bf16[512,4,3,32]{0,3,2,1:T(8,128)(2,1)S(1)} %bitcast.194), kind=kOutput, calls=%fused_computation.65 | convolution fusion | flops 1612185600 | bytes 52166656 | tf_op jit(solution)/shard_map/tkgd,nkd->kgtn/dot_general | solution.py:540
  287.5 15.0 %shard_map.233.other_ref = bf16[2,24,2,384,256]{4,3,2,1,0:T(8,128)(2,1)} custom-call(bf16[2,24,2,384,256]{4,3,2,1,0:T(8,128)(2,1)} %get-tuple-element.32.src_ref.own_ref), custom_call_target="tpu_custom_call" | custom-call | bytes 18874368 | tf_op jit(solution)/shard_map/pallas_call | solution.py:248
  302.6 11.4 %shard_map.234 = bf16[24,2,384,256]{3,2,1,0:T(8,128)(2,1)} custom-call(s32[1]{0:T(128)} %bitcast.18.me_ref, bf16[2,24,2,384,256]{4,3,2,1,0:T(8,128)(2,1)} %get-tuple-element.32.src_ref.own_ref, bf16[2,24,2,384,256]{4,3,2,1,0:T(8,128)(2,1)} %shard_map.233.other_ref), custom_call_target="tpu_custom_call" | custom-call | flops 4718592 | bytes 28311552 | tf_op jit(solution)/shard_map/pallas_call | solution.py:292
  314.0 46.4 %shard_map.235 = (f32[512,1536]{1,0:T(8,128)}, f32[24,512,1]{2,1,0:T(8,128)}, f32[512,1536]{1,0:T(8,128)}) custom-call(bf16[24,512,256]{2,1,0:T(8,128)(2,1)} %get-tuple-element.36.hid_ref, bf16[24,512,256]{2,1,0:T(8,128)(2,1)} %get-tuple-element.37.dga_ref, bf16[24,512,256]{2,1,0:T(8,128)(2,1)} %get-tuple-element.38.dua_ref, bf16[512,1536]{1,0:T(8,128)(2,1)} %dy_ref.3, ...), custom_call_target="tpu_custom_call" | custom-call | flops 28991029248 | bytes 83361792 | tf_op jit(solution)/shard_map/pallas_call | solution.py:169
  363.7 36.7 %shard_map.237 = bf16[2,512,1536]{2,1,0:T(8,128)(2,1)} custom-call(bf16[512,1536]{1,0:T(8,128)(2,1)} %convert_element_type.182.src_ref), custom_call_target="tpu_custom_call" | custom-call | bytes 3145728 | tf_op jit(solution)/shard_map/pallas_call | solution.py:248
  416.8 35.1 %shard_map.236 = bf16[2,512,1536]{2,1,0:T(8,128)(2,1)} custom-call(bf16[512,1536]{1,0:T(8,128)(2,1)} %convert_element_type.176.src_ref), custom_call_target="tpu_custom_call" | custom-call | bytes 3145728 | tf_op jit(solution)/shard_map/pallas_call | solution.py:248
  462.9 18.8 %fusion.31 = bf16[2048,4,64]{0,2,1:T(8,128)(2,1)S(1)} fusion(bf16[4,3,512,64]{2,3,1,0:T(8,128)(2,1)S(1)} %bitcast.202, f32[4,2048,512,3]{2,1,3,0:T(8,128)} %fusion.37, f32[4,3,512]{2,1,0:T(4,128)S(1)} %copy-done.65, pred[512,2048]{0,1:T(8,128)(4,1)S(1)} %copy-done.47), kind=kOutput, calls=%fused_computation.48 | convolution fusion | flops 1661468672 | bytes 53239808 | tf_op jit(solution)/shard_map/kgtn,kgtd->nkd/dot_general | solution.py:554
  485.2 29.2 %multiply_convert_fusion = bf16[4,3,512,2048]{2,3,1,0:T(8,128)(2,1)} fusion(f32[4,2048,512,3]{2,1,3,0:T(8,128)} %fusion.37, f32[4,3,512]{2,1,0:T(4,128)S(1)} %multiply_reduce_fusion.3, f32[4,3,512]{2,1,0:T(4,128)S(1)} %copy-done.65, pred[512,2048]{0,1:T(8,128)(4,1)} %fusion.6, bf16[4,3,512,64]{2,3,1,0:T(8,128)(2,1)S(1)} %bitcast.204, ...), kind=kOutput, calls=%fused_computation.3 | convolution fusion | flops 1686110208 | bytes 78430208 | tf_op jit(solution)/shard_map/kgtd,nkd->kgtn/dot_general | solution.py:544
  514.4 13.6 %fusion.30 = bf16[2048,4,64]{0,2,1:T(8,128)(2,1)} fusion(bf16[4,3,512,2048]{2,3,1,0:T(8,128)(2,1)} %multiply_convert_fusion, bf16[512,4,3,32]{0,3,2,1:T(8,128)(2,1)S(1)} %bitcast.198, bf16[512,4,3,32]{0,3,2,1:T(8,128)(2,1)S(1)} %bitcast.195), kind=kOutput, calls=%fused_computation.47 | convolution fusion | flops 1613234176 | bytes 27000832 | tf_op jit(solution)/shard_map/kgtn,tkgd->nkd/dot_general | solution.py:551
  533.8 100.8 %shard_map.239 = bf16[4,512,512]{2,1,0:T(8,128)(2,1)} custom-call(bf16[4,512,512]{2,1,0:T(8,128)(2,1)} %pad_maximum_fusion.src_ref), custom_call_target="tpu_custom_call" | custom-call | bytes 3145728 | tf_op jit(solution)/shard_map/pallas_call | solution.py:248
  639.2 11.5 %convolution_multiply_fusion = f32[4,3,512,64]{2,3,1,0:T(8,128)S(1)} fusion(bf16[4,3,512,2048]{2,3,1,0:T(8,128)(2,1)} %multiply_convert_fusion, bf16[2048,4,64,1]{0,2,1,3:T(8,128)(2,1)S(1)} %copy-done.23), kind=kOutput, calls=%fused_computation.58 | convolution fusion | flops 1611005952 | bytes 27787264 | tf_op jit(solution)/shard_map/kgtn,nkd->kgtd/dot_general | solution.py:548
  657.4 35.9 %shard_map.240 = bf16[2,512,1536]{2,1,0:T(8,128)(2,1)} custom-call(bf16[512,1536]{1,0:T(8,128)(2,1)} %fusion.20.src_ref), custom_call_target="tpu_custom_call" | custom-call | bytes 3145728 | tf_op jit(solution)/shard_map/pallas_call | solution.py:248
  724.4 11.1 %concatenate.58 = bf16[2,2,384,2176]{3,2,0,1:T(8,128)(2,1)} concatenate(bf16[2,2,384,768]{3,2,0,1:T(8,128)(2,1)} %convolution_convert_fusion.3, bf16[2,2,384,768]{3,2,0,1:T(8,128)(2,1)} %convolution_convert_fusion.2, bf16[2,2,384,256]{3,2,0,1:T(8,128)(2,1)S(1)} %convolution_convert_fusion.4, bf16[2,2,384,256]{3,2,0,1:T(8,128)(2,1)S(1)} %copy-done.39, ...), dimensions={3} | concatenate | bytes 13369344 | tf_op jit(solution)/shard_map/concatenate | solution.py:608
  741.5 59.3 %reduce-scatter.7.cloned.1.call-done = bf16[24,96,256]{2,1,0:T(8,128)(2,1)} async-done(((bf16[24,768,256]{2,1,0:T(8,128)(2,1)}), bf16[24,96,256]{2,1,0:T(8,128)(2,1)}) %reduce-scatter.7.cloned.1.call-update) | async-done | bytes 1179664 | tf_op jit(solution)/shard_map/reduce_scatter | solution.py:511
  803.7 6.3 shard_map.245.other_ref
  815.4 76.6 %reduce-scatter.13.cloned.1.call-done = bf16[96,2176]{1,0:T(8,128)(2,1)} async-done(((bf16[768,2176]{1,0:T(8,128)(2,1)}), bf16[96,2176]{1,0:T(8,128)(2,1)}) %reduce-scatter.13.cloned.1.call-update) | async-done | bytes 417808
  (288 shorter events, 158.4 us)
Async XLA Ops:
  7.2 113.1 %all-gather.2.cloned.1.call-start = ((), (), s32[]{:S(2)}) async-start(), calls=%async_computation.4 | async-start | bytes 7077888 | tf_op jit(solution)/shard_map/all_gather | solution.py:417
  7.9 727.6 %reduce-scatter.9.cloned.1.call-start = ((), (), s32[]{:S(2)}) async-start(), calls=%async_computation.6 | async-start | bytes 10616832 | tf_op jit(solution)/shard_map/reduce_scatter | solution.py:511
  8.6 61.7 %copy-start.68 = (s32[512]{0:T(512)}, s32[512]{0:T(512)S(1)}, u32[]{:S(2)}) copy-start(s32[512]{0:T(512)S(1)} %get-tuple-element.143) | copy-start | bytes 6148
  9.0 53.9 %copy-start.72 = (f32[512]{0:T(512)}, f32[512]{0:T(512)S(1)}, u32[]{:S(2)}) copy-start(f32[512]{0:T(512)S(1)} %add_rsqrt_fusion.1) | copy-start | bytes 6148
  10.0 56.6 %copy-start.41 = (f32[512,32]{0,1:T(8,128)}, f32[512,32]{0,1:T(8,128)S(1)}, u32[]{:S(2)}) copy-start(f32[512,32]{0,1:T(8,128)S(1)} %get-tuple-element.139) | copy-start | bytes 196612
  93.4 21.3 %copy-start.9 = (f32[4,3,512,64]{2,3,1,0:T(8,128)}, f32[4,3,512,64]{2,3,1,0:T(8,128)S(1)}, u32[]{:S(2)}) copy-start(f32[4,3,512,64]{2,3,1,0:T(8,128)S(1)} %copy.219) | copy-start | bytes 4718596
  93.5 22.4 %copy-start.25 = (bf16[4,3,512,64]{2,3,1,0:T(8,128)(2,1)}, bf16[4,3,512,64]{2,3,1,0:T(8,128)(2,1)S(1)}, u32[]{:S(2)}) copy-start(bf16[4,3,512,64]{2,3,1,0:T(8,128)(2,1)S(1)} %convert_element_type.171) | copy-start | bytes 2359300
  231.9 506.6 %reduce-scatter.11.cloned.1.call-start = ((), (), s32[]{:S(2)}) async-start(), calls=%async_computation.7 | async-start | bytes 10616832 | tf_op jit(solution)/shard_map/reduce_scatter | solution.py:511
  258.4 542.4 %reduce-scatter.7.cloned.1.call-start = ((), (), s32[]{:S(2)}) async-start(), calls=%async_computation.5 | async-start | bytes 10616832 | tf_op jit(solution)/shard_map/reduce_scatter | solution.py:511
  314.0 578.0 %reduce-scatter.13.cloned.1.call-start = ((), (), s32[]{:S(2)}) async-start(), calls=%async_computation.8 | async-start | bytes 3760128
  400.4 10.9 %copy-start.38 = (f32[512,8]{1,0:T(8,128)S(1)}, f32[512,8]{1,0:T(8,128)}, u32[]{:S(2)}) copy-start(f32[512,8]{1,0:T(8,128)} %copy-done.37) | copy-start | bytes 49156
  400.4 10.9 %copy-start.64 = (f32[512]{0:T(512)S(1)}, f32[512]{0:T(512)}, u32[]{:S(2)}) copy-start(f32[512]{0:T(512)} %copy-done.63) | copy-start | bytes 6148
  400.5 15.0 %copy-start.15 = (f32[512,1536]{1,0:T(8,128)S(1)}, f32[512,1536]{1,0:T(8,128)}, u32[]{:S(2)}) copy-start(f32[512,1536]{1,0:T(8,128)} %get-tuple-element.39) | copy-start | bytes 9437188
  416.8 35.1 %copy-start.5 = (f32[512,1536]{1,0:T(8,128)S(1)}, f32[512,1536]{1,0:T(8,128)}, u32[]{:S(2)}) copy-start(f32[512,1536]{1,0:T(8,128)} %copy-done.4) | copy-start | bytes 9437188
  416.8 35.1 %copy-start.56 = (bf16[1536,24]{0,1:T(8,128)(2,1)S(1)}, bf16[1536,24]{0,1:T(8,128)(2,1)}, u32[]{:S(2)}) copy-start(bf16[1536,24]{0,1:T(8,128)(2,1)} %param.21) | copy-start | bytes 221188
  416.8 35.2 %copy-start.60 = (f32[1536]{0:T(1024)S(1)}, f32[1536]{0:T(1024)}, u32[]{:S(2)}) copy-start(f32[1536]{0:T(1024)} %param.20) | copy-start | bytes 18436
  416.8 35.2 %copy-start.62 = (f32[512]{0:T(512)S(1)}, f32[512]{0:T(512)}, u32[]{:S(2)}) copy-start(f32[512]{0:T(512)} %copy-done.61) | copy-start | bytes 6148
  485.2 29.2 %copy-start.29 = (bf16[512,12,32]{0,2,1:T(8,128)(2,1)S(1)}, bf16[512,12,32]{0,2,1:T(8,128)(2,1)}, u32[]{:S(2)}) copy-start(bf16[512,12,32]{0,2,1:T(8,128)(2,1)} %copy-done.27) | copy-start | bytes 1179652
  485.2 29.2 %copy-start.32 = (bf16[512,12,32]{0,2,1:T(8,128)(2,1)S(1)}, bf16[512,12,32]{0,2,1:T(8,128)(2,1)}, u32[]{:S(2)}) copy-start(bf16[512,12,32]{0,2,1:T(8,128)(2,1)} %copy-done.30) | copy-start | bytes 1179652
  533.8 100.8 %copy-start.74 = (pred[4]{0:T(512)(128)(4,1)S(1)}, pred[4]{0:T(512)(128)(4,1)}, u32[]{:S(2)}) copy-start(pred[4]{0:T(512)(128)(4,1)} %iota_compare_fusion.2) | copy-start | bytes 16
  657.3 35.9 %copy-start.6 = (bf16[512,1536]{1,0:T(8,128)(2,1)S(1)}, bf16[512,1536]{1,0:T(8,128)(2,1)}, u32[]{:S(2)}) copy-start(bf16[512,1536]{1,0:T(8,128)(2,1)} %fusion.20.src_ref) | copy-start | bytes 4718596
  657.3 35.9 %copy-start.13 = (bf16[512,1536]{1,0:T(8,128)(2,1)S(1)}, bf16[512,1536]{1,0:T(8,128)(2,1)}, u32[]{:S(2)}) copy-start(bf16[512,1536]{1,0:T(8,128)(2,1)} %param.14) | copy-start | bytes 4718596
  657.3 36.0 %copy-start.67 = (f32[1536]{0:T(1024)S(1)}, f32[1536]{0:T(1024)}, u32[]{:S(2)}) copy-start(f32[1536]{0:T(1024)} %param.15) | copy-start | bytes 18436
  657.4 36.0 %copy-start.73 = (f32[512]{0:T(512)S(1)}, f32[512]{0:T(512)}, u32[]{:S(2)}) copy-start(f32[512]{0:T(512)} %copy-done.72) | copy-start | bytes 6148
  (57 other events, 156.5 us)
Sparse Core Ops, SparseCore 0:
  9.6 65.3 all-gather.1
  232.1 203.8 reduce-scatter.8
  439.6 195.9 reduce-scatter.10
  639.0 161.6 reduce-scatter.6
  815.5 76.4 reduce-scatter.12

commit v10 on v9

--- a/solution.py
+++ b/solution.py
@@ -306,9 +306,11 @@
     return own + jnp.sum(jnp.where(above, got.astype(jnp.float32), 0.0), axis=0)
 
 
-def _flash_body(ctx_ref, q_ref, k_ref, v_ref, qseg_ref, qpos_ref, kseg_ref, o_ref, lse_ref, m_sc, l_sc, acc_sc):
+def _flash_body(groups, ctx_ref, q_ref, k_ref, v_ref, qseg_ref, qpos_ref, kseg_ref, o_ref, lse_ref, m_sc, l_sc, acc_sc):
     f32 = jnp.float32
     block = pl.program_id(1)
+    depth = HEAD_SIZE
+    pair = k_ref.shape[2] // depth
 
     @pl.when(block == 0)
     def _():
@@ -318,73 +320,82 @@
 
     @pl.when(block <= ctx_ref[0])
     def _():
-        keys = k_ref[0]
-        width = keys.shape[0]
-        scores = lax.dot_general(
-            q_ref[0], keys, (((1,), (1,)), ((), ())), preferred_element_type=f32
-        ) * (1.0 / math.sqrt(HEAD_SIZE))
+        width = k_ref.shape[1]
         key_pos = block * width + lax.broadcasted_iota(jnp.int32, (1, width), 1)
         allowed = (qseg_ref[...] == kseg_ref[...]) & (key_pos <= qpos_ref[...])
-        scores = jnp.where(allowed, scores, NEGATIVE)
-        m_old = m_sc[...]
-        m_new = jnp.maximum(m_old, jnp.max(scores, axis=1, keepdims=True))
-        alpha = jnp.exp(m_old - m_new)
-        weights = jnp.where(allowed, jnp.exp(scores - m_new), 0.0)
-        l_sc[...] = alpha * l_sc[...] + jnp.sum(weights, axis=1, keepdims=True)
-        acc_sc[...] = alpha * acc_sc[...] + jnp.dot(
-            weights.astype(jnp.bfloat16), v_ref[0], preferred_element_type=f32
-        )
-        m_sc[...] = m_new
+        for kk in range(pair):
+            keys = k_ref[0, :, kk * depth : (kk + 1) * depth]
+            values = v_ref[0, :, kk * depth : (kk + 1) * depth]
+            for gi in range(groups):
+                i = kk * groups + gi
+                cols = slice(i * depth, (i + 1) * depth)
+                scores = lax.dot_general(
+                    q_ref[:, cols], keys, (((1,), (1,)), ((), ())), preferred_element_type=f32
+                ) * (1.0 / math.sqrt(HEAD_SIZE))
+                scores = jnp.where(allowed, scores, NEGATIVE)
+                m_old = m_sc[i]
+                m_new = jnp.maximum(m_old, jnp.max(scores, axis=1, keepdims=True))
+                alpha = jnp.exp(m_old - m_new)
+                weights = jnp.where(allowed, jnp.exp(scores - m_new), 0.0)
+                l_sc[i] = alpha * l_sc[i] + jnp.sum(weights, axis=1, keepdims=True)
+                acc_sc[:, cols] = alpha * acc_sc[:, cols] + jnp.dot(
+                    weights.astype(jnp.bfloat16), values, preferred_element_type=f32
+                )
+                m_sc[i] = m_new
 
     @pl.when(block == pl.num_programs(1) - 1)
     def _():
-        o_ref[0] = acc_sc[...] / l_sc[...]
-        lse_ref[0] = m_sc[...] + jnp.log(l_sc[...])
-
-
-def flash_forward(ctx_index, q, k, v, qseg, qpos, kseg, width):
-    heads, rows, depth = q.shape
-    blocks = k.shape[1] // width
+        for i in range(m_sc.shape[0]):
+            cols = slice(i * depth, (i + 1) * depth)
+            o_ref[:, cols] = acc_sc[:, cols] / l_sc[i]
+            lse_ref[0, :, i : i + 1] = m_sc[i] + jnp.log(l_sc[i])
+
+
+def flash_forward(ctx_index, q, kv, qseg, qpos, kseg, groups):
+    tokens, q_width = q.shape
+    blocks, width, kv_width = kv.shape
+    pair = 2
+    pairs = kv_width // (2 * pair * HEAD_SIZE)
+    heads_step = pair * groups
     f32 = jnp.float32
-    capped = lambda h, b, c: (h, jnp.minimum(b, c[0]), 0)
+    capped = lambda p, b, c: (jnp.minimum(b, c[0]), 0, p)
     grid_spec = pltpu.PrefetchScalarGridSpec(
         num_scalar_prefetch=1,
-        grid=(heads, blocks),
+        grid=(pairs, blocks),
         in_specs=[
-            pl.BlockSpec((1, rows, depth), lambda h, b, c: (h, 0, 0)),
-            pl.BlockSpec((1, width, depth), capped),
-            pl.BlockSpec((1, width, depth), capped),
-            pl.BlockSpec((rows, 1), lambda h, b, c: (0, 0)),
-            pl.BlockSpec((rows, 1), lambda h, b, c: (0, 0)),
-            pl.BlockSpec((1, width), lambda h, b, c: (0, jnp.minimum(b, c[0]))),
+            pl.BlockSpec((tokens, heads_step * HEAD_SIZE), lambda p, b, c: (0, p)),
+            pl.BlockSpec((1, width, pair * HEAD_SIZE), capped),
+            pl.BlockSpec((1, width, pair * HEAD_SIZE), lambda p, b, c: (jnp.minimum(b, c[0]), 0, pairs + p)),
+            pl.BlockSpec((tokens, 1), lambda p, b, c: (0, 0)),
+            pl.BlockSpec((tokens, 1), lambda p, b, c: (0, 0)),
+            pl.BlockSpec((1, width), lambda p, b, c: (0, jnp.minimum(b, c[0]))),
         ],
         out_specs=[
-            pl.BlockSpec((1, rows, depth), lambda h, b, c: (h, 0, 0)),
-            pl.BlockSpec((1, rows, 1), lambda h, b, c: (h, 0, 0)),
+            pl.BlockSpec((tokens, heads_step * HEAD_SIZE), lambda p, b, c: (0, p)),
+            pl.BlockSpec((1, tokens, heads_step), lambda p, b, c: (p, 0, 0)),
         ],
         scratch_shapes=[
-            pltpu.VMEM((rows, 1), f32),
-            pltpu.VMEM((rows, 1), f32),
-            pltpu.VMEM((rows, depth), f32),
+            pltpu.VMEM((heads_step, tokens, 1), f32),
+            pltpu.VMEM((heads_step, tokens, 1), f32),
+            pltpu.VMEM((tokens, heads_step * HEAD_SIZE), f32),
         ],
     )
     return pl.pallas_call(
-        _flash_body,
+        functools.partial(_flash_body, groups),
         grid_spec=grid_spec,
         out_shape=[
-            jax.ShapeDtypeStruct((heads, rows, depth), f32),
-            jax.ShapeDtypeStruct((heads, rows, 1), f32),
+            jax.ShapeDtypeStruct((tokens, q_width), f32),
+            jax.ShapeDtypeStruct((pairs, tokens, heads_step), f32),
         ],
         compiler_params=pltpu.CompilerParams(
             dimension_semantics=("arbitrary", "arbitrary"), vmem_limit_bytes=48 * 1024 * 1024
         ),
         cost_estimate=pl.CostEstimate(
-            flops=heads * rows * k.shape[1] * depth * 4,
-            transcendentals=heads * rows * k.shape[1],
-            bytes_accessed=(q.size + k.size + v.size) * 2 + heads * rows * depth * 4,
-        ),
-    )(jnp.reshape(ctx_index, (1,)).astype(jnp.int32), q, k, v, qseg, qpos, kseg)
-
+            flops=tokens * q_width * blocks * width * 4,
+            transcendentals=tokens * (q_width // HEAD_SIZE) * blocks * width,
+            bytes_accessed=(q.size + kv.size) * 2 + tokens * q_width * 4,
+        ),
+    )(jnp.reshape(ctx_index, (1,)).astype(jnp.int32), q, kv, kv, qseg, qpos, kseg)
 
 def per_device(
     dpx_count,
@@ -448,25 +459,22 @@
     kv_width = kv_local * HEAD_SIZE
     key_piece = kv_both[:, :, :kv_width].reshape(piece_rows, kv_local, HEAD_SIZE)
     value_piece = kv_both[:, :, kv_width:].reshape(piece_rows, kv_local, HEAD_SIZE)
-    row_segments = jnp.tile(segment_here, group_size)[:, None]
-    row_positions = jnp.tile(token_positions, group_size)[:, None]
-    attn_rows, lse_rows = flash_forward(
+    attn_flat, lse_pairs = flash_forward(
         ctx_index,
-        jnp.transpose(query_grouped, (1, 2, 0, 3)).reshape(kv_local, group_size * token_count, HEAD_SIZE),
-        jnp.transpose(key_piece, (1, 0, 2)),
-        jnp.transpose(value_piece, (1, 0, 2)),
-        row_segments,
-        row_positions,
+        query_grouped.reshape(token_count, heads_local * HEAD_SIZE),
+        kv_both,
+        segment_here[:, None],
+        token_positions[:, None],
         segments[None, :],
-        token_count,
-    )
-    attn_grouped = attn_rows.reshape(kv_local, group_size, token_count, HEAD_SIZE)
-    log_sum = lse_rows.reshape(kv_local, group_size, token_count)
-    attn_bf = (
-        jnp.transpose(attn_grouped, (2, 0, 1, 3))
-        .reshape(token_count, heads_local * HEAD_SIZE)
-        .astype(bf16)
-    )
+        group_size,
+    )
+    attn_grouped = jnp.transpose(
+        attn_flat.reshape(token_count, kv_local, group_size, HEAD_SIZE), (1, 2, 0, 3)
+    )
+    log_sum = jnp.transpose(
+        lse_pairs.reshape(kv_local // 2, token_count, 2, group_size), (0, 2, 3, 1)
+    ).reshape(kv_local, group_size, token_count)
+    attn_bf = attn_flat.astype(bf16)
     tensor_count = o_weight.shape[0] // o_weight.shape[1]
     attn_all = gather_axis(attn_bf, "tensor", tensor_count, 2)
     attn_full = jnp.transpose(attn_all, (1, 0, 2)).reshape(token_count, tensor_count * attn_bf.shape[1])

time: 909 us -> 910 us (level)
  local copies, waits for them, and re-layouts: 85.6 us -> 68.2 us
  Pallas kernels: 501 us -> 517 us
    pallas_call x11, Pallas kernels: 325 us -> 339 us  [exchange(): pl.pallas_call(functools.partial(_exchange_body, axis, n, per_peer, downw...]
    unnamed x164 -> x148, local copies, waits for them, and re-layouts: 23.8 us -> 21 us
  transfers between devices with their start and end apart: 5 -> 5, of which waited for: 2 -> 2; matrix products, arithmetic and copies ran while one was open for 24% -> 23% of each run, Pallas kernels for 43% -> 45%
where the time goes in v10:
time: 910 us; the launch traced here: 904 us
  Pallas kernels  517 us (57%)
  waiting for transfers between devices  134 us (15%)
  matrix products  124 us (14%)
  local copies, waits for them, and re-layouts  68.2 us (7%)
  other arithmetic  46 us (5%)
  between operations  15.2 us (2%)
    pallas_call x11, Pallas kernels, exchange(): pl.pallas_call(functools.partial(_exchange_body, axis, n, per_peer, downw...  339 us
    unnamed x6, waiting for transfers between devices  77.4 us
    pallas_call x1, Pallas kernels, expert_grad_kernel(): pl.pallas_call(_grad_body, grid=(experts,), in_specs=[whole((tokens, widt...  73.8 us
    reduce_scatter x3, waiting for transfers between devices, per_device(): lax.psum_scatter(g.reshape(g.shape[0], -1, g.shape[3]), ('dpx', 'ctx'), s...  56.5 us
    pallas_call x1, Pallas kernels, expert_rows_kernel(): pl.pallas_call(_rows_body, grid=(experts,), in_specs=[per_expert((tokens,...  46.7 us
    pallas_call x4, Pallas kernels, core_reduce(): pl.pallas_call(_pair_add_body, grid_spec=grid_spec, out_shape=jax.ShapeDt...  39.5 us
    dot_general x1, matrix products, per_device(): jnp.einsum('kgtd,nkd->kgtn', grad_attn_grouped, value_piece, preferred_el...  28.8 us
    unnamed x148, local copies, waits for them, and re-layouts  21 us
  transfers between devices with their start and end apart: 5, of which 2 were waited for; matrix products, arithmetic and copies ran while one was open for 23% of the time, Pallas kernels for 45%

profile of v10, /device:TPU:0, one launch (start us, length us, event | category | flops | bytes accessed | tf_op | source)
XLA Modules:
  0.0 904.1 jit_solution(6020554286084569251)
XLA Ops:
  13.2 40.1 %shard_map.229 = bf16[4,512,512]{2,1,0:T(8,128)(2,1)} custom-call(bf16[512,512]{1,0:T(8,128)(2,1)} %pad_maximum_fusion.3.src_ref), custom_call_target="tpu_custom_call" | custom-call | bytes 3145728 | tf_op jit(solution)/shard_map/pallas_call | solution.py:248
  60.8 18.3 %shard_map.230 = (f32[512,768]{1,0:T(8,128)S(1)}, f32[2,512,6]{2,1,0:T(8,128)S(1)}) custom-call(s32[1]{0:T(128)} %bitcast.ctx_ref, bf16[512,768]{1,0:T(8,128)(2,1)S(1)} %copy.190.q_ref, bf16[4,512,512]{2,1,0:T(8,128)(2,1)S(1)} %copy-done.2, bf16[4,512,512]{2,1,0:T(8,128)(2,1)S(1)} %copy-done.2, s32[512,1]{1,0:T(8,128)S(1)} %copy.191.qseg_ref, ...), custom_call_target="tpu_custom_call" | custom-call | flops 3221225472 | bytes 4456448 | tf_op jit(solution)/shard_map/pallas_call | solution.py:383
  81.0 19.7 %shard_map.231 = bf16[2,512,768]{2,1,0:T(8,128)(2,1)} custom-call(bf16[512,768]{1,0:T(8,128)(2,1)} %convert_element_type.170.src_ref), custom_call_target="tpu_custom_call" | custom-call | bytes 1572864 | tf_op jit(solution)/shard_map/pallas_call | solution.py:248
  117.2 73.8 %shard_map.232 = (bf16[2,24,2,384,256]{4,3,2,1,0:T(8,128)(2,1)}, bf16[2,24,2,384,256]{4,3,2,1,0:T(8,128)(2,1)}, bf16[2,24,2,384,256]{4,3,2,1,0:T(8,128)(2,1)}, b...) custom-call(bf16[512,1536]{1,0:T(8,128)(2,1)} %copy-done.10, ...), custom_call_target="tpu_custom_call" | custom-call | flops 57982058496 | bytes 138412032 | tf_op jit(solution)/shard_map/pallas_call | solution.py:135
  191.0 15.1 %shard_map.241.other_ref = bf16[2,24,2,384,256]{4,3,2,1,0:T(8,128)(2,1)} custom-call(bf16[2,24,2,384,256]{4,3,2,1,0:T(8,128)(2,1)} %get-tuple-element.44.src_ref.own_ref), custom_call_target="tpu_custom_call" | custom-call | bytes 18874368 | tf_op jit(solution)/shard_map/pallas_call | solution.py:248
  206.0 11.5 %shard_map.242 = bf16[24,2,384,256]{3,2,1,0:T(8,128)(2,1)} custom-call(s32[1]{0:T(128)} %bitcast.11.me_ref, bf16[2,24,2,384,256]{4,3,2,1,0:T(8,128)(2,1)} %get-tuple-element.44.src_ref.own_ref, bf16[2,24,2,384,256]{4,3,2,1,0:T(8,128)(2,1)} %shard_map.241.other_ref), custom_call_target="tpu_custom_call" | custom-call | flops 4718592 | bytes 28311552 | tf_op jit(solution)/shard_map/pallas_call | solution.py:292
  217.6 15.1 %shard_map.243.other_ref = bf16[2,24,2,384,256]{4,3,2,1,0:T(8,128)(2,1)} custom-call(bf16[2,24,2,384,256]{4,3,2,1,0:T(8,128)(2,1)} %get-tuple-element.45.src_ref.own_ref), custom_call_target="tpu_custom_call" | custom-call | bytes 18874368 | tf_op jit(solution)/shard_map/pallas_call | solution.py:248
  232.6 11.3 %shard_map.244 = bf16[24,2,384,256]{3,2,1,0:T(8,128)(2,1)} custom-call(s32[1]{0:T(128)} %bitcast.11.me_ref, bf16[2,24,2,384,256]{4,3,2,1,0:T(8,128)(2,1)} %get-tuple-element.45.src_ref.own_ref, bf16[2,24,2,384,256]{4,3,2,1,0:T(8,128)(2,1)} %shard_map.243.other_ref), custom_call_target="tpu_custom_call" | custom-call | flops 4718592 | bytes 28311552 | tf_op jit(solution)/shard_map/pallas_call | solution.py:292
  258.5 19.3 %fusion.36 = f32[4,2048,512,3]{2,1,3,0:T(8,128)} fusion(bf16[2048,4,64,1]{0,2,1,3:T(8,128)(2,1)S(1)} %reshape.373, bf16[512,4,3,32]{0,3,2,1:T(8,128)(2,1)S(1)} %bitcast.169, bf16[512,4,3,32]{0,3,2,1:T(8,128)(2,1)S(1)} %bitcast.167), kind=kOutput, calls=%fused_computation.64 | convolution fusion | flops 1612185600 | bytes 52166656 | tf_op jit(solution)/shard_map/tkgd,nkd->kgtn/dot_general | solution.py:548
  277.8 15.0 %shard_map.233.other_ref = bf16[2,24,2,384,256]{4,3,2,1,0:T(8,128)(2,1)} custom-call(bf16[2,24,2,384,256]{4,3,2,1,0:T(8,128)(2,1)} %get-tuple-element.32.src_ref.own_ref), custom_call_target="tpu_custom_call" | custom-call | bytes 18874368 | tf_op jit(solution)/shard_map/pallas_call | solution.py:248
  292.8 11.3 %shard_map.234 = bf16[24,2,384,256]{3,2,1,0:T(8,128)(2,1)} custom-call(s32[1]{0:T(128)} %bitcast.11.me_ref, bf16[2,24,2,384,256]{4,3,2,1,0:T(8,128)(2,1)} %get-tuple-element.32.src_ref.own_ref, bf16[2,24,2,384,256]{4,3,2,1,0:T(8,128)(2,1)} %shard_map.233.other_ref), custom_call_target="tpu_custom_call" | custom-call | flops 4718592 | bytes 28311552 | tf_op jit(solution)/shard_map/pallas_call | solution.py:292
  304.2 46.7 %shard_map.235 = (f32[512,1536]{1,0:T(8,128)}, f32[24,512,1]{2,1,0:T(8,128)}, f32[512,1536]{1,0:T(8,128)}) custom-call(bf16[24,512,256]{2,1,0:T(8,128)(2,1)} %get-tuple-element.36.hid_ref, bf16[24,512,256]{2,1,0:T(8,128)(2,1)} %get-tuple-element.37.dga_ref, bf16[24,512,256]{2,1,0:T(8,128)(2,1)} %get-tuple-element.38.dua_ref, bf16[512,1536]{1,0:T(8,128)(2,1)} %dy_ref.3, ...), custom_call_target="tpu_custom_call" | custom-call | flops 28991029248 | bytes 83361792 | tf_op jit(solution)/shard_map/pallas_call | solution.py:169
  354.1 37.1 %shard_map.237 = bf16[2,512,1536]{2,1,0:T(8,128)(2,1)} custom-call(bf16[512,1536]{1,0:T(8,128)(2,1)} %convert_element_type.178.src_ref), custom_call_target="tpu_custom_call" | custom-call | bytes 3145728 | tf_op jit(solution)/shard_map/pallas_call | solution.py:248
  407.6 35.4 %shard_map.236 = bf16[2,512,1536]{2,1,0:T(8,128)(2,1)} custom-call(bf16[512,1536]{1,0:T(8,128)(2,1)} %convert_element_type.172.src_ref), custom_call_target="tpu_custom_call" | custom-call | bytes 3145728 | tf_op jit(solution)/shard_map/pallas_call | solution.py:248
  456.2 28.8 %multiply_convert_fusion = bf16[4,3,512,2048]{2,3,1,0:T(8,128)(2,1)} fusion(f32[4,2048,512,3]{2,1,3,0:T(8,128)} %fusion.36, f32[4,3,512]{2,1,0:T(4,128)S(1)} %multiply_reduce_fusion.3, f32[4,3,512]{2,1,0:T(4,128)S(1)} %bitcast.193, pred[512,2048]{0,1:T(8,128)(4,1)S(1)} %copy-done.41, bf16[4,3,512,64]{2,3,1,0:T(8,128)(2,1)S(1)} %bitcast.176, ...), kind=kOutput, calls=%fused_computation.3 | convolution fusion | flops 1686110208 | bytes 78430208 | tf_op jit(solution)/shard_map/kgtd,nkd->kgtn/dot_general | solution.py:552
  485.0 12.7 %fusion.30 = bf16[2048,4,64]{0,2,1:T(8,128)(2,1)S(1)} fusion(bf16[4,3,512,2048]{2,3,1,0:T(8,128)(2,1)} %multiply_convert_fusion, bf16[512,4,3,32]{0,3,2,1:T(8,128)(2,1)S(1)} %bitcast.170, bf16[512,4,3,32]{0,3,2,1:T(8,128)(2,1)S(1)} %bitcast.168), kind=kOutput, calls=%fused_computation.48 | convolution fusion | flops 1613234176 | bytes 27000832 | tf_op jit(solution)/shard_map/kgtn,tkgd->nkd/dot_general | solution.py:559
  499.3 20.3 %fusion.31 = bf16[2048,4,64]{0,2,1:T(8,128)(2,1)S(1)} fusion(bf16[4,3,512,64]{2,3,1,0:T(8,128)(2,1)} %bitcast.177, f32[4,2048,512,3]{2,1,3,0:T(8,128)} %fusion.36, f32[4,3,512]{2,1,0:T(4,128)S(1)} %bitcast.194, pred[512,2048]{0,1:T(8,128)(4,1)} %fusion.6), kind=kOutput, calls=%fused_computation.49 | convolution fusion | flops 1661468672 | bytes 53239808 | tf_op jit(solution)/shard_map/kgtn,kgtd->nkd/dot_general | solution.py:562
  522.9 113.2 %shard_map.239 = bf16[4,512,512]{2,1,0:T(8,128)(2,1)} custom-call(bf16[4,512,512]{2,1,0:T(8,128)(2,1)} %pad_maximum_fusion.src_ref), custom_call_target="tpu_custom_call" | custom-call | bytes 3145728 | tf_op jit(solution)/shard_map/pallas_call | solution.py:248
  640.1 11.2 %convolution_multiply_fusion = f32[4,3,512,64]{2,3,1,0:T(8,128)S(1)} fusion(bf16[4,3,512,2048]{2,3,1,0:T(8,128)(2,1)} %multiply_convert_fusion, bf16[2048,4,64,1]{0,2,1,3:T(8,128)(2,1)S(1)} %copy-done.21), kind=kOutput, calls=%fused_computation.57 | convolution fusion | flops 1611005952 | bytes 27787264 | tf_op jit(solution)/shard_map/kgtn,nkd->kgtd/dot_general | solution.py:556
  658.0 36.2 %shard_map.240 = bf16[2,512,1536]{2,1,0:T(8,128)(2,1)} custom-call(bf16[512,1536]{1,0:T(8,128)(2,1)} %fusion.20.src_ref), custom_call_target="tpu_custom_call" | custom-call | bytes 3145728 | tf_op jit(solution)/shard_map/pallas_call | solution.py:248
  727.3 10.5 %concatenate.65 = bf16[2,2,384,2176]{3,2,0,1:T(8,128)(2,1)} concatenate(bf16[2,2,384,768]{3,2,0,1:T(8,128)(2,1)} %convolution_convert_fusion.3, bf16[2,2,384,768]{3,2,0,1:T(8,128)(2,1)S(1)} %copy.222, bf16[2,2,384,256]{3,2,0,1:T(8,128)(2,1)} %convolution_convert_fusion.4, bf16[2,2,384,256]{3,2,0,1:T(8,128)(2,1)S(1)} %copy.223, bf16[2,2,384,24]{3,2,0,1:T(8,128)(2,1)} %copy.224, ...), dimensions={3} | concatenate | bytes 13369344 | tf_op jit(solution)/shard_map/concatenate | solution.py:616
  743.8 56.5 %reduce-scatter.7.cloned.1.call-done = bf16[24,96,256]{2,1,0:T(8,128)(2,1)} async-done(((bf16[24,768,256]{2,1,0:T(8,128)(2,1)}), bf16[24,96,256]{2,1,0:T(8,128)(2,1)}) %reduce-scatter.7.cloned.1.call-update) | async-done | bytes 1179664 | tf_op jit(solution)/shard_map/reduce_scatter | solution.py:519
  803.2 6.3 shard_map.245.other_ref
  814.9 76.6 %reduce-scatter.13.cloned.1.call-done = bf16[96,2176]{1,0:T(8,128)(2,1)} async-done(((bf16[768,2176]{1,0:T(8,128)(2,1)}), bf16[96,2176]{1,0:T(8,128)(2,1)}) %reduce-scatter.13.cloned.1.call-update) | async-done | bytes 417808
  (268 shorter events, 147.0 us)
Async XLA Ops:
  7.2 98.9 %all-gather.2.cloned.1.call-start = ((), (), s32[]{:S(2)}) async-start(), calls=%async_computation.4 | async-start | bytes 7077888 | tf_op jit(solution)/shard_map/all_gather | solution.py:428
  7.9 729.9 %reduce-scatter.9.cloned.1.call-start = ((), (), s32[]{:S(2)}) async-start(), calls=%async_computation.6 | async-start | bytes 10616832 | tf_op jit(solution)/shard_map/reduce_scatter | solution.py:519
  10.0 46.6 %copy-start.38 = (f32[512,32]{0,1:T(8,128)}, f32[512,32]{0,1:T(8,128)S(1)}, u32[]{:S(2)}) copy-start(f32[512,32]{0,1:T(8,128)S(1)} %get-tuple-element.138) | copy-start | bytes 196612
  11.0 42.3 %copy-start.66 = (f32[512]{0:T(512)S(1)}, f32[512]{0:T(512)}, u32[]{:S(2)}) copy-start(f32[512]{0:T(512)} %copy-done.65) | copy-start | bytes 6148
  79.9 21.8 %copy-start = (f32[512,768]{1,0:T(8,128)}, f32[512,768]{1,0:T(8,128)S(1)}, u32[]{:S(2)}) copy-start(f32[512,768]{1,0:T(8,128)S(1)} %get-tuple-element.31) | copy-start | bytes 4718596
  217.5 523.3 %reduce-scatter.11.cloned.1.call-start = ((), (), s32[]{:S(2)}) async-start(), calls=%async_computation.7 | async-start | bytes 10616832 | tf_op jit(solution)/shard_map/reduce_scatter | solution.py:519
  244.0 556.2 %reduce-scatter.7.cloned.1.call-start = ((), (), s32[]{:S(2)}) async-start(), calls=%async_computation.5 | async-start | bytes 10616832 | tf_op jit(solution)/shard_map/reduce_scatter | solution.py:519
  252.3 25.5 %copy-start.20 = (bf16[2048,4,64,1]{0,2,1,3:T(8,128)(2,1)}, bf16[2048,4,64,1]{0,2,1,3:T(8,128)(2,1)S(1)}, u32[]{:S(2)}) copy-start(bf16[2048,4,64,1]{0,2,1,3:T(8,128)(2,1)S(1)} %reshape.373) | copy-start | bytes 3145732
  252.3 6.2 copy-start.24
  304.2 587.3 %reduce-scatter.13.cloned.1.call-start = ((), (), s32[]{:S(2)}) async-start(), calls=%async_computation.8 | async-start | bytes 3760128
  391.2 10.9 %copy-start.34 = (f32[512,8]{1,0:T(8,128)S(1)}, f32[512,8]{1,0:T(8,128)}, u32[]{:S(2)}) copy-start(f32[512,8]{1,0:T(8,128)} %copy-done.33) | copy-start | bytes 49156
  391.2 10.9 %copy-start.59 = (f32[512]{0:T(512)S(1)}, f32[512]{0:T(512)}, u32[]{:S(2)}) copy-start(f32[512]{0:T(512)} %copy-done.58) | copy-start | bytes 6148
  391.2 15.1 %copy-start.16 = (f32[512,1536]{1,0:T(8,128)S(1)}, f32[512,1536]{1,0:T(8,128)}, u32[]{:S(2)}) copy-start(f32[512,1536]{1,0:T(8,128)} %get-tuple-element.39) | copy-start | bytes 9437188
  407.6 35.5 %copy-start.8 = (f32[512,1536]{1,0:T(8,128)S(1)}, f32[512,1536]{1,0:T(8,128)}, u32[]{:S(2)}) copy-start(f32[512,1536]{1,0:T(8,128)} %copy-done.7) | copy-start | bytes 9437188
  407.6 35.5 %copy-start.49 = (bf16[1536,24]{0,1:T(8,128)(2,1)S(1)}, bf16[1536,24]{0,1:T(8,128)(2,1)}, u32[]{:S(2)}) copy-start(bf16[1536,24]{0,1:T(8,128)(2,1)} %param.21) | copy-start | bytes 221188
  407.6 35.5 %copy-start.55 = (f32[1536]{0:T(1024)S(1)}, f32[1536]{0:T(1024)}, u32[]{:S(2)}) copy-start(f32[1536]{0:T(1024)} %param.20) | copy-start | bytes 18436
  407.6 35.5 %copy-start.57 = (f32[512]{0:T(512)S(1)}, f32[512]{0:T(512)}, u32[]{:S(2)}) copy-start(f32[512]{0:T(512)} %copy-done.56) | copy-start | bytes 6148
  456.2 28.8 %copy-start.25 = (bf16[512,12,32]{0,2,1:T(8,128)(2,1)S(1)}, bf16[512,12,32]{0,2,1:T(8,128)(2,1)}, u32[]{:S(2)}) copy-start(bf16[512,12,32]{0,2,1:T(8,128)(2,1)} %copy-done.23) | copy-start | bytes 1179652
  456.2 28.8 %copy-start.28 = (bf16[512,12,32]{0,2,1:T(8,128)(2,1)S(1)}, bf16[512,12,32]{0,2,1:T(8,128)(2,1)}, u32[]{:S(2)}) copy-start(bf16[512,12,32]{0,2,1:T(8,128)(2,1)} %copy-done.26) | copy-start | bytes 1179652
  522.9 113.3 %copy-start.69 = (pred[4]{0:T(512)(128)(4,1)S(1)}, pred[4]{0:T(512)(128)(4,1)}, u32[]{:S(2)}) copy-start(pred[4]{0:T(512)(128)(4,1)} %iota_compare_fusion.2) | copy-start | bytes 16
  658.0 36.2 %copy-start.9 = (bf16[512,1536]{1,0:T(8,128)(2,1)S(1)}, bf16[512,1536]{1,0:T(8,128)(2,1)}, u32[]{:S(2)}) copy-start(bf16[512,1536]{1,0:T(8,128)(2,1)} %fusion.20.src_ref) | copy-start | bytes 4718596
  658.0 36.2 %copy-start.14 = (bf16[512,1536]{1,0:T(8,128)(2,1)S(1)}, bf16[512,1536]{1,0:T(8,128)(2,1)}, u32[]{:S(2)}) copy-start(bf16[512,1536]{1,0:T(8,128)(2,1)} %param.14) | copy-start | bytes 4718596
  658.0 36.2 %copy-start.62 = (f32[1536]{0:T(1024)S(1)}, f32[1536]{0:T(1024)}, u32[]{:S(2)}) copy-start(f32[1536]{0:T(1024)} %param.15) | copy-start | bytes 18436
  658.0 36.2 %copy-start.67 = (f32[512]{0:T(512)S(1)}, f32[512]{0:T(512)}, u32[]{:S(2)}) copy-start(f32[512]{0:T(512)} %copy-done.65) | copy-start | bytes 6148
  (52 other events, 129.9 us)
Sparse Core Ops, SparseCore 0:
  9.6 65.3 all-gather.1
  217.7 219.7 reduce-scatter.8
  441.0 194.1 reduce-scatter.10
  638.7 161.5 reduce-scatter.6
  815.0 76.4 reduce-scatter.12

commit v11 on v10

--- a/solution.py
+++ b/solution.py
@@ -511,8 +511,7 @@
         hid_all, dga_all, dua_all, cot_bf, gcol, gate_weight, up_weight, down_weight
     )
     cot_f32 = output_grad.astype(f32)
-    moe_total = sum_axis(moe_acc.astype(bf16), "tensor", 3)
-    output = (resid + moe_total).astype(bf16)
+    moe_acc_bf = moe_acc.astype(bf16)
     grad_rows_all = moe_grad_rows
     gate_parts = gate_parts[:, :, 0]
     grad_gate_out, grad_up_out, grad_down_out = [
@@ -623,6 +622,8 @@
     dense_all, grad_gate_out, grad_up_out, grad_down_out = lax.optimization_barrier(
         (dense_all, grad_gate_out, grad_up_out, grad_down_out)
     )
+    moe_acc_bf, dense_all = lax.optimization_barrier((moe_acc_bf, dense_all))
+    output = (resid + sum_axis(moe_acc_bf, "tensor", 3)).astype(bf16)
     dense_half = core_reduce(dense_all, 11)
     dense_here = lax.psum_scatter(
         dense_half.reshape(-1, dense_half.shape[-1]), ("dpx", "ctx"), scatter_dimension=0, tiled=True

time: 910 us -> 915 us (level)
  waiting for transfers between devices: 134 us -> 106 us
  local copies, waits for them, and re-layouts: 68.2 us -> 82.4 us
  other arithmetic: 46 us -> 57.4 us
    unnamed x6, waiting for transfers between devices: 77.4 us -> 36.8 us
    reduce_scatter x3, waiting for transfers between devices: 56.5 us -> 69.1 us  [per_device(): lax.psum_scatter(g.reshape(g.shape[0], -1, g.shape[3]), ('dpx', 'ctx'), s...]
    unnamed x148 -> x136, local copies, waits for them, and re-layouts: 21 us -> 19 us
  transfers between devices with their start and end apart: 5 -> 5, of which waited for: 2 -> 2; matrix products, arithmetic and copies ran while one was open for 23% -> 26% of each run, Pallas kernels for 45% -> 45%
where the time goes in v11:
time: 915 us; the launch traced here: 909 us
  Pallas kernels  525 us (57%)
  matrix products  123 us (13%)
  waiting for transfers between devices  106 us (12%)
  local copies, waits for them, and re-layouts  82.4 us (9%)
  other arithmetic  57.4 us (6%)
  between operations  15 us (2%)
    pallas_call x11, Pallas kernels, exchange(): pl.pallas_call(functools.partial(_exchange_body, axis, n, per_peer, downw...  347 us
    pallas_call x1, Pallas kernels, expert_grad_kernel(): pl.pallas_call(_grad_body, grid=(experts,), in_specs=[whole((tokens, widt...  74.1 us
    reduce_scatter x3, waiting for transfers between devices, per_device(): lax.psum_scatter(g.reshape(g.shape[0], -1, g.shape[3]), ('dpx', 'ctx'), s...  69.1 us
    pallas_call x1, Pallas kernels, expert_rows_kernel(): pl.pallas_call(_rows_body, grid=(experts,), in_specs=[per_expert((tokens,...  46.4 us
    pallas_call x4, Pallas kernels, core_reduce(): pl.pallas_call(_pair_add_body, grid_spec=grid_spec, out_shape=jax.ShapeDt...  39.4 us
    unnamed x6, waiting for transfers between devices  36.8 us
    dot_general x1, matrix products, per_device(): jnp.einsum('kgtd,nkd->kgtn', grad_attn_grouped, value_piece, preferred_el...  28 us
    dot_general x1, matrix products, per_device(): jnp.einsum('kgtn,kgtd->nkd', probability.astype(bf16), grad_attn_grouped,...  21.5 us
  transfers between devices with their start and end apart: 5, of which 2 were waited for; matrix products, arithmetic and copies ran while one was open for 26% of the time, Pallas kernels for 45%

profile of v11, /device:TPU:0, one launch (start us, length us, event | category | flops | bytes accessed | tf_op | source)
XLA Modules:
  0.0 909.0 jit_solution(15367049034818140605)
XLA Ops:
  13.3 40.1 %shard_map.229 = bf16[4,512,512]{2,1,0:T(8,128)(2,1)} custom-call(bf16[512,512]{1,0:T(8,128)(2,1)} %pad_maximum_fusion.3.src_ref), custom_call_target="tpu_custom_call" | custom-call | bytes 3145728 | tf_op jit(solution)/shard_map/pallas_call | solution.py:248
  60.8 18.5 %shard_map.230 = (f32[512,768]{1,0:T(8,128)S(1)}, f32[2,512,6]{2,1,0:T(8,128)S(1)}) custom-call(s32[1]{0:T(128)} %bitcast.ctx_ref, bf16[512,768]{1,0:T(8,128)(2,1)S(1)} %copy.190.q_ref, bf16[4,512,512]{2,1,0:T(8,128)(2,1)S(1)} %copy-done.2, bf16[4,512,512]{2,1,0:T(8,128)(2,1)S(1)} %copy-done.2, s32[512,1]{1,0:T(8,128)S(1)} %copy.191.qseg_ref, ...), custom_call_target="tpu_custom_call" | custom-call | flops 3221225472 | bytes 4456448 | tf_op jit(solution)/shard_map/pallas_call | solution.py:383
  81.1 19.7 %shard_map.231 = bf16[2,512,768]{2,1,0:T(8,128)(2,1)} custom-call(bf16[512,768]{1,0:T(8,128)(2,1)} %convert_element_type.170.src_ref), custom_call_target="tpu_custom_call" | custom-call | bytes 1572864 | tf_op jit(solution)/shard_map/pallas_call | solution.py:248
  117.4 74.1 %shard_map.232 = (bf16[2,24,2,384,256]{4,3,2,1,0:T(8,128)(2,1)}, bf16[2,24,2,384,256]{4,3,2,1,0:T(8,128)(2,1)}, bf16[2,24,2,384,256]{4,3,2,1,0:T(8,128)(2,1)}, b...) custom-call(bf16[512,1536]{1,0:T(8,128)(2,1)} %copy-done.10, ...), custom_call_target="tpu_custom_call" | custom-call | flops 57982058496 | bytes 138412032 | tf_op jit(solution)/shard_map/pallas_call | solution.py:135
  191.5 15.1 %shard_map.240.other_ref = bf16[2,24,2,384,256]{4,3,2,1,0:T(8,128)(2,1)} custom-call(bf16[2,24,2,384,256]{4,3,2,1,0:T(8,128)(2,1)} %get-tuple-element.46.src_ref.own_ref), custom_call_target="tpu_custom_call" | custom-call | bytes 18874368 | tf_op jit(solution)/shard_map/pallas_call | solution.py:248
  206.6 11.5 %shard_map.241 = bf16[24,2,384,256]{3,2,1,0:T(8,128)(2,1)} custom-call(s32[1]{0:T(128)} %bitcast.11.me_ref, bf16[2,24,2,384,256]{4,3,2,1,0:T(8,128)(2,1)} %get-tuple-element.46.src_ref.own_ref, bf16[2,24,2,384,256]{4,3,2,1,0:T(8,128)(2,1)} %shard_map.240.other_ref), custom_call_target="tpu_custom_call" | custom-call | flops 4718592 | bytes 28311552 | tf_op jit(solution)/shard_map/pallas_call | solution.py:292
  218.1 15.1 %shard_map.242.other_ref = bf16[2,24,2,384,256]{4,3,2,1,0:T(8,128)(2,1)} custom-call(bf16[2,24,2,384,256]{4,3,2,1,0:T(8,128)(2,1)} %get-tuple-element.47.src_ref.own_ref), custom_call_target="tpu_custom_call" | custom-call | bytes 18874368 | tf_op jit(solution)/shard_map/pallas_call | solution.py:248
  233.2 11.2 %shard_map.243 = bf16[24,2,384,256]{3,2,1,0:T(8,128)(2,1)} custom-call(s32[1]{0:T(128)} %bitcast.11.me_ref, bf16[2,24,2,384,256]{4,3,2,1,0:T(8,128)(2,1)} %get-tuple-element.47.src_ref.own_ref, bf16[2,24,2,384,256]{4,3,2,1,0:T(8,128)(2,1)} %shard_map.242.other_ref), custom_call_target="tpu_custom_call" | custom-call | flops 4718592 | bytes 28311552 | tf_op jit(solution)/shard_map/pallas_call | solution.py:292
  258.9 19.3 %fusion.36 = f32[4,2048,512,3]{2,1,3,0:T(8,128)} fusion(bf16[2048,4,64,1]{0,2,1,3:T(8,128)(2,1)S(1)} %reshape.373, bf16[512,4,3,32]{0,3,2,1:T(8,128)(2,1)S(1)} %bitcast.170, bf16[512,4,3,32]{0,3,2,1:T(8,128)(2,1)S(1)} %bitcast.167), kind=kOutput, calls=%fused_computation.64 | convolution fusion | flops 1612185600 | bytes 52166656 | tf_op jit(solution)/shard_map/tkgd,nkd->kgtn/dot_general | solution.py:547
  278.3 15.0 %shard_map.233.other_ref = bf16[2,24,2,384,256]{4,3,2,1,0:T(8,128)(2,1)} custom-call(bf16[2,24,2,384,256]{4,3,2,1,0:T(8,128)(2,1)} %get-tuple-element.34.src_ref.own_ref), custom_call_target="tpu_custom_call" | custom-call | bytes 18874368 | tf_op jit(solution)/shard_map/pallas_call | solution.py:248
  293.3 11.3 %shard_map.234 = bf16[24,2,384,256]{3,2,1,0:T(8,128)(2,1)} custom-call(s32[1]{0:T(128)} %bitcast.11.me_ref, bf16[2,24,2,384,256]{4,3,2,1,0:T(8,128)(2,1)} %get-tuple-element.34.src_ref.own_ref, bf16[2,24,2,384,256]{4,3,2,1,0:T(8,128)(2,1)} %shard_map.233.other_ref), custom_call_target="tpu_custom_call" | custom-call | flops 4718592 | bytes 28311552 | tf_op jit(solution)/shard_map/pallas_call | solution.py:292
  304.7 46.4 %shard_map.235 = (f32[512,1536]{1,0:T(8,128)}, f32[24,512,1]{2,1,0:T(8,128)}, f32[512,1536]{1,0:T(8,128)}) custom-call(bf16[24,512,256]{2,1,0:T(8,128)(2,1)} %get-tuple-element.38.hid_ref, bf16[24,512,256]{2,1,0:T(8,128)(2,1)} %get-tuple-element.39.dga_ref, bf16[24,512,256]{2,1,0:T(8,128)(2,1)} %get-tuple-element.40.dua_ref, bf16[512,1536]{1,0:T(8,128)(2,1)} %dy_ref.3, ...), custom_call_target="tpu_custom_call" | custom-call | flops 28991029248 | bytes 83361792 | tf_op jit(solution)/shard_map/pallas_call | solution.py:169
  354.3 37.3 %shard_map.236 = bf16[2,512,1536]{2,1,0:T(8,128)(2,1)} custom-call(bf16[512,1536]{1,0:T(8,128)(2,1)} %convert_element_type.174.src_ref), custom_call_target="tpu_custom_call" | custom-call | bytes 3145728 | tf_op jit(solution)/shard_map/pallas_call | solution.py:248
  422.2 28.0 %multiply_convert_fusion = bf16[4,3,512,2048]{2,3,1,0:T(8,128)(2,1)} fusion(f32[4,2048,512,3]{2,1,3,0:T(8,128)} %fusion.36, f32[4,3,512]{2,1,0:T(4,128)} %multiply_reduce_fusion.3, f32[4,3,512]{2,1,0:T(4,128)} %bitcast.193, pred[512,2048]{0,1:T(8,128)(4,1)} %fusion.6, bf16[4,3,512,64]{2,3,1,0:T(8,128)(2,1)} %bitcast.176, bf16[2048,4,64,1]{0,2,1,3:T(8,128)(2,1)} %reshape.374), kind=kOutput, calls=%fused_computation.3 | convolution fusion | flops 1686110208 | bytes 78430208 | tf_op jit(solution)/shard_map/kgtd,nkd->kgtn/dot_general | solution.py:551
  450.2 13.5 %fusion.30 = bf16[2048,4,64]{0,2,1:T(8,128)(2,1)} fusion(bf16[4,3,512,2048]{2,3,1,0:T(8,128)(2,1)} %multiply_convert_fusion, bf16[512,4,3,32]{0,3,2,1:T(8,128)(2,1)} %bitcast.169, bf16[512,4,3,32]{0,3,2,1:T(8,128)(2,1)S(1)} %bitcast.168), kind=kOutput, calls=%fused_computation.48 | convolution fusion | flops 1613234176 | bytes 27000832 | tf_op jit(solution)/shard_map/kgtn,tkgd->nkd/dot_general | solution.py:558
  468.8 21.5 %fusion.31 = bf16[2048,4,64]{0,2,1:T(8,128)(2,1)} fusion(bf16[4,3,512,64]{2,3,1,0:T(8,128)(2,1)} %bitcast.177, f32[4,2048,512,3]{2,1,3,0:T(8,128)} %fusion.36, f32[4,3,512]{2,1,0:T(4,128)S(1)} %bitcast.194, pred[512,2048]{0,1:T(8,128)(4,1)} %fusion.6), kind=kOutput, calls=%fused_computation.49 | convolution fusion | flops 1661468672 | bytes 53239808 | tf_op jit(solution)/shard_map/kgtn,kgtd->nkd/dot_general | solution.py:561
  498.3 120.0 %shard_map.238 = bf16[4,512,512]{2,1,0:T(8,128)(2,1)} custom-call(bf16[4,512,512]{2,1,0:T(8,128)(2,1)} %pad_maximum_fusion.src_ref), custom_call_target="tpu_custom_call" | custom-call | bytes 3145728 | tf_op jit(solution)/shard_map/pallas_call | solution.py:248
  625.9 11.1 %convolution_multiply_fusion = f32[4,3,512,64]{2,3,1,0:T(8,128)S(1)} fusion(bf16[4,3,512,2048]{2,3,1,0:T(8,128)(2,1)} %multiply_convert_fusion, bf16[2048,4,64,1]{0,2,1,3:T(8,128)(2,1)} %copy-done.19), kind=kOutput, calls=%fused_computation.57 | convolution fusion | flops 1611005952 | bytes 27787264 | tf_op jit(solution)/shard_map/kgtn,nkd->kgtd/dot_general | solution.py:555
  643.7 36.1 %shard_map.239 = bf16[2,512,1536]{2,1,0:T(8,128)(2,1)} custom-call(bf16[512,1536]{1,0:T(8,128)(2,1)} %fusion.20.src_ref), custom_call_target="tpu_custom_call" | custom-call | bytes 3145728 | tf_op jit(solution)/shard_map/pallas_call | solution.py:248
  718.9 11.2 %concatenate.65 = bf16[2,2,384,2176]{3,2,0,1:T(8,128)(2,1)} concatenate(bf16[2,2,384,768]{3,2,0,1:T(8,128)(2,1)} %convolution_convert_fusion.3, bf16[2,2,384,768]{3,2,0,1:T(8,128)(2,1)} %copy.222, bf16[2,2,384,256]{3,2,0,1:T(8,128)(2,1)} %convolution_convert_fusion.4, bf16[2,2,384,256]{3,2,0,1:T(8,128)(2,1)} %copy.223, bf16[2,2,384,24]{3,2,0,1:T(8,128)(2,1)} %copy.224, ...), dimensions={3} | concatenate | bytes 13369344 | tf_op jit(solution)/shard_map/concatenate | solution.py:615
  736.0 69.1 %reduce-scatter.7.cloned.1.call-done = bf16[24,96,256]{2,1,0:T(8,128)(2,1)} async-done(((bf16[24,768,256]{2,1,0:T(8,128)(2,1)}), bf16[24,96,256]{2,1,0:T(8,128)(2,1)}) %reduce-scatter.7.cloned.1.call-update) | async-done | bytes 1179664 | tf_op jit(solution)/shard_map/reduce_scatter | solution.py:518
  808.1 6.3 shard_map.245.other_ref
  819.8 36.8 %shard_map.244 = bf16[2,512,1536]{2,1,0:T(8,128)(2,1)} custom-call(bf16[512,1536]{1,0:T(8,128)(2,1)} %convert_element_type.172.src_ref), custom_call_target="tpu_custom_call" | custom-call | bytes 3145728 | tf_op jit(solution)/shard_map/pallas_call | solution.py:248
  860.4 36.1 %reduce-scatter.13.cloned.1.call-done = bf16[96,2176]{1,0:T(8,128)(2,1)} async-done(((bf16[768,2176]{1,0:T(8,128)(2,1)}), bf16[96,2176]{1,0:T(8,128)(2,1)}) %reduce-scatter.13.cloned.1.call-update) | async-done | bytes 417808
  (257 shorter events, 169.6 us)
Async XLA Ops:
  7.2 99.1 %all-gather.2.cloned.1.call-start = ((), (), s32[]{:S(2)}) async-start(), calls=%async_computation.4 | async-start | bytes 7077888 | tf_op jit(solution)/shard_map/all_gather | solution.py:428
  7.9 722.1 %reduce-scatter.9.cloned.1.call-start = ((), (), s32[]{:S(2)}) async-start(), calls=%async_computation.6 | async-start | bytes 10616832 | tf_op jit(solution)/shard_map/reduce_scatter | solution.py:518
  10.0 46.6 %copy-start.33 = (f32[512,32]{0,1:T(8,128)}, f32[512,32]{0,1:T(8,128)S(1)}, u32[]{:S(2)}) copy-start(f32[512,32]{0,1:T(8,128)S(1)} %get-tuple-element.140) | copy-start | bytes 196612
  11.0 42.4 %copy-start.60 = (f32[512]{0:T(512)S(1)}, f32[512]{0:T(512)}, u32[]{:S(2)}) copy-start(f32[512]{0:T(512)} %copy-done.59) | copy-start | bytes 6148
  80.1 21.8 %copy-start = (f32[512,768]{1,0:T(8,128)}, f32[512,768]{1,0:T(8,128)S(1)}, u32[]{:S(2)}) copy-start(f32[512,768]{1,0:T(8,128)S(1)} %get-tuple-element.33) | copy-start | bytes 4718596
  218.0 515.0 %reduce-scatter.11.cloned.1.call-start = ((), (), s32[]{:S(2)}) async-start(), calls=%async_computation.7 | async-start | bytes 10616832 | tf_op jit(solution)/shard_map/reduce_scatter | solution.py:518
  244.4 560.7 %reduce-scatter.7.cloned.1.call-start = ((), (), s32[]{:S(2)}) async-start(), calls=%async_computation.5 | async-start | bytes 10616832 | tf_op jit(solution)/shard_map/reduce_scatter | solution.py:518
  251.9 5.3 copy-start.6
  251.9 5.3 copy-start.58
  251.9 5.3 copy-start.62
  252.8 25.5 %copy-start.19 = (bf16[2048,4,64,1]{0,2,1,3:T(8,128)(2,1)}, bf16[2048,4,64,1]{0,2,1,3:T(8,128)(2,1)S(1)}, u32[]{:S(2)}) copy-start(bf16[2048,4,64,1]{0,2,1,3:T(8,128)(2,1)S(1)} %reshape.373) | copy-start | bytes 3145732
  252.8 6.2 copy-start.21
  252.8 6.2 copy-start.24
  304.6 591.9 %reduce-scatter.13.cloned.1.call-start = ((), (), s32[]{:S(2)}) async-start(), calls=%async_computation.8 | async-start | bytes 3760128
  391.6 12.4 %copy-start.30 = (f32[512,8]{1,0:T(8,128)S(1)}, f32[512,8]{1,0:T(8,128)}, u32[]{:S(2)}) copy-start(f32[512,8]{1,0:T(8,128)} %copy-done.29) | copy-start | bytes 49156
  391.6 16.6 %copy-start.8 = (f32[512,1536]{1,0:T(8,128)S(1)}, f32[512,1536]{1,0:T(8,128)}, u32[]{:S(2)}) copy-start(f32[512,1536]{1,0:T(8,128)} %copy-done.7) | copy-start | bytes 9437188
  391.6 16.6 %copy-start.44 = (bf16[1536,24]{0,1:T(8,128)(2,1)S(1)}, bf16[1536,24]{0,1:T(8,128)(2,1)}, u32[]{:S(2)}) copy-start(bf16[1536,24]{0,1:T(8,128)(2,1)} %param.21) | copy-start | bytes 221188
  391.7 16.6 %copy-start.50 = (f32[1536]{0:T(1024)S(1)}, f32[1536]{0:T(1024)}, u32[]{:S(2)}) copy-start(f32[1536]{0:T(1024)} %param.20) | copy-start | bytes 18436
  422.2 28.0 %copy-start.22 = (bf16[512,12,32]{0,2,1:T(8,128)(2,1)S(1)}, bf16[512,12,32]{0,2,1:T(8,128)(2,1)}, u32[]{:S(2)}) copy-start(bf16[512,12,32]{0,2,1:T(8,128)(2,1)} %copy-done.20) | copy-start | bytes 1179652
  463.7 5.0 copy-start.54
  498.3 120.0 %copy-start.63 = (pred[4]{0:T(512)(128)(4,1)S(1)}, pred[4]{0:T(512)(128)(4,1)}, u32[]{:S(2)}) copy-start(pred[4]{0:T(512)(128)(4,1)} %iota_compare_fusion.2) | copy-start | bytes 16
  643.7 36.1 %copy-start.56 = (f32[1536]{0:T(1024)S(1)}, f32[1536]{0:T(1024)}, u32[]{:S(2)}) copy-start(f32[1536]{0:T(1024)} %param.15) | copy-start | bytes 18436
  643.7 36.1 %copy-start.61 = (f32[512]{0:T(512)S(1)}, f32[512]{0:T(512)}, u32[]{:S(2)}) copy-start(f32[512]{0:T(512)} %copy-done.59) | copy-start | bytes 6148
  710.3 4.9 copy-start.39
  (46 other events, 111.5 us)
Sparse Core Ops, SparseCore 0:
  9.6 65.3 all-gather.1
  218.2 219.7 reduce-scatter.8
  441.5 198.6 reduce-scatter.10
  643.7 161.4 reduce-scatter.6
  820.0 76.4 reduce-scatter.12

commit v12 on v10

--- a/solution.py
+++ b/solution.py
@@ -620,10 +620,10 @@
     dense_all = jnp.transpose(
         dense_all.reshape(dpx_count, 2, width // (2 * dpx_count), dense_all.shape[1]), (1, 0, 2, 3)
     )
-    dense_all, grad_gate_out, grad_up_out, grad_down_out = lax.optimization_barrier(
-        (dense_all, grad_gate_out, grad_up_out, grad_down_out)
-    )
     dense_half = core_reduce(dense_all, 11)
+    dense_half, grad_gate_out, grad_up_out, grad_down_out = lax.optimization_barrier(
+        (dense_half, grad_gate_out, grad_up_out, grad_down_out)
+    )
     dense_here = lax.psum_scatter(
         dense_half.reshape(-1, dense_half.shape[-1]), ("dpx", "ctx"), scatter_dimension=0, tiled=True
     ).astype(f32)

time: 910 us -> 898 us (0.987)
  waiting for transfers between devices: 134 us -> 122 us
    reduce_scatter x3, waiting for transfers between devices: 56.5 us -> 44.7 us  [per_device(): lax.psum_scatter(g.reshape(g.shape[0], -1, g.shape[3]), ('dpx', 'ctx'), s...]
  transfers between devices with their start and end apart: 5 -> 5, of which waited for: 2 -> 2; matrix products, arithmetic and copies ran while one was open for 23% -> 23% of each run, Pallas kernels for 45% -> 47%
where the time goes in v12:
time: 898 us; the launch traced here: 893 us
  Pallas kernels  517 us (58%)
  matrix products  124 us (14%)
  waiting for transfers between devices  122 us (14%)
  local copies, waits for them, and re-layouts  68.2 us (8%)
  other arithmetic  46 us (5%)
  between operations  15.2 us (2%)
    pallas_call x11, Pallas kernels, exchange(): pl.pallas_call(functools.partial(_exchange_body, axis, n, per_peer, downw...  339 us
    unnamed x6, waiting for transfers between devices  77.6 us
    pallas_call x1, Pallas kernels, expert_grad_kernel(): pl.pallas_call(_grad_body, grid=(experts,), in_specs=[whole((tokens, widt...  73.8 us
    pallas_call x1, Pallas kernels, expert_rows_kernel(): pl.pallas_call(_rows_body, grid=(experts,), in_specs=[per_expert((tokens,...  46.7 us
    reduce_scatter x3, waiting for transfers between devices, per_device(): lax.psum_scatter(g.reshape(g.shape[0], -1, g.shape[3]), ('dpx', 'ctx'), s...  44.7 us
    pallas_call x4, Pallas kernels, core_reduce(): pl.pallas_call(_pair_add_body, grid_spec=grid_spec, out_shape=jax.ShapeDt...  39.5 us
    dot_general x1, matrix products, per_device(): jnp.einsum('kgtd,nkd->kgtn', grad_attn_grouped, value_piece, preferred_el...  28.8 us
    unnamed x148, local copies, waits for them, and re-layouts  21 us
  transfers between devices with their start and end apart: 5, of which 2 were waited for; matrix products, arithmetic and copies ran while one was open for 23% of the time, Pallas kernels for 47%

profile of v12, /device:TPU:0, one launch (start us, length us, event | category | flops | bytes accessed | tf_op | source)
XLA Modules:
  0.0 892.7 jit_solution(2043100380357996269)
XLA Ops:
  13.2 40.1 %shard_map.229 = bf16[4,512,512]{2,1,0:T(8,128)(2,1)} custom-call(bf16[512,512]{1,0:T(8,128)(2,1)} %pad_maximum_fusion.3.src_ref), custom_call_target="tpu_custom_call" | custom-call | bytes 3145728 | tf_op jit(solution)/shard_map/pallas_call | solution.py:248
  60.8 18.3 %shard_map.230 = (f32[512,768]{1,0:T(8,128)S(1)}, f32[2,512,6]{2,1,0:T(8,128)S(1)}) custom-call(s32[1]{0:T(128)} %bitcast.ctx_ref, bf16[512,768]{1,0:T(8,128)(2,1)S(1)} %copy.190.q_ref, bf16[4,512,512]{2,1,0:T(8,128)(2,1)S(1)} %copy-done.2, bf16[4,512,512]{2,1,0:T(8,128)(2,1)S(1)} %copy-done.2, s32[512,1]{1,0:T(8,128)S(1)} %copy.191.qseg_ref, ...), custom_call_target="tpu_custom_call" | custom-call | flops 3221225472 | bytes 4456448 | tf_op jit(solution)/shard_map/pallas_call | solution.py:383
  81.0 19.7 %shard_map.231 = bf16[2,512,768]{2,1,0:T(8,128)(2,1)} custom-call(bf16[512,768]{1,0:T(8,128)(2,1)} %convert_element_type.170.src_ref), custom_call_target="tpu_custom_call" | custom-call | bytes 1572864 | tf_op jit(solution)/shard_map/pallas_call | solution.py:248
  117.2 73.8 %shard_map.232 = (bf16[2,24,2,384,256]{4,3,2,1,0:T(8,128)(2,1)}, bf16[2,24,2,384,256]{4,3,2,1,0:T(8,128)(2,1)}, bf16[2,24,2,384,256]{4,3,2,1,0:T(8,128)(2,1)}, b...) custom-call(bf16[512,1536]{1,0:T(8,128)(2,1)} %copy-done.10, ...), custom_call_target="tpu_custom_call" | custom-call | flops 57982058496 | bytes 138412032 | tf_op jit(solution)/shard_map/pallas_call | solution.py:135
  191.0 15.1 %shard_map.243.other_ref = bf16[2,24,2,384,256]{4,3,2,1,0:T(8,128)(2,1)} custom-call(bf16[2,24,2,384,256]{4,3,2,1,0:T(8,128)(2,1)} %get-tuple-element.44.src_ref.own_ref), custom_call_target="tpu_custom_call" | custom-call | bytes 18874368 | tf_op jit(solution)/shard_map/pallas_call | solution.py:248
  206.0 11.5 %shard_map.244 = bf16[24,2,384,256]{3,2,1,0:T(8,128)(2,1)} custom-call(s32[1]{0:T(128)} %bitcast.11.me_ref, bf16[2,24,2,384,256]{4,3,2,1,0:T(8,128)(2,1)} %get-tuple-element.44.src_ref.own_ref, bf16[2,24,2,384,256]{4,3,2,1,0:T(8,128)(2,1)} %shard_map.243.other_ref), custom_call_target="tpu_custom_call" | custom-call | flops 4718592 | bytes 28311552 | tf_op jit(solution)/shard_map/pallas_call | solution.py:292
  217.6 15.1 %shard_map.245.other_ref = bf16[2,24,2,384,256]{4,3,2,1,0:T(8,128)(2,1)} custom-call(bf16[2,24,2,384,256]{4,3,2,1,0:T(8,128)(2,1)} %get-tuple-element.45.src_ref.own_ref), custom_call_target="tpu_custom_call" | custom-call | bytes 18874368 | tf_op jit(solution)/shard_map/pallas_call | solution.py:248
  232.6 11.3 %shard_map.246 = bf16[24,2,384,256]{3,2,1,0:T(8,128)(2,1)} custom-call(s32[1]{0:T(128)} %bitcast.11.me_ref, bf16[2,24,2,384,256]{4,3,2,1,0:T(8,128)(2,1)} %get-tuple-element.45.src_ref.own_ref, bf16[2,24,2,384,256]{4,3,2,1,0:T(8,128)(2,1)} %shard_map.245.other_ref), custom_call_target="tpu_custom_call" | custom-call | flops 4718592 | bytes 28311552 | tf_op jit(solution)/shard_map/pallas_call | solution.py:292
  258.5 19.3 %fusion.36 = f32[4,2048,512,3]{2,1,3,0:T(8,128)} fusion(bf16[2048,4,64,1]{0,2,1,3:T(8,128)(2,1)S(1)} %reshape.373, bf16[512,4,3,32]{0,3,2,1:T(8,128)(2,1)S(1)} %bitcast.169, bf16[512,4,3,32]{0,3,2,1:T(8,128)(2,1)S(1)} %bitcast.167), kind=kOutput, calls=%fused_computation.64 | convolution fusion | flops 1612185600 | bytes 52166656 | tf_op jit(solution)/shard_map/tkgd,nkd->kgtn/dot_general | solution.py:548
  277.8 15.0 %shard_map.233.other_ref = bf16[2,24,2,384,256]{4,3,2,1,0:T(8,128)(2,1)} custom-call(bf16[2,24,2,384,256]{4,3,2,1,0:T(8,128)(2,1)} %get-tuple-element.32.src_ref.own_ref), custom_call_target="tpu_custom_call" | custom-call | bytes 18874368 | tf_op jit(solution)/shard_map/pallas_call | solution.py:248
  292.8 11.3 %shard_map.234 = bf16[24,2,384,256]{3,2,1,0:T(8,128)(2,1)} custom-call(s32[1]{0:T(128)} %bitcast.11.me_ref, bf16[2,24,2,384,256]{4,3,2,1,0:T(8,128)(2,1)} %get-tuple-element.32.src_ref.own_ref, bf16[2,24,2,384,256]{4,3,2,1,0:T(8,128)(2,1)} %shard_map.233.other_ref), custom_call_target="tpu_custom_call" | custom-call | flops 4718592 | bytes 28311552 | tf_op jit(solution)/shard_map/pallas_call | solution.py:292
  304.2 46.7 %shard_map.235 = (f32[512,1536]{1,0:T(8,128)}, f32[24,512,1]{2,1,0:T(8,128)}, f32[512,1536]{1,0:T(8,128)}) custom-call(bf16[24,512,256]{2,1,0:T(8,128)(2,1)} %get-tuple-element.36.hid_ref, bf16[24,512,256]{2,1,0:T(8,128)(2,1)} %get-tuple-element.37.dga_ref, bf16[24,512,256]{2,1,0:T(8,128)(2,1)} %get-tuple-element.38.dua_ref, bf16[512,1536]{1,0:T(8,128)(2,1)} %dy_ref.3, ...), custom_call_target="tpu_custom_call" | custom-call | flops 28991029248 | bytes 83361792 | tf_op jit(solution)/shard_map/pallas_call | solution.py:169
  354.1 37.1 %shard_map.237 = bf16[2,512,1536]{2,1,0:T(8,128)(2,1)} custom-call(bf16[512,1536]{1,0:T(8,128)(2,1)} %convert_element_type.178.src_ref), custom_call_target="tpu_custom_call" | custom-call | bytes 3145728 | tf_op jit(solution)/shard_map/pallas_call | solution.py:248
  407.6 35.4 %shard_map.236 = bf16[2,512,1536]{2,1,0:T(8,128)(2,1)} custom-call(bf16[512,1536]{1,0:T(8,128)(2,1)} %convert_element_type.172.src_ref), custom_call_target="tpu_custom_call" | custom-call | bytes 3145728 | tf_op jit(solution)/shard_map/pallas_call | solution.py:248
  456.2 28.8 %multiply_convert_fusion = bf16[4,3,512,2048]{2,3,1,0:T(8,128)(2,1)} fusion(f32[4,2048,512,3]{2,1,3,0:T(8,128)} %fusion.36, f32[4,3,512]{2,1,0:T(4,128)S(1)} %multiply_reduce_fusion.3, f32[4,3,512]{2,1,0:T(4,128)S(1)} %bitcast.193, pred[512,2048]{0,1:T(8,128)(4,1)S(1)} %copy-done.41, bf16[4,3,512,64]{2,3,1,0:T(8,128)(2,1)S(1)} %bitcast.176, ...), kind=kOutput, calls=%fused_computation.3 | convolution fusion | flops 1686110208 | bytes 78430208 | tf_op jit(solution)/shard_map/kgtd,nkd->kgtn/dot_general | solution.py:552
  485.0 12.7 %fusion.30 = bf16[2048,4,64]{0,2,1:T(8,128)(2,1)S(1)} fusion(bf16[4,3,512,2048]{2,3,1,0:T(8,128)(2,1)} %multiply_convert_fusion, bf16[512,4,3,32]{0,3,2,1:T(8,128)(2,1)S(1)} %bitcast.170, bf16[512,4,3,32]{0,3,2,1:T(8,128)(2,1)S(1)} %bitcast.168), kind=kOutput, calls=%fused_computation.48 | convolution fusion | flops 1613234176 | bytes 27000832 | tf_op jit(solution)/shard_map/kgtn,tkgd->nkd/dot_general | solution.py:559
  499.3 20.3 %fusion.31 = bf16[2048,4,64]{0,2,1:T(8,128)(2,1)S(1)} fusion(bf16[4,3,512,64]{2,3,1,0:T(8,128)(2,1)} %bitcast.177, f32[4,2048,512,3]{2,1,3,0:T(8,128)} %fusion.36, f32[4,3,512]{2,1,0:T(4,128)S(1)} %bitcast.194, pred[512,2048]{0,1:T(8,128)(4,1)} %fusion.6), kind=kOutput, calls=%fused_computation.49 | convolution fusion | flops 1661468672 | bytes 53239808 | tf_op jit(solution)/shard_map/kgtn,kgtd->nkd/dot_general | solution.py:562
  522.9 113.2 %shard_map.239 = bf16[4,512,512]{2,1,0:T(8,128)(2,1)} custom-call(bf16[4,512,512]{2,1,0:T(8,128)(2,1)} %pad_maximum_fusion.src_ref), custom_call_target="tpu_custom_call" | custom-call | bytes 3145728 | tf_op jit(solution)/shard_map/pallas_call | solution.py:248
  640.1 11.2 %convolution_multiply_fusion = f32[4,3,512,64]{2,3,1,0:T(8,128)S(1)} fusion(bf16[4,3,512,2048]{2,3,1,0:T(8,128)(2,1)} %multiply_convert_fusion, bf16[2048,4,64,1]{0,2,1,3:T(8,128)(2,1)S(1)} %copy-done.21), kind=kOutput, calls=%fused_computation.57 | convolution fusion | flops 1611005952 | bytes 27787264 | tf_op jit(solution)/shard_map/kgtn,nkd->kgtd/dot_general | solution.py:556
  658.0 36.2 %shard_map.240 = bf16[2,512,1536]{2,1,0:T(8,128)(2,1)} custom-call(bf16[512,1536]{1,0:T(8,128)(2,1)} %fusion.20.src_ref), custom_call_target="tpu_custom_call" | custom-call | bytes 3145728 | tf_op jit(solution)/shard_map/pallas_call | solution.py:248
  727.3 10.5 %concatenate.65 = bf16[2,2,384,2176]{3,2,0,1:T(8,128)(2,1)} concatenate(bf16[2,2,384,768]{3,2,0,1:T(8,128)(2,1)} %convolution_convert_fusion.3, bf16[2,2,384,768]{3,2,0,1:T(8,128)(2,1)S(1)} %copy.222, bf16[2,2,384,256]{3,2,0,1:T(8,128)(2,1)} %convolution_convert_fusion.4, bf16[2,2,384,256]{3,2,0,1:T(8,128)(2,1)S(1)} %copy.223, bf16[2,2,384,24]{3,2,0,1:T(8,128)(2,1)} %copy.224, ...), dimensions={3} | concatenate | bytes 13369344 | tf_op jit(solution)/shard_map/concatenate | solution.py:616
  737.8 6.3 shard_map.241.other_ref
  755.5 44.7 %reduce-scatter.7.cloned.1.call-done = bf16[24,96,256]{2,1,0:T(8,128)(2,1)} async-done(((bf16[24,768,256]{2,1,0:T(8,128)(2,1)}), bf16[24,96,256]{2,1,0:T(8,128)(2,1)}) %reduce-scatter.7.cloned.1.call-update) | async-done | bytes 1179664 | tf_op jit(solution)/shard_map/reduce_scatter | solution.py:519
  803.2 76.9 %reduce-scatter.13.cloned.1.call-done = bf16[96,2176]{1,0:T(8,128)(2,1)} async-done(((bf16[768,2176]{1,0:T(8,128)(2,1)}), bf16[96,2176]{1,0:T(8,128)(2,1)}) %reduce-scatter.13.cloned.1.call-update) | async-done | bytes 417808
  (268 shorter events, 147.1 us)
Async XLA Ops:
  7.2 98.9 %all-gather.2.cloned.1.call-start = ((), (), s32[]{:S(2)}) async-start(), calls=%async_computation.4 | async-start | bytes 7077888 | tf_op jit(solution)/shard_map/all_gather | solution.py:428
  7.9 741.6 %reduce-scatter.9.cloned.1.call-start = ((), (), s32[]{:S(2)}) async-start(), calls=%async_computation.6 | async-start | bytes 10616832 | tf_op jit(solution)/shard_map/reduce_scatter | solution.py:519
  10.0 46.6 %copy-start.38 = (f32[512,32]{0,1:T(8,128)}, f32[512,32]{0,1:T(8,128)S(1)}, u32[]{:S(2)}) copy-start(f32[512,32]{0,1:T(8,128)S(1)} %get-tuple-element.138) | copy-start | bytes 196612
  11.0 42.3 %copy-start.66 = (f32[512]{0:T(512)S(1)}, f32[512]{0:T(512)}, u32[]{:S(2)}) copy-start(f32[512]{0:T(512)} %copy-done.65) | copy-start | bytes 6148
  79.9 21.8 %copy-start = (f32[512,768]{1,0:T(8,128)}, f32[512,768]{1,0:T(8,128)S(1)}, u32[]{:S(2)}) copy-start(f32[512,768]{1,0:T(8,128)S(1)} %get-tuple-element.31) | copy-start | bytes 4718596
  217.5 535.0 %reduce-scatter.11.cloned.1.call-start = ((), (), s32[]{:S(2)}) async-start(), calls=%async_computation.7 | async-start | bytes 10616832 | tf_op jit(solution)/shard_map/reduce_scatter | solution.py:519
  244.0 556.2 %reduce-scatter.7.cloned.1.call-start = ((), (), s32[]{:S(2)}) async-start(), calls=%async_computation.5 | async-start | bytes 10616832 | tf_op jit(solution)/shard_map/reduce_scatter | solution.py:519
  252.3 25.5 %copy-start.20 = (bf16[2048,4,64,1]{0,2,1,3:T(8,128)(2,1)}, bf16[2048,4,64,1]{0,2,1,3:T(8,128)(2,1)S(1)}, u32[]{:S(2)}) copy-start(bf16[2048,4,64,1]{0,2,1,3:T(8,128)(2,1)S(1)} %reshape.373) | copy-start | bytes 3145732
  252.3 6.2 copy-start.24
  304.2 575.9 %reduce-scatter.13.cloned.1.call-start = ((), (), s32[]{:S(2)}) async-start(), calls=%async_computation.8 | async-start | bytes 3760128
  391.2 10.9 %copy-start.34 = (f32[512,8]{1,0:T(8,128)S(1)}, f32[512,8]{1,0:T(8,128)}, u32[]{:S(2)}) copy-start(f32[512,8]{1,0:T(8,128)} %copy-done.33) | copy-start | bytes 49156
  391.2 10.9 %copy-start.59 = (f32[512]{0:T(512)S(1)}, f32[512]{0:T(512)}, u32[]{:S(2)}) copy-start(f32[512]{0:T(512)} %copy-done.58) | copy-start | bytes 6148
  391.2 15.1 %copy-start.16 = (f32[512,1536]{1,0:T(8,128)S(1)}, f32[512,1536]{1,0:T(8,128)}, u32[]{:S(2)}) copy-start(f32[512,1536]{1,0:T(8,128)} %get-tuple-element.39) | copy-start | bytes 9437188
  407.6 35.5 %copy-start.8 = (f32[512,1536]{1,0:T(8,128)S(1)}, f32[512,1536]{1,0:T(8,128)}, u32[]{:S(2)}) copy-start(f32[512,1536]{1,0:T(8,128)} %copy-done.7) | copy-start | bytes 9437188
  407.6 35.5 %copy-start.49 = (bf16[1536,24]{0,1:T(8,128)(2,1)S(1)}, bf16[1536,24]{0,1:T(8,128)(2,1)}, u32[]{:S(2)}) copy-start(bf16[1536,24]{0,1:T(8,128)(2,1)} %param.21) | copy-start | bytes 221188
  407.6 35.5 %copy-start.55 = (f32[1536]{0:T(1024)S(1)}, f32[1536]{0:T(1024)}, u32[]{:S(2)}) copy-start(f32[1536]{0:T(1024)} %param.20) | copy-start | bytes 18436
  407.6 35.5 %copy-start.57 = (f32[512]{0:T(512)S(1)}, f32[512]{0:T(512)}, u32[]{:S(2)}) copy-start(f32[512]{0:T(512)} %copy-done.56) | copy-start | bytes 6148
  456.2 28.8 %copy-start.25 = (bf16[512,12,32]{0,2,1:T(8,128)(2,1)S(1)}, bf16[512,12,32]{0,2,1:T(8,128)(2,1)}, u32[]{:S(2)}) copy-start(bf16[512,12,32]{0,2,1:T(8,128)(2,1)} %copy-done.23) | copy-start | bytes 1179652
  456.2 28.8 %copy-start.28 = (bf16[512,12,32]{0,2,1:T(8,128)(2,1)S(1)}, bf16[512,12,32]{0,2,1:T(8,128)(2,1)}, u32[]{:S(2)}) copy-start(bf16[512,12,32]{0,2,1:T(8,128)(2,1)} %copy-done.26) | copy-start | bytes 1179652
  522.9 113.3 %copy-start.69 = (pred[4]{0:T(512)(128)(4,1)S(1)}, pred[4]{0:T(512)(128)(4,1)}, u32[]{:S(2)}) copy-start(pred[4]{0:T(512)(128)(4,1)} %iota_compare_fusion.2) | copy-start | bytes 16
  658.0 36.2 %copy-start.9 = (bf16[512,1536]{1,0:T(8,128)(2,1)S(1)}, bf16[512,1536]{1,0:T(8,128)(2,1)}, u32[]{:S(2)}) copy-start(bf16[512,1536]{1,0:T(8,128)(2,1)} %fusion.20.src_ref) | copy-start | bytes 4718596
  658.0 36.2 %copy-start.14 = (bf16[512,1536]{1,0:T(8,128)(2,1)S(1)}, bf16[512,1536]{1,0:T(8,128)(2,1)}, u32[]{:S(2)}) copy-start(bf16[512,1536]{1,0:T(8,128)(2,1)} %param.14) | copy-start | bytes 4718596
  658.0 36.2 %copy-start.62 = (f32[1536]{0:T(1024)S(1)}, f32[1536]{0:T(1024)}, u32[]{:S(2)}) copy-start(f32[1536]{0:T(1024)} %param.15) | copy-start | bytes 18436
  658.0 36.2 %copy-start.67 = (f32[512]{0:T(512)S(1)}, f32[512]{0:T(512)}, u32[]{:S(2)}) copy-start(f32[512]{0:T(512)} %copy-done.65) | copy-start | bytes 6148
  (52 other events, 129.9 us)
Sparse Core Ops, SparseCore 0:
  9.6 65.3 all-gather.1
  217.7 219.7 reduce-scatter.8
  441.0 194.1 reduce-scatter.10
  638.7 161.5 reduce-scatter.6
  803.7 76.3 reduce-scatter.12

commit v13 on v12

--- a/solution.py
+++ b/solution.py
@@ -397,6 +397,75 @@
         ),
     )(jnp.reshape(ctx_index, (1,)).astype(jnp.int32), q, kv, kv, qseg, qpos, kseg)
 
+def _chain_down_body(axis, n, x_ref, out_ref, recv, send, send_sems, recv_sems):
+    f32 = jnp.float32
+    me = lax.axis_index(axis)
+    below = lax.rem(me + n - 1, n)
+    above = lax.rem(me + 1, n)
+    barrier = pltpu.get_barrier_semaphore()
+    pl.semaphore_signal(barrier, 1, device_id={axis: below}, device_id_type=MESH)
+    pl.semaphore_signal(barrier, 1, device_id={axis: above}, device_id_type=MESH)
+    pl.semaphore_wait(barrier, 2)
+    copies = []
+    for j in range(n - 1):
+        copy = pltpu.make_async_remote_copy(
+            src_ref=send.at[j],
+            dst_ref=recv.at[j],
+            send_sem=send_sems.at[j],
+            recv_sem=recv_sems.at[j],
+            device_id={axis: below},
+            device_id_type=MESH,
+        )
+        copies.append(copy)
+
+        @pl.when((j < me) & (me < n - 1))
+        def _():
+            copy.wait_recv()
+            send[j] = (x_ref[j].astype(f32) + recv[j].astype(f32)).astype(send.dtype)
+
+        @pl.when((j < me) & (me == n - 1))
+        def _():
+            send[j] = x_ref[j]
+
+        @pl.when(j < me)
+        def _():
+            copy.start()
+
+        @pl.when(j == me)
+        def _():
+            copy.wait_recv()
+            out_ref[...] = x_ref[j].astype(f32) + recv[j].astype(f32)
+
+    @pl.when(me == n - 1)
+    def _():
+        out_ref[...] = x_ref[n - 1].astype(f32)
+
+    for j in range(n - 1):
+        pl.when(j < me)(copies[j].wait_send)
+
+
+def chain_sum_down(x, axis, n, collective_id):
+    _, rows, cols = x.shape
+    return pl.pallas_call(
+        functools.partial(_chain_down_body, axis, n),
+        out_shape=jax.ShapeDtypeStruct((rows, cols), jnp.float32),
+        in_specs=[pl.BlockSpec(memory_space=pltpu.VMEM)],
+        out_specs=pl.BlockSpec(memory_space=pltpu.VMEM),
+        scratch_shapes=[
+            pltpu.VMEM((n - 1, rows, cols), x.dtype),
+            pltpu.VMEM((n - 1, rows, cols), x.dtype),
+            pltpu.SemaphoreType.DMA((n - 1,)),
+            pltpu.SemaphoreType.DMA((n - 1,)),
+        ],
+        compiler_params=pltpu.CompilerParams(
+            collective_id=collective_id, has_side_effects=True, vmem_limit_bytes=32 * 1024 * 1024
+        ),
+        cost_estimate=pl.CostEstimate(
+            flops=(n - 1) * rows * cols, transcendentals=0, bytes_accessed=3 * n * rows * cols * 2
+        ),
+    )(x)
+
+
 def per_device(
     dpx_count,
     hidden_in,
@@ -566,7 +635,7 @@
     grad_values_all = value_part.reshape(piece_rows, kv_local * HEAD_SIZE)
     back_state = (grad_query, grad_keys_all, grad_values_all)
     grad_query, grad_keys_all, grad_values_all = back_state
-    grad_kv_here = scatter_sum_downward(
+    grad_kv_here = chain_sum_down(
         jnp.concatenate([grad_keys_all, grad_values_all], axis=1)
         .astype(bf16)
         .reshape(ctx_count, token_count, 2 * kv_width),

time: 898 us -> 889 us (0.990)
  Pallas kernels: 517 us -> 507 us
    pallas_call x11 -> x10, Pallas kernels: 339 us -> 221 us  [exchange(): pl.pallas_call(functools.partial(_exchange_body, axis, n, per_peer, downw...]
    pallas_call x0 -> x1, Pallas kernels: none -> 108 us  [chain_sum_down(): pl.pallas_call(functools.partial(_chain_down_body, axis, n), out_shape=ja...]
  transfers between devices with their start and end apart: 5 -> 5, of which waited for: 2 -> 2; matrix products, arithmetic and copies ran while one was open for 23% -> 23% of each run, Pallas kernels for 47% -> 46%
where the time goes in v13:
time: 889 us; the launch traced here: 883 us
  Pallas kernels  507 us (57%)
  waiting for transfers between devices  126 us (14%)
  matrix products  122 us (14%)
  local copies, waits for them, and re-layouts  70.8 us (8%)
  other arithmetic  42.3 us (5%)
  between operations  15.2 us (2%)
    pallas_call x10, Pallas kernels, exchange(): pl.pallas_call(functools.partial(_exchange_body, axis, n, per_peer, downw...  221 us
    pallas_call x1, Pallas kernels, chain_sum_down(): pl.pallas_call(functools.partial(_chain_down_body, axis, n), out_shape=ja...  108 us
    unnamed x6, waiting for transfers between devices  77.7 us
    pallas_call x1, Pallas kernels, expert_grad_kernel(): pl.pallas_call(_grad_body, grid=(experts,), in_specs=[whole((tokens, widt...  73.8 us
    reduce_scatter x3, waiting for transfers between devices, per_device(): lax.psum_scatter(g.reshape(g.shape[0], -1, g.shape[3]), ('dpx', 'ctx'), s...  48 us
    pallas_call x1, Pallas kernels, expert_rows_kernel(): pl.pallas_call(_rows_body, grid=(experts,), in_specs=[per_expert((tokens,...  46.5 us
    pallas_call x4, Pallas kernels, core_reduce(): pl.pallas_call(_pair_add_body, grid_spec=grid_spec, out_shape=jax.ShapeDt...  39.4 us
    dot_general x1, matrix products, per_device(): jnp.einsum('kgtd,nkd->kgtn', grad_attn_grouped, value_piece, preferred_el...  28.8 us
  transfers between devices with their start and end apart: 5, of which 2 were waited for; matrix products, arithmetic and copies ran while one was open for 23% of the time, Pallas kernels for 46%

profile of v13, /device:TPU:0, one launch (start us, length us, event | category | flops | bytes accessed | tf_op | source)
XLA Modules:
  0.0 883.1 jit_solution(846873103371655196)
XLA Ops:
  13.3 40.1 %shard_map.229 = bf16[4,512,512]{2,1,0:T(8,128)(2,1)} custom-call(bf16[512,512]{1,0:T(8,128)(2,1)} %pad_maximum_fusion.3.src_ref), custom_call_target="tpu_custom_call" | custom-call | bytes 3145728 | tf_op jit(solution)/shard_map/pallas_call | solution.py:248
  60.8 18.3 %shard_map.230 = (f32[512,768]{1,0:T(8,128)S(1)}, f32[2,512,6]{2,1,0:T(8,128)S(1)}) custom-call(s32[1]{0:T(128)} %bitcast.ctx_ref, bf16[512,768]{1,0:T(8,128)(2,1)S(1)} %copy.190.q_ref, bf16[4,512,512]{2,1,0:T(8,128)(2,1)S(1)} %copy-done.2, bf16[4,512,512]{2,1,0:T(8,128)(2,1)S(1)} %copy-done.2, s32[512,1]{1,0:T(8,128)S(1)} %copy.191.qseg_ref, ...), custom_call_target="tpu_custom_call" | custom-call | flops 3221225472 | bytes 4456448 | tf_op jit(solution)/shard_map/pallas_call | solution.py:383
  81.0 19.7 %shard_map.231 = bf16[2,512,768]{2,1,0:T(8,128)(2,1)} custom-call(bf16[512,768]{1,0:T(8,128)(2,1)} %convert_element_type.161.src_ref), custom_call_target="tpu_custom_call" | custom-call | bytes 1572864 | tf_op jit(solution)/shard_map/pallas_call | solution.py:248
  117.3 73.8 %shard_map.232 = (bf16[2,24,2,384,256]{4,3,2,1,0:T(8,128)(2,1)}, bf16[2,24,2,384,256]{4,3,2,1,0:T(8,128)(2,1)}, bf16[2,24,2,384,256]{4,3,2,1,0:T(8,128)(2,1)}, b...) custom-call(bf16[512,1536]{1,0:T(8,128)(2,1)} %copy-done.10, ...), custom_call_target="tpu_custom_call" | custom-call | flops 57982058496 | bytes 138412032 | tf_op jit(solution)/shard_map/pallas_call | solution.py:135
  191.1 15.1 %shard_map.243.other_ref = bf16[2,24,2,384,256]{4,3,2,1,0:T(8,128)(2,1)} custom-call(bf16[2,24,2,384,256]{4,3,2,1,0:T(8,128)(2,1)} %get-tuple-element.44.src_ref.own_ref), custom_call_target="tpu_custom_call" | custom-call | bytes 18874368 | tf_op jit(solution)/shard_map/pallas_call | solution.py:248
  206.1 11.5 %shard_map.244 = bf16[24,2,384,256]{3,2,1,0:T(8,128)(2,1)} custom-call(s32[1]{0:T(128)} %bitcast.11.me_ref, bf16[2,24,2,384,256]{4,3,2,1,0:T(8,128)(2,1)} %get-tuple-element.44.src_ref.own_ref, bf16[2,24,2,384,256]{4,3,2,1,0:T(8,128)(2,1)} %shard_map.243.other_ref), custom_call_target="tpu_custom_call" | custom-call | flops 4718592 | bytes 28311552 | tf_op jit(solution)/shard_map/pallas_call | solution.py:292
  217.7 15.1 %shard_map.245.other_ref = bf16[2,24,2,384,256]{4,3,2,1,0:T(8,128)(2,1)} custom-call(bf16[2,24,2,384,256]{4,3,2,1,0:T(8,128)(2,1)} %get-tuple-element.45.src_ref.own_ref), custom_call_target="tpu_custom_call" | custom-call | bytes 18874368 | tf_op jit(solution)/shard_map/pallas_call | solution.py:248
  232.7 11.3 %shard_map.246 = bf16[24,2,384,256]{3,2,1,0:T(8,128)(2,1)} custom-call(s32[1]{0:T(128)} %bitcast.11.me_ref, bf16[2,24,2,384,256]{4,3,2,1,0:T(8,128)(2,1)} %get-tuple-element.45.src_ref.own_ref, bf16[2,24,2,384,256]{4,3,2,1,0:T(8,128)(2,1)} %shard_map.245.other_ref), custom_call_target="tpu_custom_call" | custom-call | flops 4718592 | bytes 28311552 | tf_op jit(solution)/shard_map/pallas_call | solution.py:292
  258.1 19.3 %fusion.36 = f32[4,2048,512,3]{2,1,3,0:T(8,128)} fusion(bf16[2048,4,64,1]{0,2,1,3:T(8,128)(2,1)S(1)} %reshape.365, bf16[512,4,3,32]{0,3,2,1:T(8,128)(2,1)S(1)} %bitcast.164, bf16[512,4,3,32]{0,3,2,1:T(8,128)(2,1)S(1)} %bitcast.162), kind=kOutput, calls=%fused_computation.60 | convolution fusion | flops 1612185600 | bytes 52166656 | tf_op jit(solution)/shard_map/tkgd,nkd->kgtn/dot_general | solution.py:617
  277.4 15.0 %shard_map.233.other_ref = bf16[2,24,2,384,256]{4,3,2,1,0:T(8,128)(2,1)} custom-call(bf16[2,24,2,384,256]{4,3,2,1,0:T(8,128)(2,1)} %get-tuple-element.32.src_ref.own_ref), custom_call_target="tpu_custom_call" | custom-call | bytes 18874368 | tf_op jit(solution)/shard_map/pallas_call | solution.py:248
  292.4 11.3 %shard_map.234 = bf16[24,2,384,256]{3,2,1,0:T(8,128)(2,1)} custom-call(s32[1]{0:T(128)} %bitcast.11.me_ref, bf16[2,24,2,384,256]{4,3,2,1,0:T(8,128)(2,1)} %get-tuple-element.32.src_ref.own_ref, bf16[2,24,2,384,256]{4,3,2,1,0:T(8,128)(2,1)} %shard_map.233.other_ref), custom_call_target="tpu_custom_call" | custom-call | flops 4718592 | bytes 28311552 | tf_op jit(solution)/shard_map/pallas_call | solution.py:292
  303.8 46.5 %shard_map.235 = (f32[512,1536]{1,0:T(8,128)}, f32[24,512,1]{2,1,0:T(8,128)}, f32[512,1536]{1,0:T(8,128)}) custom-call(bf16[24,512,256]{2,1,0:T(8,128)(2,1)} %get-tuple-element.36.hid_ref, bf16[24,512,256]{2,1,0:T(8,128)(2,1)} %get-tuple-element.37.dga_ref, bf16[24,512,256]{2,1,0:T(8,128)(2,1)} %get-tuple-element.38.dua_ref, bf16[512,1536]{1,0:T(8,128)(2,1)} %dy_ref.3, ...), custom_call_target="tpu_custom_call" | custom-call | flops 28991029248 | bytes 83361792 | tf_op jit(solution)/shard_map/pallas_call | solution.py:169
  353.5 37.1 %shard_map.237 = bf16[2,512,1536]{2,1,0:T(8,128)(2,1)} custom-call(bf16[512,1536]{1,0:T(8,128)(2,1)} %convert_element_type.169.src_ref), custom_call_target="tpu_custom_call" | custom-call | bytes 3145728 | tf_op jit(solution)/shard_map/pallas_call | solution.py:248
  407.0 35.4 %shard_map.236 = bf16[2,512,1536]{2,1,0:T(8,128)(2,1)} custom-call(bf16[512,1536]{1,0:T(8,128)(2,1)} %convert_element_type.163.src_ref), custom_call_target="tpu_custom_call" | custom-call | bytes 3145728 | tf_op jit(solution)/shard_map/pallas_call | solution.py:248
  455.5 28.8 %multiply_convert_fusion = bf16[4,3,512,2048]{2,3,1,0:T(8,128)(2,1)} fusion(f32[4,2048,512,3]{2,1,3,0:T(8,128)} %fusion.36, f32[4,3,512]{2,1,0:T(4,128)S(1)} %multiply_reduce_fusion.3, f32[4,3,512]{2,1,0:T(4,128)S(1)} %bitcast.188, pred[512,2048]{0,1:T(8,128)(4,1)S(1)} %copy-done.42, bf16[4,3,512,64]{2,3,1,0:T(8,128)(2,1)S(1)} %bitcast.171, ...), kind=kOutput, calls=%fused_computation.3 | convolution fusion | flops 1686110208 | bytes 78430208 | tf_op jit(solution)/shard_map/kgtd,nkd->kgtn/dot_general | solution.py:621
  484.4 12.7 %fusion.30 = bf16[2048,4,64]{0,2,1:T(8,128)(2,1)S(1)} fusion(bf16[4,3,512,2048]{2,3,1,0:T(8,128)(2,1)} %multiply_convert_fusion, bf16[512,4,3,32]{0,3,2,1:T(8,128)(2,1)S(1)} %bitcast.165, bf16[512,4,3,32]{0,3,2,1:T(8,128)(2,1)S(1)} %bitcast.163), kind=kOutput, calls=%fused_computation.47 | convolution fusion | flops 1613234176 | bytes 27000832 | tf_op jit(solution)/shard_map/kgtn,tkgd->nkd/dot_general | solution.py:628
  499.5 19.0 %fusion.31 = bf16[2048,4,64]{0,2,1:T(8,128)(2,1)S(1)} fusion(bf16[4,3,512,64]{2,3,1,0:T(8,128)(2,1)S(1)} %bitcast.172, f32[4,2048,512,3]{2,1,3,0:T(8,128)} %fusion.36, f32[4,3,512]{2,1,0:T(4,128)S(1)} %bitcast.189, pred[512,2048]{0,1:T(8,128)(4,1)} %fusion.6), kind=kOutput, calls=%fused_computation.48 | convolution fusion | flops 1661468672 | bytes 53239808 | tf_op jit(solution)/shard_map/kgtn,kgtd->nkd/dot_general | solution.py:631
  520.3 107.9 %shard_map.239 = f32[512,512]{1,0:T(8,128)S(1)} custom-call(bf16[4,512,512]{2,1,0:T(8,128)(2,1)S(1)} %pad_maximum_fusion.x_ref), custom_call_target="tpu_custom_call" | custom-call | flops 786432 | bytes 6291456 | tf_op jit(solution)/shard_map/pallas_call | solution.py:449
  628.7 11.4 %convolution_multiply_fusion = f32[4,3,512,64]{2,3,1,0:T(8,128)S(1)} fusion(bf16[4,3,512,2048]{2,3,1,0:T(8,128)(2,1)} %multiply_convert_fusion, bf16[2048,4,64,1]{0,2,1,3:T(8,128)(2,1)S(1)} %copy-done.22), kind=kOutput, calls=%fused_computation.54 | convolution fusion | flops 1611005952 | bytes 27787264 | tf_op jit(solution)/shard_map/kgtn,nkd->kgtd/dot_general | solution.py:625
  646.5 32.0 %shard_map.240 = bf16[2,512,1536]{2,1,0:T(8,128)(2,1)} custom-call(bf16[512,1536]{1,0:T(8,128)(2,1)} %fusion.20.src_ref), custom_call_target="tpu_custom_call" | custom-call | bytes 3145728 | tf_op jit(solution)/shard_map/pallas_call | solution.py:248
  714.6 10.5 %concatenate.65 = bf16[2,2,384,2176]{3,2,0,1:T(8,128)(2,1)} concatenate(bf16[2,2,384,768]{3,2,0,1:T(8,128)(2,1)} %convolution_convert_fusion.3, bf16[2,2,384,768]{3,2,0,1:T(8,128)(2,1)S(1)} %copy.222, bf16[2,2,384,256]{3,2,0,1:T(8,128)(2,1)} %convolution_convert_fusion.4, bf16[2,2,384,256]{3,2,0,1:T(8,128)(2,1)S(1)} %copy.223, bf16[2,2,384,24]{3,2,0,1:T(8,128)(2,1)} %copy.224, ...), dimensions={3} | concatenate | bytes 13369344 | tf_op jit(solution)/shard_map/concatenate | solution.py:685
  725.0 6.3 shard_map.241.other_ref
  742.7 48.0 %reduce-scatter.7.cloned.1.call-done = bf16[24,96,256]{2,1,0:T(8,128)(2,1)} async-done(((bf16[24,768,256]{2,1,0:T(8,128)(2,1)}), bf16[24,96,256]{2,1,0:T(8,128)(2,1)}) %reduce-scatter.7.cloned.1.call-update) | async-done | bytes 1179664 | tf_op jit(solution)/shard_map/reduce_scatter | solution.py:588
  793.6 76.9 %reduce-scatter.13.cloned.1.call-done = bf16[96,2176]{1,0:T(8,128)(2,1)} async-done(((bf16[768,2176]{1,0:T(8,128)(2,1)}), bf16[96,2176]{1,0:T(8,128)(2,1)}) %reduce-scatter.13.cloned.1.call-update) | async-done | bytes 417808
  (265 shorter events, 144.9 us)
Async XLA Ops:
  7.2 99.0 %all-gather.2.cloned.1.call-start = ((), (), s32[]{:S(2)}) async-start(), calls=%async_computation.4 | async-start | bytes 7077888 | tf_op jit(solution)/shard_map/all_gather | solution.py:497
  7.9 728.8 %reduce-scatter.9.cloned.1.call-start = ((), (), s32[]{:S(2)}) async-start(), calls=%async_computation.6 | async-start | bytes 10616832 | tf_op jit(solution)/shard_map/reduce_scatter | solution.py:588
  10.0 46.6 %copy-start.39 = (f32[512,32]{0,1:T(8,128)}, f32[512,32]{0,1:T(8,128)S(1)}, u32[]{:S(2)}) copy-start(f32[512,32]{0,1:T(8,128)S(1)} %get-tuple-element.138) | copy-start | bytes 196612
  11.0 42.3 %copy-start.67 = (f32[512]{0:T(512)S(1)}, f32[512]{0:T(512)}, u32[]{:S(2)}) copy-start(f32[512]{0:T(512)} %copy-done.66) | copy-start | bytes 6148
  80.0 21.8 %copy-start = (f32[512,768]{1,0:T(8,128)}, f32[512,768]{1,0:T(8,128)S(1)}, u32[]{:S(2)}) copy-start(f32[512,768]{1,0:T(8,128)S(1)} %get-tuple-element.31) | copy-start | bytes 4718596
  217.6 522.1 %reduce-scatter.11.cloned.1.call-start = ((), (), s32[]{:S(2)}) async-start(), calls=%async_computation.7 | async-start | bytes 10616832 | tf_op jit(solution)/shard_map/reduce_scatter | solution.py:588
  244.0 546.6 %reduce-scatter.7.cloned.1.call-start = ((), (), s32[]{:S(2)}) async-start(), calls=%async_computation.5 | async-start | bytes 10616832 | tf_op jit(solution)/shard_map/reduce_scatter | solution.py:588
  252.4 25.0 %copy-start.21 = (bf16[2048,4,64,1]{0,2,1,3:T(8,128)(2,1)}, bf16[2048,4,64,1]{0,2,1,3:T(8,128)(2,1)S(1)}, u32[]{:S(2)}) copy-start(bf16[2048,4,64,1]{0,2,1,3:T(8,128)(2,1)S(1)} %reshape.365) | copy-start | bytes 3145732
  303.7 566.8 %reduce-scatter.13.cloned.1.call-start = ((), (), s32[]{:S(2)}) async-start(), calls=%async_computation.8 | async-start | bytes 3760128
  390.6 10.9 %copy-start.33 = (f32[512,8]{1,0:T(8,128)S(1)}, f32[512,8]{1,0:T(8,128)}, u32[]{:S(2)}) copy-start(f32[512,8]{1,0:T(8,128)} %copy-done.32) | copy-start | bytes 49156
  390.6 10.9 %copy-start.60 = (f32[512]{0:T(512)S(1)}, f32[512]{0:T(512)}, u32[]{:S(2)}) copy-start(f32[512]{0:T(512)} %copy-done.59) | copy-start | bytes 6148
  390.6 15.1 %copy-start.17 = (f32[512,1536]{1,0:T(8,128)S(1)}, f32[512,1536]{1,0:T(8,128)}, u32[]{:S(2)}) copy-start(f32[512,1536]{1,0:T(8,128)} %get-tuple-element.39) | copy-start | bytes 9437188
  407.0 35.5 %copy-start.8 = (f32[512,1536]{1,0:T(8,128)S(1)}, f32[512,1536]{1,0:T(8,128)}, u32[]{:S(2)}) copy-start(f32[512,1536]{1,0:T(8,128)} %copy-done.7) | copy-start | bytes 9437188
  407.0 35.5 %copy-start.50 = (bf16[1536,24]{0,1:T(8,128)(2,1)S(1)}, bf16[1536,24]{0,1:T(8,128)(2,1)}, u32[]{:S(2)}) copy-start(bf16[1536,24]{0,1:T(8,128)(2,1)} %param.21) | copy-start | bytes 221188
  407.0 35.5 %copy-start.56 = (f32[1536]{0:T(1024)S(1)}, f32[1536]{0:T(1024)}, u32[]{:S(2)}) copy-start(f32[1536]{0:T(1024)} %param.20) | copy-start | bytes 18436
  407.0 35.5 %copy-start.58 = (f32[512]{0:T(512)S(1)}, f32[512]{0:T(512)}, u32[]{:S(2)}) copy-start(f32[512]{0:T(512)} %copy-done.57) | copy-start | bytes 6148
  455.5 28.8 %copy-start.26 = (bf16[512,12,32]{0,2,1:T(8,128)(2,1)S(1)}, bf16[512,12,32]{0,2,1:T(8,128)(2,1)}, u32[]{:S(2)}) copy-start(bf16[512,12,32]{0,2,1:T(8,128)(2,1)} %copy-done.24) | copy-start | bytes 1179652
  455.5 28.8 %copy-start.29 = (bf16[512,12,32]{0,2,1:T(8,128)(2,1)S(1)}, bf16[512,12,32]{0,2,1:T(8,128)(2,1)}, u32[]{:S(2)}) copy-start(bf16[512,12,32]{0,2,1:T(8,128)(2,1)} %copy-done.27) | copy-start | bytes 1179652
  520.3 108.2 %copy-start.40 = (f32[512,32]{0,1:T(8,128)S(1)}, f32[512,32]{0,1:T(8,128)}, u32[]{:S(2)}) copy-start(f32[512,32]{0,1:T(8,128)} %copy-done.39) | copy-start | bytes 196612
  520.3 108.2 %copy-start.48 = (f32[512,32]{0,1:T(8,128)S(1)}, f32[512,32]{0,1:T(8,128)}, u32[]{:S(2)}) copy-start(f32[512,32]{0,1:T(8,128)} %get-tuple-element.136) | copy-start | bytes 196612
  520.3 108.3 %copy-start.22 = (bf16[2048,4,64,1]{0,2,1,3:T(8,128)(2,1)S(1)}, bf16[2048,4,64,1]{0,2,1,3:T(8,128)(2,1)}, u32[]{:S(2)}) copy-start(bf16[2048,4,64,1]{0,2,1,3:T(8,128)(2,1)} %copy-done.21) | copy-start | bytes 3145732
  646.5 32.1 %copy-start.9 = (bf16[512,1536]{1,0:T(8,128)(2,1)S(1)}, bf16[512,1536]{1,0:T(8,128)(2,1)}, u32[]{:S(2)}) copy-start(bf16[512,1536]{1,0:T(8,128)(2,1)} %fusion.20.src_ref) | copy-start | bytes 4718596
  646.5 32.1 %copy-start.63 = (f32[1536]{0:T(1024)S(1)}, f32[1536]{0:T(1024)}, u32[]{:S(2)}) copy-start(f32[1536]{0:T(1024)} %param.15) | copy-start | bytes 18436
  646.5 32.1 %copy-start.68 = (f32[512]{0:T(512)S(1)}, f32[512]{0:T(512)}, u32[]{:S(2)}) copy-start(f32[512]{0:T(512)} %copy-done.66) | copy-start | bytes 6148
  (52 other events, 144.7 us)
Sparse Core Ops, SparseCore 0:
  9.6 65.3 all-gather.1
  217.7 219.6 reduce-scatter.8
  441.1 162.9 reduce-scatter.10
  607.5 183.1 reduce-scatter.6
  794.1 76.3 reduce-scatter.12

commit v14 on v13

--- a/solution.py
+++ b/solution.py
@@ -306,7 +306,7 @@
     return own + jnp.sum(jnp.where(above, got.astype(jnp.float32), 0.0), axis=0)
 
 
-def _flash_body(groups, ctx_ref, q_ref, k_ref, v_ref, qseg_ref, qpos_ref, kseg_ref, o_ref, lse_ref, m_sc, l_sc, acc_sc):
+def _flash_body(groups, ctx_ref, live_ref, q_ref, k_ref, v_ref, qseg_ref, qpos_ref, kseg_ref, o_ref, lse_ref, m_sc, l_sc, acc_sc):
     f32 = jnp.float32
     block = pl.program_id(1)
     depth = HEAD_SIZE
@@ -318,7 +318,7 @@
         l_sc[...] = jnp.zeros_like(l_sc)
         acc_sc[...] = jnp.zeros_like(acc_sc)
 
-    @pl.when(block <= ctx_ref[0])
+    @pl.when((block <= ctx_ref[0]) & (live_ref[block] != 0))
     def _():
         width = k_ref.shape[1]
         key_pos = block * width + lax.broadcasted_iota(jnp.int32, (1, width), 1)
@@ -329,14 +329,15 @@
             for gi in range(groups):
                 i = kk * groups + gi
                 cols = slice(i * depth, (i + 1) * depth)
+                queries = q_ref[:, cols] * jnp.asarray(1.0 / math.sqrt(HEAD_SIZE), q_ref.dtype)
                 scores = lax.dot_general(
-                    q_ref[:, cols], keys, (((1,), (1,)), ((), ())), preferred_element_type=f32
-                ) * (1.0 / math.sqrt(HEAD_SIZE))
+                    queries, keys, (((1,), (1,)), ((), ())), preferred_element_type=f32
+                )
                 scores = jnp.where(allowed, scores, NEGATIVE)
                 m_old = m_sc[i]
                 m_new = jnp.maximum(m_old, jnp.max(scores, axis=1, keepdims=True))
                 alpha = jnp.exp(m_old - m_new)
-                weights = jnp.where(allowed, jnp.exp(scores - m_new), 0.0)
+                weights = jnp.exp(scores - m_new)
                 l_sc[i] = alpha * l_sc[i] + jnp.sum(weights, axis=1, keepdims=True)
                 acc_sc[:, cols] = alpha * acc_sc[:, cols] + jnp.dot(
                     weights.astype(jnp.bfloat16), values, preferred_element_type=f32
@@ -351,28 +352,30 @@
             lse_ref[0, :, i : i + 1] = m_sc[i] + jnp.log(l_sc[i])
 
 
-def flash_forward(ctx_index, q, kv, qseg, qpos, kseg, groups):
+def flash_forward(ctx_index, live, q, kv, qseg, qpos, kseg, groups):
     tokens, q_width = q.shape
     blocks, width, kv_width = kv.shape
     pair = 2
     pairs = kv_width // (2 * pair * HEAD_SIZE)
     heads_step = pair * groups
     f32 = jnp.float32
-    capped = lambda p, b, c: (jnp.minimum(b, c[0]), 0, p)
+    capped = lambda p, b, c, f: (jnp.minimum(b, c[0]), 0, p)
     grid_spec = pltpu.PrefetchScalarGridSpec(
-        num_scalar_prefetch=1,
+        num_scalar_prefetch=2,
         grid=(pairs, blocks),
         in_specs=[
-            pl.BlockSpec((tokens, heads_step * HEAD_SIZE), lambda p, b, c: (0, p)),
+            pl.BlockSpec((tokens, heads_step * HEAD_SIZE), lambda p, b, c, f: (0, p)),
             pl.BlockSpec((1, width, pair * HEAD_SIZE), capped),
-            pl.BlockSpec((1, width, pair * HEAD_SIZE), lambda p, b, c: (jnp.minimum(b, c[0]), 0, pairs + p)),
-            pl.BlockSpec((tokens, 1), lambda p, b, c: (0, 0)),
-            pl.BlockSpec((tokens, 1), lambda p, b, c: (0, 0)),
-            pl.BlockSpec((1, width), lambda p, b, c: (0, jnp.minimum(b, c[0]))),
+            pl.BlockSpec(
+                (1, width, pair * HEAD_SIZE), lambda p, b, c, f: (jnp.minimum(b, c[0]), 0, pairs + p)
+            ),
+            pl.BlockSpec((tokens, 1), lambda p, b, c, f: (0, 0)),
+            pl.BlockSpec((tokens, 1), lambda p, b, c, f: (0, 0)),
+            pl.BlockSpec((1, width), lambda p, b, c, f: (0, jnp.minimum(b, c[0]))),
         ],
         out_specs=[
-            pl.BlockSpec((tokens, heads_step * HEAD_SIZE), lambda p, b, c: (0, p)),
-            pl.BlockSpec((1, tokens, heads_step), lambda p, b, c: (p, 0, 0)),
+            pl.BlockSpec((tokens, heads_step * HEAD_SIZE), lambda p, b, c, f: (0, p)),
+            pl.BlockSpec((1, tokens, heads_step), lambda p, b, c, f: (p, 0, 0)),
         ],
         scratch_shapes=[
             pltpu.VMEM((heads_step, tokens, 1), f32),
@@ -395,7 +398,7 @@
             transcendentals=tokens * (q_width // HEAD_SIZE) * blocks * width,
             bytes_accessed=(q.size + kv.size) * 2 + tokens * q_width * 4,
         ),
-    )(jnp.reshape(ctx_index, (1,)).astype(jnp.int32), q, kv, kv, qseg, qpos, kseg)
+    )(jnp.reshape(ctx_index, (1,)).astype(jnp.int32), live, q, kv, kv, qseg, qpos, kseg)
 
 def _chain_down_body(axis, n, x_ref, out_ref, recv, send, send_sems, recv_sems):
     f32 = jnp.float32
@@ -528,8 +531,17 @@
     kv_width = kv_local * HEAD_SIZE
     key_piece = kv_both[:, :, :kv_width].reshape(piece_rows, kv_local, HEAD_SIZE)
     value_piece = kv_both[:, :, kv_width:].reshape(piece_rows, kv_local, HEAD_SIZE)
+    key_blocks = segments.shape[0] // token_count
+    live_blocks = jnp.any(
+        (
+            (segment_here[:, None] == segments[None, :])
+            & (jnp.arange(segments.shape[0], dtype=jnp.int32)[None, :] <= token_positions[:, None])
+        ).reshape(token_count, key_blocks, token_count),
+        axis=(0, 2),
+    ).astype(jnp.int32)
     attn_flat, lse_pairs = flash_forward(
         ctx_index,
+        live_blocks,
         query_grouped.reshape(token_count, heads_local * HEAD_SIZE),
         kv_both,
         segment_here[:, None],

time: 889 us -> 883 us (level)
  Pallas kernels: 507 us -> 497 us
    pallas_call x1, Pallas kernels: 108 us -> 98.7 us  [chain_sum_down(): pl.pallas_call(functools.partial(_chain_down_body, axis, n), out_shape=ja...]
    unnamed x148 -> x150, local copies, waits for them, and re-layouts: 20.6 us -> 20.7 us
  transfers between devices with their start and end apart: 5 -> 5, of which waited for: 2 -> 2; matrix products, arithmetic and copies ran while one was open for 23% -> 24% of each run, Pallas kernels for 46% -> 45%
where the time goes in v14:
time: 883 us; the launch traced here: 875 us
  Pallas kernels  497 us (56%)
  waiting for transfers between devices  125 us (14%)
  matrix products  123 us (14%)
  local copies, waits for them, and re-layouts  71 us (8%)
  other arithmetic  44 us (5%)
  between operations  15.4 us (2%)
    pallas_call x10, Pallas kernels, exchange(): pl.pallas_call(functools.partial(_exchange_body, axis, n, per_peer, downw...  219 us
    pallas_call x1, Pallas kernels, chain_sum_down(): pl.pallas_call(functools.partial(_chain_down_body, axis, n), out_shape=ja...  98.7 us
    unnamed x6, waiting for transfers between devices  77.8 us
    pallas_call x1, Pallas kernels, expert_grad_kernel(): pl.pallas_call(_grad_body, grid=(experts,), in_specs=[whole((tokens, widt...  73.9 us
    reduce_scatter x3, waiting for transfers between devices, per_device(): lax.psum_scatter(g.reshape(g.shape[0], -1, g.shape[3]), ('dpx', 'ctx'), s...  47.2 us
    pallas_call x1, Pallas kernels, expert_rows_kernel(): pl.pallas_call(_rows_body, grid=(experts,), in_specs=[per_expert((tokens,...  46.6 us
    pallas_call x4, Pallas kernels, core_reduce(): pl.pallas_call(_pair_add_body, grid_spec=grid_spec, out_shape=jax.ShapeDt...  39.6 us
    dot_general x1, matrix products, per_device(): jnp.einsum('kgtd,nkd->kgtn', grad_attn_grouped, value_piece, preferred_el...  29.1 us
  transfers between devices with their start and end apart: 5, of which 2 were waited for; matrix products, arithmetic and copies ran while one was open for 24% of the time, Pallas kernels for 45%

profile of v14, /device:TPU:0, one launch (start us, length us, event | category | flops | bytes accessed | tf_op | source)
XLA Modules:
  0.0 875.2 jit_solution(8654414772461109578)
XLA Ops:
  13.2 40.1 %shard_map.229 = bf16[4,512,512]{2,1,0:T(8,128)(2,1)} custom-call(bf16[512,512]{1,0:T(8,128)(2,1)} %pad_maximum_fusion.3.src_ref), custom_call_target="tpu_custom_call" | custom-call | bytes 3145728 | tf_op jit(solution)/shard_map/pallas_call | solution.py:248
  62.4 18.6 %shard_map.230 = (f32[512,768]{1,0:T(8,128)S(1)}, f32[2,512,6]{2,1,0:T(8,128)S(1)}) custom-call(s32[1]{0:T(128)} %bitcast.ctx_ref, s32[4]{0:T(128)S(1)} %convert_element_type.159.live_ref, bf16[512,768]{1,0:T(8,128)(2,1)S(1)} %copy.190.q_ref, bf16[4,512,512]{2,1,0:T(8,128)(2,1)S(1)} %copy-done.2, bf16[4,512,512]{2,1,0:T(8,128)(2,1)S(1)} %copy-done.2, ...), custom_call_target="tpu_custom_call" | custom-call | flops 3221225472 | bytes 4456448 | tf_op jit(solution)/shard_map/pallas_call | solution.py:386
  82.8 19.7 %shard_map.231 = bf16[2,512,768]{2,1,0:T(8,128)(2,1)} custom-call(bf16[512,768]{1,0:T(8,128)(2,1)} %convert_element_type.165.src_ref), custom_call_target="tpu_custom_call" | custom-call | bytes 1572864 | tf_op jit(solution)/shard_map/pallas_call | solution.py:248
  119.0 73.9 %shard_map.232 = (bf16[2,24,2,384,256]{4,3,2,1,0:T(8,128)(2,1)}, bf16[2,24,2,384,256]{4,3,2,1,0:T(8,128)(2,1)}, bf16[2,24,2,384,256]{4,3,2,1,0:T(8,128)(2,1)}, b...) custom-call(bf16[512,1536]{1,0:T(8,128)(2,1)} %copy-done.10, ...), custom_call_target="tpu_custom_call" | custom-call | flops 57982058496 | bytes 138412032 | tf_op jit(solution)/shard_map/pallas_call | solution.py:135
  193.0 15.1 %shard_map.243.other_ref = bf16[2,24,2,384,256]{4,3,2,1,0:T(8,128)(2,1)} custom-call(bf16[2,24,2,384,256]{4,3,2,1,0:T(8,128)(2,1)} %get-tuple-element.44.src_ref.own_ref), custom_call_target="tpu_custom_call" | custom-call | bytes 18874368 | tf_op jit(solution)/shard_map/pallas_call | solution.py:248
  208.0 11.5 %shard_map.244 = bf16[24,2,384,256]{3,2,1,0:T(8,128)(2,1)} custom-call(s32[1]{0:T(128)} %bitcast.11.me_ref, bf16[2,24,2,384,256]{4,3,2,1,0:T(8,128)(2,1)} %get-tuple-element.44.src_ref.own_ref, bf16[2,24,2,384,256]{4,3,2,1,0:T(8,128)(2,1)} %shard_map.243.other_ref), custom_call_target="tpu_custom_call" | custom-call | flops 4718592 | bytes 28311552 | tf_op jit(solution)/shard_map/pallas_call | solution.py:292
  219.6 15.1 %shard_map.245.other_ref = bf16[2,24,2,384,256]{4,3,2,1,0:T(8,128)(2,1)} custom-call(bf16[2,24,2,384,256]{4,3,2,1,0:T(8,128)(2,1)} %get-tuple-element.45.src_ref.own_ref), custom_call_target="tpu_custom_call" | custom-call | bytes 18874368 | tf_op jit(solution)/shard_map/pallas_call | solution.py:248
  234.7 11.3 %shard_map.246 = bf16[24,2,384,256]{3,2,1,0:T(8,128)(2,1)} custom-call(s32[1]{0:T(128)} %bitcast.11.me_ref, bf16[2,24,2,384,256]{4,3,2,1,0:T(8,128)(2,1)} %get-tuple-element.45.src_ref.own_ref, bf16[2,24,2,384,256]{4,3,2,1,0:T(8,128)(2,1)} %shard_map.245.other_ref), custom_call_target="tpu_custom_call" | custom-call | flops 4718592 | bytes 28311552 | tf_op jit(solution)/shard_map/pallas_call | solution.py:292
  260.0 20.2 %fusion.36 = f32[4,2048,512,3]{2,1,3,0:T(8,128)} fusion(bf16[2048,4,64,1]{0,2,1,3:T(8,128)(2,1)S(1)} %reshape.390, bf16[512,4,3,32]{0,3,2,1:T(8,128)(2,1)S(1)} %bitcast.164, bf16[512,4,3,32]{0,3,2,1:T(8,128)(2,1)S(1)} %bitcast.162), kind=kOutput, calls=%fused_computation.61 | convolution fusion | flops 1612185600 | bytes 52166656 | tf_op jit(solution)/shard_map/tkgd,nkd->kgtn/dot_general | solution.py:629
  280.2 15.0 %shard_map.233.other_ref = bf16[2,24,2,384,256]{4,3,2,1,0:T(8,128)(2,1)} custom-call(bf16[2,24,2,384,256]{4,3,2,1,0:T(8,128)(2,1)} %get-tuple-element.32.src_ref.own_ref), custom_call_target="tpu_custom_call" | custom-call | bytes 18874368 | tf_op jit(solution)/shard_map/pallas_call | solution.py:248
  295.2 11.4 %shard_map.234 = bf16[24,2,384,256]{3,2,1,0:T(8,128)(2,1)} custom-call(s32[1]{0:T(128)} %bitcast.11.me_ref, bf16[2,24,2,384,256]{4,3,2,1,0:T(8,128)(2,1)} %get-tuple-element.32.src_ref.own_ref, bf16[2,24,2,384,256]{4,3,2,1,0:T(8,128)(2,1)} %shard_map.233.other_ref), custom_call_target="tpu_custom_call" | custom-call | flops 4718592 | bytes 28311552 | tf_op jit(solution)/shard_map/pallas_call | solution.py:292
  306.7 46.6 %shard_map.235 = (f32[512,1536]{1,0:T(8,128)}, f32[24,512,1]{2,1,0:T(8,128)}, f32[512,1536]{1,0:T(8,128)}) custom-call(bf16[24,512,256]{2,1,0:T(8,128)(2,1)} %get-tuple-element.36.hid_ref, bf16[24,512,256]{2,1,0:T(8,128)(2,1)} %get-tuple-element.37.dga_ref, bf16[24,512,256]{2,1,0:T(8,128)(2,1)} %get-tuple-element.38.dua_ref, bf16[512,1536]{1,0:T(8,128)(2,1)} %dy_ref.3, ...), custom_call_target="tpu_custom_call" | custom-call | flops 28991029248 | bytes 83361792 | tf_op jit(solution)/shard_map/pallas_call | solution.py:169
  356.6 36.6 %shard_map.237 = bf16[2,512,1536]{2,1,0:T(8,128)(2,1)} custom-call(bf16[512,1536]{1,0:T(8,128)(2,1)} %convert_element_type.173.src_ref), custom_call_target="tpu_custom_call" | custom-call | bytes 3145728 | tf_op jit(solution)/shard_map/pallas_call | solution.py:248
  409.6 34.9 %shard_map.236 = bf16[2,512,1536]{2,1,0:T(8,128)(2,1)} custom-call(bf16[512,1536]{1,0:T(8,128)(2,1)} %convert_element_type.167.src_ref), custom_call_target="tpu_custom_call" | custom-call | bytes 3145728 | tf_op jit(solution)/shard_map/pallas_call | solution.py:248
  457.7 29.1 %multiply_convert_fusion = bf16[4,3,512,2048]{2,3,1,0:T(8,128)(2,1)} fusion(f32[4,2048,512,3]{2,1,3,0:T(8,128)} %fusion.36, f32[4,3,512]{2,1,0:T(4,128)S(1)} %multiply_reduce_fusion.3, f32[4,3,512]{2,1,0:T(4,128)S(1)} %bitcast.189, pred[512,2048]{0,1:T(8,128)(4,1)S(1)} %copy-done.42, bf16[4,3,512,64]{2,3,1,0:T(8,128)(2,1)S(1)} %bitcast.171, ...), kind=kOutput, calls=%fused_computation.3 | convolution fusion | flops 1686110208 | bytes 78430208 | tf_op jit(solution)/shard_map/kgtd,nkd->kgtn/dot_general | solution.py:633
  486.7 12.5 %fusion.30 = bf16[2048,4,64]{0,2,1:T(8,128)(2,1)S(1)} fusion(bf16[4,3,512,2048]{2,3,1,0:T(8,128)(2,1)} %multiply_convert_fusion, bf16[512,4,3,32]{0,3,2,1:T(8,128)(2,1)S(1)} %bitcast.165, bf16[512,4,3,32]{0,3,2,1:T(8,128)(2,1)S(1)} %bitcast.163), kind=kOutput, calls=%fused_computation.48 | convolution fusion | flops 1613234176 | bytes 27000832 | tf_op jit(solution)/shard_map/kgtn,tkgd->nkd/dot_general | solution.py:640
  501.6 19.1 %fusion.31 = bf16[2048,4,64]{0,2,1:T(8,128)(2,1)S(1)} fusion(bf16[4,3,512,64]{2,3,1,0:T(8,128)(2,1)S(1)} %bitcast.172, f32[4,2048,512,3]{2,1,3,0:T(8,128)} %fusion.36, f32[4,3,512]{2,1,0:T(4,128)S(1)} %bitcast.190, pred[512,2048]{0,1:T(8,128)(4,1)} %fusion.6), kind=kOutput, calls=%fused_computation.49 | convolution fusion | flops 1661468672 | bytes 53239808 | tf_op jit(solution)/shard_map/kgtn,kgtd->nkd/dot_general | solution.py:643
  522.6 98.7 %shard_map.239 = f32[512,512]{1,0:T(8,128)S(1)} custom-call(bf16[4,512,512]{2,1,0:T(8,128)(2,1)S(1)} %pad_maximum_fusion.x_ref), custom_call_target="tpu_custom_call" | custom-call | flops 786432 | bytes 6291456 | tf_op jit(solution)/shard_map/pallas_call | solution.py:452
  621.7 11.5 %convolution_multiply_fusion = f32[4,3,512,64]{2,3,1,0:T(8,128)S(1)} fusion(bf16[4,3,512,2048]{2,3,1,0:T(8,128)(2,1)} %multiply_convert_fusion, bf16[2048,4,64,1]{0,2,1,3:T(8,128)(2,1)S(1)} %copy-done.22), kind=kOutput, calls=%fused_computation.55 | convolution fusion | flops 1611005952 | bytes 27787264 | tf_op jit(solution)/shard_map/kgtn,nkd->kgtd/dot_general | solution.py:637
  639.6 31.3 %shard_map.240 = bf16[2,512,1536]{2,1,0:T(8,128)(2,1)} custom-call(bf16[512,1536]{1,0:T(8,128)(2,1)} %fusion.20.src_ref), custom_call_target="tpu_custom_call" | custom-call | bytes 3145728 | tf_op jit(solution)/shard_map/pallas_call | solution.py:248
  706.9 10.5 %concatenate.65 = bf16[2,2,384,2176]{3,2,0,1:T(8,128)(2,1)} concatenate(bf16[2,2,384,768]{3,2,0,1:T(8,128)(2,1)} %convolution_convert_fusion.3, bf16[2,2,384,768]{3,2,0,1:T(8,128)(2,1)S(1)} %copy.222, bf16[2,2,384,256]{3,2,0,1:T(8,128)(2,1)} %convolution_convert_fusion.4, bf16[2,2,384,256]{3,2,0,1:T(8,128)(2,1)S(1)} %copy.223, bf16[2,2,384,24]{3,2,0,1:T(8,128)(2,1)} %copy.224, ...), dimensions={3} | concatenate | bytes 13369344 | tf_op jit(solution)/shard_map/concatenate | solution.py:697
  717.4 6.3 shard_map.241.other_ref
  735.1 47.2 %reduce-scatter.7.cloned.1.call-done = bf16[24,96,256]{2,1,0:T(8,128)(2,1)} async-done(((bf16[24,768,256]{2,1,0:T(8,128)(2,1)}), bf16[24,96,256]{2,1,0:T(8,128)(2,1)}) %reduce-scatter.7.cloned.1.call-update) | async-done | bytes 1179664 | tf_op jit(solution)/shard_map/reduce_scatter | solution.py:600
  785.2 77.1 %reduce-scatter.13.cloned.1.call-done = bf16[96,2176]{1,0:T(8,128)(2,1)} async-done(((bf16[768,2176]{1,0:T(8,128)(2,1)}), bf16[96,2176]{1,0:T(8,128)(2,1)}) %reduce-scatter.13.cloned.1.call-update) | async-done | bytes 417808
  (271 shorter events, 146.7 us)
Async XLA Ops:
  7.2 100.7 %all-gather.2.cloned.1.call-start = ((), (), s32[]{:S(2)}) async-start(), calls=%async_computation.4 | async-start | bytes 7077888 | tf_op jit(solution)/shard_map/all_gather | solution.py:500
  7.9 721.2 %reduce-scatter.9.cloned.1.call-start = ((), (), s32[]{:S(2)}) async-start(), calls=%async_computation.6 | async-start | bytes 10616832 | tf_op jit(solution)/shard_map/reduce_scatter | solution.py:600
  10.0 46.6 %copy-start.39 = (f32[512,32]{0,1:T(8,128)}, f32[512,32]{0,1:T(8,128)S(1)}, u32[]{:S(2)}) copy-start(f32[512,32]{0,1:T(8,128)S(1)} %get-tuple-element.138) | copy-start | bytes 196612
  11.0 42.3 %copy-start.69 = (f32[512]{0:T(512)S(1)}, f32[512]{0:T(512)}, u32[]{:S(2)}) copy-start(f32[512]{0:T(512)} %copy-done.68) | copy-start | bytes 6148
  81.8 21.8 %copy-start = (f32[512,768]{1,0:T(8,128)}, f32[512,768]{1,0:T(8,128)S(1)}, u32[]{:S(2)}) copy-start(f32[512,768]{1,0:T(8,128)S(1)} %get-tuple-element.31) | copy-start | bytes 4718596
  219.5 512.5 %reduce-scatter.11.cloned.1.call-start = ((), (), s32[]{:S(2)}) async-start(), calls=%async_computation.7 | async-start | bytes 10616832 | tf_op jit(solution)/shard_map/reduce_scatter | solution.py:600
  246.0 536.3 %reduce-scatter.7.cloned.1.call-start = ((), (), s32[]{:S(2)}) async-start(), calls=%async_computation.5 | async-start | bytes 10616832 | tf_op jit(solution)/shard_map/reduce_scatter | solution.py:600
  254.3 25.9 %copy-start.21 = (bf16[2048,4,64,1]{0,2,1,3:T(8,128)(2,1)}, bf16[2048,4,64,1]{0,2,1,3:T(8,128)(2,1)S(1)}, u32[]{:S(2)}) copy-start(bf16[2048,4,64,1]{0,2,1,3:T(8,128)(2,1)S(1)} %reshape.390) | copy-start | bytes 3145732
  306.7 555.7 %reduce-scatter.13.cloned.1.call-start = ((), (), s32[]{:S(2)}) async-start(), calls=%async_computation.8 | async-start | bytes 3760128
  393.2 10.9 %copy-start.33 = (f32[512,8]{1,0:T(8,128)S(1)}, f32[512,8]{1,0:T(8,128)}, u32[]{:S(2)}) copy-start(f32[512,8]{1,0:T(8,128)} %copy-done.32) | copy-start | bytes 49156
  393.2 10.9 %copy-start.60 = (f32[512]{0:T(512)S(1)}, f32[512]{0:T(512)}, u32[]{:S(2)}) copy-start(f32[512]{0:T(512)} %copy-done.59) | copy-start | bytes 6148
  393.2 15.0 %copy-start.17 = (f32[512,1536]{1,0:T(8,128)S(1)}, f32[512,1536]{1,0:T(8,128)}, u32[]{:S(2)}) copy-start(f32[512,1536]{1,0:T(8,128)} %get-tuple-element.39) | copy-start | bytes 9437188
  409.6 35.0 %copy-start.8 = (f32[512,1536]{1,0:T(8,128)S(1)}, f32[512,1536]{1,0:T(8,128)}, u32[]{:S(2)}) copy-start(f32[512,1536]{1,0:T(8,128)} %copy-done.7) | copy-start | bytes 9437188
  409.6 35.0 %copy-start.50 = (bf16[1536,24]{0,1:T(8,128)(2,1)S(1)}, bf16[1536,24]{0,1:T(8,128)(2,1)}, u32[]{:S(2)}) copy-start(bf16[1536,24]{0,1:T(8,128)(2,1)} %param.21) | copy-start | bytes 221188
  409.6 35.0 %copy-start.56 = (f32[1536]{0:T(1024)S(1)}, f32[1536]{0:T(1024)}, u32[]{:S(2)}) copy-start(f32[1536]{0:T(1024)} %param.20) | copy-start | bytes 18436
  409.6 35.0 %copy-start.58 = (f32[512]{0:T(512)S(1)}, f32[512]{0:T(512)}, u32[]{:S(2)}) copy-start(f32[512]{0:T(512)} %copy-done.57) | copy-start | bytes 6148
  457.7 29.1 %copy-start.26 = (bf16[512,12,32]{0,2,1:T(8,128)(2,1)S(1)}, bf16[512,12,32]{0,2,1:T(8,128)(2,1)}, u32[]{:S(2)}) copy-start(bf16[512,12,32]{0,2,1:T(8,128)(2,1)} %copy-done.24) | copy-start | bytes 1179652
  457.7 29.1 %copy-start.29 = (bf16[512,12,32]{0,2,1:T(8,128)(2,1)S(1)}, bf16[512,12,32]{0,2,1:T(8,128)(2,1)}, u32[]{:S(2)}) copy-start(bf16[512,12,32]{0,2,1:T(8,128)(2,1)} %copy-done.27) | copy-start | bytes 1179652
  522.6 99.0 %copy-start.40 = (f32[512,32]{0,1:T(8,128)S(1)}, f32[512,32]{0,1:T(8,128)}, u32[]{:S(2)}) copy-start(f32[512,32]{0,1:T(8,128)} %copy-done.39) | copy-start | bytes 196612
  522.6 99.0 %copy-start.48 = (f32[512,32]{0,1:T(8,128)S(1)}, f32[512,32]{0,1:T(8,128)}, u32[]{:S(2)}) copy-start(f32[512,32]{0,1:T(8,128)} %get-tuple-element.136) | copy-start | bytes 196612
  522.6 99.1 %copy-start.22 = (bf16[2048,4,64,1]{0,2,1,3:T(8,128)(2,1)S(1)}, bf16[2048,4,64,1]{0,2,1,3:T(8,128)(2,1)}, u32[]{:S(2)}) copy-start(bf16[2048,4,64,1]{0,2,1,3:T(8,128)(2,1)} %copy-done.21) | copy-start | bytes 3145732
  639.6 31.3 %copy-start.9 = (bf16[512,1536]{1,0:T(8,128)(2,1)S(1)}, bf16[512,1536]{1,0:T(8,128)(2,1)}, u32[]{:S(2)}) copy-start(bf16[512,1536]{1,0:T(8,128)(2,1)} %fusion.20.src_ref) | copy-start | bytes 4718596
  639.6 31.4 %copy-start.65 = (f32[1536]{0:T(1024)S(1)}, f32[1536]{0:T(1024)}, u32[]{:S(2)}) copy-start(f32[1536]{0:T(1024)} %param.15) | copy-start | bytes 18436
  639.6 31.4 %copy-start.70 = (f32[512]{0:T(512)S(1)}, f32[512]{0:T(512)}, u32[]{:S(2)}) copy-start(f32[512]{0:T(512)} %copy-done.68) | copy-start | bytes 6148
  (53 other events, 148.2 us)
Sparse Core Ops, SparseCore 0:
  9.6 65.3 all-gather.1
  219.7 209.4 reduce-scatter.8
  432.8 162.5 reduce-scatter.10
  598.8 183.3 reduce-scatter.6
  785.7 76.5 reduce-scatter.12

commit v15 on v13

--- a/solution.py
+++ b/solution.py
@@ -466,6 +466,68 @@
     )(x)
 
 
+def _chain_up_body(axis, n, x_ref, out_ref, send_sems, recv_sems):
+    me = lax.axis_index(axis)
+    below = lax.rem(me + n - 1, n)
+    above = lax.rem(me + 1, n)
+    barrier = pltpu.get_barrier_semaphore()
+    pl.semaphore_signal(barrier, 1, device_id={axis: below}, device_id_type=MESH)
+    pl.semaphore_signal(barrier, 1, device_id={axis: above}, device_id_type=MESH)
+    pl.semaphore_wait(barrier, 2)
+    own = pltpu.make_async_remote_copy(
+        src_ref=x_ref,
+        dst_ref=out_ref.at[me],
+        send_sem=send_sems.at[me],
+        recv_sem=recv_sems.at[me],
+        device_id={axis: above},
+        device_id_type=MESH,
+    )
+    pl.when(me < n - 1)(own.start)
+    forwards = []
+    for k in range(1, n):
+        block = jnp.maximum(me - k, 0)
+        incoming = pltpu.make_async_remote_copy(
+            src_ref=out_ref.at[block],
+            dst_ref=out_ref.at[block],
+            send_sem=send_sems.at[block],
+            recv_sem=recv_sems.at[block],
+            device_id={axis: below},
+            device_id_type=MESH,
+        )
+        forward = pltpu.make_async_remote_copy(
+            src_ref=out_ref.at[block],
+            dst_ref=out_ref.at[block],
+            send_sem=send_sems.at[block],
+            recv_sem=recv_sems.at[block],
+            device_id={axis: above},
+            device_id_type=MESH,
+        )
+        forwards.append((k, forward))
+        pl.when(k <= me)(incoming.wait_recv)
+        pl.when((k <= me) & (me < n - 1))(forward.start)
+    pl.when(me < n - 1)(own.wait_send)
+    for k, forward in forwards:
+        pl.when((k <= me) & (me < n - 1))(forward.wait_send)
+
+
+def gather_up(x, axis, n, collective_id):
+    got = pl.pallas_call(
+        functools.partial(_chain_up_body, axis, n),
+        out_shape=jax.ShapeDtypeStruct((n,) + x.shape, x.dtype),
+        in_specs=[pl.BlockSpec(memory_space=pl.ANY)],
+        out_specs=pl.BlockSpec(memory_space=pl.ANY),
+        scratch_shapes=[pltpu.SemaphoreType.DMA((n,)), pltpu.SemaphoreType.DMA((n,))],
+        compiler_params=pltpu.CompilerParams(collective_id=collective_id, has_side_effects=True),
+        cost_estimate=pl.CostEstimate(
+            flops=0, transcendentals=0, bytes_accessed=2 * (n - 1) * x.size * x.dtype.itemsize
+        ),
+    )(x)
+    me = lax.axis_index(axis)
+    below = (jnp.arange(n, dtype=jnp.int32) < me).reshape((n,) + (1,) * x.ndim)
+    got = jnp.where(below, got, jnp.zeros_like(got))
+    return lax.dynamic_update_slice_in_dim(got, x[None], me, 0)
+
+
 def per_device(
     dpx_count,
     hidden_in,
@@ -523,7 +585,7 @@
         )
 
     ctx_count = segments.shape[0] // token_count
-    kv_both = gather_axis(jnp.concatenate([key_flat, value_flat], axis=1), "ctx", ctx_count, 1)
+    kv_both = gather_up(jnp.concatenate([key_flat, value_flat], axis=1), "ctx", ctx_count, 1)
     piece_rows = ctx_count * token_count
     kv_width = kv_local * HEAD_SIZE
     key_piece = kv_both[:, :, :kv_width].reshape(piece_rows, kv_local, HEAD_SIZE)

time: 889 us -> 878 us (0.988)
  Pallas kernels: 507 us -> 495 us
    pallas_call x10 -> x9, Pallas kernels: 221 us -> 195 us  [exchange(): pl.pallas_call(functools.partial(_exchange_body, axis, n, per_peer, downw...]
    pallas_call x0 -> x1, Pallas kernels: none -> 16.6 us  [gather_up(): pl.pallas_call(functools.partial(_chain_up_body, axis, n), out_shape=jax....]
  transfers between devices with their start and end apart: 5 -> 5, of which waited for: 2 -> 2; matrix products, arithmetic and copies ran while one was open for 23% -> 24% of each run, Pallas kernels for 46% -> 45%
where the time goes in v15:
time: 878 us; the launch traced here: 872 us
  Pallas kernels  495 us (56%)
  waiting for transfers between devices  126 us (14%)
  matrix products  122 us (14%)
  local copies, waits for them, and re-layouts  70 us (8%)
  other arithmetic  44.1 us (5%)
  between operations  15.2 us (2%)
    pallas_call x9, Pallas kernels, exchange(): pl.pallas_call(functools.partial(_exchange_body, axis, n, per_peer, downw...  195 us
    pallas_call x1, Pallas kernels, chain_sum_down(): pl.pallas_call(functools.partial(_chain_down_body, axis, n), out_shape=ja...  105 us
    unnamed x6, waiting for transfers between devices  77.7 us
    pallas_call x1, Pallas kernels, expert_grad_kernel(): pl.pallas_call(_grad_body, grid=(experts,), in_specs=[whole((tokens, widt...  73.8 us
    reduce_scatter x3, waiting for transfers between devices, per_device(): lax.psum_scatter(g.reshape(g.shape[0], -1, g.shape[3]), ('dpx', 'ctx'), s...  48.3 us
    pallas_call x1, Pallas kernels, expert_rows_kernel(): pl.pallas_call(_rows_body, grid=(experts,), in_specs=[per_expert((tokens,...  46.8 us
    pallas_call x4, Pallas kernels, core_reduce(): pl.pallas_call(_pair_add_body, grid_spec=grid_spec, out_shape=jax.ShapeDt...  39.5 us
    dot_general x1, matrix products, per_device(): jnp.einsum('kgtd,nkd->kgtn', grad_attn_grouped, value_piece, preferred_el...  28.8 us
  transfers between devices with their start and end apart: 5, of which 2 were waited for; matrix products, arithmetic and copies ran while one was open for 24% of the time, Pallas kernels for 45%

profile of v15, /device:TPU:0, one launch (start us, length us, event | category | flops | bytes accessed | tf_op | source)
XLA Modules:
  0.0 872.2 jit_solution(524090597183368598)
XLA Ops:
  13.3 16.6 %shard_map.229 = bf16[4,512,512]{2,1,0:T(8,128)(2,1)} custom-call(bf16[512,512]{1,0:T(8,128)(2,1)} %pad_maximum_fusion.3.x_ref), custom_call_target="tpu_custom_call" | custom-call | bytes 3145728 | tf_op jit(solution)/shard_map/pallas_call | solution.py:514
  36.8 18.4 %shard_map.230 = (f32[512,768]{1,0:T(8,128)S(1)}, f32[2,512,6]{2,1,0:T(8,128)S(1)}) custom-call(s32[1]{0:T(128)} %bitcast.ctx_ref, bf16[512,768]{1,0:T(8,128)(2,1)S(1)} %copy.190.q_ref, bf16[4,512,512]{2,1,0:T(8,128)(2,1)S(1)} %bitcast_dynamic-update-slice_fusion.1.k_ref.v_ref, bf16[4,512,512]{2,1,0:T(8,128)(2,1)S(1)} %bitcast_dynamic-update-slice_fusion.1.k_ref.v_ref, ...), custom_call_target="tpu_custom_call" | custom-call | flops 3221225472 | bytes 4456448 | tf_op jit(solution)/shard_map/pallas_call | solution.py:383
  57.0 34.7 %shard_map.231 = bf16[2,512,768]{2,1,0:T(8,128)(2,1)} custom-call(bf16[512,768]{1,0:T(8,128)(2,1)} %convert_element_type.161.src_ref), custom_call_target="tpu_custom_call" | custom-call | bytes 1572864 | tf_op jit(solution)/shard_map/pallas_call | solution.py:248
  108.3 73.8 %shard_map.232 = (bf16[2,24,2,384,256]{4,3,2,1,0:T(8,128)(2,1)}, bf16[2,24,2,384,256]{4,3,2,1,0:T(8,128)(2,1)}, bf16[2,24,2,384,256]{4,3,2,1,0:T(8,128)(2,1)}, b...) custom-call(bf16[512,1536]{1,0:T(8,128)(2,1)} %copy-done.10, ...), custom_call_target="tpu_custom_call" | custom-call | flops 57982058496 | bytes 138412032 | tf_op jit(solution)/shard_map/pallas_call | solution.py:135
  182.0 15.1 %shard_map.243.other_ref = bf16[2,24,2,384,256]{4,3,2,1,0:T(8,128)(2,1)} custom-call(bf16[2,24,2,384,256]{4,3,2,1,0:T(8,128)(2,1)} %get-tuple-element.44.src_ref.own_ref), custom_call_target="tpu_custom_call" | custom-call | bytes 18874368 | tf_op jit(solution)/shard_map/pallas_call | solution.py:248
  197.1 11.5 %shard_map.244 = bf16[24,2,384,256]{3,2,1,0:T(8,128)(2,1)} custom-call(s32[1]{0:T(128)} %bitcast.11.me_ref, bf16[2,24,2,384,256]{4,3,2,1,0:T(8,128)(2,1)} %get-tuple-element.44.src_ref.own_ref, bf16[2,24,2,384,256]{4,3,2,1,0:T(8,128)(2,1)} %shard_map.243.other_ref), custom_call_target="tpu_custom_call" | custom-call | flops 4718592 | bytes 28311552 | tf_op jit(solution)/shard_map/pallas_call | solution.py:292
  208.6 15.1 %shard_map.245.other_ref = bf16[2,24,2,384,256]{4,3,2,1,0:T(8,128)(2,1)} custom-call(bf16[2,24,2,384,256]{4,3,2,1,0:T(8,128)(2,1)} %get-tuple-element.45.src_ref.own_ref), custom_call_target="tpu_custom_call" | custom-call | bytes 18874368 | tf_op jit(solution)/shard_map/pallas_call | solution.py:248
  223.7 11.3 %shard_map.246 = bf16[24,2,384,256]{3,2,1,0:T(8,128)(2,1)} custom-call(s32[1]{0:T(128)} %bitcast.11.me_ref, bf16[2,24,2,384,256]{4,3,2,1,0:T(8,128)(2,1)} %get-tuple-element.45.src_ref.own_ref, bf16[2,24,2,384,256]{4,3,2,1,0:T(8,128)(2,1)} %shard_map.245.other_ref), custom_call_target="tpu_custom_call" | custom-call | flops 4718592 | bytes 28311552 | tf_op jit(solution)/shard_map/pallas_call | solution.py:292
  249.0 19.3 %fusion.36 = f32[4,2048,512,3]{2,1,3,0:T(8,128)} fusion(bf16[2048,4,64,1]{0,2,1,3:T(8,128)(2,1)S(1)} %reshape.370, bf16[512,4,3,32]{0,3,2,1:T(8,128)(2,1)S(1)} %bitcast.164, bf16[512,4,3,32]{0,3,2,1:T(8,128)(2,1)S(1)} %bitcast.162), kind=kOutput, calls=%fused_computation.61 | convolution fusion | flops 1612185600 | bytes 52166656 | tf_op jit(solution)/shard_map/tkgd,nkd->kgtn/dot_general | solution.py:679
  268.4 15.0 %shard_map.233.other_ref = bf16[2,24,2,384,256]{4,3,2,1,0:T(8,128)(2,1)} custom-call(bf16[2,24,2,384,256]{4,3,2,1,0:T(8,128)(2,1)} %get-tuple-element.32.src_ref.own_ref), custom_call_target="tpu_custom_call" | custom-call | bytes 18874368 | tf_op jit(solution)/shard_map/pallas_call | solution.py:248
  283.4 11.3 %shard_map.234 = bf16[24,2,384,256]{3,2,1,0:T(8,128)(2,1)} custom-call(s32[1]{0:T(128)} %bitcast.11.me_ref, bf16[2,24,2,384,256]{4,3,2,1,0:T(8,128)(2,1)} %get-tuple-element.32.src_ref.own_ref, bf16[2,24,2,384,256]{4,3,2,1,0:T(8,128)(2,1)} %shard_map.233.other_ref), custom_call_target="tpu_custom_call" | custom-call | flops 4718592 | bytes 28311552 | tf_op jit(solution)/shard_map/pallas_call | solution.py:292
  294.8 46.8 %shard_map.235 = (f32[512,1536]{1,0:T(8,128)}, f32[24,512,1]{2,1,0:T(8,128)}, f32[512,1536]{1,0:T(8,128)}) custom-call(bf16[24,512,256]{2,1,0:T(8,128)(2,1)} %get-tuple-element.36.hid_ref, bf16[24,512,256]{2,1,0:T(8,128)(2,1)} %get-tuple-element.37.dga_ref, bf16[24,512,256]{2,1,0:T(8,128)(2,1)} %get-tuple-element.38.dua_ref, bf16[512,1536]{1,0:T(8,128)(2,1)} %dy_ref.3, ...), custom_call_target="tpu_custom_call" | custom-call | flops 28991029248 | bytes 83361792 | tf_op jit(solution)/shard_map/pallas_call | solution.py:169
  344.9 36.7 %shard_map.237 = bf16[2,512,1536]{2,1,0:T(8,128)(2,1)} custom-call(bf16[512,1536]{1,0:T(8,128)(2,1)} %convert_element_type.169.src_ref), custom_call_target="tpu_custom_call" | custom-call | bytes 3145728 | tf_op jit(solution)/shard_map/pallas_call | solution.py:248
  398.8 34.3 %shard_map.236 = bf16[2,512,1536]{2,1,0:T(8,128)(2,1)} custom-call(bf16[512,1536]{1,0:T(8,128)(2,1)} %convert_element_type.163.src_ref), custom_call_target="tpu_custom_call" | custom-call | bytes 3145728 | tf_op jit(solution)/shard_map/pallas_call | solution.py:248
  447.0 28.8 %multiply_convert_fusion = bf16[4,3,512,2048]{2,3,1,0:T(8,128)(2,1)} fusion(f32[4,2048,512,3]{2,1,3,0:T(8,128)} %fusion.36, f32[4,3,512]{2,1,0:T(4,128)S(1)} %multiply_reduce_fusion.3, f32[4,3,512]{2,1,0:T(4,128)S(1)} %bitcast.188, pred[512,2048]{0,1:T(8,128)(4,1)S(1)} %copy-done.42, bf16[4,3,512,64]{2,3,1,0:T(8,128)(2,1)S(1)} %bitcast.171, ...), kind=kOutput, calls=%fused_computation.3 | convolution fusion | flops 1686110208 | bytes 78430208 | tf_op jit(solution)/shard_map/kgtd,nkd->kgtn/dot_general | solution.py:683
  475.9 12.8 %fusion.30 = bf16[2048,4,64]{0,2,1:T(8,128)(2,1)S(1)} fusion(bf16[4,3,512,2048]{2,3,1,0:T(8,128)(2,1)} %multiply_convert_fusion, bf16[512,4,3,32]{0,3,2,1:T(8,128)(2,1)S(1)} %bitcast.165, bf16[512,4,3,32]{0,3,2,1:T(8,128)(2,1)S(1)} %bitcast.163), kind=kOutput, calls=%fused_computation.47 | convolution fusion | flops 1613234176 | bytes 27000832 | tf_op jit(solution)/shard_map/kgtn,tkgd->nkd/dot_general | solution.py:690
  491.1 19.0 %fusion.31 = bf16[2048,4,64]{0,2,1:T(8,128)(2,1)S(1)} fusion(bf16[4,3,512,64]{2,3,1,0:T(8,128)(2,1)S(1)} %bitcast.172, f32[4,2048,512,3]{2,1,3,0:T(8,128)} %fusion.36, f32[4,3,512]{2,1,0:T(4,128)S(1)} %bitcast.189, pred[512,2048]{0,1:T(8,128)(4,1)} %fusion.6), kind=kOutput, calls=%fused_computation.48 | convolution fusion | flops 1661468672 | bytes 53239808 | tf_op jit(solution)/shard_map/kgtn,kgtd->nkd/dot_general | solution.py:693
  511.9 104.9 %shard_map.239 = f32[512,512]{1,0:T(8,128)S(1)} custom-call(bf16[4,512,512]{2,1,0:T(8,128)(2,1)S(1)} %pad_maximum_fusion.x_ref), custom_call_target="tpu_custom_call" | custom-call | flops 786432 | bytes 6291456 | tf_op jit(solution)/shard_map/pallas_call | solution.py:449
  617.2 11.4 %convolution_multiply_fusion = f32[4,3,512,64]{2,3,1,0:T(8,128)S(1)} fusion(bf16[4,3,512,2048]{2,3,1,0:T(8,128)(2,1)} %multiply_convert_fusion, bf16[2048,4,64,1]{0,2,1,3:T(8,128)(2,1)S(1)} %copy-done.22), kind=kOutput, calls=%fused_computation.55 | convolution fusion | flops 1611005952 | bytes 27787264 | tf_op jit(solution)/shard_map/kgtn,nkd->kgtd/dot_general | solution.py:687
  635.0 32.1 %shard_map.240 = bf16[2,512,1536]{2,1,0:T(8,128)(2,1)} custom-call(bf16[512,1536]{1,0:T(8,128)(2,1)} %fusion.20.src_ref), custom_call_target="tpu_custom_call" | custom-call | bytes 3145728 | tf_op jit(solution)/shard_map/pallas_call | solution.py:248
  703.3 10.5 %concatenate.65 = bf16[2,2,384,2176]{3,2,0,1:T(8,128)(2,1)} concatenate(bf16[2,2,384,768]{3,2,0,1:T(8,128)(2,1)} %convolution_convert_fusion.3, bf16[2,2,384,768]{3,2,0,1:T(8,128)(2,1)S(1)} %copy.222, bf16[2,2,384,256]{3,2,0,1:T(8,128)(2,1)} %convolution_convert_fusion.4, bf16[2,2,384,256]{3,2,0,1:T(8,128)(2,1)S(1)} %copy.223, bf16[2,2,384,24]{3,2,0,1:T(8,128)(2,1)} %copy.224, ...), dimensions={3} | concatenate | bytes 13369344 | tf_op jit(solution)/shard_map/concatenate | solution.py:747
  713.7 6.3 shard_map.241.other_ref
  731.4 48.3 %reduce-scatter.7.cloned.1.call-done = bf16[24,96,256]{2,1,0:T(8,128)(2,1)} async-done(((bf16[24,768,256]{2,1,0:T(8,128)(2,1)}), bf16[24,96,256]{2,1,0:T(8,128)(2,1)}) %reduce-scatter.7.cloned.1.call-update) | async-done | bytes 1179664 | tf_op jit(solution)/shard_map/reduce_scatter | solution.py:650
  782.6 76.9 %reduce-scatter.13.cloned.1.call-done = bf16[96,2176]{1,0:T(8,128)(2,1)} async-done(((bf16[768,2176]{1,0:T(8,128)(2,1)}), bf16[96,2176]{1,0:T(8,128)(2,1)}) %reduce-scatter.13.cloned.1.call-update) | async-done | bytes 417808
  (267 shorter events, 146.0 us)
Async XLA Ops:
  7.2 90.0 %all-gather.2.cloned.1.call-start = ((), (), s32[]{:S(2)}) async-start(), calls=%async_computation.4 | async-start | bytes 7077888 | tf_op jit(solution)/shard_map/all_gather | solution.py:559
  7.9 717.5 %reduce-scatter.9.cloned.1.call-start = ((), (), s32[]{:S(2)}) async-start(), calls=%async_computation.6 | async-start | bytes 10616832 | tf_op jit(solution)/shard_map/reduce_scatter | solution.py:650
  10.0 23.1 %copy-start.39 = (f32[512,32]{0,1:T(8,128)}, f32[512,32]{0,1:T(8,128)S(1)}, u32[]{:S(2)}) copy-start(f32[512,32]{0,1:T(8,128)S(1)} %get-tuple-element.138) | copy-start | bytes 196612
  11.0 18.8 %copy-start.67 = (f32[512]{0:T(512)S(1)}, f32[512]{0:T(512)}, u32[]{:S(2)}) copy-start(f32[512]{0:T(512)} %copy-done.66) | copy-start | bytes 6148
  36.8 18.4 %copy-start.2 = (bf16[4,512,512]{2,1,0:T(8,128)(2,1)}, bf16[4,512,512]{2,1,0:T(8,128)(2,1)S(1)}, u32[]{:S(2)}) copy-start(bf16[4,512,512]{2,1,0:T(8,128)(2,1)S(1)} %bitcast_dynamic-update-slice_fusion.1.k_ref.v_ref) | copy-start | bytes 6291460
  56.0 36.8 %copy-start = (f32[512,768]{1,0:T(8,128)}, f32[512,768]{1,0:T(8,128)S(1)}, u32[]{:S(2)}) copy-start(f32[512,768]{1,0:T(8,128)S(1)} %get-tuple-element.31) | copy-start | bytes 4718596
  208.6 519.8 %reduce-scatter.11.cloned.1.call-start = ((), (), s32[]{:S(2)}) async-start(), calls=%async_computation.7 | async-start | bytes 10616832 | tf_op jit(solution)/shard_map/reduce_scatter | solution.py:650
  235.0 544.6 %reduce-scatter.7.cloned.1.call-start = ((), (), s32[]{:S(2)}) async-start(), calls=%async_computation.5 | async-start | bytes 10616832 | tf_op jit(solution)/shard_map/reduce_scatter | solution.py:650
  243.4 25.0 %copy-start.21 = (bf16[2048,4,64,1]{0,2,1,3:T(8,128)(2,1)}, bf16[2048,4,64,1]{0,2,1,3:T(8,128)(2,1)S(1)}, u32[]{:S(2)}) copy-start(bf16[2048,4,64,1]{0,2,1,3:T(8,128)(2,1)S(1)} %reshape.370) | copy-start | bytes 3145732
  294.8 564.8 %reduce-scatter.13.cloned.1.call-start = ((), (), s32[]{:S(2)}) async-start(), calls=%async_computation.8 | async-start | bytes 3760128
  381.6 11.7 %copy-start.33 = (f32[512,8]{1,0:T(8,128)S(1)}, f32[512,8]{1,0:T(8,128)}, u32[]{:S(2)}) copy-start(f32[512,8]{1,0:T(8,128)} %copy-done.32) | copy-start | bytes 49156
  381.6 15.8 %copy-start.17 = (f32[512,1536]{1,0:T(8,128)S(1)}, f32[512,1536]{1,0:T(8,128)}, u32[]{:S(2)}) copy-start(f32[512,1536]{1,0:T(8,128)} %get-tuple-element.39) | copy-start | bytes 9437188
  398.8 34.4 %copy-start.8 = (f32[512,1536]{1,0:T(8,128)S(1)}, f32[512,1536]{1,0:T(8,128)}, u32[]{:S(2)}) copy-start(f32[512,1536]{1,0:T(8,128)} %copy-done.7) | copy-start | bytes 9437188
  398.8 34.4 %copy-start.50 = (bf16[1536,24]{0,1:T(8,128)(2,1)S(1)}, bf16[1536,24]{0,1:T(8,128)(2,1)}, u32[]{:S(2)}) copy-start(bf16[1536,24]{0,1:T(8,128)(2,1)} %param.21) | copy-start | bytes 221188
  398.8 34.4 %copy-start.56 = (f32[1536]{0:T(1024)S(1)}, f32[1536]{0:T(1024)}, u32[]{:S(2)}) copy-start(f32[1536]{0:T(1024)} %param.20) | copy-start | bytes 18436
  398.8 34.4 %copy-start.58 = (f32[512]{0:T(512)S(1)}, f32[512]{0:T(512)}, u32[]{:S(2)}) copy-start(f32[512]{0:T(512)} %copy-done.57) | copy-start | bytes 6148
  447.0 28.9 %copy-start.26 = (bf16[512,12,32]{0,2,1:T(8,128)(2,1)S(1)}, bf16[512,12,32]{0,2,1:T(8,128)(2,1)}, u32[]{:S(2)}) copy-start(bf16[512,12,32]{0,2,1:T(8,128)(2,1)} %copy-done.24) | copy-start | bytes 1179652
  447.0 28.9 %copy-start.29 = (bf16[512,12,32]{0,2,1:T(8,128)(2,1)S(1)}, bf16[512,12,32]{0,2,1:T(8,128)(2,1)}, u32[]{:S(2)}) copy-start(bf16[512,12,32]{0,2,1:T(8,128)(2,1)} %copy-done.27) | copy-start | bytes 1179652
  511.9 105.2 %copy-start.40 = (f32[512,32]{0,1:T(8,128)S(1)}, f32[512,32]{0,1:T(8,128)}, u32[]{:S(2)}) copy-start(f32[512,32]{0,1:T(8,128)} %copy-done.39) | copy-start | bytes 196612
  511.9 105.2 %copy-start.48 = (f32[512,32]{0,1:T(8,128)S(1)}, f32[512,32]{0,1:T(8,128)}, u32[]{:S(2)}) copy-start(f32[512,32]{0,1:T(8,128)} %get-tuple-element.136) | copy-start | bytes 196612
  511.9 105.3 %copy-start.22 = (bf16[2048,4,64,1]{0,2,1,3:T(8,128)(2,1)S(1)}, bf16[2048,4,64,1]{0,2,1,3:T(8,128)(2,1)}, u32[]{:S(2)}) copy-start(bf16[2048,4,64,1]{0,2,1,3:T(8,128)(2,1)} %copy-done.21) | copy-start | bytes 3145732
  635.0 32.1 %copy-start.9 = (bf16[512,1536]{1,0:T(8,128)(2,1)S(1)}, bf16[512,1536]{1,0:T(8,128)(2,1)}, u32[]{:S(2)}) copy-start(bf16[512,1536]{1,0:T(8,128)(2,1)} %fusion.20.src_ref) | copy-start | bytes 4718596
  635.0 32.2 %copy-start.63 = (f32[1536]{0:T(1024)S(1)}, f32[1536]{0:T(1024)}, u32[]{:S(2)}) copy-start(f32[1536]{0:T(1024)} %param.15) | copy-start | bytes 18436
  635.0 32.2 %copy-start.68 = (f32[512]{0:T(512)S(1)}, f32[512]{0:T(512)}, u32[]{:S(2)}) copy-start(f32[512]{0:T(512)} %copy-done.66) | copy-start | bytes 6148
  (52 other events, 158.2 us)
Sparse Core Ops, SparseCore 0:
  9.6 80.8 all-gather.1
  208.7 217.3 reduce-scatter.8
  429.7 163.2 reduce-scatter.10
  596.4 183.2 reduce-scatter.6
  783.1 76.3 reduce-scatter.12

commit v16 on v15

--- a/solution.py
+++ b/solution.py
@@ -306,17 +306,23 @@
     return own + jnp.sum(jnp.where(above, got.astype(jnp.float32), 0.0), axis=0)
 
 
-def _flash_body(groups, ctx_ref, q_ref, k_ref, v_ref, qseg_ref, qpos_ref, kseg_ref, o_ref, lse_ref, m_sc, l_sc, acc_sc):
+def _flash_body(groups, ctx_ref, q_ref, k_ref, v_ref, qseg_ref, qpos_ref, kseg_ref, o_ref, lse_ref, qs_sc, m_sc, l_sc, acc_sc):
     f32 = jnp.float32
     block = pl.program_id(1)
     depth = HEAD_SIZE
     pair = k_ref.shape[2] // depth
+    tokens = q_ref.shape[0]
 
     @pl.when(block == 0)
     def _():
         m_sc[...] = jnp.full_like(m_sc, NEGATIVE)
         l_sc[...] = jnp.zeros_like(l_sc)
         acc_sc[...] = jnp.zeros_like(acc_sc)
+        scale = jnp.asarray(1.0 / math.sqrt(HEAD_SIZE), q_ref.dtype)
+        for kk in range(pair):
+            for gi in range(groups):
+                i = kk * groups + gi
+                qs_sc[kk, gi * tokens : (gi + 1) * tokens, :] = q_ref[:, i * depth : (i + 1) * depth] * scale
 
     @pl.when(block <= ctx_ref[0])
     def _():
@@ -326,29 +332,28 @@
         for kk in range(pair):
             keys = k_ref[0, :, kk * depth : (kk + 1) * depth]
             values = v_ref[0, :, kk * depth : (kk + 1) * depth]
+            scores = lax.dot_general(
+                qs_sc[kk], keys, (((1,), (1,)), ((), ())), preferred_element_type=f32
+            )
+            scores = jnp.where(allowed, scores, NEGATIVE)
+            m_old = m_sc[kk]
+            m_new = jnp.maximum(m_old, jnp.max(scores, axis=1, keepdims=True))
+            alpha = jnp.exp(m_old - m_new)
+            weights = jnp.where(allowed, jnp.exp(scores - m_new), 0.0)
+            l_sc[kk] = alpha * l_sc[kk] + jnp.sum(weights, axis=1, keepdims=True)
+            acc_sc[kk] = alpha * acc_sc[kk] + jnp.dot(
+                weights.astype(jnp.bfloat16), values, preferred_element_type=f32
+            )
+            m_sc[kk] = m_new
+
+    @pl.when(block == pl.num_programs(1) - 1)
+    def _():
+        for kk in range(pair):
             for gi in range(groups):
                 i = kk * groups + gi
-                cols = slice(i * depth, (i + 1) * depth)
-                scores = lax.dot_general(
-                    q_ref[:, cols], keys, (((1,), (1,)), ((), ())), preferred_element_type=f32
-                ) * (1.0 / math.sqrt(HEAD_SIZE))
-                scores = jnp.where(allowed, scores, NEGATIVE)
-                m_old = m_sc[i]
-                m_new = jnp.maximum(m_old, jnp.max(scores, axis=1, keepdims=True))
-                alpha = jnp.exp(m_old - m_new)
-                weights = jnp.where(allowed, jnp.exp(scores - m_new), 0.0)
-                l_sc[i] = alpha * l_sc[i] + jnp.sum(weights, axis=1, keepdims=True)
-                acc_sc[:, cols] = alpha * acc_sc[:, cols] + jnp.dot(
-                    weights.astype(jnp.bfloat16), values, preferred_element_type=f32
-                )
-                m_sc[i] = m_new
-
-    @pl.when(block == pl.num_programs(1) - 1)
-    def _():
-        for i in range(m_sc.shape[0]):
-            cols = slice(i * depth, (i + 1) * depth)
-            o_ref[:, cols] = acc_sc[:, cols] / l_sc[i]
-            lse_ref[0, :, i : i + 1] = m_sc[i] + jnp.log(l_sc[i])
+                rows = slice(gi * tokens, (gi + 1) * tokens)
+                o_ref[:, i * depth : (i + 1) * depth] = acc_sc[kk, rows, :] / l_sc[kk, rows, :]
+                lse_ref[0, :, i : i + 1] = m_sc[kk, rows, :] + jnp.log(l_sc[kk, rows, :])
 
 
 def flash_forward(ctx_index, q, kv, qseg, qpos, kseg, groups):
@@ -366,8 +371,8 @@
             pl.BlockSpec((tokens, heads_step * HEAD_SIZE), lambda p, b, c: (0, p)),
             pl.BlockSpec((1, width, pair * HEAD_SIZE), capped),
             pl.BlockSpec((1, width, pair * HEAD_SIZE), lambda p, b, c: (jnp.minimum(b, c[0]), 0, pairs + p)),
-            pl.BlockSpec((tokens, 1), lambda p, b, c: (0, 0)),
-            pl.BlockSpec((tokens, 1), lambda p, b, c: (0, 0)),
+            pl.BlockSpec((groups * tokens, 1), lambda p, b, c: (0, 0)),
+            pl.BlockSpec((groups * tokens, 1), lambda p, b, c: (0, 0)),
             pl.BlockSpec((1, width), lambda p, b, c: (0, jnp.minimum(b, c[0]))),
         ],
         out_specs=[
@@ -375,9 +380,10 @@
             pl.BlockSpec((1, tokens, heads_step), lambda p, b, c: (p, 0, 0)),
         ],
         scratch_shapes=[
-            pltpu.VMEM((heads_step, tokens, 1), f32),
-            pltpu.VMEM((heads_step, tokens, 1), f32),
-            pltpu.VMEM((tokens, heads_step * HEAD_SIZE), f32),
+            pltpu.VMEM((pair, groups * tokens, HEAD_SIZE), q.dtype),
+            pltpu.VMEM((pair, groups * tokens, 1), f32),
+            pltpu.VMEM((pair, groups * tokens, 1), f32),
+            pltpu.VMEM((pair, groups * tokens, HEAD_SIZE), f32),
         ],
     )
     return pl.pallas_call(
@@ -594,8 +600,8 @@
         ctx_index,
         query_grouped.reshape(token_count, heads_local * HEAD_SIZE),
         kv_both,
-        segment_here[:, None],
-        token_positions[:, None],
+        jnp.tile(segment_here, group_size)[:, None],
+        jnp.tile(token_positions, group_size)[:, None],
         segments[None, :],
         group_size,
     )

time: 878 us -> 858 us (0.977)
  Pallas kernels: 495 us -> 473 us
    pallas_call x1, Pallas kernels: 105 us -> 85.7 us  [chain_sum_down(): pl.pallas_call(functools.partial(_chain_down_body, axis, n), out_shape=ja...]
    unnamed x148 -> x158, local copies, waits for them, and re-layouts: 19.8 us -> 22.5 us
  transfers between devices with their start and end apart: 5 -> 5, of which waited for: 2 -> 2; matrix products, arithmetic and copies ran while one was open for 24% -> 24% of each run, Pallas kernels for 45% -> 44%
where the time goes in v16:
time: 858 us; the launch traced here: 852 us
  Pallas kernels  473 us (55%)
  waiting for transfers between devices  126 us (15%)
  matrix products  123 us (14%)
  local copies, waits for them, and re-layouts  72.5 us (8%)
  other arithmetic  43.5 us (5%)
  between operations  15.2 us (2%)
    pallas_call x9, Pallas kernels, exchange(): pl.pallas_call(functools.partial(_exchange_body, axis, n, per_peer, downw...  196 us
    pallas_call x1, Pallas kernels, chain_sum_down(): pl.pallas_call(functools.partial(_chain_down_body, axis, n), out_shape=ja...  85.7 us
    unnamed x6, waiting for transfers between devices  77.7 us
    pallas_call x1, Pallas kernels, expert_grad_kernel(): pl.pallas_call(_grad_body, grid=(experts,), in_specs=[whole((tokens, widt...  73.8 us
    reduce_scatter x3, waiting for transfers between devices, per_device(): lax.psum_scatter(g.reshape(g.shape[0], -1, g.shape[3]), ('dpx', 'ctx'), s...  47.9 us
    pallas_call x1, Pallas kernels, expert_rows_kernel(): pl.pallas_call(_rows_body, grid=(experts,), in_specs=[per_expert((tokens,...  46.5 us
    pallas_call x4, Pallas kernels, core_reduce(): pl.pallas_call(_pair_add_body, grid_spec=grid_spec, out_shape=jax.ShapeDt...  39.8 us
    dot_general x1, matrix products, per_device(): jnp.einsum('kgtd,nkd->kgtn', grad_attn_grouped, value_piece, preferred_el...  29.1 us
  transfers between devices with their start and end apart: 5, of which 2 were waited for; matrix products, arithmetic and copies ran while one was open for 24% of the time, Pallas kernels for 44%

profile of v16, /device:TPU:0, one launch (start us, length us, event | category | flops | bytes accessed | tf_op | source)
XLA Modules:
  0.0 852.4 jit_solution(12684916360826545862)
XLA Ops:
  13.3 16.6 %shard_map.229 = bf16[4,512,512]{2,1,0:T(8,128)(2,1)} custom-call(bf16[512,512]{1,0:T(8,128)(2,1)} %pad_maximum_fusion.3.x_ref), custom_call_target="tpu_custom_call" | custom-call | bytes 3145728 | tf_op jit(solution)/shard_map/pallas_call | solution.py:520
  40.1 14.3 %shard_map.230 = (f32[512,768]{1,0:T(8,128)S(1)}, f32[2,512,6]{2,1,0:T(8,128)S(1)}) custom-call(s32[1]{0:T(128)} %bitcast.ctx_ref, bf16[512,768]{1,0:T(8,128)(2,1)S(1)} %copy.193.q_ref, bf16[4,512,512]{2,1,0:T(8,128)(2,1)} %copy-done.23, bf16[4,512,512]{2,1,0:T(8,128)(2,1)} %copy-done.23, s32[1536,1]{1,0:T(8,128)S(1)} %bitcast.164, s32[1536,1]{1,0:T(8,128)S(1)} %bitcast.165, ...), custom_call_target="tpu_custom_call" | custom-call | flops 3221225472 | bytes 4456448 | tf_op jit(solution)/shard_map/pallas_call | solution.py:389
  56.2 35.5 %shard_map.231 = bf16[2,512,768]{2,1,0:T(8,128)(2,1)} custom-call(bf16[512,768]{1,0:T(8,128)(2,1)} %convert_element_type.161.src_ref), custom_call_target="tpu_custom_call" | custom-call | bytes 1572864 | tf_op jit(solution)/shard_map/pallas_call | solution.py:248
  108.2 73.8 %shard_map.232 = (bf16[2,24,2,384,256]{4,3,2,1,0:T(8,128)(2,1)}, bf16[2,24,2,384,256]{4,3,2,1,0:T(8,128)(2,1)}, bf16[2,24,2,384,256]{4,3,2,1,0:T(8,128)(2,1)}, b...) custom-call(bf16[512,1536]{1,0:T(8,128)(2,1)} %copy-done.10, ...), custom_call_target="tpu_custom_call" | custom-call | flops 57982058496 | bytes 138412032 | tf_op jit(solution)/shard_map/pallas_call | solution.py:135
  182.0 15.1 %shard_map.243.other_ref = bf16[2,24,2,384,256]{4,3,2,1,0:T(8,128)(2,1)} custom-call(bf16[2,24,2,384,256]{4,3,2,1,0:T(8,128)(2,1)} %get-tuple-element.44.src_ref.own_ref), custom_call_target="tpu_custom_call" | custom-call | bytes 18874368 | tf_op jit(solution)/shard_map/pallas_call | solution.py:248
  197.1 11.5 %shard_map.244 = bf16[24,2,384,256]{3,2,1,0:T(8,128)(2,1)} custom-call(s32[1]{0:T(128)} %bitcast.10.me_ref, bf16[2,24,2,384,256]{4,3,2,1,0:T(8,128)(2,1)} %get-tuple-element.44.src_ref.own_ref, bf16[2,24,2,384,256]{4,3,2,1,0:T(8,128)(2,1)} %shard_map.243.other_ref), custom_call_target="tpu_custom_call" | custom-call | flops 4718592 | bytes 28311552 | tf_op jit(solution)/shard_map/pallas_call | solution.py:292
  208.6 15.1 %shard_map.245.other_ref = bf16[2,24,2,384,256]{4,3,2,1,0:T(8,128)(2,1)} custom-call(bf16[2,24,2,384,256]{4,3,2,1,0:T(8,128)(2,1)} %get-tuple-element.45.src_ref.own_ref), custom_call_target="tpu_custom_call" | custom-call | bytes 18874368 | tf_op jit(solution)/shard_map/pallas_call | solution.py:248
  223.7 11.3 %shard_map.246 = bf16[24,2,384,256]{3,2,1,0:T(8,128)(2,1)} custom-call(s32[1]{0:T(128)} %bitcast.10.me_ref, bf16[2,24,2,384,256]{4,3,2,1,0:T(8,128)(2,1)} %get-tuple-element.45.src_ref.own_ref, bf16[2,24,2,384,256]{4,3,2,1,0:T(8,128)(2,1)} %shard_map.245.other_ref), custom_call_target="tpu_custom_call" | custom-call | flops 4718592 | bytes 28311552 | tf_op jit(solution)/shard_map/pallas_call | solution.py:292
  249.0 19.6 %fusion.36 = f32[4,2048,512,3]{2,1,3,0:T(8,128)} fusion(bf16[2048,4,64,1]{0,2,1,3:T(8,128)(2,1)S(1)} %reshape.371, bf16[512,4,3,32]{0,3,2,1:T(8,128)(2,1)S(1)} %bitcast.175, bf16[512,4,3,32]{0,3,2,1:T(8,128)(2,1)S(1)} %bitcast.173), kind=kOutput, calls=%fused_computation.61 | convolution fusion | flops 1612185600 | bytes 52166656 | tf_op jit(solution)/shard_map/tkgd,nkd->kgtn/dot_general | solution.py:685
  268.5 15.0 %shard_map.233.other_ref = bf16[2,24,2,384,256]{4,3,2,1,0:T(8,128)(2,1)} custom-call(bf16[2,24,2,384,256]{4,3,2,1,0:T(8,128)(2,1)} %get-tuple-element.32.src_ref.own_ref), custom_call_target="tpu_custom_call" | custom-call | bytes 18874368 | tf_op jit(solution)/shard_map/pallas_call | solution.py:248
  283.6 11.7 %shard_map.234 = bf16[24,2,384,256]{3,2,1,0:T(8,128)(2,1)} custom-call(s32[1]{0:T(128)} %bitcast.10.me_ref, bf16[2,24,2,384,256]{4,3,2,1,0:T(8,128)(2,1)} %get-tuple-element.32.src_ref.own_ref, bf16[2,24,2,384,256]{4,3,2,1,0:T(8,128)(2,1)} %shard_map.233.other_ref), custom_call_target="tpu_custom_call" | custom-call | flops 4718592 | bytes 28311552 | tf_op jit(solution)/shard_map/pallas_call | solution.py:292
  295.3 46.5 %shard_map.235 = (f32[512,1536]{1,0:T(8,128)}, f32[24,512,1]{2,1,0:T(8,128)}, f32[512,1536]{1,0:T(8,128)}) custom-call(bf16[24,512,256]{2,1,0:T(8,128)(2,1)} %get-tuple-element.36.hid_ref, bf16[24,512,256]{2,1,0:T(8,128)(2,1)} %get-tuple-element.37.dga_ref, bf16[24,512,256]{2,1,0:T(8,128)(2,1)} %get-tuple-element.38.dua_ref, bf16[512,1536]{1,0:T(8,128)(2,1)} %dy_ref.3, ...), custom_call_target="tpu_custom_call" | custom-call | flops 28991029248 | bytes 83361792 | tf_op jit(solution)/shard_map/pallas_call | solution.py:169
  345.2 36.7 %shard_map.237 = bf16[2,512,1536]{2,1,0:T(8,128)(2,1)} custom-call(bf16[512,1536]{1,0:T(8,128)(2,1)} %convert_element_type.169.src_ref), custom_call_target="tpu_custom_call" | custom-call | bytes 3145728 | tf_op jit(solution)/shard_map/pallas_call | solution.py:248
  398.3 35.0 %shard_map.236 = bf16[2,512,1536]{2,1,0:T(8,128)(2,1)} custom-call(bf16[512,1536]{1,0:T(8,128)(2,1)} %convert_element_type.163.src_ref), custom_call_target="tpu_custom_call" | custom-call | bytes 3145728 | tf_op jit(solution)/shard_map/pallas_call | solution.py:248
  446.6 29.1 %multiply_convert_fusion = bf16[4,3,512,2048]{2,3,1,0:T(8,128)(2,1)} fusion(f32[4,2048,512,3]{2,1,3,0:T(8,128)} %fusion.36, f32[4,3,512]{2,1,0:T(4,128)S(1)} %multiply_reduce_fusion.3, f32[4,3,512]{2,1,0:T(4,128)S(1)} %bitcast.199, pred[512,2048]{0,1:T(8,128)(4,1)S(1)} %copy-done.43, bf16[4,3,512,64]{2,3,1,0:T(8,128)(2,1)S(1)} %bitcast.182, ...), kind=kOutput, calls=%fused_computation.3 | convolution fusion | flops 1686110208 | bytes 78430208 | tf_op jit(solution)/shard_map/kgtd,nkd->kgtn/dot_general | solution.py:689
  475.7 12.6 %fusion.30 = bf16[2048,4,64]{0,2,1:T(8,128)(2,1)S(1)} fusion(bf16[4,3,512,2048]{2,3,1,0:T(8,128)(2,1)} %multiply_convert_fusion, bf16[512,4,3,32]{0,3,2,1:T(8,128)(2,1)S(1)} %bitcast.176, bf16[512,4,3,32]{0,3,2,1:T(8,128)(2,1)S(1)} %bitcast.174), kind=kOutput, calls=%fused_computation.47 | convolution fusion | flops 1613234176 | bytes 27000832 | tf_op jit(solution)/shard_map/kgtn,tkgd->nkd/dot_general | solution.py:696
  490.7 19.3 %fusion.31 = bf16[2048,4,64]{0,2,1:T(8,128)(2,1)S(1)} fusion(bf16[4,3,512,64]{2,3,1,0:T(8,128)(2,1)S(1)} %bitcast.183, f32[4,2048,512,3]{2,1,3,0:T(8,128)} %fusion.36, f32[4,3,512]{2,1,0:T(4,128)S(1)} %bitcast.200, pred[512,2048]{0,1:T(8,128)(4,1)} %fusion.6), kind=kOutput, calls=%fused_computation.48 | convolution fusion | flops 1661468672 | bytes 53239808 | tf_op jit(solution)/shard_map/kgtn,kgtd->nkd/dot_general | solution.py:699
  511.8 85.7 %shard_map.239 = f32[512,512]{1,0:T(8,128)S(1)} custom-call(bf16[4,512,512]{2,1,0:T(8,128)(2,1)S(1)} %pad_maximum_fusion.x_ref), custom_call_target="tpu_custom_call" | custom-call | flops 786432 | bytes 6291456 | tf_op jit(solution)/shard_map/pallas_call | solution.py:455
  598.0 11.4 %convolution_multiply_fusion = f32[4,3,512,64]{2,3,1,0:T(8,128)S(1)} fusion(bf16[4,3,512,2048]{2,3,1,0:T(8,128)(2,1)} %multiply_convert_fusion, bf16[2048,4,64,1]{0,2,1,3:T(8,128)(2,1)S(1)} %copy-done.22), kind=kOutput, calls=%fused_computation.55 | convolution fusion | flops 1611005952 | bytes 27787264 | tf_op jit(solution)/shard_map/kgtn,nkd->kgtd/dot_general | solution.py:693
  615.7 32.1 %shard_map.240 = bf16[2,512,1536]{2,1,0:T(8,128)(2,1)} custom-call(bf16[512,1536]{1,0:T(8,128)(2,1)} %fusion.20.src_ref), custom_call_target="tpu_custom_call" | custom-call | bytes 3145728 | tf_op jit(solution)/shard_map/pallas_call | solution.py:248
  683.9 10.4 %concatenate.65 = bf16[2,2,384,2176]{3,2,0,1:T(8,128)(2,1)} concatenate(bf16[2,2,384,768]{3,2,0,1:T(8,128)(2,1)} %convolution_convert_fusion.3, bf16[2,2,384,768]{3,2,0,1:T(8,128)(2,1)S(1)} %copy.226, bf16[2,2,384,256]{3,2,0,1:T(8,128)(2,1)} %convolution_convert_fusion.4, bf16[2,2,384,256]{3,2,0,1:T(8,128)(2,1)S(1)} %copy.227, bf16[2,2,384,24]{3,2,0,1:T(8,128)(2,1)} %copy.228, ...), dimensions={3} | concatenate | bytes 13369344 | tf_op jit(solution)/shard_map/concatenate | solution.py:753
  694.3 6.3 shard_map.241.other_ref
  711.9 47.9 %reduce-scatter.7.cloned.1.call-done = bf16[24,96,256]{2,1,0:T(8,128)(2,1)} async-done(((bf16[24,768,256]{2,1,0:T(8,128)(2,1)}), bf16[24,96,256]{2,1,0:T(8,128)(2,1)}) %reduce-scatter.7.cloned.1.call-update) | async-done | bytes 1179664 | tf_op jit(solution)/shard_map/reduce_scatter | solution.py:656
  762.8 76.9 %reduce-scatter.13.cloned.1.call-done = bf16[96,2176]{1,0:T(8,128)(2,1)} async-done(((bf16[768,2176]{1,0:T(8,128)(2,1)}), bf16[96,2176]{1,0:T(8,128)(2,1)}) %reduce-scatter.13.cloned.1.call-update) | async-done | bytes 417808
  (275 shorter events, 147.8 us)
Async XLA Ops:
  7.2 89.9 %all-gather.2.cloned.1.call-start = ((), (), s32[]{:S(2)}) async-start(), calls=%async_computation.4 | async-start | bytes 7077888 | tf_op jit(solution)/shard_map/all_gather | solution.py:565
  7.9 698.1 %reduce-scatter.9.cloned.1.call-start = ((), (), s32[]{:S(2)}) async-start(), calls=%async_computation.6 | async-start | bytes 10616832 | tf_op jit(solution)/shard_map/reduce_scatter | solution.py:656
  10.0 23.1 %copy-start.40 = (f32[512,32]{0,1:T(8,128)}, f32[512,32]{0,1:T(8,128)S(1)}, u32[]{:S(2)}) copy-start(f32[512,32]{0,1:T(8,128)S(1)} %get-tuple-element.138) | copy-start | bytes 196612
  11.0 18.8 %copy-start.70 = (f32[512]{0:T(512)S(1)}, f32[512]{0:T(512)}, u32[]{:S(2)}) copy-start(f32[512]{0:T(512)} %copy-done.69) | copy-start | bytes 6148
  55.2 37.5 %copy-start = (f32[512,768]{1,0:T(8,128)}, f32[512,768]{1,0:T(8,128)S(1)}, u32[]{:S(2)}) copy-start(f32[512,768]{1,0:T(8,128)S(1)} %get-tuple-element.31) | copy-start | bytes 4718596
  208.6 500.4 %reduce-scatter.11.cloned.1.call-start = ((), (), s32[]{:S(2)}) async-start(), calls=%async_computation.7 | async-start | bytes 10616832 | tf_op jit(solution)/shard_map/reduce_scatter | solution.py:656
  235.0 524.9 %reduce-scatter.7.cloned.1.call-start = ((), (), s32[]{:S(2)}) async-start(), calls=%async_computation.5 | async-start | bytes 10616832 | tf_op jit(solution)/shard_map/reduce_scatter | solution.py:656
  243.3 25.2 %copy-start.21 = (bf16[2048,4,64,1]{0,2,1,3:T(8,128)(2,1)}, bf16[2048,4,64,1]{0,2,1,3:T(8,128)(2,1)S(1)}, u32[]{:S(2)}) copy-start(bf16[2048,4,64,1]{0,2,1,3:T(8,128)(2,1)S(1)} %reshape.371) | copy-start | bytes 3145732
  295.3 544.5 %reduce-scatter.13.cloned.1.call-start = ((), (), s32[]{:S(2)}) async-start(), calls=%async_computation.8 | async-start | bytes 3760128
  381.9 10.9 %copy-start.34 = (f32[512,8]{1,0:T(8,128)S(1)}, f32[512,8]{1,0:T(8,128)}, u32[]{:S(2)}) copy-start(f32[512,8]{1,0:T(8,128)} %copy-done.33) | copy-start | bytes 49156
  381.9 10.9 %copy-start.61 = (f32[512]{0:T(512)S(1)}, f32[512]{0:T(512)}, u32[]{:S(2)}) copy-start(f32[512]{0:T(512)} %copy-done.60) | copy-start | bytes 6148
  381.9 15.1 %copy-start.17 = (f32[512,1536]{1,0:T(8,128)S(1)}, f32[512,1536]{1,0:T(8,128)}, u32[]{:S(2)}) copy-start(f32[512,1536]{1,0:T(8,128)} %get-tuple-element.39) | copy-start | bytes 9437188
  398.3 35.1 %copy-start.8 = (f32[512,1536]{1,0:T(8,128)S(1)}, f32[512,1536]{1,0:T(8,128)}, u32[]{:S(2)}) copy-start(f32[512,1536]{1,0:T(8,128)} %copy-done.7) | copy-start | bytes 9437188
  398.3 35.1 %copy-start.51 = (bf16[1536,24]{0,1:T(8,128)(2,1)S(1)}, bf16[1536,24]{0,1:T(8,128)(2,1)}, u32[]{:S(2)}) copy-start(bf16[1536,24]{0,1:T(8,128)(2,1)} %param.21) | copy-start | bytes 221188
  398.3 35.1 %copy-start.57 = (f32[1536]{0:T(1024)S(1)}, f32[1536]{0:T(1024)}, u32[]{:S(2)}) copy-start(f32[1536]{0:T(1024)} %param.20) | copy-start | bytes 18436
  398.3 35.1 %copy-start.59 = (f32[512]{0:T(512)S(1)}, f32[512]{0:T(512)}, u32[]{:S(2)}) copy-start(f32[512]{0:T(512)} %copy-done.58) | copy-start | bytes 6148
  446.6 29.1 %copy-start.27 = (bf16[512,12,32]{0,2,1:T(8,128)(2,1)S(1)}, bf16[512,12,32]{0,2,1:T(8,128)(2,1)}, u32[]{:S(2)}) copy-start(bf16[512,12,32]{0,2,1:T(8,128)(2,1)} %copy-done.25) | copy-start | bytes 1179652
  446.6 29.1 %copy-start.30 = (bf16[512,12,32]{0,2,1:T(8,128)(2,1)S(1)}, bf16[512,12,32]{0,2,1:T(8,128)(2,1)}, u32[]{:S(2)}) copy-start(bf16[512,12,32]{0,2,1:T(8,128)(2,1)} %copy-done.28) | copy-start | bytes 1179652
  511.8 86.0 %copy-start.41 = (f32[512,32]{0,1:T(8,128)S(1)}, f32[512,32]{0,1:T(8,128)}, u32[]{:S(2)}) copy-start(f32[512,32]{0,1:T(8,128)} %copy-done.40) | copy-start | bytes 196612
  511.8 86.0 %copy-start.49 = (f32[512,32]{0,1:T(8,128)S(1)}, f32[512,32]{0,1:T(8,128)}, u32[]{:S(2)}) copy-start(f32[512,32]{0,1:T(8,128)} %get-tuple-element.136) | copy-start | bytes 196612
  511.8 86.1 %copy-start.22 = (bf16[2048,4,64,1]{0,2,1,3:T(8,128)(2,1)S(1)}, bf16[2048,4,64,1]{0,2,1,3:T(8,128)(2,1)}, u32[]{:S(2)}) copy-start(bf16[2048,4,64,1]{0,2,1,3:T(8,128)(2,1)} %copy-done.21) | copy-start | bytes 3145732
  615.7 32.1 %copy-start.9 = (bf16[512,1536]{1,0:T(8,128)(2,1)S(1)}, bf16[512,1536]{1,0:T(8,128)(2,1)}, u32[]{:S(2)}) copy-start(bf16[512,1536]{1,0:T(8,128)(2,1)} %fusion.20.src_ref) | copy-start | bytes 4718596
  615.7 32.1 %copy-start.64 = (f32[1536]{0:T(1024)S(1)}, f32[1536]{0:T(1024)}, u32[]{:S(2)}) copy-start(f32[1536]{0:T(1024)} %param.15) | copy-start | bytes 18436
  615.7 32.1 %copy-start.71 = (f32[512]{0:T(512)S(1)}, f32[512]{0:T(512)}, u32[]{:S(2)}) copy-start(f32[512]{0:T(512)} %copy-done.69) | copy-start | bytes 6148
  (54 other events, 150.0 us)
Sparse Core Ops, SparseCore 0:
  9.6 81.6 all-gather.1
  208.7 197.7 reduce-scatter.8
  410.1 163.0 reduce-scatter.10
  576.6 183.1 reduce-scatter.6
  763.3 76.3 reduce-scatter.12

commit v17 on v16

--- a/solution.py
+++ b/solution.py
@@ -534,6 +534,162 @@
     return lax.dynamic_update_slice_in_dim(got, x[None], me, 0)
 
 
+def _attend_block(groups, kv_heads, q_sc, kv_buf, qseg_ref, qpos_ref, kseg_ref, m_sc, l_sc, acc_sc, block):
+    f32 = jnp.float32
+    depth = HEAD_SIZE
+    width = kv_buf.shape[0]
+    start = pl.multiple_of(block * width, width)
+    key_pos = start + lax.broadcasted_iota(jnp.int32, (1, width), 1)
+    allowed = (qseg_ref[...] == kseg_ref[:, pl.ds(start, width)]) & (key_pos <= qpos_ref[...])
+    for kk in range(kv_heads):
+        keys = kv_buf[:, kk * depth : (kk + 1) * depth]
+        values = kv_buf[:, (kv_heads + kk) * depth : (kv_heads + kk + 1) * depth]
+        scores = lax.dot_general(q_sc[kk], keys, (((1,), (1,)), ((), ())), preferred_element_type=f32)
+        scores = jnp.where(allowed, scores, NEGATIVE)
+        m_old = m_sc[kk]
+        m_new = jnp.maximum(m_old, jnp.max(scores, axis=1, keepdims=True))
+        alpha = jnp.exp(m_old - m_new)
+        weights = jnp.where(allowed, jnp.exp(scores - m_new), 0.0)
+        l_sc[kk] = alpha * l_sc[kk] + jnp.sum(weights, axis=1, keepdims=True)
+        acc_sc[kk] = alpha * acc_sc[kk] + jnp.dot(
+            weights.astype(jnp.bfloat16), values, preferred_element_type=f32
+        )
+        m_sc[kk] = m_new
+
+
+def _gather_attend_body(
+    axis, n, groups, q_ref, own_ref, qseg_ref, qpos_ref, kseg_ref,
+    kv_ref, o_ref, lse_ref,
+    q_sc, m_sc, l_sc, acc_sc, kv_buf, send_sems, recv_sems, copy_sem,
+):
+    depth = HEAD_SIZE
+    tokens = q_ref.shape[0]
+    kv_heads = own_ref.shape[1] // (2 * depth)
+    me = lax.axis_index(axis)
+    below = lax.rem(me + n - 1, n)
+    above = lax.rem(me + 1, n)
+    barrier = pltpu.get_barrier_semaphore()
+    pl.semaphore_signal(barrier, 1, device_id={axis: below}, device_id_type=MESH)
+    pl.semaphore_signal(barrier, 1, device_id={axis: above}, device_id_type=MESH)
+    pl.semaphore_wait(barrier, 2)
+    own = pltpu.make_async_remote_copy(
+        src_ref=own_ref,
+        dst_ref=kv_ref.at[me],
+        send_sem=send_sems.at[me],
+        recv_sem=recv_sems.at[me],
+        device_id={axis: above},
+        device_id_type=MESH,
+    )
+    pl.when(me < n - 1)(own.start)
+
+    m_sc[...] = jnp.full_like(m_sc, NEGATIVE)
+    l_sc[...] = jnp.zeros_like(l_sc)
+    acc_sc[...] = jnp.zeros_like(acc_sc)
+    scale = jnp.asarray(1.0 / math.sqrt(HEAD_SIZE), q_ref.dtype)
+    for kk in range(kv_heads):
+        for gi in range(groups):
+            i = kk * groups + gi
+            q_sc[kk, gi * tokens : (gi + 1) * tokens, :] = q_ref[:, i * depth : (i + 1) * depth] * scale
+
+    local = pltpu.make_async_copy(own_ref, kv_buf, copy_sem)
+    local.start()
+    local.wait()
+    _attend_block(groups, kv_heads, q_sc, kv_buf, qseg_ref, qpos_ref, kseg_ref, m_sc, l_sc, acc_sc, me)
+
+    def step(k, carry):
+        block = me - k
+        incoming = pltpu.make_async_remote_copy(
+            src_ref=kv_ref.at[block],
+            dst_ref=kv_ref.at[block],
+            send_sem=send_sems.at[block],
+            recv_sem=recv_sems.at[block],
+            device_id={axis: below},
+            device_id_type=MESH,
+        )
+        incoming.wait_recv()
+        forward = pltpu.make_async_remote_copy(
+            src_ref=kv_ref.at[block],
+            dst_ref=kv_ref.at[block],
+            send_sem=send_sems.at[block],
+            recv_sem=recv_sems.at[block],
+            device_id={axis: above},
+            device_id_type=MESH,
+        )
+        pl.when(me < n - 1)(forward.start)
+        fetch = pltpu.make_async_copy(kv_ref.at[block], kv_buf, copy_sem)
+        fetch.start()
+        fetch.wait()
+        _attend_block(groups, kv_heads, q_sc, kv_buf, qseg_ref, qpos_ref, kseg_ref, m_sc, l_sc, acc_sc, block)
+        return carry
+
+    lax.fori_loop(1, me + 1, step, 0)
+
+    for kk in range(kv_heads):
+        for gi in range(groups):
+            i = kk * groups + gi
+            rows = slice(gi * tokens, (gi + 1) * tokens)
+            o_ref[:, i * depth : (i + 1) * depth] = acc_sc[kk, rows, :] / l_sc[kk, rows, :]
+            lse_ref[:, i : i + 1] = m_sc[kk, rows, :] + jnp.log(l_sc[kk, rows, :])
+
+    pl.when(me < n - 1)(own.wait_send)
+
+    def drain(k, carry):
+        block = me - k
+        pltpu.make_async_remote_copy(
+            src_ref=kv_ref.at[block],
+            dst_ref=kv_ref.at[block],
+            send_sem=send_sems.at[block],
+            recv_sem=recv_sems.at[block],
+            device_id={axis: above},
+            device_id_type=MESH,
+        ).wait_send()
+        return carry
+
+    lax.fori_loop(1, jnp.where(me < n - 1, me + 1, 1), drain, 0)
+
+
+def gather_attend(q, own, qseg, qpos, kseg, axis, n, groups, collective_id):
+    tokens, q_width = q.shape
+    rows, kv_width = own.shape
+    heads = q_width // HEAD_SIZE
+    kv_heads = kv_width // (2 * HEAD_SIZE)
+    f32 = jnp.float32
+    vmem = pl.BlockSpec(memory_space=pltpu.VMEM)
+    anywhere = pl.BlockSpec(memory_space=pl.ANY)
+    kv_all, attn, lse = pl.pallas_call(
+        functools.partial(_gather_attend_body, axis, n, groups),
+        out_shape=[
+            jax.ShapeDtypeStruct((n, rows, kv_width), own.dtype),
+            jax.ShapeDtypeStruct((tokens, q_width), f32),
+            jax.ShapeDtypeStruct((tokens, heads), f32),
+        ],
+        in_specs=[vmem, anywhere, vmem, vmem, vmem],
+        out_specs=[anywhere, vmem, vmem],
+        scratch_shapes=[
+            pltpu.VMEM((kv_heads, groups * tokens, HEAD_SIZE), q.dtype),
+            pltpu.VMEM((kv_heads, groups * tokens, 1), f32),
+            pltpu.VMEM((kv_heads, groups * tokens, 1), f32),
+            pltpu.VMEM((kv_heads, groups * tokens, HEAD_SIZE), f32),
+            pltpu.VMEM((rows, kv_width), own.dtype),
+            pltpu.SemaphoreType.DMA((n,)),
+            pltpu.SemaphoreType.DMA((n,)),
+            pltpu.SemaphoreType.DMA(()),
+        ],
+        compiler_params=pltpu.CompilerParams(
+            collective_id=collective_id, has_side_effects=True, vmem_limit_bytes=48 * 1024 * 1024
+        ),
+        cost_estimate=pl.CostEstimate(
+            flops=tokens * q_width * n * rows * 4,
+            transcendentals=tokens * heads * n * rows,
+            bytes_accessed=2 * n * own.size * own.dtype.itemsize + tokens * q_width * 6,
+        ),
+    )(q, own, qseg, qpos, kseg)
+    me = lax.axis_index(axis)
+    below = (jnp.arange(n, dtype=jnp.int32) < me).reshape((n, 1, 1))
+    kv_all = jnp.where(below, kv_all, jnp.zeros_like(kv_all))
+    return attn, lse, lax.dynamic_update_slice_in_dim(kv_all, own[None], me, 0)
+
+
 def per_device(
     dpx_count,
     hidden_in,
@@ -591,26 +747,25 @@
         )
 
     ctx_count = segments.shape[0] // token_count
-    kv_both = gather_up(jnp.concatenate([key_flat, value_flat], axis=1), "ctx", ctx_count, 1)
+    attn_flat, lse_heads, kv_both = gather_attend(
+        query_grouped.reshape(token_count, heads_local * HEAD_SIZE),
+        jnp.concatenate([key_flat, value_flat], axis=1),
+        jnp.tile(segment_here, group_size)[:, None],
+        jnp.tile(token_positions, group_size)[:, None],
+        segments[None, :],
+        "ctx",
+        ctx_count,
+        group_size,
+        1,
+    )
     piece_rows = ctx_count * token_count
     kv_width = kv_local * HEAD_SIZE
     key_piece = kv_both[:, :, :kv_width].reshape(piece_rows, kv_local, HEAD_SIZE)
     value_piece = kv_both[:, :, kv_width:].reshape(piece_rows, kv_local, HEAD_SIZE)
-    attn_flat, lse_pairs = flash_forward(
-        ctx_index,
-        query_grouped.reshape(token_count, heads_local * HEAD_SIZE),
-        kv_both,
-        jnp.tile(segment_here, group_size)[:, None],
-        jnp.tile(token_positions, group_size)[:, None],
-        segments[None, :],
-        group_size,
-    )
     attn_grouped = jnp.transpose(
         attn_flat.reshape(token_count, kv_local, group_size, HEAD_SIZE), (1, 2, 0, 3)
     )
-    log_sum = jnp.transpose(
-        lse_pairs.reshape(kv_local // 2, token_count, 2, group_size), (0, 2, 3, 1)
-    ).reshape(kv_local, group_size, token_count)
+    log_sum = jnp.transpose(lse_heads.reshape(token_count, kv_local, group_size), (1, 2, 0))
     attn_bf = attn_flat.astype(bf16)
     tensor_count = o_weight.shape[0] // o_weight.shape[1]
     attn_all = gather_axis(attn_bf, "tensor", tensor_count, 2)

time: 858 us -> 827 us (0.964)
  Pallas kernels: 473 us -> 435 us
    pallas_call x1, Pallas kernels: 85.7 us -> 55.5 us  [chain_sum_down(): pl.pallas_call(functools.partial(_chain_down_body, axis, n), out_shape=ja...]
    pallas_call x2 -> x1, Pallas kernels: 30.9 us -> 21.9 us  [gather_attend(): pl.pallas_call(functools.partial(_gather_attend_body, axis, n, groups), o...]
    unnamed x158 -> x160, local copies, waits for them, and re-layouts: 22.5 us -> 22 us
  transfers between devices with their start and end apart: 5 -> 5, of which waited for: 2 -> 3; matrix products, arithmetic and copies ran while one was open for 24% -> 25% of each run, Pallas kernels for 44% -> 41%
where the time goes in v17:
time: 827 us; the launch traced here: 821 us
  Pallas kernels  435 us (53%)
  waiting for transfers between devices  134 us (16%)
  matrix products  124 us (15%)
  local copies, waits for them, and re-layouts  70.4 us (9%)
  other arithmetic  42 us (5%)
  between operations  15.2 us (2%)
    pallas_call x9, Pallas kernels, exchange(): pl.pallas_call(functools.partial(_exchange_body, axis, n, per_peer, downw...  197 us
    unnamed x6, waiting for transfers between devices  77.6 us
    pallas_call x1, Pallas kernels, expert_grad_kernel(): pl.pallas_call(_grad_body, grid=(experts,), in_specs=[whole((tokens, widt...  73.6 us
    pallas_call x1, Pallas kernels, chain_sum_down(): pl.pallas_call(functools.partial(_chain_down_body, axis, n), out_shape=ja...  55.5 us
    reduce_scatter x3, waiting for transfers between devices, per_device(): lax.psum_scatter(g.reshape(g.shape[0], -1, g.shape[3]), ('dpx', 'ctx'), s...  51 us
    pallas_call x1, Pallas kernels, expert_rows_kernel(): pl.pallas_call(_rows_body, grid=(experts,), in_specs=[per_expert((tokens,...  46.8 us
    pallas_call x4, Pallas kernels, core_reduce(): pl.pallas_call(_pair_add_body, grid_spec=grid_spec, out_shape=jax.ShapeDt...  39.6 us
    dot_general x1, matrix products, per_device(): jnp.einsum('kgtd,nkd->kgtn', grad_attn_grouped, value_piece, preferred_el...  28.3 us
  transfers between devices with their start and end apart: 5, of which 3 were waited for; matrix products, arithmetic and copies ran while one was open for 25% of the time, Pallas kernels for 41%

profile of v17, /device:TPU:0, one launch (start us, length us, event | category | flops | bytes accessed | tf_op | source)
XLA Modules:
  0.0 820.5 jit_solution(4249973373149800865)
XLA Ops:
  20.7 21.9 %shard_map.229 = (bf16[4,512,512]{2,1,0:T(8,128)(2,1)}, f32[512,768]{1,0:T(8,128)S(1)}, f32[512,12]{1,0:T(8,128)S(1)}) custom-call(bf16[512,768]{1,0:T(8,128)(2,1)S(1)} %copy.188.q_ref, bf16[512,512]{1,0:T(8,128)(2,1)S(1)} %pad_maximum_fusion.3.own_ref, s32[1536,1]{1,0:T(8,128)S(1)} %bitcast.162, s32[1536,1]{1,0:T(8,128)S(1)} %bitcast.163, ...), custom_call_target="tpu_custom_call" | custom-call | flops 3221225472 | bytes 6553600 | tf_op jit(solution)/shard_map/pallas_call | solution.py:659
  44.4 37.1 %shard_map.230 = bf16[2,512,768]{2,1,0:T(8,128)(2,1)} custom-call(bf16[512,768]{1,0:T(8,128)(2,1)} %convert_element_type.161.src_ref), custom_call_target="tpu_custom_call" | custom-call | bytes 1572864 | tf_op jit(solution)/shard_map/pallas_call | solution.py:248
  102.9 73.6 %shard_map.231 = (bf16[2,24,2,384,256]{4,3,2,1,0:T(8,128)(2,1)}, bf16[2,24,2,384,256]{4,3,2,1,0:T(8,128)(2,1)}, bf16[2,24,2,384,256]{4,3,2,1,0:T(8,128)(2,1)}, b...) custom-call(bf16[512,1536]{1,0:T(8,128)(2,1)} %copy-done.10, ...), custom_call_target="tpu_custom_call" | custom-call | flops 57982058496 | bytes 138412032 | tf_op jit(solution)/shard_map/pallas_call | solution.py:135
  176.5 15.1 %shard_map.242.other_ref = bf16[2,24,2,384,256]{4,3,2,1,0:T(8,128)(2,1)} custom-call(bf16[2,24,2,384,256]{4,3,2,1,0:T(8,128)(2,1)} %get-tuple-element.46.src_ref.own_ref), custom_call_target="tpu_custom_call" | custom-call | bytes 18874368 | tf_op jit(solution)/shard_map/pallas_call | solution.py:248
  191.5 11.5 %shard_map.243 = bf16[24,2,384,256]{3,2,1,0:T(8,128)(2,1)} custom-call(s32[1]{0:T(128)} %bitcast.8.me_ref, bf16[2,24,2,384,256]{4,3,2,1,0:T(8,128)(2,1)} %get-tuple-element.46.src_ref.own_ref, bf16[2,24,2,384,256]{4,3,2,1,0:T(8,128)(2,1)} %shard_map.242.other_ref), custom_call_target="tpu_custom_call" | custom-call | flops 4718592 | bytes 28311552 | tf_op jit(solution)/shard_map/pallas_call | solution.py:292
  203.1 15.1 %shard_map.244.other_ref = bf16[2,24,2,384,256]{4,3,2,1,0:T(8,128)(2,1)} custom-call(bf16[2,24,2,384,256]{4,3,2,1,0:T(8,128)(2,1)} %get-tuple-element.47.src_ref.own_ref), custom_call_target="tpu_custom_call" | custom-call | bytes 18874368 | tf_op jit(solution)/shard_map/pallas_call | solution.py:248
  218.1 11.3 %shard_map.245 = bf16[24,2,384,256]{3,2,1,0:T(8,128)(2,1)} custom-call(s32[1]{0:T(128)} %bitcast.8.me_ref, bf16[2,24,2,384,256]{4,3,2,1,0:T(8,128)(2,1)} %get-tuple-element.47.src_ref.own_ref, bf16[2,24,2,384,256]{4,3,2,1,0:T(8,128)(2,1)} %shard_map.244.other_ref), custom_call_target="tpu_custom_call" | custom-call | flops 4718592 | bytes 28311552 | tf_op jit(solution)/shard_map/pallas_call | solution.py:292
  243.8 20.5 %fusion.36 = f32[4,2048,512,3]{2,1,3,0:T(8,128)} fusion(bf16[2048,4,64,1]{0,2,1,3:T(8,128)(2,1)S(1)} %reshape.367, bf16[512,4,3,32]{0,3,2,1:T(8,128)(2,1)S(1)} %bitcast.173, bf16[512,4,3,32]{0,3,2,1:T(8,128)(2,1)S(1)} %bitcast.171), kind=kOutput, calls=%fused_computation.61 | convolution fusion | flops 1612185600 | bytes 52166656 | tf_op jit(solution)/shard_map/tkgd,nkd->kgtn/dot_general | solution.py:840
  264.2 15.0 %shard_map.232.other_ref = bf16[2,24,2,384,256]{4,3,2,1,0:T(8,128)(2,1)} custom-call(bf16[2,24,2,384,256]{4,3,2,1,0:T(8,128)(2,1)} %get-tuple-element.33.src_ref.own_ref), custom_call_target="tpu_custom_call" | custom-call | bytes 18874368 | tf_op jit(solution)/shard_map/pallas_call | solution.py:248
  279.2 11.3 %shard_map.233 = bf16[24,2,384,256]{3,2,1,0:T(8,128)(2,1)} custom-call(s32[1]{0:T(128)} %bitcast.8.me_ref, bf16[2,24,2,384,256]{4,3,2,1,0:T(8,128)(2,1)} %get-tuple-element.33.src_ref.own_ref, bf16[2,24,2,384,256]{4,3,2,1,0:T(8,128)(2,1)} %shard_map.232.other_ref), custom_call_target="tpu_custom_call" | custom-call | flops 4718592 | bytes 28311552 | tf_op jit(solution)/shard_map/pallas_call | solution.py:292
  291.1 46.8 %shard_map.234 = (f32[512,1536]{1,0:T(8,128)}, f32[24,512,1]{2,1,0:T(8,128)}, f32[512,1536]{1,0:T(8,128)}) custom-call(bf16[24,512,256]{2,1,0:T(8,128)(2,1)} %get-tuple-element.37.hid_ref, bf16[24,512,256]{2,1,0:T(8,128)(2,1)} %get-tuple-element.38.dga_ref, bf16[24,512,256]{2,1,0:T(8,128)(2,1)} %get-tuple-element.39.dua_ref, bf16[512,1536]{1,0:T(8,128)(2,1)} %dy_ref.3, ...), custom_call_target="tpu_custom_call" | custom-call | flops 28991029248 | bytes 83361792 | tf_op jit(solution)/shard_map/pallas_call | solution.py:169
  341.2 36.8 %shard_map.236 = bf16[2,512,1536]{2,1,0:T(8,128)(2,1)} custom-call(bf16[512,1536]{1,0:T(8,128)(2,1)} %convert_element_type.169.src_ref), custom_call_target="tpu_custom_call" | custom-call | bytes 3145728 | tf_op jit(solution)/shard_map/pallas_call | solution.py:248
  394.4 35.2 %shard_map.235 = bf16[2,512,1536]{2,1,0:T(8,128)(2,1)} custom-call(bf16[512,1536]{1,0:T(8,128)(2,1)} %convert_element_type.163.src_ref), custom_call_target="tpu_custom_call" | custom-call | bytes 3145728 | tf_op jit(solution)/shard_map/pallas_call | solution.py:248
  442.7 28.3 %multiply_convert_fusion = bf16[4,3,512,2048]{2,3,1,0:T(8,128)(2,1)} fusion(f32[4,2048,512,3]{2,1,3,0:T(8,128)} %fusion.36, f32[4,3,512]{2,1,0:T(4,128)S(1)} %multiply_reduce_fusion.3, f32[4,3,512]{2,1,0:T(4,128)S(1)} %bitcast.196, pred[512,2048]{0,1:T(8,128)(4,1)} %fusion.6, bf16[4,3,512,64]{2,3,1,0:T(8,128)(2,1)S(1)} %bitcast.180, ...), kind=kOutput, calls=%fused_computation.3 | convolution fusion | flops 1686110208 | bytes 78430208 | tf_op jit(solution)/shard_map/kgtd,nkd->kgtn/dot_general | solution.py:844
  470.9 12.9 %fusion.30 = bf16[2048,4,64]{0,2,1:T(8,128)(2,1)S(1)} fusion(bf16[4,3,512,2048]{2,3,1,0:T(8,128)(2,1)} %multiply_convert_fusion, bf16[512,4,3,32]{0,3,2,1:T(8,128)(2,1)S(1)} %bitcast.174, bf16[512,4,3,32]{0,3,2,1:T(8,128)(2,1)S(1)} %bitcast.172), kind=kOutput, calls=%fused_computation.47 | convolution fusion | flops 1613234176 | bytes 27000832 | tf_op jit(solution)/shard_map/kgtn,tkgd->nkd/dot_general | solution.py:851
  486.3 19.6 %fusion.31 = bf16[2048,4,64]{0,2,1:T(8,128)(2,1)S(1)} fusion(bf16[4,3,512,64]{2,3,1,0:T(8,128)(2,1)S(1)} %bitcast.181, f32[4,2048,512,3]{2,1,3,0:T(8,128)} %fusion.36, f32[4,3,512]{2,1,0:T(4,128)S(1)} %bitcast.197, pred[512,2048]{0,1:T(8,128)(4,1)} %fusion.6), kind=kOutput, calls=%fused_computation.48 | convolution fusion | flops 1661468672 | bytes 53239808 | tf_op jit(solution)/shard_map/kgtn,kgtd->nkd/dot_general | solution.py:854
  507.7 55.5 %shard_map.238 = f32[512,512]{1,0:T(8,128)S(1)} custom-call(bf16[4,512,512]{2,1,0:T(8,128)(2,1)S(1)} %pad_maximum_fusion.x_ref), custom_call_target="tpu_custom_call" | custom-call | flops 786432 | bytes 6291456 | tf_op jit(solution)/shard_map/pallas_call | solution.py:455
  563.6 11.3 %convolution_multiply_fusion = f32[4,3,512,64]{2,3,1,0:T(8,128)S(1)} fusion(bf16[4,3,512,2048]{2,3,1,0:T(8,128)(2,1)} %multiply_convert_fusion, bf16[2048,4,64,1]{0,2,1,3:T(8,128)(2,1)S(1)} %copy-done.22), kind=kOutput, calls=%fused_computation.55 | convolution fusion | flops 1611005952 | bytes 27787264 | tf_op jit(solution)/shard_map/kgtn,nkd->kgtd/dot_general | solution.py:848
  581.3 31.5 %shard_map.239 = bf16[2,512,1536]{2,1,0:T(8,128)(2,1)} custom-call(bf16[512,1536]{1,0:T(8,128)(2,1)} %fusion.20.src_ref), custom_call_target="tpu_custom_call" | custom-call | bytes 3145728 | tf_op jit(solution)/shard_map/pallas_call | solution.py:248
  616.5 5.6 fusion.48
  649.1 10.4 %concatenate.65 = bf16[2,2,384,2176]{3,2,0,1:T(8,128)(2,1)} concatenate(bf16[2,2,384,768]{3,2,0,1:T(8,128)(2,1)} %convolution_convert_fusion.3, bf16[2,2,384,768]{3,2,0,1:T(8,128)(2,1)S(1)} %copy.219, bf16[2,2,384,256]{3,2,0,1:T(8,128)(2,1)} %convolution_convert_fusion.4, bf16[2,2,384,256]{3,2,0,1:T(8,128)(2,1)S(1)} %copy.220, bf16[2,2,384,24]{3,2,0,1:T(8,128)(2,1)} %copy.221, ...), dimensions={3} | concatenate | bytes 13369344 | tf_op jit(solution)/shard_map/concatenate | solution.py:908
  659.5 6.3 shard_map.240.other_ref
  677.1 51.0 %reduce-scatter.7.cloned.1.call-done = bf16[24,96,256]{2,1,0:T(8,128)(2,1)} async-done(((bf16[24,768,256]{2,1,0:T(8,128)(2,1)}), bf16[24,96,256]{2,1,0:T(8,128)(2,1)}) %reduce-scatter.7.cloned.1.call-update) | async-done | bytes 1179664 | tf_op jit(solution)/shard_map/reduce_scatter | solution.py:811
  731.1 76.8 %reduce-scatter.13.cloned.1.call-done = bf16[96,2176]{1,0:T(8,128)(2,1)} async-done(((bf16[768,2176]{1,0:T(8,128)(2,1)}), bf16[96,2176]{1,0:T(8,128)(2,1)}) %reduce-scatter.13.cloned.1.call-update) | async-done | bytes 417808
  (276 shorter events, 145.0 us)
Async XLA Ops:
  7.2 84.6 %all-gather.2.cloned.1.call-start = ((), (), s32[]{:S(2)}) async-start(), calls=%async_computation.4 | async-start | bytes 7077888 | tf_op jit(solution)/shard_map/all_gather | solution.py:721
  7.9 663.3 %reduce-scatter.9.cloned.1.call-start = ((), (), s32[]{:S(2)}) async-start(), calls=%async_computation.6 | async-start | bytes 10616832 | tf_op jit(solution)/shard_map/reduce_scatter | solution.py:811
  43.4 39.1 %copy-start = (f32[512,768]{1,0:T(8,128)}, f32[512,768]{1,0:T(8,128)S(1)}, u32[]{:S(2)}) copy-start(f32[512,768]{1,0:T(8,128)S(1)} %get-tuple-element.32) | copy-start | bytes 4718596
  82.5 9.4 %copy-start.13 = (bf16[512,1536]{1,0:T(8,128)(2,1)S(1)}, bf16[512,1536]{1,0:T(8,128)(2,1)}, u32[]{:S(2)}) copy-start(bf16[512,1536]{1,0:T(8,128)(2,1)} %param.14) | copy-start | bytes 4718596
  203.0 471.1 %reduce-scatter.11.cloned.1.call-start = ((), (), s32[]{:S(2)}) async-start(), calls=%async_computation.7 | async-start | bytes 10616832 | tf_op jit(solution)/shard_map/reduce_scatter | solution.py:811
  229.5 498.6 %reduce-scatter.7.cloned.1.call-start = ((), (), s32[]{:S(2)}) async-start(), calls=%async_computation.5 | async-start | bytes 10616832 | tf_op jit(solution)/shard_map/reduce_scatter | solution.py:811
  237.4 26.9 %copy-start.21 = (bf16[2048,4,64,1]{0,2,1,3:T(8,128)(2,1)}, bf16[2048,4,64,1]{0,2,1,3:T(8,128)(2,1)S(1)}, u32[]{:S(2)}) copy-start(bf16[2048,4,64,1]{0,2,1,3:T(8,128)(2,1)S(1)} %reshape.367) | copy-start | bytes 3145732
  290.6 517.3 %reduce-scatter.13.cloned.1.call-start = ((), (), s32[]{:S(2)}) async-start(), calls=%async_computation.8 | async-start | bytes 3760128
  378.0 10.9 %copy-start.33 = (f32[512,8]{1,0:T(8,128)S(1)}, f32[512,8]{1,0:T(8,128)}, u32[]{:S(2)}) copy-start(f32[512,8]{1,0:T(8,128)} %copy-done.32) | copy-start | bytes 49156
  378.0 10.9 %copy-start.63 = (f32[512]{0:T(512)S(1)}, f32[512]{0:T(512)}, u32[]{:S(2)}) copy-start(f32[512]{0:T(512)} %copy-done.62) | copy-start | bytes 6148
  378.0 15.0 %copy-start.17 = (f32[512,1536]{1,0:T(8,128)S(1)}, f32[512,1536]{1,0:T(8,128)}, u32[]{:S(2)}) copy-start(f32[512,1536]{1,0:T(8,128)} %get-tuple-element.40) | copy-start | bytes 9437188
  394.4 35.2 %copy-start.8 = (f32[512,1536]{1,0:T(8,128)S(1)}, f32[512,1536]{1,0:T(8,128)}, u32[]{:S(2)}) copy-start(f32[512,1536]{1,0:T(8,128)} %copy-done.7) | copy-start | bytes 9437188
  394.4 35.3 %copy-start.53 = (bf16[1536,24]{0,1:T(8,128)(2,1)S(1)}, bf16[1536,24]{0,1:T(8,128)(2,1)}, u32[]{:S(2)}) copy-start(bf16[1536,24]{0,1:T(8,128)(2,1)} %param.21) | copy-start | bytes 221188
  394.4 35.3 %copy-start.59 = (f32[1536]{0:T(1024)S(1)}, f32[1536]{0:T(1024)}, u32[]{:S(2)}) copy-start(f32[1536]{0:T(1024)} %param.20) | copy-start | bytes 18436
  394.4 35.3 %copy-start.61 = (f32[512]{0:T(512)S(1)}, f32[512]{0:T(512)}, u32[]{:S(2)}) copy-start(f32[512]{0:T(512)} %copy-done.60) | copy-start | bytes 6148
  442.7 28.3 %copy-start.26 = (bf16[512,12,32]{0,2,1:T(8,128)(2,1)S(1)}, bf16[512,12,32]{0,2,1:T(8,128)(2,1)}, u32[]{:S(2)}) copy-start(bf16[512,12,32]{0,2,1:T(8,128)(2,1)} %copy-done.24) | copy-start | bytes 1179652
  442.7 28.3 %copy-start.29 = (bf16[512,12,32]{0,2,1:T(8,128)(2,1)S(1)}, bf16[512,12,32]{0,2,1:T(8,128)(2,1)}, u32[]{:S(2)}) copy-start(bf16[512,12,32]{0,2,1:T(8,128)(2,1)} %copy-done.27) | copy-start | bytes 1179652
  507.7 55.8 %copy-start.42 = (f32[512,32]{0,1:T(8,128)S(1)}, f32[512,32]{0,1:T(8,128)}, u32[]{:S(2)}) copy-start(f32[512,32]{0,1:T(8,128)} %copy-done.41) | copy-start | bytes 196612
  507.7 55.8 %copy-start.51 = (f32[512,32]{0,1:T(8,128)S(1)}, f32[512,32]{0,1:T(8,128)}, u32[]{:S(2)}) copy-start(f32[512,32]{0,1:T(8,128)} %get-tuple-element.138) | copy-start | bytes 196612
  507.7 55.9 %copy-start.22 = (bf16[2048,4,64,1]{0,2,1,3:T(8,128)(2,1)S(1)}, bf16[2048,4,64,1]{0,2,1,3:T(8,128)(2,1)}, u32[]{:S(2)}) copy-start(bf16[2048,4,64,1]{0,2,1,3:T(8,128)(2,1)} %copy-done.21) | copy-start | bytes 3145732
  581.3 31.5 %copy-start.9 = (bf16[512,1536]{1,0:T(8,128)(2,1)S(1)}, bf16[512,1536]{1,0:T(8,128)(2,1)}, u32[]{:S(2)}) copy-start(bf16[512,1536]{1,0:T(8,128)(2,1)} %fusion.20.src_ref) | copy-start | bytes 4718596
  581.3 31.5 %copy-start.66 = (f32[1536]{0:T(1024)S(1)}, f32[1536]{0:T(1024)}, u32[]{:S(2)}) copy-start(f32[1536]{0:T(1024)} %param.15) | copy-start | bytes 18436
  581.3 31.5 %copy-start.72 = (f32[512]{0:T(512)S(1)}, f32[512]{0:T(512)}, u32[]{:S(2)}) copy-start(f32[512]{0:T(512)} %copy-done.71) | copy-start | bytes 6148
  622.0 10.8 %copy-start.15 = (bf16[512,1536]{1,0:T(8,128)(2,1)S(1)}, bf16[512,1536]{1,0:T(8,128)(2,1)}, u32[]{:S(2)}) copy-start(bf16[512,1536]{1,0:T(8,128)(2,1)} %param.14) | copy-start | bytes 4718596
  (55 other events, 173.0 us)
Sparse Core Ops, SparseCore 0:
  9.6 82.1 all-gather.1
  203.1 170.5 reduce-scatter.8
  377.3 164.1 reduce-scatter.10
  544.9 183.1 reduce-scatter.6
  731.6 76.3 reduce-scatter.12

commit v18 on v17

--- a/solution.py
+++ b/solution.py
@@ -79,30 +79,30 @@
 
 
 def _grad_body(
-    n2_ref, n2t_ref, dy_ref, dyt_ref, gcol_ref, grow_ref, wg_ref, wu_ref, wd_ref,
-    gg_ref, gu_ref, gd_ref, hid_ref, dga_ref, dua_ref,
+    n2_ref, n2t_ref, dy_ref, gcol_ref, wg_ref, wu_ref, wd_ref,
+    gg_ref, hid_ref, dga_ref, dua_ref,
 ):
     f32 = jnp.float32
     bf16 = jnp.bfloat16
     n2 = n2_ref[...]
-    wd = wd_ref[0]
     gate_act = jnp.dot(n2, wg_ref[0], preferred_element_type=f32)
     up_act = jnp.dot(n2, wu_ref[0], preferred_element_type=f32)
     sig = 1.0 / (1.0 + jnp.exp(-gate_act))
     silu = gate_act * sig
-    hidden = (silu * up_act).astype(bf16)
-    hid_ref[0] = hidden
+    hid_ref[0] = (silu * up_act).astype(bf16)
     deo = (_gate_column(gcol_ref) * dy_ref[...].astype(f32)).astype(bf16)
-    grad_hidden = jnp.dot(deo, wd, preferred_element_type=f32)
-    deo_t = (grow_ref[0] * dyt_ref[...].astype(f32)).astype(bf16)
-    _store_split(gd_ref, jnp.dot(deo_t, hidden, preferred_element_type=f32))
+    grad_hidden = jnp.dot(deo, wd_ref[0], preferred_element_type=f32)
     grad_gate_act = (grad_hidden * up_act * sig * (1.0 + gate_act * (1.0 - sig))).astype(bf16)
-    grad_up_act = (grad_hidden * silu).astype(bf16)
     dga_ref[0] = grad_gate_act
-    dua_ref[0] = grad_up_act
-    n2t = n2t_ref[...]
-    _store_split(gg_ref, jnp.dot(n2t, grad_gate_act, preferred_element_type=f32))
-    _store_split(gu_ref, jnp.dot(n2t, grad_up_act, preferred_element_type=f32))
+    dua_ref[0] = (grad_hidden * silu).astype(bf16)
+    _store_split(gg_ref, jnp.dot(n2t_ref[...], grad_gate_act, preferred_element_type=f32))
+
+
+def _grad_rest_body(n2t_ref, dyt_ref, grow_ref, hid_ref, dua_ref, gu_ref, gd_ref):
+    f32 = jnp.float32
+    deo_t = (grow_ref[0] * dyt_ref[...].astype(f32)).astype(jnp.bfloat16)
+    _store_split(gd_ref, jnp.dot(deo_t, hid_ref[0], preferred_element_type=f32))
+    _store_split(gu_ref, jnp.dot(n2t_ref[...], dua_ref[0], preferred_element_type=f32))
 
 
 def _rows_body(hid_ref, dga_ref, dua_ref, dy_ref, gcol_ref, wg_ref, wu_ref, wd_ref, acc_ref, dgate_ref, dn2_ref):
@@ -122,7 +122,7 @@
     ) + lax.dot_general(dua_ref[0], wu_ref[0], nt, preferred_element_type=f32)
 
 
-def expert_grad_kernel(n2, n2t, dy, dyt, gcol, grow, wg, wu, wd, groups):
+def expert_grad_kernel(n2, n2t, dy, gcol, wg, wu, wd, groups):
     tokens, width = n2.shape
     experts, _, hidden = wg.shape
     bf16 = jnp.bfloat16
@@ -139,25 +139,54 @@
             whole((tokens, width)),
             whole((width, tokens)),
             whole((tokens, width)),
-            whole((width, tokens)),
             whole((tokens, experts)),
-            per_expert((1, tokens)),
             per_expert((width, hidden)),
             per_expert((width, hidden)),
             per_expert((width, hidden)),
         ],
-        out_specs=[split, split, split]
-        + [per_expert((tokens, hidden))] * 3,
-        out_shape=[split_shape] * 3 + [act_shape] * 3,
+        out_specs=[split] + [per_expert((tokens, hidden))] * 3,
+        out_shape=[split_shape] + [act_shape] * 3,
         compiler_params=pltpu.CompilerParams(
             dimension_semantics=("arbitrary",), vmem_limit_bytes=64 * 1024 * 1024
         ),
         cost_estimate=pl.CostEstimate(
-            flops=experts * tokens * width * hidden * 2 * 6,
+            flops=experts * tokens * width * hidden * 2 * 4,
             transcendentals=experts * tokens * hidden,
-            bytes_accessed=experts * width * hidden * 12 + tokens * width * 8 + experts * tokens * hidden * 6,
-        ),
-    )(n2, n2t, dy, dyt, gcol, grow, wg, wu, wd)
+            bytes_accessed=experts * width * hidden * 8 + tokens * width * 6 + experts * tokens * hidden * 6,
+        ),
+    )(n2, n2t, dy, gcol, wg, wu, wd)
+
+
+def expert_grad_rest_kernel(n2t, dyt, grow, hid, dua, groups):
+    width, tokens = n2t.shape
+    experts, _, hidden = hid.shape
+    bf16 = jnp.bfloat16
+    whole = lambda shape: pl.BlockSpec(shape, lambda e: (0,) * len(shape))
+    per_expert = lambda shape: pl.BlockSpec((1,) + shape, lambda e: (e,) + (0,) * len(shape))
+    split_rows = width // (groups * 2)
+    split = pl.BlockSpec((2, 1, groups, split_rows, hidden), lambda e: (0, e, 0, 0, 0))
+    split_shape = jax.ShapeDtypeStruct((2, experts, groups, split_rows, hidden), bf16)
+    return pl.pallas_call(
+        _grad_rest_body,
+        grid=(experts,),
+        in_specs=[
+            whole((width, tokens)),
+            whole((width, tokens)),
+            per_expert((1, tokens)),
+            per_expert((tokens, hidden)),
+            per_expert((tokens, hidden)),
+        ],
+        out_specs=[split, split],
+        out_shape=[split_shape, split_shape],
+        compiler_params=pltpu.CompilerParams(
+            dimension_semantics=("arbitrary",), vmem_limit_bytes=64 * 1024 * 1024
+        ),
+        cost_estimate=pl.CostEstimate(
+            flops=experts * tokens * width * hidden * 2 * 2,
+            transcendentals=0,
+            bytes_accessed=experts * width * hidden * 4 + tokens * width * 4 + experts * tokens * hidden * 4,
+        ),
+    )(n2t, dyt, grow, hid, dua)
 
 
 def expert_rows_kernel(hid, dga, dua, dy, gcol, wg, wu, wd):
@@ -783,13 +812,12 @@
     gates_by_expert = jnp.transpose(gates_dense)
     cot_bf = output_grad
     gcol = gates_dense
-    grad_gate, grad_up, grad_down, hid_all, dga_all, dua_all = expert_grad_kernel(
+    normed_two_t = jnp.transpose(normed_two)
+    grad_gate, hid_all, dga_all, dua_all = expert_grad_kernel(
         normed_two,
-        jnp.transpose(normed_two),
+        normed_two_t,
         cot_bf,
-        jnp.transpose(cot_bf),
         gcol,
-        gates_by_expert[:, None, :],
         gate_weight,
         up_weight,
         down_weight,
@@ -798,6 +826,14 @@
     gate_half = core_reduce(grad_gate, 8)
     gate_half, hid_all, dga_all, dua_all = lax.optimization_barrier(
         (gate_half, hid_all, dga_all, dua_all)
+    )
+    grad_up, grad_down = expert_grad_rest_kernel(
+        normed_two_t,
+        jnp.transpose(cot_bf),
+        gates_by_expert[:, None, :],
+        hid_all,
+        dua_all,
+        dpx_count,
     )
     moe_acc, gate_parts, moe_grad_rows = expert_rows_kernel(
         hid_all, dga_all, dua_all, cot_bf, gcol, gate_weight, up_weight, down_weight

time: 827 us -> 845 us (1.022)
  waiting for transfers between devices: 134 us -> 80.3 us
  Pallas kernels: 435 us -> 478 us
  local copies, waits for them, and re-layouts: 70.4 us -> 99.2 us
    reduce_scatter x3, waiting for transfers between devices: 51 us -> 9 us  [per_device(): lax.psum_scatter(g.reshape(g.shape[0], -1, g.shape[3]), ('dpx', 'ctx'), s...]
    pallas_call x0 -> x1, Pallas kernels: none -> 32.6 us  [expert_grad_rest_kernel(): pl.pallas_call(_grad_rest_body, grid=(experts,), in_specs=[whole((width,...]
    unnamed x160 -> x158, local copies, waits for them, and re-layouts: 22 us -> 35.6 us
    pallas_call x1, Pallas kernels: 55.5 us -> 68 us  [chain_sum_down(): pl.pallas_call(functools.partial(_chain_down_body, axis, n), out_shape=ja...]
    dot_general x2 -> x0, local copies, waits for them, and re-layouts: 9.83 us -> none  [contract_rows(): lax.dot_general(left, right, (((0,), (0,)), ((), ())), preferred_element_...]
  transfers between devices with their start and end apart: 5 -> 5, of which waited for: 3 -> 2; matrix products, arithmetic and copies ran while one was open for 25% -> 28% of each run, Pallas kernels for 41% -> 45%
where the time goes in v18:
time: 845 us; the launch traced here: 837 us
  Pallas kernels  478 us (57%)
  matrix products  122 us (14%)
  local copies, waits for them, and re-layouts  99.2 us (12%)
  waiting for transfers between devices  80.3 us (10%)
  other arithmetic  42.4 us (5%)
  between operations  15 us (2%)
    pallas_call x9, Pallas kernels, exchange(): pl.pallas_call(functools.partial(_exchange_body, axis, n, per_peer, downw...  193 us
    unnamed x6, waiting for transfers between devices  71.2 us
    pallas_call x1, Pallas kernels, expert_grad_kernel(): pl.pallas_call(_grad_body, grid=(experts,), in_specs=[whole((tokens, widt...  71 us
    pallas_call x1, Pallas kernels, chain_sum_down(): pl.pallas_call(functools.partial(_chain_down_body, axis, n), out_shape=ja...  68 us
    pallas_call x1, Pallas kernels, expert_rows_kernel(): pl.pallas_call(_rows_body, grid=(experts,), in_specs=[per_expert((tokens,...  46.1 us
    pallas_call x4, Pallas kernels, core_reduce(): pl.pallas_call(_pair_add_body, grid_spec=grid_spec, out_shape=jax.ShapeDt...  40 us
    unnamed x158, local copies, waits for them, and re-layouts  35.6 us
    pallas_call x1, Pallas kernels, expert_grad_rest_kernel(): pl.pallas_call(_grad_rest_body, grid=(experts,), in_specs=[whole((width,...  32.6 us
  transfers between devices with their start and end apart: 5, of which 2 were waited for; matrix products, arithmetic and copies ran while one was open for 28% of the time, Pallas kernels for 45%

profile of v18, /device:TPU:0, one launch (start us, length us, event | category | flops | bytes accessed | tf_op | source)
XLA Modules:
  0.0 837.1 jit_solution(3936564976225726692)
XLA Ops:
  26.1 27.0 %shard_map.229 = (bf16[4,512,512]{2,1,0:T(8,128)(2,1)}, f32[512,768]{1,0:T(8,128)S(1)}, f32[512,12]{1,0:T(8,128)S(1)}) custom-call(bf16[512,768]{1,0:T(8,128)(2,1)S(1)} %copy-done.2, bf16[512,512]{1,0:T(8,128)(2,1)S(1)} %pad_maximum_fusion.3.own_ref, s32[1536,1]{1,0:T(8,128)S(1)} %bitcast.163, s32[1536,1]{1,0:T(8,128)S(1)} %bitcast.164, s32[1,2048]{1,0:T(1,128)S(1)} %bitcast.165), custom_call_target="tpu_custom_call" | custom-call | flops 3221225472 | bytes 6553600 | tf_op jit(solution)/shard_map/pallas_call | solution.py:688
  54.9 36.8 %shard_map.230 = bf16[2,512,768]{2,1,0:T(8,128)(2,1)} custom-call(bf16[512,768]{1,0:T(8,128)(2,1)} %convert_element_type.161.src_ref), custom_call_target="tpu_custom_call" | custom-call | bytes 1572864 | tf_op jit(solution)/shard_map/pallas_call | solution.py:277
  106.9 71.0 %shard_map.231 = (bf16[2,24,2,384,256]{4,3,2,1,0:T(8,128)(2,1)}, bf16[24,512,256]{2,1,0:T(8,128)(2,1)}, bf16[24,512,256]{2,1,0:T(8,128)(2,1)}, bf16[24,512,256]{2,1,0:T(8,128)(2,1)}) custom-call(bf16[512,1536]{1,0:T(8,128)(2,1)} %copy.261.n2_ref, bf16[1536,512]{1,0:T(8,128)(2,1)} %fusion.87.n2t_ref, bf16[512,1536]{1,0:T(8,128)(2,1)} %dy_ref.3, ...), custom_call_target="tpu_custom_call" | custom-call | flops 38654705664 | bytes 99090432 | tf_op jit(solution)/shard_map/pallas_call | solution.py:135
  177.9 15.0 %shard_map.232.other_ref = bf16[2,24,2,384,256]{4,3,2,1,0:T(8,128)(2,1)} custom-call(bf16[2,24,2,384,256]{4,3,2,1,0:T(8,128)(2,1)} %get-tuple-element.33.src_ref.own_ref), custom_call_target="tpu_custom_call" | custom-call | bytes 18874368 | tf_op jit(solution)/shard_map/pallas_call | solution.py:277
  192.9 11.5 %shard_map.233 = bf16[24,2,384,256]{3,2,1,0:T(8,128)(2,1)} custom-call(s32[1]{0:T(128)} %bitcast.8.me_ref, bf16[2,24,2,384,256]{4,3,2,1,0:T(8,128)(2,1)} %get-tuple-element.33.src_ref.own_ref, bf16[2,24,2,384,256]{4,3,2,1,0:T(8,128)(2,1)} %shard_map.232.other_ref), custom_call_target="tpu_custom_call" | custom-call | flops 4718592 | bytes 28311552 | tf_op jit(solution)/shard_map/pallas_call | solution.py:321
  208.0 32.6 %shard_map.242 = (bf16[2,24,2,384,256]{4,3,2,1,0:T(8,128)(2,1)}, bf16[2,24,2,384,256]{4,3,2,1,0:T(8,128)(2,1)}) custom-call(bf16[1536,512]{1,0:T(8,128)(2,1)} %fusion.87.n2t_ref, bf16[1536,512]{1,0:T(8,128)(2,1)} %bitcast.180, f32[24,1,512]{2,1,0:T(1,128)} %broadcast_in_dim.122.grow_ref, bf16[24,512,256]{2,1,0:T(8,128)(2,1)} %get-tuple-element.37.hid_ref, ...), custom_call_target="tpu_custom_call" | custom-call | flops 19327352832 | bytes 53477376 | tf_op jit(solution)/shard_map/pallas_call | solution.py:169
  240.6 15.0 %shard_map.243.other_ref = bf16[2,24,2,384,256]{4,3,2,1,0:T(8,128)(2,1)} custom-call(bf16[2,24,2,384,256]{4,3,2,1,0:T(8,128)(2,1)} %get-tuple-element.46.src_ref.own_ref), custom_call_target="tpu_custom_call" | custom-call | bytes 18874368 | tf_op jit(solution)/shard_map/pallas_call | solution.py:277
  255.6 11.7 %shard_map.244 = bf16[24,2,384,256]{3,2,1,0:T(8,128)(2,1)} custom-call(s32[1]{0:T(128)} %bitcast.8.me_ref, bf16[2,24,2,384,256]{4,3,2,1,0:T(8,128)(2,1)} %get-tuple-element.46.src_ref.own_ref, bf16[2,24,2,384,256]{4,3,2,1,0:T(8,128)(2,1)} %shard_map.243.other_ref), custom_call_target="tpu_custom_call" | custom-call | flops 4718592 | bytes 28311552 | tf_op jit(solution)/shard_map/pallas_call | solution.py:321
  281.4 20.0 %fusion.39 = f32[4,2048,512,3]{2,1,3,0:T(8,128)} fusion(bf16[2048,4,64,1]{0,2,1,3:T(8,128)(2,1)S(1)} %reshape.367, bf16[512,4,3,32]{0,3,2,1:T(8,128)(2,1)S(1)} %bitcast.174, bf16[512,4,3,32]{0,3,2,1:T(8,128)(2,1)S(1)} %bitcast.172), kind=kOutput, calls=%fused_computation.63 | convolution fusion | flops 1612185600 | bytes 52166656 | tf_op jit(solution)/shard_map/tkgd,nkd->kgtn/dot_general | solution.py:876
  301.4 15.0 %shard_map.245.other_ref = bf16[2,24,2,384,256]{4,3,2,1,0:T(8,128)(2,1)} custom-call(bf16[2,24,2,384,256]{4,3,2,1,0:T(8,128)(2,1)} %get-tuple-element.47.src_ref.own_ref), custom_call_target="tpu_custom_call" | custom-call | bytes 18874368 | tf_op jit(solution)/shard_map/pallas_call | solution.py:277
  316.4 11.3 %shard_map.246 = bf16[24,2,384,256]{3,2,1,0:T(8,128)(2,1)} custom-call(s32[1]{0:T(128)} %bitcast.8.me_ref, bf16[2,24,2,384,256]{4,3,2,1,0:T(8,128)(2,1)} %get-tuple-element.47.src_ref.own_ref, bf16[2,24,2,384,256]{4,3,2,1,0:T(8,128)(2,1)} %shard_map.245.other_ref), custom_call_target="tpu_custom_call" | custom-call | flops 4718592 | bytes 28311552 | tf_op jit(solution)/shard_map/pallas_call | solution.py:321
  327.8 46.1 %shard_map.234 = (f32[512,1536]{1,0:T(8,128)}, f32[24,512,1]{2,1,0:T(8,128)}, f32[512,1536]{1,0:T(8,128)}) custom-call(bf16[24,512,256]{2,1,0:T(8,128)(2,1)} %get-tuple-element.37.hid_ref, bf16[24,512,256]{2,1,0:T(8,128)(2,1)} %get-tuple-element.38.dga_ref, bf16[24,512,256]{2,1,0:T(8,128)(2,1)} %get-tuple-element.39.dua_ref, bf16[512,1536]{1,0:T(8,128)(2,1)} %dy_ref.3, ...), custom_call_target="tpu_custom_call" | custom-call | flops 28991029248 | bytes 83361792 | tf_op jit(solution)/shard_map/pallas_call | solution.py:198
  396.5 35.8 %shard_map.236 = bf16[2,512,1536]{2,1,0:T(8,128)(2,1)} custom-call(bf16[512,1536]{1,0:T(8,128)(2,1)} %copy.269.src_ref), custom_call_target="tpu_custom_call" | custom-call | bytes 3145728 | tf_op jit(solution)/shard_map/pallas_call | solution.py:277
  446.2 34.9 %shard_map.235 = bf16[2,512,1536]{2,1,0:T(8,128)(2,1)} custom-call(bf16[512,1536]{1,0:T(8,128)(2,1)} %copy.265.src_ref), custom_call_target="tpu_custom_call" | custom-call | bytes 3145728 | tf_op jit(solution)/shard_map/pallas_call | solution.py:277
  500.1 19.9 %fusion.32 = bf16[2048,4,64]{0,2,1:T(8,128)(2,1)} fusion(bf16[4,3,512,64]{2,3,1,0:T(8,128)(2,1)S(1)} %bitcast.183, f32[4,2048,512,3]{2,1,3,0:T(8,128)} %fusion.39, f32[4,3,512]{2,1,0:T(4,128)S(1)} %bitcast.199, pred[512,2048]{0,1:T(8,128)(4,1)S(1)} %copy-done.39), kind=kOutput, calls=%fused_computation.48 | convolution fusion | flops 1661468672 | bytes 53239808 | tf_op jit(solution)/shard_map/kgtn,kgtd->nkd/dot_general | solution.py:890
  523.9 28.9 %multiply_convert_fusion = bf16[4,3,512,2048]{2,3,1,0:T(8,128)(2,1)} fusion(f32[4,2048,512,3]{2,1,3,0:T(8,128)} %fusion.39, f32[4,3,512]{2,1,0:T(4,128)S(1)} %multiply_reduce_fusion.3, f32[4,3,512]{2,1,0:T(4,128)S(1)} %bitcast.200, pred[512,2048]{0,1:T(8,128)(4,1)} %fusion.6, bf16[4,3,512,64]{2,3,1,0:T(8,128)(2,1)S(1)} %bitcast.185, ...), kind=kOutput, calls=%fused_computation.3 | convolution fusion | flops 1686110208 | bytes 78430208 | tf_op jit(solution)/shard_map/kgtd,nkd->kgtn/dot_general | solution.py:880
  552.9 12.5 %fusion.31 = bf16[2048,4,64]{0,2,1:T(8,128)(2,1)S(1)} fusion(bf16[4,3,512,2048]{2,3,1,0:T(8,128)(2,1)} %multiply_convert_fusion, bf16[512,4,3,32]{0,3,2,1:T(8,128)(2,1)S(1)} %bitcast.175, bf16[512,4,3,32]{0,3,2,1:T(8,128)(2,1)S(1)} %bitcast.173), kind=kOutput, calls=%fused_computation.47 | convolution fusion | flops 1613234176 | bytes 27000832 | tf_op jit(solution)/shard_map/kgtn,tkgd->nkd/dot_general | solution.py:887
  568.3 68.0 %shard_map.238 = f32[512,512]{1,0:T(8,128)S(1)} custom-call(bf16[4,512,512]{2,1,0:T(8,128)(2,1)S(1)} %pad_maximum_fusion.x_ref), custom_call_target="tpu_custom_call" | custom-call | flops 786432 | bytes 6291456 | tf_op jit(solution)/shard_map/pallas_call | solution.py:484
  640.2 10.8 %convolution_multiply_fusion = f32[4,3,512,64]{2,3,1,0:T(8,128)S(1)} fusion(bf16[4,3,512,2048]{2,3,1,0:T(8,128)(2,1)} %multiply_convert_fusion, bf16[2048,4,64,1]{0,2,1,3:T(8,128)(2,1)S(1)} %copy-done.18), kind=kOutput, calls=%fused_computation.55 | convolution fusion | flops 1611005952 | bytes 27787264 | tf_op jit(solution)/shard_map/kgtn,nkd->kgtd/dot_general | solution.py:884
  657.6 28.3 %shard_map.239 = bf16[2,512,1536]{2,1,0:T(8,128)(2,1)} custom-call(bf16[512,1536]{1,0:T(8,128)(2,1)} %copy.289.src_ref), custom_call_target="tpu_custom_call" | custom-call | bytes 3145728 | tf_op jit(solution)/shard_map/pallas_call | solution.py:277
  701.9 11.1 %concatenate.65 = bf16[2,2,384,2176]{3,2,0,1:T(8,128)(2,1)} concatenate(bf16[2,2,384,768]{3,2,0,1:T(8,128)(2,1)} %convolution_convert_fusion.3, bf16[2,2,384,768]{3,2,0,1:T(8,128)(2,1)} %copy.294, bf16[2,2,384,256]{3,2,0,1:T(8,128)(2,1)} %convolution_convert_fusion.4, bf16[2,2,384,256]{3,2,0,1:T(8,128)(2,1)} %copy.295, bf16[2,2,384,24]{3,2,0,1:T(8,128)(2,1)S(1)} %copy-done.38, ...), dimensions={3} | concatenate | bytes 13369344 | tf_op jit(solution)/shard_map/concatenate | solution.py:944
  713.0 6.3 shard_map.240.other_ref
  730.7 9.0 %reduce-scatter.11.cloned.1.call-done = bf16[24,96,256]{2,1,0:T(8,128)(2,1)} async-done(((bf16[24,768,256]{2,1,0:T(8,128)(2,1)}), bf16[24,96,256]{2,1,0:T(8,128)(2,1)}) %reduce-scatter.11.cloned.1.call-update) | async-done | bytes 1179664 | tf_op jit(solution)/shard_map/reduce_scatter | solution.py:847
  754.1 70.5 %reduce-scatter.13.cloned.1.call-done = bf16[96,2176]{1,0:T(8,128)(2,1)} async-done(((bf16[768,2176]{1,0:T(8,128)(2,1)}), bf16[96,2176]{1,0:T(8,128)(2,1)}) %reduce-scatter.13.cloned.1.call-update) | async-done | bytes 417808
  (280 shorter events, 172.9 us)
Async XLA Ops:
  7.2 87.3 %all-gather.2.cloned.1.call-start = ((), (), s32[]{:S(2)}) async-start(), calls=%async_computation.4 | async-start | bytes 7077888 | tf_op jit(solution)/shard_map/all_gather | solution.py:750
  7.9 716.9 %reduce-scatter.7.cloned.1.call-start = ((), (), s32[]{:S(2)}) async-start(), calls=%async_computation.5 | async-start | bytes 10616832 | tf_op jit(solution)/shard_map/reduce_scatter | solution.py:847
  13.7 5.5 copy-start.35
  15.5 9.9 %copy-start.33 = (bf16[512,256]{1,0:T(8,128)(2,1)}, bf16[512,256]{1,0:T(8,128)(2,1)S(1)}, u32[]{:S(2)}) copy-start(bf16[512,256]{1,0:T(8,128)(2,1)S(1)} %copy.251) | copy-start | bytes 786436
  53.8 38.9 %copy-start = (f32[512,768]{1,0:T(8,128)}, f32[512,768]{1,0:T(8,128)S(1)}, u32[]{:S(2)}) copy-start(f32[512,768]{1,0:T(8,128)S(1)} %get-tuple-element.32) | copy-start | bytes 4718596
  204.4 523.4 %reduce-scatter.9.cloned.1.call-start = ((), (), s32[]{:S(2)}) async-start(), calls=%async_computation.6 | async-start | bytes 10616832 | tf_op jit(solution)/shard_map/reduce_scatter | solution.py:847
  267.4 472.3 %reduce-scatter.11.cloned.1.call-start = ((), (), s32[]{:S(2)}) async-start(), calls=%async_computation.7 | async-start | bytes 10616832 | tf_op jit(solution)/shard_map/reduce_scatter | solution.py:847
  276.1 5.2 copy-start.23
  279.6 21.8 %copy-start.17 = (bf16[2048,4,64,1]{0,2,1,3:T(8,128)(2,1)}, bf16[2048,4,64,1]{0,2,1,3:T(8,128)(2,1)S(1)}, u32[]{:S(2)}) copy-start(bf16[2048,4,64,1]{0,2,1,3:T(8,128)(2,1)S(1)} %reshape.367) | copy-start | bytes 3145732
  327.8 496.8 %reduce-scatter.13.cloned.1.call-start = ((), (), s32[]{:S(2)}) async-start(), calls=%async_computation.8 | async-start | bytes 3760128
  377.1 11.3 %copy-start.31 = (f32[512,8]{1,0:T(8,128)S(1)}, f32[512,8]{1,0:T(8,128)}, u32[]{:S(2)}) copy-start(f32[512,8]{1,0:T(8,128)} %copy-done.30) | copy-start | bytes 49156
  377.1 11.3 %copy-start.61 = (f32[512]{0:T(512)S(1)}, f32[512]{0:T(512)}, u32[]{:S(2)}) copy-start(f32[512]{0:T(512)} %copy-done.60) | copy-start | bytes 6148
  377.1 13.8 %copy-start.14 = (bf16[512,1536]{0,1:T(8,128)(2,1)S(1)}, bf16[512,1536]{0,1:T(8,128)(2,1)}, u32[]{:S(2)}) copy-start(bf16[512,1536]{0,1:T(8,128)(2,1)} %copy-done.13) | copy-start | bytes 4718596
  432.3 5.4 copy-start.8
  432.3 5.4 copy-start.51
  432.3 5.4 copy-start.55
  432.3 5.4 copy-start.59
  486.4 6.8 copy-start.16
  523.9 29.0 %copy-start.21 = (bf16[512,12,32]{0,2,1:T(8,128)(2,1)S(1)}, bf16[512,12,32]{0,2,1:T(8,128)(2,1)}, u32[]{:S(2)}) copy-start(bf16[512,12,32]{0,2,1:T(8,128)(2,1)} %copy-done.19) | copy-start | bytes 1179652
  523.9 28.9 %copy-start.24 = (bf16[512,12,32]{0,2,1:T(8,128)(2,1)S(1)}, bf16[512,12,32]{0,2,1:T(8,128)(2,1)}, u32[]{:S(2)}) copy-start(bf16[512,12,32]{0,2,1:T(8,128)(2,1)} %copy-done.22) | copy-start | bytes 1179652
  568.3 70.1 %copy-start.28 = (bf16[512,1536]{0,1:T(8,128)(2,1)S(1)}, bf16[512,1536]{0,1:T(8,128)(2,1)}, u32[]{:S(2)}) copy-start(bf16[512,1536]{0,1:T(8,128)(2,1)} %copy-done.26) | copy-start | bytes 4718596
  685.9 5.4 copy-start.11
  685.9 5.4 copy-start.57
  686.0 5.4 copy-start.64
  (51 other events, 124.7 us)
Sparse Core Ops, SparseCore 0:
  9.6 82.2 all-gather.1
  204.5 170.5 reduce-scatter.6
  378.7 162.5 reduce-scatter.8
  544.6 195.0 reduce-scatter.10
  743.2 81.3 reduce-scatter.12

commit v19 on v17

--- a/solution.py
+++ b/solution.py
@@ -79,7 +79,7 @@
 
 
 def _grad_body(
-    n2_ref, n2t_ref, dy_ref, dyt_ref, gcol_ref, grow_ref, wg_ref, wu_ref, wd_ref,
+    n2_ref, n2t_ref, dy_ref, dyt_ref, gcol_ref, wg_ref, wu_ref, wd_ref,
     gg_ref, gu_ref, gd_ref, hid_ref, dga_ref, dua_ref,
 ):
     f32 = jnp.float32
@@ -92,10 +92,10 @@
     silu = gate_act * sig
     hidden = (silu * up_act).astype(bf16)
     hid_ref[0] = hidden
-    deo = (_gate_column(gcol_ref) * dy_ref[...].astype(f32)).astype(bf16)
-    grad_hidden = jnp.dot(deo, wd, preferred_element_type=f32)
-    deo_t = (grow_ref[0] * dyt_ref[...].astype(f32)).astype(bf16)
-    _store_split(gd_ref, jnp.dot(deo_t, hidden, preferred_element_type=f32))
+    gate = _gate_column(gcol_ref)
+    grad_hidden = gate * jnp.dot(dy_ref[...], wd, preferred_element_type=f32)
+    gated_hidden = (gate * hidden.astype(f32)).astype(bf16)
+    _store_split(gd_ref, jnp.dot(dyt_ref[...], gated_hidden, preferred_element_type=f32))
     grad_gate_act = (grad_hidden * up_act * sig * (1.0 + gate_act * (1.0 - sig))).astype(bf16)
     grad_up_act = (grad_hidden * silu).astype(bf16)
     dga_ref[0] = grad_gate_act
@@ -122,7 +122,7 @@
     ) + lax.dot_general(dua_ref[0], wu_ref[0], nt, preferred_element_type=f32)
 
 
-def expert_grad_kernel(n2, n2t, dy, dyt, gcol, grow, wg, wu, wd, groups):
+def expert_grad_kernel(n2, n2t, dy, dyt, gcol, wg, wu, wd, groups):
     tokens, width = n2.shape
     experts, _, hidden = wg.shape
     bf16 = jnp.bfloat16
@@ -141,7 +141,6 @@
             whole((tokens, width)),
             whole((width, tokens)),
             whole((tokens, experts)),
-            per_expert((1, tokens)),
             per_expert((width, hidden)),
             per_expert((width, hidden)),
             per_expert((width, hidden)),
@@ -157,7 +156,7 @@
             transcendentals=experts * tokens * hidden,
             bytes_accessed=experts * width * hidden * 12 + tokens * width * 8 + experts * tokens * hidden * 6,
         ),
-    )(n2, n2t, dy, dyt, gcol, grow, wg, wu, wd)
+    )(n2, n2t, dy, dyt, gcol, wg, wu, wd)
 
 
 def expert_rows_kernel(hid, dga, dua, dy, gcol, wg, wu, wd):
@@ -789,7 +788,6 @@
         cot_bf,
         jnp.transpose(cot_bf),
         gcol,
-        gates_by_expert[:, None, :],
         gate_weight,
         up_weight,
         down_weight,
@@ -810,7 +808,7 @@
     grad_gate_out, grad_up_out, grad_down_out = [
         lax.psum_scatter(
             g.reshape(g.shape[0], -1, g.shape[3]), ("dpx", "ctx"), scatter_dimension=1, tiled=True
-        ).astype(jnp.float32)
+        )
         for g in (gate_half, core_reduce(grad_up, 9), core_reduce(grad_down, 10))
     ]
     gate_pair = jnp.sum(
@@ -915,6 +913,11 @@
     dense_half = core_reduce(dense_all, 11)
     dense_half, grad_gate_out, grad_up_out, grad_down_out = lax.optimization_barrier(
         (dense_half, grad_gate_out, grad_up_out, grad_down_out)
+    )
+    grad_gate_out, grad_up_out, grad_down_out = (
+        grad_gate_out.astype(f32),
+        grad_up_out.astype(f32),
+        grad_down_out.astype(f32),
     )
     dense_here = lax.psum_scatter(
         dense_half.reshape(-1, dense_half.shape[-1]), ("dpx", "ctx"), scatter_dimension=0, tiled=True

time: 827 us -> 826 us (level)
    unnamed x160 -> x166, local copies, waits for them, and re-layouts: 22 us -> 23.6 us
where the time goes in v19:
time: 826 us; the launch traced here: 819 us
  Pallas kernels  434 us (53%)
  waiting for transfers between devices  136 us (16%)
  matrix products  123 us (15%)
  local copies, waits for them, and re-layouts  71.3 us (9%)
  other arithmetic  38 us (5%)
  between operations  15.2 us (2%)
    pallas_call x9, Pallas kernels, exchange(): pl.pallas_call(functools.partial(_exchange_body, axis, n, per_peer, downw...  197 us
    unnamed x6, waiting for transfers between devices  74.4 us
    pallas_call x1, Pallas kernels, expert_grad_kernel(): pl.pallas_call(_grad_body, grid=(experts,), in_specs=[whole((tokens, widt...  73.6 us
    reduce_scatter x3, waiting for transfers between devices, per_device(): lax.psum_scatter(g.reshape(g.shape[0], -1, g.shape[3]), ('dpx', 'ctx'), s...  56.9 us
    pallas_call x1, Pallas kernels, chain_sum_down(): pl.pallas_call(functools.partial(_chain_down_body, axis, n), out_shape=ja...  54.9 us
    pallas_call x1, Pallas kernels, expert_rows_kernel(): pl.pallas_call(_rows_body, grid=(experts,), in_specs=[per_expert((tokens,...  46.8 us
    pallas_call x4, Pallas kernels, core_reduce(): pl.pallas_call(_pair_add_body, grid_spec=grid_spec, out_shape=jax.ShapeDt...  39.6 us
    dot_general x1, matrix products, per_device(): jnp.einsum('kgtd,nkd->kgtn', grad_attn_grouped, value_piece, preferred_el...  28.3 us
  transfers between devices with their start and end apart: 5, of which 3 were waited for; matrix products, arithmetic and copies ran while one was open for 25% of the time, Pallas kernels for 41%

profile of v19, /device:TPU:0, one launch (start us, length us, event | category | flops | bytes accessed | tf_op | source)
XLA Modules:
  0.0 819.4 jit_solution(10966171492803634951)
XLA Ops:
  20.8 21.8 %shard_map.229 = (bf16[4,512,512]{2,1,0:T(8,128)(2,1)}, f32[512,768]{1,0:T(8,128)S(1)}, f32[512,12]{1,0:T(8,128)S(1)}) custom-call(bf16[512,768]{1,0:T(8,128)(2,1)S(1)} %copy.185.q_ref, bf16[512,512]{1,0:T(8,128)(2,1)S(1)} %pad_maximum_fusion.3.own_ref, s32[1536,1]{1,0:T(8,128)S(1)} %bitcast.161, s32[1536,1]{1,0:T(8,128)S(1)} %bitcast.162, ...), custom_call_target="tpu_custom_call" | custom-call | flops 3221225472 | bytes 6553600 | tf_op jit(solution)/shard_map/pallas_call | solution.py:658
  44.3 37.1 %shard_map.230 = bf16[2,512,768]{2,1,0:T(8,128)(2,1)} custom-call(bf16[512,768]{1,0:T(8,128)(2,1)} %convert_element_type.161.src_ref), custom_call_target="tpu_custom_call" | custom-call | bytes 1572864 | tf_op jit(solution)/shard_map/pallas_call | solution.py:247
  102.3 73.6 %shard_map.231 = (bf16[2,24,2,384,256]{4,3,2,1,0:T(8,128)(2,1)}, bf16[2,24,2,384,256]{4,3,2,1,0:T(8,128)(2,1)}, bf16[2,24,2,384,256]{4,3,2,1,0:T(8,128)(2,1)}, b...) custom-call(bf16[512,1536]{1,0:T(8,128)(2,1)} %copy-done.10, ...), custom_call_target="tpu_custom_call" | custom-call | flops 57982058496 | bytes 138412032 | tf_op jit(solution)/shard_map/pallas_call | solution.py:135
  175.9 15.0 %shard_map.244.other_ref = bf16[2,24,2,384,256]{4,3,2,1,0:T(8,128)(2,1)} custom-call(bf16[2,24,2,384,256]{4,3,2,1,0:T(8,128)(2,1)} %get-tuple-element.47.src_ref.own_ref), custom_call_target="tpu_custom_call" | custom-call | bytes 18874368 | tf_op jit(solution)/shard_map/pallas_call | solution.py:247
  190.9 11.5 %shard_map.245 = bf16[24,2,384,256]{3,2,1,0:T(8,128)(2,1)} custom-call(s32[1]{0:T(128)} %bitcast.8.me_ref, bf16[2,24,2,384,256]{4,3,2,1,0:T(8,128)(2,1)} %get-tuple-element.47.src_ref.own_ref, bf16[2,24,2,384,256]{4,3,2,1,0:T(8,128)(2,1)} %shard_map.244.other_ref), custom_call_target="tpu_custom_call" | custom-call | flops 4718592 | bytes 28311552 | tf_op jit(solution)/shard_map/pallas_call | solution.py:291
  202.5 15.1 %shard_map.242.other_ref = bf16[2,24,2,384,256]{4,3,2,1,0:T(8,128)(2,1)} custom-call(bf16[2,24,2,384,256]{4,3,2,1,0:T(8,128)(2,1)} %get-tuple-element.46.src_ref.own_ref), custom_call_target="tpu_custom_call" | custom-call | bytes 18874368 | tf_op jit(solution)/shard_map/pallas_call | solution.py:247
  217.6 11.3 %shard_map.243 = bf16[24,2,384,256]{3,2,1,0:T(8,128)(2,1)} custom-call(s32[1]{0:T(128)} %bitcast.8.me_ref, bf16[2,24,2,384,256]{4,3,2,1,0:T(8,128)(2,1)} %get-tuple-element.46.src_ref.own_ref, bf16[2,24,2,384,256]{4,3,2,1,0:T(8,128)(2,1)} %shard_map.242.other_ref), custom_call_target="tpu_custom_call" | custom-call | flops 4718592 | bytes 28311552 | tf_op jit(solution)/shard_map/pallas_call | solution.py:291
  243.2 20.5 %fusion.36 = f32[4,2048,512,3]{2,1,3,0:T(8,128)} fusion(bf16[2048,4,64,1]{0,2,1,3:T(8,128)(2,1)S(1)} %reshape.367, bf16[512,4,3,32]{0,3,2,1:T(8,128)(2,1)S(1)} %bitcast.172, bf16[512,4,3,32]{0,3,2,1:T(8,128)(2,1)S(1)} %bitcast.170), kind=kOutput, calls=%fused_computation.61 | convolution fusion | flops 1612185600 | bytes 52166656 | tf_op jit(solution)/shard_map/tkgd,nkd->kgtn/dot_general | solution.py:838
  263.7 15.0 %shard_map.232.other_ref = bf16[2,24,2,384,256]{4,3,2,1,0:T(8,128)(2,1)} custom-call(bf16[2,24,2,384,256]{4,3,2,1,0:T(8,128)(2,1)} %get-tuple-element.33.src_ref.own_ref), custom_call_target="tpu_custom_call" | custom-call | bytes 18874368 | tf_op jit(solution)/shard_map/pallas_call | solution.py:247
  278.7 11.4 %shard_map.233 = bf16[24,2,384,256]{3,2,1,0:T(8,128)(2,1)} custom-call(s32[1]{0:T(128)} %bitcast.8.me_ref, bf16[2,24,2,384,256]{4,3,2,1,0:T(8,128)(2,1)} %get-tuple-element.33.src_ref.own_ref, bf16[2,24,2,384,256]{4,3,2,1,0:T(8,128)(2,1)} %shard_map.232.other_ref), custom_call_target="tpu_custom_call" | custom-call | flops 4718592 | bytes 28311552 | tf_op jit(solution)/shard_map/pallas_call | solution.py:291
  290.6 46.8 %shard_map.234 = (f32[512,1536]{1,0:T(8,128)}, f32[24,512,1]{2,1,0:T(8,128)}, f32[512,1536]{1,0:T(8,128)}) custom-call(bf16[24,512,256]{2,1,0:T(8,128)(2,1)} %get-tuple-element.37.hid_ref, bf16[24,512,256]{2,1,0:T(8,128)(2,1)} %get-tuple-element.38.dga_ref, bf16[24,512,256]{2,1,0:T(8,128)(2,1)} %get-tuple-element.39.dua_ref, bf16[512,1536]{1,0:T(8,128)(2,1)} %dy_ref.3, ...), custom_call_target="tpu_custom_call" | custom-call | flops 28991029248 | bytes 83361792 | tf_op jit(solution)/shard_map/pallas_call | solution.py:168
  340.7 36.8 %shard_map.236 = bf16[2,512,1536]{2,1,0:T(8,128)(2,1)} custom-call(bf16[512,1536]{1,0:T(8,128)(2,1)} %convert_element_type.169.src_ref), custom_call_target="tpu_custom_call" | custom-call | bytes 3145728 | tf_op jit(solution)/shard_map/pallas_call | solution.py:247
  393.8 35.2 %shard_map.235 = bf16[2,512,1536]{2,1,0:T(8,128)(2,1)} custom-call(bf16[512,1536]{1,0:T(8,128)(2,1)} %convert_element_type.163.src_ref), custom_call_target="tpu_custom_call" | custom-call | bytes 3145728 | tf_op jit(solution)/shard_map/pallas_call | solution.py:247
  442.2 28.3 %multiply_convert_fusion = bf16[4,3,512,2048]{2,3,1,0:T(8,128)(2,1)} fusion(f32[4,2048,512,3]{2,1,3,0:T(8,128)} %fusion.36, f32[4,3,512]{2,1,0:T(4,128)S(1)} %multiply_reduce_fusion.3, f32[4,3,512]{2,1,0:T(4,128)S(1)} %bitcast.194, pred[512,2048]{0,1:T(8,128)(4,1)} %fusion.6, bf16[4,3,512,64]{2,3,1,0:T(8,128)(2,1)S(1)} %bitcast.179, ...), kind=kOutput, calls=%fused_computation.3 | convolution fusion | flops 1686110208 | bytes 78430208 | tf_op jit(solution)/shard_map/kgtd,nkd->kgtn/dot_general | solution.py:842
  470.5 12.9 %fusion.30 = bf16[2048,4,64]{0,2,1:T(8,128)(2,1)S(1)} fusion(bf16[4,3,512,2048]{2,3,1,0:T(8,128)(2,1)} %multiply_convert_fusion, bf16[512,4,3,32]{0,3,2,1:T(8,128)(2,1)S(1)} %bitcast.173, bf16[512,4,3,32]{0,3,2,1:T(8,128)(2,1)S(1)} %bitcast.171), kind=kOutput, calls=%fused_computation.47 | convolution fusion | flops 1613234176 | bytes 27000832 | tf_op jit(solution)/shard_map/kgtn,tkgd->nkd/dot_general | solution.py:849
  485.8 19.6 %fusion.31 = bf16[2048,4,64]{0,2,1:T(8,128)(2,1)S(1)} fusion(bf16[4,3,512,64]{2,3,1,0:T(8,128)(2,1)S(1)} %bitcast.180, f32[4,2048,512,3]{2,1,3,0:T(8,128)} %fusion.36, f32[4,3,512]{2,1,0:T(4,128)S(1)} %bitcast.195, pred[512,2048]{0,1:T(8,128)(4,1)} %fusion.6), kind=kOutput, calls=%fused_computation.48 | convolution fusion | flops 1661468672 | bytes 53239808 | tf_op jit(solution)/shard_map/kgtn,kgtd->nkd/dot_general | solution.py:852
  507.2 54.9 %shard_map.238 = f32[512,512]{1,0:T(8,128)S(1)} custom-call(bf16[4,512,512]{2,1,0:T(8,128)(2,1)S(1)} %pad_maximum_fusion.x_ref), custom_call_target="tpu_custom_call" | custom-call | flops 786432 | bytes 6291456 | tf_op jit(solution)/shard_map/pallas_call | solution.py:454
  562.6 10.9 %convolution_multiply_fusion = f32[4,3,512,64]{2,3,1,0:T(8,128)S(1)} fusion(bf16[4,3,512,2048]{2,3,1,0:T(8,128)(2,1)} %multiply_convert_fusion, bf16[2048,4,64,1]{0,2,1,3:T(8,128)(2,1)S(1)} %copy-done.22), kind=kOutput, calls=%fused_computation.55 | convolution fusion | flops 1611005952 | bytes 27787264 | tf_op jit(solution)/shard_map/kgtn,nkd->kgtd/dot_general | solution.py:846
  579.8 31.7 %shard_map.239 = bf16[2,512,1536]{2,1,0:T(8,128)(2,1)} custom-call(bf16[512,1536]{1,0:T(8,128)(2,1)} %fusion.20.src_ref), custom_call_target="tpu_custom_call" | custom-call | bytes 3145728 | tf_op jit(solution)/shard_map/pallas_call | solution.py:247
  615.2 5.5 fusion.48
  647.8 10.4 %concatenate.65 = bf16[2,2,384,2176]{3,2,0,1:T(8,128)(2,1)} concatenate(bf16[2,2,384,768]{3,2,0,1:T(8,128)(2,1)} %convolution_convert_fusion.3, bf16[2,2,384,768]{3,2,0,1:T(8,128)(2,1)S(1)} %copy.216, bf16[2,2,384,256]{3,2,0,1:T(8,128)(2,1)} %convolution_convert_fusion.4, bf16[2,2,384,256]{3,2,0,1:T(8,128)(2,1)S(1)} %copy.217, bf16[2,2,384,24]{3,2,0,1:T(8,128)(2,1)} %copy.218, ...), dimensions={3} | concatenate | bytes 13369344 | tf_op jit(solution)/shard_map/concatenate | solution.py:906
  658.3 6.3 shard_map.240.other_ref
  670.0 56.9 %reduce-scatter.7.cloned.1.call-done = bf16[24,96,256]{2,1,0:T(8,128)(2,1)} async-done(((bf16[24,768,256]{2,1,0:T(8,128)(2,1)}), bf16[24,96,256]{2,1,0:T(8,128)(2,1)}) %reduce-scatter.7.cloned.1.call-update) | async-done | bytes 1179664 | tf_op jit(solution)/shard_map/reduce_scatter | solution.py:809
  733.2 73.6 %reduce-scatter.13.cloned.1.call-done = bf16[96,2176]{1,0:T(8,128)(2,1)} async-done(((bf16[768,2176]{1,0:T(8,128)(2,1)}), bf16[96,2176]{1,0:T(8,128)(2,1)}) %reduce-scatter.13.cloned.1.call-update) | async-done | bytes 417808
  (281 shorter events, 142.0 us)
Async XLA Ops:
  7.2 84.6 %all-gather.2.cloned.1.call-start = ((), (), s32[]{:S(2)}) async-start(), calls=%async_computation.4 | async-start | bytes 7077888 | tf_op jit(solution)/shard_map/all_gather | solution.py:720
  7.9 662.0 %reduce-scatter.11.cloned.1.call-start = ((), (), s32[]{:S(2)}) async-start(), calls=%async_computation.7 | async-start | bytes 10616832 | tf_op jit(solution)/shard_map/reduce_scatter | solution.py:809
  43.3 39.1 %copy-start = (f32[512,768]{1,0:T(8,128)}, f32[512,768]{1,0:T(8,128)S(1)}, u32[]{:S(2)}) copy-start(f32[512,768]{1,0:T(8,128)S(1)} %get-tuple-element.32) | copy-start | bytes 4718596
  82.4 9.5 %copy-start.13 = (bf16[512,1536]{1,0:T(8,128)(2,1)S(1)}, bf16[512,1536]{1,0:T(8,128)(2,1)}, u32[]{:S(2)}) copy-start(bf16[512,1536]{1,0:T(8,128)(2,1)} %param.14) | copy-start | bytes 4718596
  202.4 467.5 %reduce-scatter.9.cloned.1.call-start = ((), (), s32[]{:S(2)}) async-start(), calls=%async_computation.6 | async-start | bytes 10616832 | tf_op jit(solution)/shard_map/reduce_scatter | solution.py:809
  228.9 497.9 %reduce-scatter.7.cloned.1.call-start = ((), (), s32[]{:S(2)}) async-start(), calls=%async_computation.5 | async-start | bytes 10616832 | tf_op jit(solution)/shard_map/reduce_scatter | solution.py:809
  236.8 26.9 %copy-start.21 = (bf16[2048,4,64,1]{0,2,1,3:T(8,128)(2,1)}, bf16[2048,4,64,1]{0,2,1,3:T(8,128)(2,1)S(1)}, u32[]{:S(2)}) copy-start(bf16[2048,4,64,1]{0,2,1,3:T(8,128)(2,1)S(1)} %reshape.367) | copy-start | bytes 3145732
  290.1 516.7 %reduce-scatter.13.cloned.1.call-start = ((), (), s32[]{:S(2)}) async-start(), calls=%async_computation.8 | async-start | bytes 3760128
  377.5 10.9 %copy-start.33 = (f32[512,8]{1,0:T(8,128)S(1)}, f32[512,8]{1,0:T(8,128)}, u32[]{:S(2)}) copy-start(f32[512,8]{1,0:T(8,128)} %copy-done.32) | copy-start | bytes 49156
  377.5 10.9 %copy-start.66 = (f32[512]{0:T(512)S(1)}, f32[512]{0:T(512)}, u32[]{:S(2)}) copy-start(f32[512]{0:T(512)} %copy-done.65) | copy-start | bytes 6148
  377.5 15.0 %copy-start.17 = (f32[512,1536]{1,0:T(8,128)S(1)}, f32[512,1536]{1,0:T(8,128)}, u32[]{:S(2)}) copy-start(f32[512,1536]{1,0:T(8,128)} %get-tuple-element.40) | copy-start | bytes 9437188
  393.8 35.2 %copy-start.8 = (f32[512,1536]{1,0:T(8,128)S(1)}, f32[512,1536]{1,0:T(8,128)}, u32[]{:S(2)}) copy-start(f32[512,1536]{1,0:T(8,128)} %copy-done.7) | copy-start | bytes 9437188
  393.8 35.3 %copy-start.56 = (bf16[1536,24]{0,1:T(8,128)(2,1)S(1)}, bf16[1536,24]{0,1:T(8,128)(2,1)}, u32[]{:S(2)}) copy-start(bf16[1536,24]{0,1:T(8,128)(2,1)} %param.21) | copy-start | bytes 221188
  393.8 35.3 %copy-start.62 = (f32[1536]{0:T(1024)S(1)}, f32[1536]{0:T(1024)}, u32[]{:S(2)}) copy-start(f32[1536]{0:T(1024)} %param.20) | copy-start | bytes 18436
  393.8 35.3 %copy-start.64 = (f32[512]{0:T(512)S(1)}, f32[512]{0:T(512)}, u32[]{:S(2)}) copy-start(f32[512]{0:T(512)} %copy-done.63) | copy-start | bytes 6148
  442.1 28.3 %copy-start.26 = (bf16[512,12,32]{0,2,1:T(8,128)(2,1)S(1)}, bf16[512,12,32]{0,2,1:T(8,128)(2,1)}, u32[]{:S(2)}) copy-start(bf16[512,12,32]{0,2,1:T(8,128)(2,1)} %copy-done.24) | copy-start | bytes 1179652
  442.2 28.3 %copy-start.29 = (bf16[512,12,32]{0,2,1:T(8,128)(2,1)S(1)}, bf16[512,12,32]{0,2,1:T(8,128)(2,1)}, u32[]{:S(2)}) copy-start(bf16[512,12,32]{0,2,1:T(8,128)(2,1)} %copy-done.27) | copy-start | bytes 1179652
  507.2 55.2 %copy-start.42 = (f32[512,32]{0,1:T(8,128)S(1)}, f32[512,32]{0,1:T(8,128)}, u32[]{:S(2)}) copy-start(f32[512,32]{0,1:T(8,128)} %copy-done.41) | copy-start | bytes 196612
  507.2 55.2 %copy-start.54 = (f32[512,32]{0,1:T(8,128)S(1)}, f32[512,32]{0,1:T(8,128)}, u32[]{:S(2)}) copy-start(f32[512,32]{0,1:T(8,128)} %get-tuple-element.138) | copy-start | bytes 196612
  507.2 55.4 %copy-start.22 = (bf16[2048,4,64,1]{0,2,1,3:T(8,128)(2,1)S(1)}, bf16[2048,4,64,1]{0,2,1,3:T(8,128)(2,1)}, u32[]{:S(2)}) copy-start(bf16[2048,4,64,1]{0,2,1,3:T(8,128)(2,1)} %copy-done.21) | copy-start | bytes 3145732
  579.8 31.7 %copy-start.9 = (bf16[512,1536]{1,0:T(8,128)(2,1)S(1)}, bf16[512,1536]{1,0:T(8,128)(2,1)}, u32[]{:S(2)}) copy-start(bf16[512,1536]{1,0:T(8,128)(2,1)} %fusion.20.src_ref) | copy-start | bytes 4718596
  579.8 31.7 %copy-start.69 = (f32[1536]{0:T(1024)S(1)}, f32[1536]{0:T(1024)}, u32[]{:S(2)}) copy-start(f32[1536]{0:T(1024)} %param.15) | copy-start | bytes 18436
  579.8 31.7 %copy-start.75 = (f32[512]{0:T(512)S(1)}, f32[512]{0:T(512)}, u32[]{:S(2)}) copy-start(f32[512]{0:T(512)} %copy-done.74) | copy-start | bytes 6148
  620.7 10.8 %copy-start.15 = (bf16[512,1536]{1,0:T(8,128)(2,1)S(1)}, bf16[512,1536]{1,0:T(8,128)(2,1)}, u32[]{:S(2)}) copy-start(bf16[512,1536]{1,0:T(8,128)(2,1)} %param.14) | copy-start | bytes 4718596
  (58 other events, 180.2 us)
Sparse Core Ops, SparseCore 0:
  9.6 82.1 all-gather.1
  202.6 170.6 reduce-scatter.10
  376.8 163.5 reduce-scatter.8
  543.9 182.8 reduce-scatter.6
  730.3 76.4 reduce-scatter.12

commit v20 on v19

--- a/solution.py
+++ b/solution.py
@@ -79,7 +79,7 @@
 
 
 def _grad_body(
-    n2_ref, n2t_ref, dy_ref, dyt_ref, gcol_ref, wg_ref, wu_ref, wd_ref,
+    n2_ref, dy_ref, gcol_ref, wg_ref, wu_ref, wd_ref,
     gg_ref, gu_ref, gd_ref, hid_ref, dga_ref, dua_ref,
 ):
     f32 = jnp.float32
@@ -95,14 +95,14 @@
     gate = _gate_column(gcol_ref)
     grad_hidden = gate * jnp.dot(dy_ref[...], wd, preferred_element_type=f32)
     gated_hidden = (gate * hidden.astype(f32)).astype(bf16)
-    _store_split(gd_ref, jnp.dot(dyt_ref[...], gated_hidden, preferred_element_type=f32))
+    tn = (((0,), (0,)), ((), ()))
+    _store_split(gd_ref, lax.dot_general(dy_ref[...], gated_hidden, tn, preferred_element_type=f32))
     grad_gate_act = (grad_hidden * up_act * sig * (1.0 + gate_act * (1.0 - sig))).astype(bf16)
     grad_up_act = (grad_hidden * silu).astype(bf16)
     dga_ref[0] = grad_gate_act
     dua_ref[0] = grad_up_act
-    n2t = n2t_ref[...]
-    _store_split(gg_ref, jnp.dot(n2t, grad_gate_act, preferred_element_type=f32))
-    _store_split(gu_ref, jnp.dot(n2t, grad_up_act, preferred_element_type=f32))
+    _store_split(gg_ref, lax.dot_general(n2, grad_gate_act, tn, preferred_element_type=f32))
+    _store_split(gu_ref, lax.dot_general(n2, grad_up_act, tn, preferred_element_type=f32))
 
 
 def _rows_body(hid_ref, dga_ref, dua_ref, dy_ref, gcol_ref, wg_ref, wu_ref, wd_ref, acc_ref, dgate_ref, dn2_ref):
@@ -122,7 +122,7 @@
     ) + lax.dot_general(dua_ref[0], wu_ref[0], nt, preferred_element_type=f32)
 
 
-def expert_grad_kernel(n2, n2t, dy, dyt, gcol, wg, wu, wd, groups):
+def expert_grad_kernel(n2, dy, gcol, wg, wu, wd, groups):
     tokens, width = n2.shape
     experts, _, hidden = wg.shape
     bf16 = jnp.bfloat16
@@ -137,9 +137,7 @@
         grid=(experts,),
         in_specs=[
             whole((tokens, width)),
-            whole((width, tokens)),
             whole((tokens, width)),
-            whole((width, tokens)),
             whole((tokens, experts)),
             per_expert((width, hidden)),
             per_expert((width, hidden)),
@@ -156,7 +154,7 @@
             transcendentals=experts * tokens * hidden,
             bytes_accessed=experts * width * hidden * 12 + tokens * width * 8 + experts * tokens * hidden * 6,
         ),
-    )(n2, n2t, dy, dyt, gcol, wg, wu, wd)
+    )(n2, dy, gcol, wg, wu, wd)
 
 
 def expert_rows_kernel(hid, dga, dua, dy, gcol, wg, wu, wd):
@@ -717,7 +715,7 @@
     token_positions = ctx_index * token_count + jnp.arange(token_count, dtype=jnp.int32)
     segment_here = lax.dynamic_slice_in_dim(segments, ctx_index * token_count, token_count)
     inputs_f32 = hidden_in.astype(f32)
-    o_full = lax.all_gather(o_weight, "tensor", axis=1, tiled=True)
+    o_full = lax.all_gather(o_weight, "tensor", axis=0, tiled=False)
     normed_f32, scale_one = normalize(inputs_f32, attn_gain)
     normed_one = normed_f32.astype(bf16)
     query_rows = jnp.dot(normed_one, q_weight, preferred_element_type=f32).reshape(
@@ -768,8 +766,9 @@
     attn_bf = attn_flat.astype(bf16)
     tensor_count = o_weight.shape[0] // o_weight.shape[1]
     attn_all = gather_axis(attn_bf, "tensor", tensor_count, 2)
-    attn_full = jnp.transpose(attn_all, (1, 0, 2)).reshape(token_count, tensor_count * attn_bf.shape[1])
-    mixed_attn = contract_cols(attn_full, o_full)
+    mixed_attn = lax.dot_general(
+        attn_all, o_full, (((0, 2), (0, 2)), ((), ())), preferred_element_type=f32
+    )
     resid = inputs_f32 + mixed_attn
     normed_two_f32, scale_two = normalize(resid, moe_gain)
     normed_two = normed_two_f32.astype(bf16)
@@ -784,9 +783,7 @@
     gcol = gates_dense
     grad_gate, grad_up, grad_down, hid_all, dga_all, dua_all = expert_grad_kernel(
         normed_two,
-        jnp.transpose(normed_two),
         cot_bf,
-        jnp.transpose(cot_bf),
         gcol,
         gate_weight,
         up_weight,

time: 826 us -> 821 us (level)
    unnamed x166 -> x163, local copies, waits for them, and re-layouts: 23.6 us -> 21.6 us
  transfers between devices with their start and end apart: 5 -> 5, of which waited for: 3 -> 3; matrix products, arithmetic and copies ran while one was open for 25% -> 25% of each run, Pallas kernels for 41% -> 40%
where the time goes in v20:
time: 821 us; the launch traced here: 815 us
  Pallas kernels  429 us (52%)
  waiting for transfers between devices  140 us (17%)
  matrix products  125 us (15%)
  local copies, waits for them, and re-layouts  65.9 us (8%)
  other arithmetic  39 us (5%)
  between operations  15.2 us (2%)
    pallas_call x9, Pallas kernels, exchange(): pl.pallas_call(functools.partial(_exchange_body, axis, n, per_peer, downw...  197 us
    unnamed x6, waiting for transfers between devices  74.4 us
    pallas_call x1, Pallas kernels, expert_grad_kernel(): pl.pallas_call(_grad_body, grid=(experts,), in_specs=[whole((tokens, widt...  72.5 us
    reduce_scatter x3, waiting for transfers between devices, per_device(): lax.psum_scatter(g.reshape(g.shape[0], -1, g.shape[3]), ('dpx', 'ctx'), s...  56.1 us
    pallas_call x1, Pallas kernels, chain_sum_down(): pl.pallas_call(functools.partial(_chain_down_body, axis, n), out_shape=ja...  52.5 us
    pallas_call x1, Pallas kernels, expert_rows_kernel(): pl.pallas_call(_rows_body, grid=(experts,), in_specs=[per_expert((tokens,...  46.2 us
    pallas_call x4, Pallas kernels, core_reduce(): pl.pallas_call(_pair_add_body, grid_spec=grid_spec, out_shape=jax.ShapeDt...  39.6 us
    dot_general x1, matrix products, per_device(): jnp.einsum('kgtd,nkd->kgtn', grad_attn_grouped, value_piece, preferred_el...  28.3 us
  transfers between devices with their start and end apart: 5, of which 3 were waited for; matrix products, arithmetic and copies ran while one was open for 25% of the time, Pallas kernels for 40%

profile of v20, /device:TPU:0, one launch (start us, length us, event | category | flops | bytes accessed | tf_op | source)
XLA Modules:
  0.0 814.7 jit_solution(9497697921453162139)
XLA Ops:
  20.7 21.4 %shard_map.229 = (bf16[4,512,512]{2,1,0:T(8,128)(2,1)}, f32[512,768]{1,0:T(8,128)S(1)}, f32[512,12]{1,0:T(8,128)S(1)}) custom-call(bf16[512,768]{1,0:T(8,128)(2,1)S(1)} %copy.174.q_ref, bf16[512,512]{1,0:T(8,128)(2,1)S(1)} %pad_maximum_fusion.3.own_ref, s32[1536,1]{1,0:T(8,128)S(1)} %bitcast.161, s32[1536,1]{1,0:T(8,128)S(1)} %bitcast.162, ...), custom_call_target="tpu_custom_call" | custom-call | flops 3221225472 | bytes 6553600 | tf_op jit(solution)/shard_map/pallas_call | solution.py:656
  43.9 37.1 %shard_map.230 = bf16[2,512,768]{2,1,0:T(8,128)(2,1)} custom-call(bf16[512,768]{1,0:T(8,128)(2,1)} %convert_element_type.161.src_ref), custom_call_target="tpu_custom_call" | custom-call | bytes 1572864 | tf_op jit(solution)/shard_map/pallas_call | solution.py:245
  82.0 9.9 %all-gather.3.cloned.1.call-done = bf16[3072,768]{1,0:T(8,128)(2,1)} async-done(((bf16[1536,768]{1,0:T(8,128)(2,1)}), bf16[3072,768]{1,0:T(8,128)(2,1)}) %all-gather.3.cloned.1.call-update) | async-done | bytes 4718608 | tf_op jit(solution)/shard_map/all_gather | solution.py:718
  102.7 72.5 %shard_map.231 = (bf16[2,24,2,384,256]{4,3,2,1,0:T(8,128)(2,1)}, bf16[2,24,2,384,256]{4,3,2,1,0:T(8,128)(2,1)}, bf16[2,24,2,384,256]{4,3,2,1,0:T(8,128)(2,1)}, b...) custom-call(bf16[512,1536]{1,0:T(8,128)(2,1)} %copy-done.10, ...), custom_call_target="tpu_custom_call" | custom-call | flops 57982058496 | bytes 138412032 | tf_op jit(solution)/shard_map/pallas_call | solution.py:135
  175.2 15.0 %shard_map.244.other_ref = bf16[2,24,2,384,256]{4,3,2,1,0:T(8,128)(2,1)} custom-call(bf16[2,24,2,384,256]{4,3,2,1,0:T(8,128)(2,1)} %get-tuple-element.47.src_ref.own_ref), custom_call_target="tpu_custom_call" | custom-call | bytes 18874368 | tf_op jit(solution)/shard_map/pallas_call | solution.py:245
  190.3 11.5 %shard_map.245 = bf16[24,2,384,256]{3,2,1,0:T(8,128)(2,1)} custom-call(s32[1]{0:T(128)} %bitcast.8.me_ref, bf16[2,24,2,384,256]{4,3,2,1,0:T(8,128)(2,1)} %get-tuple-element.47.src_ref.own_ref, bf16[2,24,2,384,256]{4,3,2,1,0:T(8,128)(2,1)} %shard_map.244.other_ref), custom_call_target="tpu_custom_call" | custom-call | flops 4718592 | bytes 28311552 | tf_op jit(solution)/shard_map/pallas_call | solution.py:289
  201.8 15.1 %shard_map.242.other_ref = bf16[2,24,2,384,256]{4,3,2,1,0:T(8,128)(2,1)} custom-call(bf16[2,24,2,384,256]{4,3,2,1,0:T(8,128)(2,1)} %get-tuple-element.46.src_ref.own_ref), custom_call_target="tpu_custom_call" | custom-call | bytes 18874368 | tf_op jit(solution)/shard_map/pallas_call | solution.py:245
  216.9 11.3 %shard_map.243 = bf16[24,2,384,256]{3,2,1,0:T(8,128)(2,1)} custom-call(s32[1]{0:T(128)} %bitcast.8.me_ref, bf16[2,24,2,384,256]{4,3,2,1,0:T(8,128)(2,1)} %get-tuple-element.46.src_ref.own_ref, bf16[2,24,2,384,256]{4,3,2,1,0:T(8,128)(2,1)} %shard_map.242.other_ref), custom_call_target="tpu_custom_call" | custom-call | flops 4718592 | bytes 28311552 | tf_op jit(solution)/shard_map/pallas_call | solution.py:289
  242.6 20.3 %fusion.36 = f32[4,2048,512,3]{2,1,3,0:T(8,128)} fusion(bf16[2048,4,64,1]{0,2,1,3:T(8,128)(2,1)S(1)} %reshape.365, bf16[512,4,3,32]{0,3,2,1:T(8,128)(2,1)S(1)} %bitcast.172, bf16[512,4,3,32]{0,3,2,1:T(8,128)(2,1)S(1)} %bitcast.170), kind=kOutput, calls=%fused_computation.62 | convolution fusion | flops 1612185600 | bytes 52166656 | tf_op jit(solution)/shard_map/tkgd,nkd->kgtn/dot_general | solution.py:835
  262.8 15.0 %shard_map.232.other_ref = bf16[2,24,2,384,256]{4,3,2,1,0:T(8,128)(2,1)} custom-call(bf16[2,24,2,384,256]{4,3,2,1,0:T(8,128)(2,1)} %get-tuple-element.33.src_ref.own_ref), custom_call_target="tpu_custom_call" | custom-call | bytes 18874368 | tf_op jit(solution)/shard_map/pallas_call | solution.py:245
  277.9 11.4 %shard_map.233 = bf16[24,2,384,256]{3,2,1,0:T(8,128)(2,1)} custom-call(s32[1]{0:T(128)} %bitcast.8.me_ref, bf16[2,24,2,384,256]{4,3,2,1,0:T(8,128)(2,1)} %get-tuple-element.33.src_ref.own_ref, bf16[2,24,2,384,256]{4,3,2,1,0:T(8,128)(2,1)} %shard_map.232.other_ref), custom_call_target="tpu_custom_call" | custom-call | flops 4718592 | bytes 28311552 | tf_op jit(solution)/shard_map/pallas_call | solution.py:289
  289.8 46.2 %shard_map.234 = (f32[512,1536]{1,0:T(8,128)}, f32[24,512,1]{2,1,0:T(8,128)}, f32[512,1536]{1,0:T(8,128)}) custom-call(bf16[24,512,256]{2,1,0:T(8,128)(2,1)} %get-tuple-element.37.hid_ref, bf16[24,512,256]{2,1,0:T(8,128)(2,1)} %get-tuple-element.38.dga_ref, bf16[24,512,256]{2,1,0:T(8,128)(2,1)} %get-tuple-element.39.dua_ref, bf16[512,1536]{1,0:T(8,128)(2,1)} %dy_ref.3, ...), custom_call_target="tpu_custom_call" | custom-call | flops 28991029248 | bytes 83361792 | tf_op jit(solution)/shard_map/pallas_call | solution.py:166
  339.2 36.8 %shard_map.236 = bf16[2,512,1536]{2,1,0:T(8,128)(2,1)} custom-call(bf16[512,1536]{1,0:T(8,128)(2,1)} %convert_element_type.169.src_ref), custom_call_target="tpu_custom_call" | custom-call | bytes 3145728 | tf_op jit(solution)/shard_map/pallas_call | solution.py:245
  393.2 34.4 %shard_map.235 = bf16[2,512,1536]{2,1,0:T(8,128)(2,1)} custom-call(bf16[512,1536]{1,0:T(8,128)(2,1)} %convert_element_type.163.src_ref), custom_call_target="tpu_custom_call" | custom-call | bytes 3145728 | tf_op jit(solution)/shard_map/pallas_call | solution.py:245
  440.8 28.3 %multiply_convert_fusion = bf16[4,3,512,2048]{2,3,1,0:T(8,128)(2,1)} fusion(f32[4,2048,512,3]{2,1,3,0:T(8,128)} %fusion.36, f32[4,3,512]{2,1,0:T(4,128)S(1)} %multiply_reduce_fusion.3, f32[4,3,512]{2,1,0:T(4,128)S(1)} %bitcast.191, pred[512,2048]{0,1:T(8,128)(4,1)} %fusion.6, bf16[4,3,512,64]{2,3,1,0:T(8,128)(2,1)S(1)} %bitcast.178, ...), kind=kOutput, calls=%fused_computation.3 | convolution fusion | flops 1686110208 | bytes 78430208 | tf_op jit(solution)/shard_map/kgtd,nkd->kgtn/dot_general | solution.py:839
  469.1 12.6 %fusion.30 = bf16[2048,4,64]{0,2,1:T(8,128)(2,1)S(1)} fusion(bf16[4,3,512,2048]{2,3,1,0:T(8,128)(2,1)} %multiply_convert_fusion, bf16[512,4,3,32]{0,3,2,1:T(8,128)(2,1)S(1)} %bitcast.173, bf16[512,4,3,32]{0,3,2,1:T(8,128)(2,1)S(1)} %bitcast.171), kind=kOutput, calls=%fused_computation.48 | convolution fusion | flops 1613234176 | bytes 27000832 | tf_op jit(solution)/shard_map/kgtn,tkgd->nkd/dot_general | solution.py:846
  484.1 19.4 %fusion.31 = bf16[2048,4,64]{0,2,1:T(8,128)(2,1)S(1)} fusion(bf16[4,3,512,64]{2,3,1,0:T(8,128)(2,1)S(1)} %bitcast.179, f32[4,2048,512,3]{2,1,3,0:T(8,128)} %fusion.36, f32[4,3,512]{2,1,0:T(4,128)S(1)} %bitcast.192, pred[512,2048]{0,1:T(8,128)(4,1)} %fusion.6), kind=kOutput, calls=%fused_computation.49 | convolution fusion | flops 1661468672 | bytes 53239808 | tf_op jit(solution)/shard_map/kgtn,kgtd->nkd/dot_general | solution.py:849
  505.4 52.5 %shard_map.238 = f32[512,512]{1,0:T(8,128)S(1)} custom-call(bf16[4,512,512]{2,1,0:T(8,128)(2,1)S(1)} %pad_maximum_fusion.x_ref), custom_call_target="tpu_custom_call" | custom-call | flops 786432 | bytes 6291456 | tf_op jit(solution)/shard_map/pallas_call | solution.py:452
  558.3 11.4 %convolution_multiply_fusion = f32[4,3,512,64]{2,3,1,0:T(8,128)S(1)} fusion(bf16[4,3,512,2048]{2,3,1,0:T(8,128)(2,1)} %multiply_convert_fusion, bf16[2048,4,64,1]{0,2,1,3:T(8,128)(2,1)S(1)} %copy-done.21), kind=kOutput, calls=%fused_computation.56 | convolution fusion | flops 1611005952 | bytes 27787264 | tf_op jit(solution)/shard_map/kgtn,nkd->kgtd/dot_general | solution.py:843
  576.1 31.7 %shard_map.239 = bf16[2,512,1536]{2,1,0:T(8,128)(2,1)} custom-call(bf16[512,1536]{1,0:T(8,128)(2,1)} %fusion.20.src_ref), custom_call_target="tpu_custom_call" | custom-call | bytes 3145728 | tf_op jit(solution)/shard_map/pallas_call | solution.py:245
  643.9 10.4 %concatenate.65 = bf16[2,2,384,2176]{3,2,0,1:T(8,128)(2,1)} concatenate(bf16[2,2,384,768]{3,2,0,1:T(8,128)(2,1)} %convolution_convert_fusion.3, bf16[2,2,384,768]{3,2,0,1:T(8,128)(2,1)S(1)} %copy.202, bf16[2,2,384,256]{3,2,0,1:T(8,128)(2,1)} %convolution_convert_fusion.4, bf16[2,2,384,256]{3,2,0,1:T(8,128)(2,1)S(1)} %copy.203, bf16[2,2,384,24]{3,2,0,1:T(8,128)(2,1)} %copy.204, ...), dimensions={3} | concatenate | bytes 13369344 | tf_op jit(solution)/shard_map/concatenate | solution.py:903
  654.4 6.3 shard_map.240.other_ref
  666.1 56.1 %reduce-scatter.7.cloned.1.call-done = bf16[24,96,256]{2,1,0:T(8,128)(2,1)} async-done(((bf16[24,768,256]{2,1,0:T(8,128)(2,1)}), bf16[24,96,256]{2,1,0:T(8,128)(2,1)}) %reduce-scatter.7.cloned.1.call-update) | async-done | bytes 1179664 | tf_op jit(solution)/shard_map/reduce_scatter | solution.py:806
  728.5 73.6 %reduce-scatter.13.cloned.1.call-done = bf16[96,2176]{1,0:T(8,128)(2,1)} async-done(((bf16[768,2176]{1,0:T(8,128)(2,1)}), bf16[96,2176]{1,0:T(8,128)(2,1)}) %reduce-scatter.13.cloned.1.call-update) | async-done | bytes 417808
  (275 shorter events, 139.3 us)
Async XLA Ops:
  7.2 84.6 %all-gather.3.cloned.1.call-start = ((), (), s32[]{:S(2)}) async-start(), calls=%async_computation.7 | async-start | bytes 7077888 | tf_op jit(solution)/shard_map/all_gather | solution.py:718
  7.9 658.1 %reduce-scatter.11.cloned.1.call-start = ((), (), s32[]{:S(2)}) async-start(), calls=%async_computation.6 | async-start | bytes 10616832 | tf_op jit(solution)/shard_map/reduce_scatter | solution.py:806
  9.0 9.0 %copy-start.73 = (f32[512]{0:T(512)}, f32[512]{0:T(512)S(1)}, u32[]{:S(2)}) copy-start(f32[512]{0:T(512)S(1)} %add_rsqrt_fusion.1) | copy-start | bytes 6148
  42.8 39.2 %copy-start = (f32[512,768]{1,0:T(8,128)}, f32[512,768]{1,0:T(8,128)S(1)}, u32[]{:S(2)}) copy-start(f32[512,768]{1,0:T(8,128)S(1)} %get-tuple-element.32) | copy-start | bytes 4718596
  201.8 464.3 %reduce-scatter.9.cloned.1.call-start = ((), (), s32[]{:S(2)}) async-start(), calls=%async_computation.5 | async-start | bytes 10616832 | tf_op jit(solution)/shard_map/reduce_scatter | solution.py:806
  228.3 493.9 %reduce-scatter.7.cloned.1.call-start = ((), (), s32[]{:S(2)}) async-start(), calls=%async_computation.4 | async-start | bytes 10616832 | tf_op jit(solution)/shard_map/reduce_scatter | solution.py:806
  236.2 26.6 %copy-start.20 = (bf16[2048,4,64,1]{0,2,1,3:T(8,128)(2,1)}, bf16[2048,4,64,1]{0,2,1,3:T(8,128)(2,1)S(1)}, u32[]{:S(2)}) copy-start(bf16[2048,4,64,1]{0,2,1,3:T(8,128)(2,1)S(1)} %reshape.365) | copy-start | bytes 3145732
  289.3 512.8 %reduce-scatter.13.cloned.1.call-start = ((), (), s32[]{:S(2)}) async-start(), calls=%async_computation.8 | async-start | bytes 3760128
  376.1 11.7 %copy-start.31 = (f32[512,8]{1,0:T(8,128)S(1)}, f32[512,8]{1,0:T(8,128)}, u32[]{:S(2)}) copy-start(f32[512,8]{1,0:T(8,128)} %copy-done.30) | copy-start | bytes 49156
  376.1 11.7 %copy-start.63 = (f32[512]{0:T(512)S(1)}, f32[512]{0:T(512)}, u32[]{:S(2)}) copy-start(f32[512]{0:T(512)} %copy-done.62) | copy-start | bytes 6148
  376.1 15.8 %copy-start.16 = (f32[512,1536]{1,0:T(8,128)S(1)}, f32[512,1536]{1,0:T(8,128)}, u32[]{:S(2)}) copy-start(f32[512,1536]{1,0:T(8,128)} %get-tuple-element.40) | copy-start | bytes 9437188
  393.2 34.5 %copy-start.8 = (f32[512,1536]{1,0:T(8,128)S(1)}, f32[512,1536]{1,0:T(8,128)}, u32[]{:S(2)}) copy-start(f32[512,1536]{1,0:T(8,128)} %copy-done.7) | copy-start | bytes 9437188
  393.2 34.5 %copy-start.55 = (bf16[1536,24]{0,1:T(8,128)(2,1)S(1)}, bf16[1536,24]{0,1:T(8,128)(2,1)}, u32[]{:S(2)}) copy-start(bf16[1536,24]{0,1:T(8,128)(2,1)} %param.21) | copy-start | bytes 221188
  393.2 34.5 %copy-start.61 = (f32[1536]{0:T(1024)S(1)}, f32[1536]{0:T(1024)}, u32[]{:S(2)}) copy-start(f32[1536]{0:T(1024)} %param.20) | copy-start | bytes 18436
  393.2 34.5 %copy-start.68 = (f32[512]{0:T(512)S(1)}, f32[512]{0:T(512)}, u32[]{:S(2)}) copy-start(f32[512]{0:T(512)} %copy-done.67) | copy-start | bytes 6148
  440.8 28.3 %copy-start.25 = (bf16[512,12,32]{0,2,1:T(8,128)(2,1)S(1)}, bf16[512,12,32]{0,2,1:T(8,128)(2,1)}, u32[]{:S(2)}) copy-start(bf16[512,12,32]{0,2,1:T(8,128)(2,1)} %copy-done.23) | copy-start | bytes 1179652
  440.8 28.3 %copy-start.28 = (bf16[512,12,32]{0,2,1:T(8,128)(2,1)S(1)}, bf16[512,12,32]{0,2,1:T(8,128)(2,1)}, u32[]{:S(2)}) copy-start(bf16[512,12,32]{0,2,1:T(8,128)(2,1)} %copy-done.26) | copy-start | bytes 1179652
  505.4 52.8 %copy-start.40 = (f32[512,32]{0,1:T(8,128)S(1)}, f32[512,32]{0,1:T(8,128)}, u32[]{:S(2)}) copy-start(f32[512,32]{0,1:T(8,128)} %copy-done.39) | copy-start | bytes 196612
  505.4 52.8 %copy-start.53 = (f32[512,32]{0,1:T(8,128)S(1)}, f32[512,32]{0,1:T(8,128)}, u32[]{:S(2)}) copy-start(f32[512,32]{0,1:T(8,128)} %get-tuple-element.138) | copy-start | bytes 196612
  505.4 52.9 %copy-start.21 = (bf16[2048,4,64,1]{0,2,1,3:T(8,128)(2,1)S(1)}, bf16[2048,4,64,1]{0,2,1,3:T(8,128)(2,1)}, u32[]{:S(2)}) copy-start(bf16[2048,4,64,1]{0,2,1,3:T(8,128)(2,1)} %copy-done.20) | copy-start | bytes 3145732
  576.1 31.7 %copy-start.9 = (bf16[512,1536]{1,0:T(8,128)(2,1)S(1)}, bf16[512,1536]{1,0:T(8,128)(2,1)}, u32[]{:S(2)}) copy-start(bf16[512,1536]{1,0:T(8,128)(2,1)} %fusion.20.src_ref) | copy-start | bytes 4718596
  576.1 31.7 %copy-start.66 = (f32[1536]{0:T(1024)S(1)}, f32[1536]{0:T(1024)}, u32[]{:S(2)}) copy-start(f32[1536]{0:T(1024)} %param.15) | copy-start | bytes 18436
  576.1 31.7 %copy-start.74 = (f32[512]{0:T(512)S(1)}, f32[512]{0:T(512)}, u32[]{:S(2)}) copy-start(f32[512]{0:T(512)} %copy-done.73) | copy-start | bytes 6148
  617.0 10.8 %copy-start.14 = (bf16[512,1536]{1,0:T(8,128)(2,1)S(1)}, bf16[512,1536]{1,0:T(8,128)(2,1)}, u32[]{:S(2)}) copy-start(bf16[512,1536]{1,0:T(8,128)(2,1)} %param.14) | copy-start | bytes 4718596
  (57 other events, 174.0 us)
Sparse Core Ops, SparseCore 0:
  9.6 82.1 all-gather.2
  201.9 166.1 reduce-scatter.10
  371.7 164.3 reduce-scatter.8
  539.6 182.5 reduce-scatter.6
  725.6 76.4 reduce-scatter.12

commit v21 on v20

--- a/solution.py
+++ b/solution.py
@@ -276,7 +276,9 @@
     rest = x.shape[2:]
     zeros = (0,) * len(rest)
     item_bytes = math.prod(rest) * x.dtype.itemsize
-    step = max(d for d in range(1, count + 1) if count % d == 0 and d * item_bytes <= 4 * 1024 * 1024)
+    step = max(
+        [1] + [d for d in range(1, count + 1) if count % d == 0 and d * item_bytes <= 3 * 1024 * 1024 // 2]
+    )
     grid_spec = pltpu.PrefetchScalarGridSpec(
         num_scalar_prefetch=1,
         grid=(count // step,),

time: 821 us -> 821 us (level)
  no operation moved by 1% of the time
where the time goes in v21:
time: 821 us; the launch traced here: 814 us
  Pallas kernels  427 us (52%)
  waiting for transfers between devices  141 us (17%)
  matrix products  124 us (15%)
  local copies, waits for them, and re-layouts  65.9 us (8%)
  other arithmetic  39 us (5%)
  between operations  15.2 us (2%)
    pallas_call x9, Pallas kernels, exchange(): pl.pallas_call(functools.partial(_exchange_body, axis, n, per_peer, downw...  197 us
    unnamed x6, waiting for transfers between devices  74.3 us
    pallas_call x1, Pallas kernels, expert_grad_kernel(): pl.pallas_call(_grad_body, grid=(experts,), in_specs=[whole((tokens, widt...  72.5 us
    reduce_scatter x3, waiting for transfers between devices, per_device(): lax.psum_scatter(g.reshape(g.shape[0], -1, g.shape[3]), ('dpx', 'ctx'), s...  56.8 us
    pallas_call x1, Pallas kernels, chain_sum_down(): pl.pallas_call(functools.partial(_chain_down_body, axis, n), out_shape=ja...  52.2 us
    pallas_call x1, Pallas kernels, expert_rows_kernel(): pl.pallas_call(_rows_body, grid=(experts,), in_specs=[per_expert((tokens,...  46.2 us
    pallas_call x4, Pallas kernels, core_reduce(): pl.pallas_call(_pair_add_body, grid_spec=grid_spec, out_shape=jax.ShapeDt...  38.6 us
    dot_general x1, matrix products, per_device(): jnp.einsum('kgtd,nkd->kgtn', grad_attn_grouped, value_piece, preferred_el...  28.2 us
  transfers between devices with their start and end apart: 5, of which 3 were waited for; matrix products, arithmetic and copies ran while one was open for 25% of the time, Pallas kernels for 40%

profile of v21, /device:TPU:0, one launch (start us, length us, event | category | flops | bytes accessed | tf_op | source)
XLA Modules:
  0.0 814.2 jit_solution(4528677736628606084)
XLA Ops:
  20.7 20.9 %shard_map.229 = (bf16[4,512,512]{2,1,0:T(8,128)(2,1)}, f32[512,768]{1,0:T(8,128)S(1)}, f32[512,12]{1,0:T(8,128)S(1)}) custom-call(bf16[512,768]{1,0:T(8,128)(2,1)S(1)} %copy.174.q_ref, bf16[512,512]{1,0:T(8,128)(2,1)S(1)} %pad_maximum_fusion.3.own_ref, s32[1536,1]{1,0:T(8,128)S(1)} %bitcast.161, s32[1536,1]{1,0:T(8,128)S(1)} %bitcast.162, ...), custom_call_target="tpu_custom_call" | custom-call | flops 3221225472 | bytes 6553600 | tf_op jit(solution)/shard_map/pallas_call | solution.py:658
  43.4 37.1 %shard_map.230 = bf16[2,512,768]{2,1,0:T(8,128)(2,1)} custom-call(bf16[512,768]{1,0:T(8,128)(2,1)} %convert_element_type.161.src_ref), custom_call_target="tpu_custom_call" | custom-call | bytes 1572864 | tf_op jit(solution)/shard_map/pallas_call | solution.py:245
  81.5 10.3 %all-gather.3.cloned.1.call-done = bf16[3072,768]{1,0:T(8,128)(2,1)} async-done(((bf16[1536,768]{1,0:T(8,128)(2,1)}), bf16[3072,768]{1,0:T(8,128)(2,1)}) %all-gather.3.cloned.1.call-update) | async-done | bytes 4718608 | tf_op jit(solution)/shard_map/all_gather | solution.py:720
  102.7 72.5 %shard_map.231 = (bf16[2,24,2,384,256]{4,3,2,1,0:T(8,128)(2,1)}, bf16[2,24,2,384,256]{4,3,2,1,0:T(8,128)(2,1)}, bf16[2,24,2,384,256]{4,3,2,1,0:T(8,128)(2,1)}, b...) custom-call(bf16[512,1536]{1,0:T(8,128)(2,1)} %copy-done.10, ...), custom_call_target="tpu_custom_call" | custom-call | flops 57982058496 | bytes 138412032 | tf_op jit(solution)/shard_map/pallas_call | solution.py:135
  175.2 15.0 %shard_map.244.other_ref = bf16[2,24,2,384,256]{4,3,2,1,0:T(8,128)(2,1)} custom-call(bf16[2,24,2,384,256]{4,3,2,1,0:T(8,128)(2,1)} %get-tuple-element.47.src_ref.own_ref), custom_call_target="tpu_custom_call" | custom-call | bytes 18874368 | tf_op jit(solution)/shard_map/pallas_call | solution.py:245
  190.3 11.4 %shard_map.245 = bf16[24,2,384,256]{3,2,1,0:T(8,128)(2,1)} custom-call(s32[1]{0:T(128)} %bitcast.8.me_ref, bf16[2,24,2,384,256]{4,3,2,1,0:T(8,128)(2,1)} %get-tuple-element.47.src_ref.own_ref, bf16[2,24,2,384,256]{4,3,2,1,0:T(8,128)(2,1)} %shard_map.244.other_ref), custom_call_target="tpu_custom_call" | custom-call | flops 4718592 | bytes 28311552 | tf_op jit(solution)/shard_map/pallas_call | solution.py:291
  201.7 15.1 %shard_map.242.other_ref = bf16[2,24,2,384,256]{4,3,2,1,0:T(8,128)(2,1)} custom-call(bf16[2,24,2,384,256]{4,3,2,1,0:T(8,128)(2,1)} %get-tuple-element.46.src_ref.own_ref), custom_call_target="tpu_custom_call" | custom-call | bytes 18874368 | tf_op jit(solution)/shard_map/pallas_call | solution.py:245
  216.8 11.3 %shard_map.243 = bf16[24,2,384,256]{3,2,1,0:T(8,128)(2,1)} custom-call(s32[1]{0:T(128)} %bitcast.8.me_ref, bf16[2,24,2,384,256]{4,3,2,1,0:T(8,128)(2,1)} %get-tuple-element.46.src_ref.own_ref, bf16[2,24,2,384,256]{4,3,2,1,0:T(8,128)(2,1)} %shard_map.242.other_ref), custom_call_target="tpu_custom_call" | custom-call | flops 4718592 | bytes 28311552 | tf_op jit(solution)/shard_map/pallas_call | solution.py:291
  242.4 20.3 %fusion.36 = f32[4,2048,512,3]{2,1,3,0:T(8,128)} fusion(bf16[2048,4,64,1]{0,2,1,3:T(8,128)(2,1)S(1)} %reshape.365, bf16[512,4,3,32]{0,3,2,1:T(8,128)(2,1)S(1)} %bitcast.172, bf16[512,4,3,32]{0,3,2,1:T(8,128)(2,1)S(1)} %bitcast.170), kind=kOutput, calls=%fused_computation.62 | convolution fusion | flops 1612185600 | bytes 52166656 | tf_op jit(solution)/shard_map/tkgd,nkd->kgtn/dot_general | solution.py:837
  262.7 15.0 %shard_map.232.other_ref = bf16[2,24,2,384,256]{4,3,2,1,0:T(8,128)(2,1)} custom-call(bf16[2,24,2,384,256]{4,3,2,1,0:T(8,128)(2,1)} %get-tuple-element.33.src_ref.own_ref), custom_call_target="tpu_custom_call" | custom-call | bytes 18874368 | tf_op jit(solution)/shard_map/pallas_call | solution.py:245
  277.7 11.4 %shard_map.233 = bf16[24,2,384,256]{3,2,1,0:T(8,128)(2,1)} custom-call(s32[1]{0:T(128)} %bitcast.8.me_ref, bf16[2,24,2,384,256]{4,3,2,1,0:T(8,128)(2,1)} %get-tuple-element.33.src_ref.own_ref, bf16[2,24,2,384,256]{4,3,2,1,0:T(8,128)(2,1)} %shard_map.232.other_ref), custom_call_target="tpu_custom_call" | custom-call | flops 4718592 | bytes 28311552 | tf_op jit(solution)/shard_map/pallas_call | solution.py:291
  289.7 46.2 %shard_map.234 = (f32[512,1536]{1,0:T(8,128)}, f32[24,512,1]{2,1,0:T(8,128)}, f32[512,1536]{1,0:T(8,128)}) custom-call(bf16[24,512,256]{2,1,0:T(8,128)(2,1)} %get-tuple-element.37.hid_ref, bf16[24,512,256]{2,1,0:T(8,128)(2,1)} %get-tuple-element.38.dga_ref, bf16[24,512,256]{2,1,0:T(8,128)(2,1)} %get-tuple-element.39.dua_ref, bf16[512,1536]{1,0:T(8,128)(2,1)} %dy_ref.3, ...), custom_call_target="tpu_custom_call" | custom-call | flops 28991029248 | bytes 83361792 | tf_op jit(solution)/shard_map/pallas_call | solution.py:166
  339.1 36.9 %shard_map.236 = bf16[2,512,1536]{2,1,0:T(8,128)(2,1)} custom-call(bf16[512,1536]{1,0:T(8,128)(2,1)} %convert_element_type.169.src_ref), custom_call_target="tpu_custom_call" | custom-call | bytes 3145728 | tf_op jit(solution)/shard_map/pallas_call | solution.py:245
  393.2 34.6 %shard_map.235 = bf16[2,512,1536]{2,1,0:T(8,128)(2,1)} custom-call(bf16[512,1536]{1,0:T(8,128)(2,1)} %convert_element_type.163.src_ref), custom_call_target="tpu_custom_call" | custom-call | bytes 3145728 | tf_op jit(solution)/shard_map/pallas_call | solution.py:245
  440.9 28.2 %multiply_convert_fusion = bf16[4,3,512,2048]{2,3,1,0:T(8,128)(2,1)} fusion(f32[4,2048,512,3]{2,1,3,0:T(8,128)} %fusion.36, f32[4,3,512]{2,1,0:T(4,128)S(1)} %multiply_reduce_fusion.3, f32[4,3,512]{2,1,0:T(4,128)S(1)} %bitcast.191, pred[512,2048]{0,1:T(8,128)(4,1)} %fusion.6, bf16[4,3,512,64]{2,3,1,0:T(8,128)(2,1)S(1)} %bitcast.178, ...), kind=kOutput, calls=%fused_computation.3 | convolution fusion | flops 1686110208 | bytes 78430208 | tf_op jit(solution)/shard_map/kgtd,nkd->kgtn/dot_general | solution.py:841
  469.1 12.6 %fusion.30 = bf16[2048,4,64]{0,2,1:T(8,128)(2,1)S(1)} fusion(bf16[4,3,512,2048]{2,3,1,0:T(8,128)(2,1)} %multiply_convert_fusion, bf16[512,4,3,32]{0,3,2,1:T(8,128)(2,1)S(1)} %bitcast.173, bf16[512,4,3,32]{0,3,2,1:T(8,128)(2,1)S(1)} %bitcast.171), kind=kOutput, calls=%fused_computation.48 | convolution fusion | flops 1613234176 | bytes 27000832 | tf_op jit(solution)/shard_map/kgtn,tkgd->nkd/dot_general | solution.py:848
  484.1 19.4 %fusion.31 = bf16[2048,4,64]{0,2,1:T(8,128)(2,1)S(1)} fusion(bf16[4,3,512,64]{2,3,1,0:T(8,128)(2,1)S(1)} %bitcast.179, f32[4,2048,512,3]{2,1,3,0:T(8,128)} %fusion.36, f32[4,3,512]{2,1,0:T(4,128)S(1)} %bitcast.192, pred[512,2048]{0,1:T(8,128)(4,1)} %fusion.6), kind=kOutput, calls=%fused_computation.49 | convolution fusion | flops 1661468672 | bytes 53239808 | tf_op jit(solution)/shard_map/kgtn,kgtd->nkd/dot_general | solution.py:851
  505.4 52.2 %shard_map.238 = f32[512,512]{1,0:T(8,128)S(1)} custom-call(bf16[4,512,512]{2,1,0:T(8,128)(2,1)S(1)} %pad_maximum_fusion.x_ref), custom_call_target="tpu_custom_call" | custom-call | flops 786432 | bytes 6291456 | tf_op jit(solution)/shard_map/pallas_call | solution.py:454
  558.1 11.4 %convolution_multiply_fusion = f32[4,3,512,64]{2,3,1,0:T(8,128)S(1)} fusion(bf16[4,3,512,2048]{2,3,1,0:T(8,128)(2,1)} %multiply_convert_fusion, bf16[2048,4,64,1]{0,2,1,3:T(8,128)(2,1)S(1)} %copy-done.21), kind=kOutput, calls=%fused_computation.56 | convolution fusion | flops 1611005952 | bytes 27787264 | tf_op jit(solution)/shard_map/kgtn,nkd->kgtd/dot_general | solution.py:845
  575.8 31.6 %shard_map.239 = bf16[2,512,1536]{2,1,0:T(8,128)(2,1)} custom-call(bf16[512,1536]{1,0:T(8,128)(2,1)} %fusion.20.src_ref), custom_call_target="tpu_custom_call" | custom-call | bytes 3145728 | tf_op jit(solution)/shard_map/pallas_call | solution.py:245
  643.6 10.4 %concatenate.65 = bf16[2,2,384,2176]{3,2,0,1:T(8,128)(2,1)} concatenate(bf16[2,2,384,768]{3,2,0,1:T(8,128)(2,1)} %convolution_convert_fusion.3, bf16[2,2,384,768]{3,2,0,1:T(8,128)(2,1)S(1)} %copy.202, bf16[2,2,384,256]{3,2,0,1:T(8,128)(2,1)} %convolution_convert_fusion.4, bf16[2,2,384,256]{3,2,0,1:T(8,128)(2,1)S(1)} %copy.203, bf16[2,2,384,24]{3,2,0,1:T(8,128)(2,1)} %copy.204, ...), dimensions={3} | concatenate | bytes 13369344 | tf_op jit(solution)/shard_map/concatenate | solution.py:905
  654.0 6.3 shard_map.240.other_ref
  664.9 56.8 %reduce-scatter.7.cloned.1.call-done = bf16[24,96,256]{2,1,0:T(8,128)(2,1)} async-done(((bf16[24,768,256]{2,1,0:T(8,128)(2,1)}), bf16[24,96,256]{2,1,0:T(8,128)(2,1)}) %reduce-scatter.7.cloned.1.call-update) | async-done | bytes 1179664 | tf_op jit(solution)/shard_map/reduce_scatter | solution.py:808
  728.0 73.5 %reduce-scatter.13.cloned.1.call-done = bf16[96,2176]{1,0:T(8,128)(2,1)} async-done(((bf16[768,2176]{1,0:T(8,128)(2,1)}), bf16[96,2176]{1,0:T(8,128)(2,1)}) %reduce-scatter.13.cloned.1.call-update) | async-done | bytes 417808
  (275 shorter events, 138.4 us)
Async XLA Ops:
  7.2 84.6 %all-gather.3.cloned.1.call-start = ((), (), s32[]{:S(2)}) async-start(), calls=%async_computation.7 | async-start | bytes 7077888 | tf_op jit(solution)/shard_map/all_gather | solution.py:720
  7.9 656.9 %reduce-scatter.11.cloned.1.call-start = ((), (), s32[]{:S(2)}) async-start(), calls=%async_computation.6 | async-start | bytes 10616832 | tf_op jit(solution)/shard_map/reduce_scatter | solution.py:808
  9.0 9.0 %copy-start.73 = (f32[512]{0:T(512)}, f32[512]{0:T(512)S(1)}, u32[]{:S(2)}) copy-start(f32[512]{0:T(512)S(1)} %add_rsqrt_fusion.1) | copy-start | bytes 6148
  42.3 39.2 %copy-start = (f32[512,768]{1,0:T(8,128)}, f32[512,768]{1,0:T(8,128)S(1)}, u32[]{:S(2)}) copy-start(f32[512,768]{1,0:T(8,128)S(1)} %get-tuple-element.32) | copy-start | bytes 4718596
  201.7 463.2 %reduce-scatter.9.cloned.1.call-start = ((), (), s32[]{:S(2)}) async-start(), calls=%async_computation.5 | async-start | bytes 10616832 | tf_op jit(solution)/shard_map/reduce_scatter | solution.py:808
  228.1 493.6 %reduce-scatter.7.cloned.1.call-start = ((), (), s32[]{:S(2)}) async-start(), calls=%async_computation.4 | async-start | bytes 10616832 | tf_op jit(solution)/shard_map/reduce_scatter | solution.py:808
  236.0 26.6 %copy-start.20 = (bf16[2048,4,64,1]{0,2,1,3:T(8,128)(2,1)}, bf16[2048,4,64,1]{0,2,1,3:T(8,128)(2,1)S(1)}, u32[]{:S(2)}) copy-start(bf16[2048,4,64,1]{0,2,1,3:T(8,128)(2,1)S(1)} %reshape.365) | copy-start | bytes 3145732
  289.2 512.4 %reduce-scatter.13.cloned.1.call-start = ((), (), s32[]{:S(2)}) async-start(), calls=%async_computation.8 | async-start | bytes 3760128
  376.0 11.7 %copy-start.31 = (f32[512,8]{1,0:T(8,128)S(1)}, f32[512,8]{1,0:T(8,128)}, u32[]{:S(2)}) copy-start(f32[512,8]{1,0:T(8,128)} %copy-done.30) | copy-start | bytes 49156
  376.0 11.7 %copy-start.63 = (f32[512]{0:T(512)S(1)}, f32[512]{0:T(512)}, u32[]{:S(2)}) copy-start(f32[512]{0:T(512)} %copy-done.62) | copy-start | bytes 6148
  376.0 15.8 %copy-start.16 = (f32[512,1536]{1,0:T(8,128)S(1)}, f32[512,1536]{1,0:T(8,128)}, u32[]{:S(2)}) copy-start(f32[512,1536]{1,0:T(8,128)} %get-tuple-element.40) | copy-start | bytes 9437188
  393.2 34.7 %copy-start.8 = (f32[512,1536]{1,0:T(8,128)S(1)}, f32[512,1536]{1,0:T(8,128)}, u32[]{:S(2)}) copy-start(f32[512,1536]{1,0:T(8,128)} %copy-done.7) | copy-start | bytes 9437188
  393.2 34.7 %copy-start.55 = (bf16[1536,24]{0,1:T(8,128)(2,1)S(1)}, bf16[1536,24]{0,1:T(8,128)(2,1)}, u32[]{:S(2)}) copy-start(bf16[1536,24]{0,1:T(8,128)(2,1)} %param.21) | copy-start | bytes 221188
  393.2 34.7 %copy-start.61 = (f32[1536]{0:T(1024)S(1)}, f32[1536]{0:T(1024)}, u32[]{:S(2)}) copy-start(f32[1536]{0:T(1024)} %param.20) | copy-start | bytes 18436
  393.2 34.7 %copy-start.68 = (f32[512]{0:T(512)S(1)}, f32[512]{0:T(512)}, u32[]{:S(2)}) copy-start(f32[512]{0:T(512)} %copy-done.67) | copy-start | bytes 6148
  440.9 28.2 %copy-start.25 = (bf16[512,12,32]{0,2,1:T(8,128)(2,1)S(1)}, bf16[512,12,32]{0,2,1:T(8,128)(2,1)}, u32[]{:S(2)}) copy-start(bf16[512,12,32]{0,2,1:T(8,128)(2,1)} %copy-done.23) | copy-start | bytes 1179652
  440.9 28.2 %copy-start.28 = (bf16[512,12,32]{0,2,1:T(8,128)(2,1)S(1)}, bf16[512,12,32]{0,2,1:T(8,128)(2,1)}, u32[]{:S(2)}) copy-start(bf16[512,12,32]{0,2,1:T(8,128)(2,1)} %copy-done.26) | copy-start | bytes 1179652
  505.4 52.5 %copy-start.40 = (f32[512,32]{0,1:T(8,128)S(1)}, f32[512,32]{0,1:T(8,128)}, u32[]{:S(2)}) copy-start(f32[512,32]{0,1:T(8,128)} %copy-done.39) | copy-start | bytes 196612
  505.4 52.5 %copy-start.53 = (f32[512,32]{0,1:T(8,128)S(1)}, f32[512,32]{0,1:T(8,128)}, u32[]{:S(2)}) copy-start(f32[512,32]{0,1:T(8,128)} %get-tuple-element.138) | copy-start | bytes 196612
  505.4 52.6 %copy-start.21 = (bf16[2048,4,64,1]{0,2,1,3:T(8,128)(2,1)S(1)}, bf16[2048,4,64,1]{0,2,1,3:T(8,128)(2,1)}, u32[]{:S(2)}) copy-start(bf16[2048,4,64,1]{0,2,1,3:T(8,128)(2,1)} %copy-done.20) | copy-start | bytes 3145732
  575.8 31.6 %copy-start.9 = (bf16[512,1536]{1,0:T(8,128)(2,1)S(1)}, bf16[512,1536]{1,0:T(8,128)(2,1)}, u32[]{:S(2)}) copy-start(bf16[512,1536]{1,0:T(8,128)(2,1)} %fusion.20.src_ref) | copy-start | bytes 4718596
  575.8 31.6 %copy-start.66 = (f32[1536]{0:T(1024)S(1)}, f32[1536]{0:T(1024)}, u32[]{:S(2)}) copy-start(f32[1536]{0:T(1024)} %param.15) | copy-start | bytes 18436
  575.8 31.6 %copy-start.74 = (f32[512]{0:T(512)S(1)}, f32[512]{0:T(512)}, u32[]{:S(2)}) copy-start(f32[512]{0:T(512)} %copy-done.73) | copy-start | bytes 6148
  616.7 10.8 %copy-start.14 = (bf16[512,1536]{1,0:T(8,128)(2,1)S(1)}, bf16[512,1536]{1,0:T(8,128)(2,1)}, u32[]{:S(2)}) copy-start(bf16[512,1536]{1,0:T(8,128)(2,1)} %param.14) | copy-start | bytes 4718596
  (57 other events, 174.0 us)
Sparse Core Ops, SparseCore 0:
  9.6 82.1 all-gather.2
  201.8 166.1 reduce-scatter.10
  371.6 164.2 reduce-scatter.8
  539.4 182.3 reduce-scatter.6
  725.2 76.3 reduce-scatter.12

commit v22 on v21

--- a/solution.py
+++ b/solution.py
@@ -64,18 +64,19 @@
     )
 
 
-def _store_split(out_ref, value):
+def _store_split(out_ref, value, slot=0):
     cores, _, groups, rows, _ = out_ref.shape
     for x in range(groups):
         for c in range(cores):
             start = (x * cores + c) * rows
-            out_ref[c, 0, x] = value[start : start + rows].astype(out_ref.dtype)
-
-
-def _gate_column(gates_ref):
+            out_ref[c, slot, x] = value[start : start + rows].astype(out_ref.dtype)
+
+
+def _gate_column(gates_ref, expert=None):
     gates = gates_ref[...]
     lane = lax.broadcasted_iota(jnp.int32, gates.shape, 1)
-    return jnp.sum(jnp.where(lane == pl.program_id(0), gates, 0.0), axis=1, keepdims=True)
+    expert = pl.program_id(0) if expert is None else expert
+    return jnp.sum(jnp.where(lane == expert, gates, 0.0), axis=1, keepdims=True)
 
 
 def _grad_body(
@@ -84,25 +85,27 @@
 ):
     f32 = jnp.float32
     bf16 = jnp.bfloat16
+    tn = (((0,), (0,)), ((), ()))
     n2 = n2_ref[...]
-    wd = wd_ref[0]
-    gate_act = jnp.dot(n2, wg_ref[0], preferred_element_type=f32)
-    up_act = jnp.dot(n2, wu_ref[0], preferred_element_type=f32)
-    sig = 1.0 / (1.0 + jnp.exp(-gate_act))
-    silu = gate_act * sig
-    hidden = (silu * up_act).astype(bf16)
-    hid_ref[0] = hidden
-    gate = _gate_column(gcol_ref)
-    grad_hidden = gate * jnp.dot(dy_ref[...], wd, preferred_element_type=f32)
-    gated_hidden = (gate * hidden.astype(f32)).astype(bf16)
-    tn = (((0,), (0,)), ((), ()))
-    _store_split(gd_ref, lax.dot_general(dy_ref[...], gated_hidden, tn, preferred_element_type=f32))
-    grad_gate_act = (grad_hidden * up_act * sig * (1.0 + gate_act * (1.0 - sig))).astype(bf16)
-    grad_up_act = (grad_hidden * silu).astype(bf16)
-    dga_ref[0] = grad_gate_act
-    dua_ref[0] = grad_up_act
-    _store_split(gg_ref, lax.dot_general(n2, grad_gate_act, tn, preferred_element_type=f32))
-    _store_split(gu_ref, lax.dot_general(n2, grad_up_act, tn, preferred_element_type=f32))
+    per_step = wg_ref.shape[0]
+    for i in range(per_step):
+        wd = wd_ref[i]
+        gate_act = jnp.dot(n2, wg_ref[i], preferred_element_type=f32)
+        up_act = jnp.dot(n2, wu_ref[i], preferred_element_type=f32)
+        sig = 1.0 / (1.0 + jnp.exp(-gate_act))
+        silu = gate_act * sig
+        hidden = (silu * up_act).astype(bf16)
+        hid_ref[i] = hidden
+        gate = _gate_column(gcol_ref, pl.program_id(0) * per_step + i)
+        grad_hidden = gate * jnp.dot(dy_ref[...], wd, preferred_element_type=f32)
+        gated_hidden = (gate * hidden.astype(f32)).astype(bf16)
+        _store_split(gd_ref, lax.dot_general(dy_ref[...], gated_hidden, tn, preferred_element_type=f32), i)
+        grad_gate_act = (grad_hidden * up_act * sig * (1.0 + gate_act * (1.0 - sig))).astype(bf16)
+        grad_up_act = (grad_hidden * silu).astype(bf16)
+        dga_ref[i] = grad_gate_act
+        dua_ref[i] = grad_up_act
+        _store_split(gg_ref, lax.dot_general(n2, grad_gate_act, tn, preferred_element_type=f32), i)
+        _store_split(gu_ref, lax.dot_general(n2, grad_up_act, tn, preferred_element_type=f32), i)
 
 
 def _rows_body(hid_ref, dga_ref, dua_ref, dy_ref, gcol_ref, wg_ref, wu_ref, wd_ref, acc_ref, dgate_ref, dn2_ref):
@@ -127,14 +130,15 @@
     experts, _, hidden = wg.shape
     bf16 = jnp.bfloat16
     whole = lambda shape: pl.BlockSpec(shape, lambda e: (0,) * len(shape))
-    per_expert = lambda shape: pl.BlockSpec((1,) + shape, lambda e: (e,) + (0,) * len(shape))
+    step = 2 if experts % 2 == 0 else 1
+    per_expert = lambda shape: pl.BlockSpec((step,) + shape, lambda e: (e,) + (0,) * len(shape))
     split_rows = width // (groups * 2)
-    split = pl.BlockSpec((2, 1, groups, split_rows, hidden), lambda e: (0, e, 0, 0, 0))
+    split = pl.BlockSpec((2, step, groups, split_rows, hidden), lambda e: (0, e, 0, 0, 0))
     split_shape = jax.ShapeDtypeStruct((2, experts, groups, split_rows, hidden), bf16)
     act_shape = jax.ShapeDtypeStruct((experts, tokens, hidden), bf16)
     return pl.pallas_call(
         _grad_body,
-        grid=(experts,),
+        grid=(experts // step,),
         in_specs=[
             whole((tokens, width)),
             whole((tokens, width)),

time: 821 us -> 819 us (level)
  transfers between devices with their start and end apart: 5 -> 5, of which waited for: 3 -> 3; matrix products, arithmetic and copies ran while one was open for 25% -> 25% of each run, Pallas kernels for 40% -> 41%
where the time goes in v22:
time: 819 us; the launch traced here: 813 us
  Pallas kernels  427 us (52%)
  waiting for transfers between devices  141 us (17%)
  matrix products  124 us (15%)
  local copies, waits for them, and re-layouts  66.3 us (8%)
  other arithmetic  38.6 us (5%)
  between operations  15.2 us (2%)
    pallas_call x9, Pallas kernels, exchange(): pl.pallas_call(functools.partial(_exchange_body, axis, n, per_peer, downw...  197 us
    unnamed x6, waiting for transfers between devices  74.2 us
    pallas_call x1, Pallas kernels, expert_grad_kernel(): pl.pallas_call(_grad_body, grid=(experts // step,), in_specs=[whole((toke...  71.2 us
    reduce_scatter x3, waiting for transfers between devices, per_device(): lax.psum_scatter(g.reshape(g.shape[0], -1, g.shape[3]), ('dpx', 'ctx'), s...  57.7 us
    pallas_call x1, Pallas kernels, chain_sum_down(): pl.pallas_call(functools.partial(_chain_down_body, axis, n), out_shape=ja...  51.9 us
    pallas_call x1, Pallas kernels, expert_rows_kernel(): pl.pallas_call(_rows_body, grid=(experts,), in_specs=[per_expert((tokens,...  46.2 us
    pallas_call x4, Pallas kernels, core_reduce(): pl.pallas_call(_pair_add_body, grid_spec=grid_spec, out_shape=jax.ShapeDt...  38.6 us
    dot_general x1, matrix products, per_device(): jnp.einsum('kgtd,nkd->kgtn', grad_attn_grouped, value_piece, preferred_el...  28.2 us
  transfers between devices with their start and end apart: 5, of which 3 were waited for; matrix products, arithmetic and copies ran while one was open for 25% of the time, Pallas kernels for 41%

profile of v22, /device:TPU:0, one launch (start us, length us, event | category | flops | bytes accessed | tf_op | source)
XLA Modules:
  0.0 812.9 jit_solution(13888971666243713410)
XLA Ops:
  20.7 22.4 %shard_map.229 = (bf16[4,512,512]{2,1,0:T(8,128)(2,1)}, f32[512,768]{1,0:T(8,128)S(1)}, f32[512,12]{1,0:T(8,128)S(1)}) custom-call(bf16[512,768]{1,0:T(8,128)(2,1)S(1)} %copy.174.q_ref, bf16[512,512]{1,0:T(8,128)(2,1)S(1)} %pad_maximum_fusion.3.own_ref, s32[1536,1]{1,0:T(8,128)S(1)} %bitcast.161, s32[1536,1]{1,0:T(8,128)S(1)} %bitcast.162, ...), custom_call_target="tpu_custom_call" | custom-call | flops 3221225472 | bytes 6553600 | tf_op jit(solution)/shard_map/pallas_call | solution.py:662
  44.9 37.1 %shard_map.230 = bf16[2,512,768]{2,1,0:T(8,128)(2,1)} custom-call(bf16[512,768]{1,0:T(8,128)(2,1)} %convert_element_type.161.src_ref), custom_call_target="tpu_custom_call" | custom-call | bytes 1572864 | tf_op jit(solution)/shard_map/pallas_call | solution.py:249
  83.0 8.9 %all-gather.3.cloned.1.call-done = bf16[3072,768]{1,0:T(8,128)(2,1)} async-done(((bf16[1536,768]{1,0:T(8,128)(2,1)}), bf16[3072,768]{1,0:T(8,128)(2,1)}) %all-gather.3.cloned.1.call-update) | async-done | bytes 4718608 | tf_op jit(solution)/shard_map/all_gather | solution.py:724
  102.7 71.2 %shard_map.231 = (bf16[2,24,2,384,256]{4,3,2,1,0:T(8,128)(2,1)}, bf16[2,24,2,384,256]{4,3,2,1,0:T(8,128)(2,1)}, bf16[2,24,2,384,256]{4,3,2,1,0:T(8,128)(2,1)}, b...) custom-call(bf16[512,1536]{1,0:T(8,128)(2,1)} %copy-done.10, ...), custom_call_target="tpu_custom_call" | custom-call | flops 57982058496 | bytes 138412032 | tf_op jit(solution)/shard_map/pallas_call | solution.py:139
  173.9 15.0 %shard_map.244.other_ref = bf16[2,24,2,384,256]{4,3,2,1,0:T(8,128)(2,1)} custom-call(bf16[2,24,2,384,256]{4,3,2,1,0:T(8,128)(2,1)} %get-tuple-element.47.src_ref.own_ref), custom_call_target="tpu_custom_call" | custom-call | bytes 18874368 | tf_op jit(solution)/shard_map/pallas_call | solution.py:249
  188.9 11.4 %shard_map.245 = bf16[24,2,384,256]{3,2,1,0:T(8,128)(2,1)} custom-call(s32[1]{0:T(128)} %bitcast.8.me_ref, bf16[2,24,2,384,256]{4,3,2,1,0:T(8,128)(2,1)} %get-tuple-element.47.src_ref.own_ref, bf16[2,24,2,384,256]{4,3,2,1,0:T(8,128)(2,1)} %shard_map.244.other_ref), custom_call_target="tpu_custom_call" | custom-call | flops 4718592 | bytes 28311552 | tf_op jit(solution)/shard_map/pallas_call | solution.py:295
  200.3 15.1 %shard_map.242.other_ref = bf16[2,24,2,384,256]{4,3,2,1,0:T(8,128)(2,1)} custom-call(bf16[2,24,2,384,256]{4,3,2,1,0:T(8,128)(2,1)} %get-tuple-element.46.src_ref.own_ref), custom_call_target="tpu_custom_call" | custom-call | bytes 18874368 | tf_op jit(solution)/shard_map/pallas_call | solution.py:249
  215.4 11.3 %shard_map.243 = bf16[24,2,384,256]{3,2,1,0:T(8,128)(2,1)} custom-call(s32[1]{0:T(128)} %bitcast.8.me_ref, bf16[2,24,2,384,256]{4,3,2,1,0:T(8,128)(2,1)} %get-tuple-element.46.src_ref.own_ref, bf16[2,24,2,384,256]{4,3,2,1,0:T(8,128)(2,1)} %shard_map.242.other_ref), custom_call_target="tpu_custom_call" | custom-call | flops 4718592 | bytes 28311552 | tf_op jit(solution)/shard_map/pallas_call | solution.py:295
  241.0 20.3 %fusion.36 = f32[4,2048,512,3]{2,1,3,0:T(8,128)} fusion(bf16[2048,4,64,1]{0,2,1,3:T(8,128)(2,1)S(1)} %reshape.365, bf16[512,4,3,32]{0,3,2,1:T(8,128)(2,1)S(1)} %bitcast.172, bf16[512,4,3,32]{0,3,2,1:T(8,128)(2,1)S(1)} %bitcast.170), kind=kOutput, calls=%fused_computation.62 | convolution fusion | flops 1612185600 | bytes 52166656 | tf_op jit(solution)/shard_map/tkgd,nkd->kgtn/dot_general | solution.py:841
  261.3 15.0 %shard_map.232.other_ref = bf16[2,24,2,384,256]{4,3,2,1,0:T(8,128)(2,1)} custom-call(bf16[2,24,2,384,256]{4,3,2,1,0:T(8,128)(2,1)} %get-tuple-element.33.src_ref.own_ref), custom_call_target="tpu_custom_call" | custom-call | bytes 18874368 | tf_op jit(solution)/shard_map/pallas_call | solution.py:249
  276.3 11.4 %shard_map.233 = bf16[24,2,384,256]{3,2,1,0:T(8,128)(2,1)} custom-call(s32[1]{0:T(128)} %bitcast.8.me_ref, bf16[2,24,2,384,256]{4,3,2,1,0:T(8,128)(2,1)} %get-tuple-element.33.src_ref.own_ref, bf16[2,24,2,384,256]{4,3,2,1,0:T(8,128)(2,1)} %shard_map.232.other_ref), custom_call_target="tpu_custom_call" | custom-call | flops 4718592 | bytes 28311552 | tf_op jit(solution)/shard_map/pallas_call | solution.py:295
  288.3 46.2 %shard_map.234 = (f32[512,1536]{1,0:T(8,128)}, f32[24,512,1]{2,1,0:T(8,128)}, f32[512,1536]{1,0:T(8,128)}) custom-call(bf16[24,512,256]{2,1,0:T(8,128)(2,1)} %get-tuple-element.37.hid_ref, bf16[24,512,256]{2,1,0:T(8,128)(2,1)} %get-tuple-element.38.dga_ref, bf16[24,512,256]{2,1,0:T(8,128)(2,1)} %get-tuple-element.39.dua_ref, bf16[512,1536]{1,0:T(8,128)(2,1)} %dy_ref.3, ...), custom_call_target="tpu_custom_call" | custom-call | flops 28991029248 | bytes 83361792 | tf_op jit(solution)/shard_map/pallas_call | solution.py:170
  337.7 36.9 %shard_map.236 = bf16[2,512,1536]{2,1,0:T(8,128)(2,1)} custom-call(bf16[512,1536]{1,0:T(8,128)(2,1)} %convert_element_type.169.src_ref), custom_call_target="tpu_custom_call" | custom-call | bytes 3145728 | tf_op jit(solution)/shard_map/pallas_call | solution.py:249
  391.8 34.6 %shard_map.235 = bf16[2,512,1536]{2,1,0:T(8,128)(2,1)} custom-call(bf16[512,1536]{1,0:T(8,128)(2,1)} %convert_element_type.163.src_ref), custom_call_target="tpu_custom_call" | custom-call | bytes 3145728 | tf_op jit(solution)/shard_map/pallas_call | solution.py:249
  439.5 28.2 %multiply_convert_fusion = bf16[4,3,512,2048]{2,3,1,0:T(8,128)(2,1)} fusion(f32[4,2048,512,3]{2,1,3,0:T(8,128)} %fusion.36, f32[4,3,512]{2,1,0:T(4,128)S(1)} %multiply_reduce_fusion.3, f32[4,3,512]{2,1,0:T(4,128)S(1)} %bitcast.191, pred[512,2048]{0,1:T(8,128)(4,1)} %fusion.6, bf16[4,3,512,64]{2,3,1,0:T(8,128)(2,1)S(1)} %bitcast.178, ...), kind=kOutput, calls=%fused_computation.3 | convolution fusion | flops 1686110208 | bytes 78430208 | tf_op jit(solution)/shard_map/kgtd,nkd->kgtn/dot_general | solution.py:845
  467.7 12.6 %fusion.30 = bf16[2048,4,64]{0,2,1:T(8,128)(2,1)S(1)} fusion(bf16[4,3,512,2048]{2,3,1,0:T(8,128)(2,1)} %multiply_convert_fusion, bf16[512,4,3,32]{0,3,2,1:T(8,128)(2,1)S(1)} %bitcast.173, bf16[512,4,3,32]{0,3,2,1:T(8,128)(2,1)S(1)} %bitcast.171), kind=kOutput, calls=%fused_computation.48 | convolution fusion | flops 1613234176 | bytes 27000832 | tf_op jit(solution)/shard_map/kgtn,tkgd->nkd/dot_general | solution.py:852
  482.7 19.4 %fusion.31 = bf16[2048,4,64]{0,2,1:T(8,128)(2,1)S(1)} fusion(bf16[4,3,512,64]{2,3,1,0:T(8,128)(2,1)S(1)} %bitcast.179, f32[4,2048,512,3]{2,1,3,0:T(8,128)} %fusion.36, f32[4,3,512]{2,1,0:T(4,128)S(1)} %bitcast.192, pred[512,2048]{0,1:T(8,128)(4,1)} %fusion.6), kind=kOutput, calls=%fused_computation.49 | convolution fusion | flops 1661468672 | bytes 53239808 | tf_op jit(solution)/shard_map/kgtn,kgtd->nkd/dot_general | solution.py:855
  504.0 51.9 %shard_map.238 = f32[512,512]{1,0:T(8,128)S(1)} custom-call(bf16[4,512,512]{2,1,0:T(8,128)(2,1)S(1)} %pad_maximum_fusion.x_ref), custom_call_target="tpu_custom_call" | custom-call | flops 786432 | bytes 6291456 | tf_op jit(solution)/shard_map/pallas_call | solution.py:458
  556.4 11.2 %convolution_multiply_fusion = f32[4,3,512,64]{2,3,1,0:T(8,128)S(1)} fusion(bf16[4,3,512,2048]{2,3,1,0:T(8,128)(2,1)} %multiply_convert_fusion, bf16[2048,4,64,1]{0,2,1,3:T(8,128)(2,1)S(1)} %copy-done.21), kind=kOutput, calls=%fused_computation.56 | convolution fusion | flops 1611005952 | bytes 27787264 | tf_op jit(solution)/shard_map/kgtn,nkd->kgtd/dot_general | solution.py:849
  573.9 31.4 %shard_map.239 = bf16[2,512,1536]{2,1,0:T(8,128)(2,1)} custom-call(bf16[512,1536]{1,0:T(8,128)(2,1)} %fusion.20.src_ref), custom_call_target="tpu_custom_call" | custom-call | bytes 3145728 | tf_op jit(solution)/shard_map/pallas_call | solution.py:249
  641.5 10.4 %concatenate.65 = bf16[2,2,384,2176]{3,2,0,1:T(8,128)(2,1)} concatenate(bf16[2,2,384,768]{3,2,0,1:T(8,128)(2,1)} %convolution_convert_fusion.3, bf16[2,2,384,768]{3,2,0,1:T(8,128)(2,1)S(1)} %copy.202, bf16[2,2,384,256]{3,2,0,1:T(8,128)(2,1)} %convolution_convert_fusion.4, bf16[2,2,384,256]{3,2,0,1:T(8,128)(2,1)S(1)} %copy.203, bf16[2,2,384,24]{3,2,0,1:T(8,128)(2,1)} %copy.204, ...), dimensions={3} | concatenate | bytes 13369344 | tf_op jit(solution)/shard_map/concatenate | solution.py:909
  652.0 6.3 shard_map.240.other_ref
  662.8 57.7 %reduce-scatter.7.cloned.1.call-done = bf16[24,96,256]{2,1,0:T(8,128)(2,1)} async-done(((bf16[24,768,256]{2,1,0:T(8,128)(2,1)}), bf16[24,96,256]{2,1,0:T(8,128)(2,1)}) %reduce-scatter.7.cloned.1.call-update) | async-done | bytes 1179664 | tf_op jit(solution)/shard_map/reduce_scatter | solution.py:812
  726.8 73.5 %reduce-scatter.13.cloned.1.call-done = bf16[96,2176]{1,0:T(8,128)(2,1)} async-done(((bf16[768,2176]{1,0:T(8,128)(2,1)}), bf16[96,2176]{1,0:T(8,128)(2,1)}) %reduce-scatter.13.cloned.1.call-update) | async-done | bytes 417808
  (275 shorter events, 138.5 us)
Async XLA Ops:
  7.2 84.6 %all-gather.3.cloned.1.call-start = ((), (), s32[]{:S(2)}) async-start(), calls=%async_computation.7 | async-start | bytes 7077888 | tf_op jit(solution)/shard_map/all_gather | solution.py:724
  7.9 654.9 %reduce-scatter.11.cloned.1.call-start = ((), (), s32[]{:S(2)}) async-start(), calls=%async_computation.6 | async-start | bytes 10616832 | tf_op jit(solution)/shard_map/reduce_scatter | solution.py:812
  9.0 9.0 %copy-start.73 = (f32[512]{0:T(512)}, f32[512]{0:T(512)S(1)}, u32[]{:S(2)}) copy-start(f32[512]{0:T(512)S(1)} %add_rsqrt_fusion.1) | copy-start | bytes 6148
  43.8 39.2 %copy-start = (f32[512,768]{1,0:T(8,128)}, f32[512,768]{1,0:T(8,128)S(1)}, u32[]{:S(2)}) copy-start(f32[512,768]{1,0:T(8,128)S(1)} %get-tuple-element.32) | copy-start | bytes 4718596
  200.3 462.5 %reduce-scatter.9.cloned.1.call-start = ((), (), s32[]{:S(2)}) async-start(), calls=%async_computation.5 | async-start | bytes 10616832 | tf_op jit(solution)/shard_map/reduce_scatter | solution.py:812
  226.7 493.8 %reduce-scatter.7.cloned.1.call-start = ((), (), s32[]{:S(2)}) async-start(), calls=%async_computation.4 | async-start | bytes 10616832 | tf_op jit(solution)/shard_map/reduce_scatter | solution.py:812
  234.6 26.6 %copy-start.20 = (bf16[2048,4,64,1]{0,2,1,3:T(8,128)(2,1)}, bf16[2048,4,64,1]{0,2,1,3:T(8,128)(2,1)S(1)}, u32[]{:S(2)}) copy-start(bf16[2048,4,64,1]{0,2,1,3:T(8,128)(2,1)S(1)} %reshape.365) | copy-start | bytes 3145732
  287.8 512.5 %reduce-scatter.13.cloned.1.call-start = ((), (), s32[]{:S(2)}) async-start(), calls=%async_computation.8 | async-start | bytes 3760128
  374.6 11.7 %copy-start.31 = (f32[512,8]{1,0:T(8,128)S(1)}, f32[512,8]{1,0:T(8,128)}, u32[]{:S(2)}) copy-start(f32[512,8]{1,0:T(8,128)} %copy-done.30) | copy-start | bytes 49156
  374.6 11.7 %copy-start.63 = (f32[512]{0:T(512)S(1)}, f32[512]{0:T(512)}, u32[]{:S(2)}) copy-start(f32[512]{0:T(512)} %copy-done.62) | copy-start | bytes 6148
  374.6 15.8 %copy-start.16 = (f32[512,1536]{1,0:T(8,128)S(1)}, f32[512,1536]{1,0:T(8,128)}, u32[]{:S(2)}) copy-start(f32[512,1536]{1,0:T(8,128)} %get-tuple-element.40) | copy-start | bytes 9437188
  391.8 34.7 %copy-start.8 = (f32[512,1536]{1,0:T(8,128)S(1)}, f32[512,1536]{1,0:T(8,128)}, u32[]{:S(2)}) copy-start(f32[512,1536]{1,0:T(8,128)} %copy-done.7) | copy-start | bytes 9437188
  391.8 34.7 %copy-start.55 = (bf16[1536,24]{0,1:T(8,128)(2,1)S(1)}, bf16[1536,24]{0,1:T(8,128)(2,1)}, u32[]{:S(2)}) copy-start(bf16[1536,24]{0,1:T(8,128)(2,1)} %param.21) | copy-start | bytes 221188
  391.8 34.7 %copy-start.61 = (f32[1536]{0:T(1024)S(1)}, f32[1536]{0:T(1024)}, u32[]{:S(2)}) copy-start(f32[1536]{0:T(1024)} %param.20) | copy-start | bytes 18436
  391.8 34.7 %copy-start.68 = (f32[512]{0:T(512)S(1)}, f32[512]{0:T(512)}, u32[]{:S(2)}) copy-start(f32[512]{0:T(512)} %copy-done.67) | copy-start | bytes 6148
  439.5 28.2 %copy-start.25 = (bf16[512,12,32]{0,2,1:T(8,128)(2,1)S(1)}, bf16[512,12,32]{0,2,1:T(8,128)(2,1)}, u32[]{:S(2)}) copy-start(bf16[512,12,32]{0,2,1:T(8,128)(2,1)} %copy-done.23) | copy-start | bytes 1179652
  439.5 28.2 %copy-start.28 = (bf16[512,12,32]{0,2,1:T(8,128)(2,1)S(1)}, bf16[512,12,32]{0,2,1:T(8,128)(2,1)}, u32[]{:S(2)}) copy-start(bf16[512,12,32]{0,2,1:T(8,128)(2,1)} %copy-done.26) | copy-start | bytes 1179652
  504.0 52.2 %copy-start.40 = (f32[512,32]{0,1:T(8,128)S(1)}, f32[512,32]{0,1:T(8,128)}, u32[]{:S(2)}) copy-start(f32[512,32]{0,1:T(8,128)} %copy-done.39) | copy-start | bytes 196612
  504.0 52.2 %copy-start.53 = (f32[512,32]{0,1:T(8,128)S(1)}, f32[512,32]{0,1:T(8,128)}, u32[]{:S(2)}) copy-start(f32[512,32]{0,1:T(8,128)} %get-tuple-element.138) | copy-start | bytes 196612
  504.0 52.3 %copy-start.21 = (bf16[2048,4,64,1]{0,2,1,3:T(8,128)(2,1)S(1)}, bf16[2048,4,64,1]{0,2,1,3:T(8,128)(2,1)}, u32[]{:S(2)}) copy-start(bf16[2048,4,64,1]{0,2,1,3:T(8,128)(2,1)} %copy-done.20) | copy-start | bytes 3145732
  573.9 31.4 %copy-start.9 = (bf16[512,1536]{1,0:T(8,128)(2,1)S(1)}, bf16[512,1536]{1,0:T(8,128)(2,1)}, u32[]{:S(2)}) copy-start(bf16[512,1536]{1,0:T(8,128)(2,1)} %fusion.20.src_ref) | copy-start | bytes 4718596
  573.9 31.4 %copy-start.66 = (f32[1536]{0:T(1024)S(1)}, f32[1536]{0:T(1024)}, u32[]{:S(2)}) copy-start(f32[1536]{0:T(1024)} %param.15) | copy-start | bytes 18436
  573.9 31.4 %copy-start.74 = (f32[512]{0:T(512)S(1)}, f32[512]{0:T(512)}, u32[]{:S(2)}) copy-start(f32[512]{0:T(512)} %copy-done.73) | copy-start | bytes 6148
  614.4 10.8 %copy-start.14 = (bf16[512,1536]{1,0:T(8,128)(2,1)S(1)}, bf16[512,1536]{1,0:T(8,128)(2,1)}, u32[]{:S(2)}) copy-start(bf16[512,1536]{1,0:T(8,128)(2,1)} %param.14) | copy-start | bytes 4718596
  (57 other events, 174.0 us)
Sparse Core Ops, SparseCore 0:
  9.6 82.1 all-gather.2
  200.4 166.1 reduce-scatter.10
  370.2 163.9 reduce-scatter.8
  537.7 182.8 reduce-scatter.6
  724.0 76.2 reduce-scatter.12
